TPU v7x, 128 devices: a whole 4x4x4 slice. The times are simulated.
128 devices in a mesh: tile: 32 (over x, z, core), member: 4 (over y).
Axes of the slice: x: 4, y: 4, z: 4, core: 2. Of those that a mesh axis runs over, the one named last changes fastest.
Arguments:
- log_perm: float32 [128, 4, 256, 256], P('member', None, 'tile'), may hold values from -3.4 to 3.4
- start_pressure: float32 [4, 256, 256], P(None, 'tile'), may hold values from -5 to 5
- start_sat: float32 [4, 256, 256], P(None, 'tile'), may hold values from 0.1 to 0.9
- source: float32 [4, 256, 256], P(None, 'tile'), may hold values from -5 to 5
- storage: float32 [4, 256, 256], P(None, 'tile'), may hold values from 0.05 to 0.5
- well_press: float32 [1024], replicated, may hold values from -4 to 4
- perf_cell: int32 [8192], P('tile'), may hold values from 0 to 8191
- perf_well: int32 [8192], P('tile'), may hold values from 0 to 1023
- perf_count: int32 [32], P('tile'), may hold values from 64 to 256, as said below
- observed: float32 [1024], replicated, may hold values from -8 to 8
- obs_var: float32 [1024], replicated, may hold values from 0.5 to 5
- obs_noise: float32 [128, 1024], P('member'), may hold values from -5 to 5
Outputs:
- new_log_perm: float32 [128, 4, 256, 256], P('member', None, 'tile')
- pressure: float32 [128, 4, 256, 256], P('member', None, 'tile')
- saturation: float32 [128, 4, 256, 256], P('member', None, 'tile')
- well_rates: float32 [128, 1024], P('member', 'tile')
Inputs may be any that keep to these rules, and one draw needn't show every extreme that they name: `perf_count`: one strip has all 256 slots live.
All inputs are finite; a program needn't handle non-finite values.
Results may differ from a plain program's by a relative error of at most 0.017.
Values may be sent and summed in bfloat16 or wider, within the bound.
A program may use at most 64 MiB of HBM per device.

v0:
```python
import jax
import jax.numpy as jnp
from jax import lax
from jax.sharding import PartitionSpec as P

SWEEPS = 2


VERTICAL = 0.5
VISCOSITY_RATIO = 2.0
STEP_COEF = 0.1
INFLATION = 4.0


def extended_2(block, sides, width):
    for axis, dim in sides:
        count = lax.axis_size(axis)
        forward = [(i, i + 1) for i in range(count - 1)]
        backward = [(target, source) for source, target in forward]
        low = lax.ppermute(
            lax.slice_in_dim(block, block.shape[dim] - width, None, axis=dim), axis, forward
        )
        high = lax.ppermute(lax.slice_in_dim(block, 0, width, axis=dim), axis, backward)
        block = jnp.concatenate([low, block, high], axis=dim)
    return block


def harmonic(lower_val, upper_val):
    return 2.0 * lower_val * upper_val / (lower_val + upper_val)


def pad_face(values_in, along_dim, before):
    widths = [(0, 0)] * values_in.ndim
    widths[along_dim] = (1, 0) if before else (0, 1)
    return jnp.pad(values_in, widths)


def slide_by(values_in, along_dim, before):
    extent = values_in.shape[along_dim]
    if before:
        remain = lax.slice_in_dim(values_in, 0, extent - 1, axis=along_dim)
    else:
        remain = lax.slice_in_dim(values_in, 1, extent, axis=along_dim)
    return pad_face(remain, along_dim, before)


def face_terms(permeab, inside):
    face_x = (
        harmonic(permeab[:, :, :-1, :], permeab[:, :, 1:, :]) * (inside[:-1] * inside[1:])[:, None]
    )
    face_y = harmonic(permeab[:, :, :, :-1], permeab[:, :, :, 1:])
    face_z = VERTICAL * harmonic(permeab[:, :-1], permeab[:, 1:])
    return (face_x, face_y, face_z)


def neighbours(face_sets, values_in):
    flow_sum = 0.0
    weight_sum = 0.0
    for faces_dim, along_dim in zip(face_sets, (2, 3, 1)):
        lower = pad_face(faces_dim, along_dim, True)
        upper = pad_face(faces_dim, along_dim, False)
        flow_sum = (
            flow_sum
            + lower * slide_by(values_in, along_dim, True)
            + upper * slide_by(values_in, along_dim, False)
        )
        weight_sum = weight_sum + lower + upper
    return (flow_sum, weight_sum)


def jacobi(pressure, baseline, storage_term, face_sets):
    flow_sum, weight_sum = neighbours(face_sets, pressure)
    return (baseline + flow_sum) / (storage_term + weight_sum)


def water_frac(values_in):
    squared = values_in * values_in
    return squared / (squared + VISCOSITY_RATIO * (1.0 - values_in) * (1.0 - values_in))


def transport(pressure, saturation, face_sets):
    fraction = water_frac(saturation)
    change = 0.0
    for faces_dim, along_dim in zip(face_sets, (2, 3, 1)):
        extent = pressure.shape[along_dim]
        lower_press = lax.slice_in_dim(pressure, 0, extent - 1, axis=along_dim)
        upper_press = lax.slice_in_dim(pressure, 1, extent, axis=along_dim)
        lower_frac = lax.slice_in_dim(fraction, 0, extent - 1, axis=along_dim)
        upper_frac = lax.slice_in_dim(fraction, 1, extent, axis=along_dim)
        velocity = faces_dim * (lower_press - upper_press)
        carried = velocity * jnp.where(velocity > 0, lower_frac, upper_frac)
        change = change + pad_face(carried, along_dim, True) - pad_face(carried, along_dim, False)
    return saturation + STEP_COEF * change


def solve_spd(gram_matrix, cross_matrix):
    factor = jnp.linalg.cholesky(gram_matrix + jnp.eye(gram_matrix.shape[0], dtype=jnp.float32))
    halfway = lax.linalg.triangular_solve(factor, cross_matrix, left_side=True, lower=True)
    return lax.linalg.triangular_solve(
        factor, halfway, left_side=True, lower=True, transpose_a=True
    )


def trim_rim(values_in, rim_cut):
    return values_in[:, :, rim_cut : values_in.shape[2] - rim_cut, :]


def per_device(
    log_perm,
    start_pressure,
    start_sat,
    source,
    storage,
    well_press,
    perf_cell,
    perf_well,
    perf_count,
    observed,
    obs_var,
    obs_noise,
):
    local_count, layers, strip_width, strip_depth = log_perm.shape
    tile_count = lax.axis_size("tile")
    members = local_count * lax.axis_size("member")
    well_count = well_press.shape[0]
    well_share = well_count // tile_count
    tile_rank = lax.axis_index("tile")
    member_rank = lax.axis_index("member")
    permeab = jnp.exp(extended_2(log_perm, (("tile", 2),), 1))
    shared = extended_2(jnp.stack([start_pressure, start_sat]), (("tile", 2),), 1)
    column = tile_rank * strip_width - 1 + jnp.arange(strip_width + 2 * 1, dtype=jnp.int32)
    face_sets = face_terms(
        permeab, ((column >= 0) & (column < strip_width * tile_count)).astype(jnp.float32)
    )
    baseline = jnp.pad(source + storage * start_pressure, ((0, 0), (1, 1), (0, 0)))[None]
    storage_term = jnp.pad(storage, ((0, 0), (1, 1), (0, 0)), constant_values=1.0)[None]
    extended = jnp.broadcast_to(shared[0:1], (local_count,) + shared.shape[1:])
    for sweep_idx in range(SWEEPS):
        pressure = trim_rim(jacobi(extended, baseline, storage_term, face_sets), 1)
        extended = extended_2(pressure, (("tile", 2),), 1)
    saturation = trim_rim(transport(extended, shared[1:2], face_sets), 1)
    permeab = trim_rim(permeab, 1)
    cell_count = layers * strip_width * strip_depth
    mobility = (permeab * water_frac(saturation)).reshape(local_count, cell_count)
    cell_press = pressure.reshape(local_count, cell_count)
    perf_mob = jnp.take(mobility, perf_cell, axis=1)
    perf_press = jnp.take(cell_press, perf_cell, axis=1)
    selector = (perf_well[:, None] == jnp.arange(well_count, dtype=jnp.int32)[None, :]).astype(
        jnp.float32
    )
    perf_bhp = jnp.dot(selector, well_press, precision=lax.Precision.HIGHEST)
    live_mask = (jnp.arange(perf_cell.shape[0], dtype=jnp.int32) < perf_count[0]).astype(
        jnp.float32
    )
    perf_terms = perf_mob * (perf_press - perf_bhp[None]) * live_mask[None]
    partial_rates = jnp.dot(
        perf_terms, selector, precision=lax.Precision.HIGHEST, preferred_element_type=jnp.float32
    )
    member_root = (members - 1) ** 0.5
    spread = jnp.sqrt(INFLATION * obs_var)
    well_rates = lax.psum_scatter(partial_rates, "tile", scatter_dimension=1, tiled=True)
    well_first = tile_rank * well_share
    spread_part = lax.dynamic_slice_in_dim(spread, well_first, well_share, 0)
    observed_part = lax.dynamic_slice_in_dim(observed, well_first, well_share, 0)
    noise_part = lax.dynamic_slice_in_dim(obs_noise, well_first, well_share, 1)
    mean_rate = lax.psum(jnp.sum(well_rates, 0), "member") / members
    scaled = (well_rates - mean_rate) / (spread_part * member_root)
    innovation = (observed_part - well_rates) / spread_part + noise_part
    scaled_all, innov_all = (
        lax.all_gather(scaled, "member", axis=0, tiled=True),
        lax.all_gather(innovation, "member", axis=0, tiled=True),
    )
    gram_part = jnp.dot(
        scaled_all,
        scaled_all.T,
        precision=lax.Precision.HIGHEST,
        preferred_element_type=jnp.float32,
    )
    cross_part = jnp.dot(
        scaled_all, innov_all.T, precision=lax.Precision.HIGHEST, preferred_element_type=jnp.float32
    )
    gram_matrix, cross_matrix = lax.psum((gram_part, cross_part), "tile")
    weights_low = solve_spd(gram_matrix, cross_matrix).astype(jnp.bfloat16)
    anomaly = (log_perm / member_root).astype(jnp.bfloat16).reshape(local_count, cell_count)
    first_member = member_rank * local_count
    contract = (((0,), (0,)), ((), ()))
    own_rows = lax.dynamic_slice_in_dim(weights_low, first_member, local_count, 0)
    update_sum = lax.psum_scatter(
        lax.dot_general(own_rows, anomaly, contract, preferred_element_type=jnp.float32).astype(
            jnp.bfloat16
        ),
        "member",
        scatter_dimension=0,
        tiled=True,
    ).astype(jnp.float32)
    new_log_perm = log_perm + update_sum.reshape(log_perm.shape)
    return (new_log_perm, pressure, saturation, well_rates)


def solution(mesh):
    return jax.shard_map(
        per_device,
        mesh=mesh,
        in_specs=(
            P("member", None, "tile", None),
            P(None, "tile", None),
            P(None, "tile", None),
            P(None, "tile", None),
            P(None, "tile", None),
            P(),
            P("tile"),
            P("tile"),
            P("tile"),
            P(),
            P(),
            P("member", None),
        ),
        out_specs=(
            P("member", None, "tile", None),
            P("member", None, "tile", None),
            P("member", None, "tile", None),
            P("member", "tile"),
        ),
        check_vma=False,
    )
```

profile of v0, /device:TPU:1, one launch (start us, length us, event | category | flops | bytes accessed | tf_op | source)
XLA Modules:
  0.0 349.1 jit_solution(9366257711582904115)
XLA Ops:
  9.2 4.9 %collective-permute-start = (f32[32,4,1,256]{3,0,2,1:T(8,128)S(1)}, f32[32,4,1,256]{3,0,2,1:T(8,128)S(1)}, u32[]{:S(2)}, u32[]{:S(2)}) collective-permute-start(f32[32,4,1,256]{3,0,2,1:T(8,128)S(1)} %get-tuple-element.23), channel_id=1, source_target_pairs={{0,4},{4,8},{8,12},{12,16},{16,20},{20,24},{24,28},{28,32},{32,36}... | collective-permute-start | bytes 393224 | tf_op jit(solution)/shard_map/ppermute | solution.py:20
  14.1 1.9 collective-permute-start.1
  16.1 3.6 %collective-permute-start.2 = (f32[2,4,1,256]{3,2,1,0:T(1,128)S(1)}, f32[2,4,1,256]{3,2,1,0:T(1,128)S(1)}, u32[]{:S(2)}, u32[]{:S(2)}) collective-permute-start(f32[2,4,1,256]{3,2,1,0:T(1,128)S(1)} %get-tuple-element.40), channel_id=1, source_target_pairs={{0,4},{4,8},{8,12},{12,16},{16,20},{20,24},{24,28},{28,32},{32,36}... | collective-permute-start | bytes 24584 | tf_op jit(solution)/shard_map/ppermute | solution.py:20
  19.7 1.9 collective-permute-start.3
  27.2 2.1 fusion.3
  29.4 2.7 collective-permute-start.4
  32.0 1.9 collective-permute-start.5
  34.2 4.2 %collective-permute-done.5 = f32[32,4,1,256]{3,0,2,1:T(8,128)S(1)} collective-permute-done((f32[32,4,1,256]{3,0,2,1:T(8,128)S(1)}, f32[32,4,1,256]{3,0,2,1:T(8,128)S(1)}, u32[]{:S(2)}, u32[]{:S(2)}) %collective-permute-start.5) | collective-permute-done | bytes 131104 | tf_op jit(solution)/shard_map/ppermute | solution.py:23
  39.2 2.1 fusion.7
  43.3 2.4 collective-permute-start.7
  45.8 2.7 copy.23
  48.5 2.9 gather_fusion.1
  55.1 2.7 copy.22
  57.8 3.0 gather_fusion
  60.8 2.0 convolution_bitcast_fusion
  63.7 81.1 %reduce-scatter.7.cloned.1.call-done = f32[32,32]{1,0:T(8,128)} async-done(((f32[1024,32]{1,0:T(8,128)}), f32[32,32]{1,0:T(8,128)}) %reduce-scatter.7.cloned.1.call-update) | async-done | bytes 4112
  146.5 8.4 %psum.21 = f32[32]{0:T(128)S(1)} all-reduce(f32[32]{0:T(128)S(1)} %bitcast_reduce_fusion), channel_id=1, replica_groups=mesh['tile'=32,'member'=4] {'member'}, use_global_device_ids=true, to_apply=%region_2.4 | all-reduce | flops 32 | bytes 256 | tf_op jit(solution)/shard_map/psum | solution.py:166
  155.7 9.0 %all_gather.6 = f32[128,32]{1,0:T(8,128)S(1)} all-gather(f32[32,32]{1,0:T(8,128)S(1)} %get-tuple-element.43), channel_id=1, replica_groups=mesh['tile'=32,'member'=4] {'member'}, dimensions={0}, use_global_device_ids=true | all-gather | bytes 20480 | tf_op jit(solution)/shard_map/all_gather | solution.py:170
  164.7 9.1 %all_gather.7 = f32[128,32]{1,0:T(8,128)S(1)} all-gather(f32[32,32]{1,0:T(8,128)S(1)} %get-tuple-element.42), channel_id=1, replica_groups=mesh['tile'=32,'member'=4] {'member'}, dimensions={0}, use_global_device_ids=true | all-gather | bytes 20480 | tf_op jit(solution)/shard_map/all_gather | solution.py:171
  176.2 106.4 %all-reduce.29.cloned.1.call-done = (f32[128,128]{1,0:T(8,128)}, f32[128,128]{1,0:T(8,128)}) async-done(((f32[128,128]{1,0:T(8,128)}, f32[128,128]{1,0:T(8,128)}), (f32[128,128]{1,0:T(8,128)}, f32[128,128]{1,0:T(8,128)})) %all-reduce.29.cloned.1.call-update) | async-done | bytes 131088 | tf_op jit(solution)/shard_map/psum | solution.py:182
  284.4 11.7 %cholesky.17 = f32[128,128]{1,0:T(8,128)S(1)} custom-call(f32[128,128]{1,0:T(8,128)S(1)} %fusion.39), custom_call_target="Cholesky" | custom-call | tf_op jit(solution)/shard_map/jit(cholesky)/cholesky | solution.py:97
  297.5 9.8 %custom-call.8 = f32[1,128,128]{1,2,0:T(8,128)S(1)} custom-call(f32[1,128,128]{2,1,0:T(8,128)S(1)} %fusion.34), custom_call_target="InvertDiagBlocksLowerTriangular" | custom-call | tf_op jit(solution)/shard_map/triangular_solve | solution.py:99
  308.6 2.1 convolution_convert_fusion
  313.9 26.3 %reduce-scatter.5.cloned.1.call-done = bf16[32,8192]{1,0:T(8,128)(2,1)} async-done(((bf16[128,8192]{1,0:T(8,128)(2,1)}), bf16[32,8192]{1,0:T(8,128)(2,1)}) %reduce-scatter.5.cloned.1.call-update) | async-done | bytes 524304 | tf_op jit(solution)/shard_map/reduce_scatter | solution.py:188
  (108 shorter events, 29.0 us)
Async XLA Ops:
  7.2 15.3 %copy-start = (f32[1024]{0:T(1024)S(1)}, f32[1024]{0:T(1024)}, u32[]{:S(2)}) copy-start(f32[1024]{0:T(1024)} %param.19) | copy-start | bytes 12292
  7.2 8.9 %copy-start.3 = (f32[4,8,256]{2,1,0:T(8,128)S(1)}, f32[4,8,256]{2,1,0:T(8,128)}, u32[]{:S(2)}) copy-start(f32[4,8,256]{2,1,0:T(8,128)} %param.15) | copy-start | bytes 98308
  7.2 8.9 %copy-start.6 = (f32[4,8,256]{2,1,0:T(8,128)S(1)}, f32[4,8,256]{2,1,0:T(8,128)}, u32[]{:S(2)}) copy-start(f32[4,8,256]{2,1,0:T(8,128)} %param.16) | copy-start | bytes 98308
  7.2 14.6 %copy-start.9 = (s32[256]{0:T(256)S(1)}, s32[256]{0:T(256)}, u32[]{:S(2)}) copy-start(s32[256]{0:T(256)} %param.20) | copy-start | bytes 3076
  7.2 15.2 %copy-start.8 = (f32[4,8,256]{2,1,0:T(8,128)S(1)}, f32[4,8,256]{2,1,0:T(8,128)}, u32[]{:S(2)}) copy-start(f32[4,8,256]{2,1,0:T(8,128)} %param.17) | copy-start | bytes 98308
  7.2 15.2 %copy-start.5 = (f32[4,8,256]{2,1,0:T(8,128)S(1)}, f32[4,8,256]{2,1,0:T(8,128)}, u32[]{:S(2)}) copy-start(f32[4,8,256]{2,1,0:T(8,128)} %param.18) | copy-start | bytes 98308
  7.2 15.2 %copy-start.11 = (s32[256]{0:T(256)S(1)}, s32[256]{0:T(256)}, u32[]{:S(2)}) copy-start(s32[256]{0:T(256)} %param.21) | copy-start | bytes 3076
  7.2 137.6 %reduce-scatter.7.cloned.1.call-start = ((), (), s32[]{:S(2)}) async-start(), calls=%async_computation.3 | async-start | bytes 540672
  9.2 16.3 %collective-permute-start = (f32[32,4,1,256]{3,0,2,1:T(8,128)S(1)}, f32[32,4,1,256]{3,0,2,1:T(8,128)S(1)}, u32[]{:S(2)}, u32[]{:S(2)}) collective-permute-start(f32[32,4,1,256]{3,0,2,1:T(8,128)S(1)} %get-tuple-element.23), channel_id=1, source_target_pairs={{0,4},{4,8},{8,12},{12,16},{16,20},{20,24},{24,28},{28,32},{32,36}... | collective-permute-start | bytes 393224 | tf_op jit(solution)/shard_map/ppermute | solution.py:20
  14.1 11.4 %collective-permute-start.1 = (f32[32,4,1,256]{3,0,2,1:T(8,128)S(1)}, f32[32,4,1,256]{3,0,2,1:T(8,128)S(1)}, u32[]{:S(2)}, u32[]{:S(2)}) collective-permute-start(f32[32,4,1,256]{3,0,2,1:T(8,128)S(1)} %get-tuple-element.24), channel_id=1, source_target_pairs={{4,0},{8,4},{12,8},{16,12},{20,16},{24,20},{28,24},{32,28},{36,32}... | collective-permute-start | bytes 393224 | tf_op jit(solution)/shard_map/ppermute | solution.py:23
  16.1 7.6 %collective-permute-start.2 = (f32[2,4,1,256]{3,2,1,0:T(1,128)S(1)}, f32[2,4,1,256]{3,2,1,0:T(1,128)S(1)}, u32[]{:S(2)}, u32[]{:S(2)}) collective-permute-start(f32[2,4,1,256]{3,2,1,0:T(1,128)S(1)} %get-tuple-element.40), channel_id=1, source_target_pairs={{0,4},{4,8},{8,12},{12,16},{16,20},{20,24},{24,28},{28,32},{32,36}... | collective-permute-start | bytes 24584 | tf_op jit(solution)/shard_map/ppermute | solution.py:20
  19.7 5.0 %collective-permute-start.3 = (f32[2,4,1,256]{3,2,1,0:T(1,128)S(1)}, f32[2,4,1,256]{3,2,1,0:T(1,128)S(1)}, u32[]{:S(2)}, u32[]{:S(2)}) collective-permute-start(f32[2,4,1,256]{3,2,1,0:T(1,128)S(1)} %get-tuple-element.41), channel_id=1, source_target_pairs={{4,0},{8,4},{12,8},{16,12},{20,16},{24,20},{28,24},{32,28},{36,32}... | collective-permute-start | bytes 24584 | tf_op jit(solution)/shard_map/ppermute | solution.py:23
  29.4 4.8 %collective-permute-start.4 = (f32[32,4,1,256]{3,0,2,1:T(8,128)S(1)}, f32[32,4,1,256]{3,0,2,1:T(8,128)S(1)}, u32[]{:S(2)}, u32[]{:S(2)}) collective-permute-start(f32[32,4,1,256]{3,0,2,1:T(8,128)S(1)} %get-tuple-element.21), channel_id=1, source_target_pairs={{0,4},{4,8},{8,12},{12,16},{16,20},{20,24},{24,28},{28,32},{32,36}... | collective-permute-start | bytes 393224 | tf_op jit(solution)/shard_map/ppermute | solution.py:20
  32.0 6.3 %collective-permute-start.5 = (f32[32,4,1,256]{3,0,2,1:T(8,128)S(1)}, f32[32,4,1,256]{3,0,2,1:T(8,128)S(1)}, u32[]{:S(2)}, u32[]{:S(2)}) collective-permute-start(f32[32,4,1,256]{3,0,2,1:T(8,128)S(1)} %get-tuple-element.22), channel_id=1, source_target_pairs={{4,0},{8,4},{12,8},{16,12},{20,16},{24,20},{28,24},{32,28},{36,32}... | collective-permute-start | bytes 393224 | tf_op jit(solution)/shard_map/ppermute | solution.py:23
  41.4 10.0 %collective-permute-start.6 = (f32[32,4,1,256]{3,0,2,1:T(8,128)S(1)}, f32[32,4,1,256]{3,0,2,1:T(8,128)S(1)}, u32[]{:S(2)}, u32[]{:S(2)}) collective-permute-start(f32[32,4,1,256]{3,0,2,1:T(8,128)S(1)} %get-tuple-element.15), channel_id=1, source_target_pairs={{0,4},{4,8},{8,12},{12,16},{16,20},{20,24},{24,28},{28,32},{32,36}... | collective-permute-start | bytes 393224 | tf_op jit(solution)/shard_map/ppermute | solution.py:20
  43.3 8.1 %collective-permute-start.7 = (f32[32,4,1,256]{3,0,2,1:T(8,128)S(1)}, f32[32,4,1,256]{3,0,2,1:T(8,128)S(1)}, u32[]{:S(2)}, u32[]{:S(2)}) collective-permute-start(f32[32,4,1,256]{3,0,2,1:T(8,128)S(1)} %get-tuple-element.16), channel_id=1, source_target_pairs={{4,0},{8,4},{12,8},{16,12},{20,16},{24,20},{28,24},{32,28},{36,32}... | collective-permute-start | bytes 393224 | tf_op jit(solution)/shard_map/ppermute | solution.py:23
  55.1 5.7 %copy-start.12 = (s32[256]{0:T(256)S(1)}, s32[256]{0:T(256)}, u32[]{:S(2)}) copy-start(s32[256]{0:T(256)} %param.21) | copy-start | bytes 3076
  55.1 5.7 %copy-start.13 = (f32[1,256]{1,0:T(1,128)S(1)}, f32[1,256]{1,0:T(1,128)}, u32[]{:S(2)}) copy-start(f32[1,256]{1,0:T(1,128)} %fusion.24) | copy-start | bytes 3076
  57.8 5.0 %copy-start.10 = (f32[1024]{0:T(1024)S(1)}, f32[1024]{0:T(1024)}, u32[]{:S(2)}) copy-start(f32[1024]{0:T(1024)} %param.24) | copy-start | bytes 12292
  57.8 117.9 %copy-start.1 = (f32[32,4,8,256]{3,2,1,0:T(8,128)S(1)}, f32[32,4,8,256]{3,2,1,0:T(8,128)}, u32[]{:S(2)}) copy-start(f32[32,4,8,256]{3,2,1,0:T(8,128)} %param.14) | copy-start | bytes 3145732
  62.8 219.8 %all-reduce.29.cloned.1.call-start = ((), (), s32[]{:S(2)}) async-start(), calls=%async_computation.4 | async-start | bytes 262144 | tf_op jit(solution)/shard_map/psum | solution.py:182
  145.6 30.5 %copy-start.7 = (f32[32,32]{1,0:T(8,128)}, f32[32,32]{1,0:T(8,128)S(1)}, u32[]{:S(2)}) copy-start(f32[32,32]{1,0:T(8,128)S(1)} %copy.28) | copy-start | bytes 12292
  175.7 164.6 %reduce-scatter.5.cloned.1.call-start = ((), (), s32[]{:S(2)}) async-start(), calls=%async_computation.2 | async-start | bytes 2621440 | tf_op jit(solution)/shard_map/reduce_scatter | solution.py:188
  310.7 1.6 copy-start.2
  (1 other events, 0.8 us)
Sparse Core Ops, SparseCore 0:
  62.9 81.8 reduce-scatter.6
  175.8 106.7 all-reduce.28
  310.9 29.3 reduce-scatter.4
where the time goes:
time: 350 us; the launch traced here: 349 us
  waiting for transfers between devices  219 us (63%)
  other arithmetic  36.6 us (10%)
  blocking collectives  26.6 us (8%)
  local copies, waits for them, and re-layouts  21.9 us (6%)
  starting transfers between devices  21.5 us (6%)
  between operations  15 us (4%)
  matrix products  8.37 us (2%)
    psum x1, waiting for transfers between devices, per_device(): gram_matrix, cross_matrix = lax.psum((gram_part, cross_part), 'tile')  106 us
    unnamed x4, waiting for transfers between devices  81.2 us
    reduce_scatter x1, waiting for transfers between devices, per_device(): lax.psum_scatter(lax.dot_general(own_rows, anomaly, contract, preferred_e...  26.3 us
    ppermute x4, starting transfers between devices, extended_2(): lax.ppermute(lax.slice_in_dim(block, block.shape[dim] - width, None, axis...  13.2 us
    another operation x3, other arithmetic, solve_spd(): jnp.linalg.cholesky(gram_matrix + jnp.eye(gram_matrix.shape[0], dtype=jnp...  12.4 us
    another operation x2, other arithmetic, solve_spd(): lax.linalg.triangular_solve(factor, halfway, left_side=True, lower=True,...  10.5 us
    all_gather x1, blocking collectives, per_device(): lax.all_gather(innovation, 'member', axis=0, tiled=True)  9.14 us
    all_gather x1, blocking collectives, per_device(): lax.all_gather(scaled, 'member', axis=0, tiled=True)  8.97 us
  transfers between devices with their start and end apart: 11, of which 5 were waited for; matrix products, arithmetic and copies ran while one was open for 4% of the time, Pallas kernels for 0%

commit v1 on v0

--- a/solution.py
+++ b/solution.py
@@ -1,6 +1,10 @@
+import functools
+
 import jax
 import jax.numpy as jnp
 from jax import lax
+from jax.experimental import pallas as pl
+from jax.experimental.pallas import tpu as pltpu
 from jax.sharding import PartitionSpec as P
 
 SWEEPS = 2
@@ -103,6 +107,107 @@
 
 def trim_rim(values_in, rim_cut):
     return values_in[:, :, rim_cut : values_in.shape[2] - rim_cut, :]
+
+
+def exchange_kernel(member_count, part_ref, obs_ref, spr_ref, noise_ref, full_ref,
+                    recv_a, mine, send_a, recv_a_sem, send_b, recv_b_sem):
+    tile_count = part_ref.shape[0]
+    total = tile_count * member_count
+    me_t = lax.axis_index("tile")
+    me_m = lax.axis_index("member")
+    me = me_t * member_count + me_m
+    mesh_ids = pl.DeviceIdType.MESH
+
+    barrier = pltpu.get_barrier_semaphore()
+
+    def greet(k, carry):
+        peer = lax.rem(me + k, total)
+        pl.semaphore_signal(
+            barrier, 1, device_id=(peer // member_count, lax.rem(peer, member_count)),
+            device_id_type=mesh_ids,
+        )
+        return carry
+
+    lax.fori_loop(1, total, greet, 0)
+    pl.semaphore_wait(barrier, total - 1)
+
+    def copy_a(dst_t, src_t):
+        return pltpu.make_async_remote_copy(
+            src_ref=part_ref.at[dst_t], dst_ref=recv_a.at[src_t],
+            send_sem=send_a.at[dst_t], recv_sem=recv_a_sem.at[src_t],
+            device_id=(dst_t, me_m), device_id_type=mesh_ids,
+        )
+
+    def start_a(k, carry):
+        copy_a(lax.rem(me_t + k, tile_count), me_t).start()
+        return carry
+
+    lax.fori_loop(1, tile_count, start_a, 0)
+
+    def wait_a(k, acc):
+        src_t = lax.rem(me_t + k, tile_count)
+        copy_a(me_t, src_t).wait_recv()
+        return acc + recv_a[src_t]
+
+    acc = lax.fori_loop(1, tile_count, wait_a, part_ref[me_t])
+
+    def wait_a_send(k, carry):
+        copy_a(lax.rem(me_t + k, tile_count), me_t).wait_send()
+        return carry
+
+    lax.fori_loop(1, tile_count, wait_a_send, 0)
+
+    innov = (obs_ref[...] - acc) / spr_ref[...] + noise_ref[...]
+    mine[0] = acc
+    mine[1] = innov
+    full_ref[me_m, me_t, 0] = acc
+    full_ref[me_m, me_t, 1] = innov
+
+    def copy_b(dst, src):
+        return pltpu.make_async_remote_copy(
+            src_ref=mine, dst_ref=full_ref.at[lax.rem(src, member_count), src // member_count],
+            send_sem=send_b.at[dst], recv_sem=recv_b_sem.at[src],
+            device_id=(dst // member_count, lax.rem(dst, member_count)), device_id_type=mesh_ids,
+        )
+
+    def start_b(k, carry):
+        copy_b(lax.rem(me + k, total), me).start()
+        return carry
+
+    lax.fori_loop(1, total, start_b, 0)
+
+    def wait_b(k, carry):
+        copy_b(me, lax.rem(me + k, total)).wait_recv()
+        return carry
+
+    lax.fori_loop(1, total, wait_b, 0)
+
+    def wait_b_send(k, carry):
+        copy_b(lax.rem(me + k, total), me).wait_send()
+        return carry
+
+    lax.fori_loop(1, total, wait_b_send, 0)
+
+
+def rates_exchange(pieces, obs_blk, spr_blk, noise_blk, member_count):
+    tile_count, rows, lanes = pieces.shape
+    total = tile_count * member_count
+    vmem = pl.BlockSpec(memory_space=pltpu.VMEM)
+    return pl.pallas_call(
+        functools.partial(exchange_kernel, member_count),
+        out_shape=jax.ShapeDtypeStruct((member_count, tile_count, 2, rows, lanes), jnp.float32),
+        in_specs=[vmem] * 4,
+        out_specs=vmem,
+        scratch_shapes=[
+            pltpu.VMEM((tile_count, rows, lanes), jnp.float32),
+            pltpu.VMEM((2, rows, lanes), jnp.float32),
+            pltpu.SemaphoreType.DMA((tile_count,)),
+            pltpu.SemaphoreType.DMA((tile_count,)),
+            pltpu.SemaphoreType.DMA((total,)),
+            pltpu.SemaphoreType.DMA((total,)),
+        ],
+        compiler_params=pltpu.CompilerParams(collective_id=0, has_side_effects=True),
+    )(pieces, obs_blk, spr_blk, noise_blk)
 
 
 def per_device(
@@ -158,41 +263,40 @@
     )
     member_root = (members - 1) ** 0.5
     spread = jnp.sqrt(INFLATION * obs_var)
-    well_rates = lax.psum_scatter(partial_rates, "tile", scatter_dimension=1, tiled=True)
+    member_count = lax.axis_size("member")
     well_first = tile_rank * well_share
     spread_part = lax.dynamic_slice_in_dim(spread, well_first, well_share, 0)
     observed_part = lax.dynamic_slice_in_dim(observed, well_first, well_share, 0)
     noise_part = lax.dynamic_slice_in_dim(obs_noise, well_first, well_share, 1)
-    mean_rate = lax.psum(jnp.sum(well_rates, 0), "member") / members
-    scaled = (well_rates - mean_rate) / (spread_part * member_root)
-    innovation = (observed_part - well_rates) / spread_part + noise_part
-    scaled_all, innov_all = (
-        lax.all_gather(scaled, "member", axis=0, tiled=True),
-        lax.all_gather(innovation, "member", axis=0, tiled=True),
-    )
-    gram_part = jnp.dot(
-        scaled_all,
-        scaled_all.T,
-        precision=lax.Precision.HIGHEST,
-        preferred_element_type=jnp.float32,
-    )
-    cross_part = jnp.dot(
+    block_rows = local_count * well_share // 128
+    pieces = partial_rates.reshape(local_count, tile_count, well_share).transpose(1, 0, 2)
+    pieces = pieces.reshape(tile_count, block_rows, 128)
+    obs_blk = jnp.broadcast_to(observed_part[None, :], (local_count, well_share)).reshape(block_rows, 128)
+    spr_blk = jnp.broadcast_to(spread_part[None, :], (local_count, well_share)).reshape(block_rows, 128)
+    noise_blk = noise_part.reshape(block_rows, 128)
+    full = rates_exchange(pieces, obs_blk, spr_blk, noise_blk, member_count)
+    full = full.reshape(member_count, tile_count, 2, local_count, well_share)
+    rates_all = full[:, :, 0].transpose(0, 2, 1, 3).reshape(members, well_count)
+    innov_all = full[:, :, 1].transpose(0, 2, 1, 3).reshape(members, well_count)
+    own_block = lax.dynamic_index_in_dim(
+        lax.dynamic_index_in_dim(full, member_rank, 0, keepdims=False), tile_rank, 0, keepdims=False
+    )
+    well_rates = own_block[0]
+    mean_rate = jnp.sum(rates_all, 0) / members
+    scaled_all = (rates_all - mean_rate) / (spread * member_root)
+    gram_matrix = jnp.dot(
+        scaled_all, scaled_all.T, precision=lax.Precision.HIGHEST, preferred_element_type=jnp.float32
+    )
+    cross_matrix = jnp.dot(
         scaled_all, innov_all.T, precision=lax.Precision.HIGHEST, preferred_element_type=jnp.float32
     )
-    gram_matrix, cross_matrix = lax.psum((gram_part, cross_part), "tile")
     weights_low = solve_spd(gram_matrix, cross_matrix).astype(jnp.bfloat16)
     anomaly = (log_perm / member_root).astype(jnp.bfloat16).reshape(local_count, cell_count)
+    anomaly_all = lax.all_gather(anomaly, "member", axis=0, tiled=True)
     first_member = member_rank * local_count
+    own_cols = lax.dynamic_slice_in_dim(weights_low, first_member, local_count, 1)
     contract = (((0,), (0,)), ((), ()))
-    own_rows = lax.dynamic_slice_in_dim(weights_low, first_member, local_count, 0)
-    update_sum = lax.psum_scatter(
-        lax.dot_general(own_rows, anomaly, contract, preferred_element_type=jnp.float32).astype(
-            jnp.bfloat16
-        ),
-        "member",
-        scatter_dimension=0,
-        tiled=True,
-    ).astype(jnp.float32)
+    update_sum = lax.dot_general(own_cols, anomaly_all, contract, preferred_element_type=jnp.float32)
     new_log_perm = log_perm + update_sum.reshape(log_perm.shape)
     return (new_log_perm, pressure, saturation, well_rates)
 

time: 350 us -> 183 us (0.52)
  waiting for transfers between devices: 219 us -> 3.99 us
  Pallas kernels: 0 us -> 44.3 us
  blocking collectives: 26.6 us -> 0 us
  local copies, waits for them, and re-layouts: 21.9 us -> 46.6 us
  other arithmetic: 36.6 us -> 41.5 us
    psum x1 -> x0, waiting for transfers between devices: 106 us -> none  [per_device(): gram_matrix, cross_matrix = lax.psum((gram_part, cross_part), 'tile')]
    unnamed x4 -> x1, waiting for transfers between devices: 81.2 us -> 0.02 us
    pallas_call x0 -> x1, Pallas kernels: none -> 44.3 us  [rates_exchange(): pl.pallas_call(functools.partial(exchange_kernel, member_count), out_shap...]
    reduce_scatter x1 -> x0, waiting for transfers between devices: 26.3 us -> none  [per_device(): lax.psum_scatter(lax.dot_general(own_rows, anomaly, contract, preferred_e...]
    all_gather x2 -> x0, blocking collectives: 18.1 us -> none  [the longest x1 9.14 us: per_device(): lax.all_gather(innovation, 'member', axis=0, tiled=True)]
    psum x1 -> x0, blocking collectives: 8.45 us -> none  [per_device(): mean_rate = lax.psum(jnp.sum(well_rates, 0), 'member') / members]
    reshape x0 -> x6, local copies, waits for them, and re-layouts: none -> 7.5 us  [the longest x1 3.75 us: per_device(): full = full.reshape(member_count, tile_count, 2, local_count, well_share)]
    unnamed x34 -> x69, local copies, waits for them, and re-layouts: 7.55 us -> 10.1 us
  transfers between devices with their start and end apart: 11 -> 9, of which waited for: 5 -> 1; matrix products, arithmetic and copies ran while one was open for 4% -> 48% of each run, Pallas kernels for 0% -> 24%
where the time goes in v1:
time: 183 us; the launch traced here: 182 us
  local copies, waits for them, and re-layouts  46.6 us (25%)
  Pallas kernels  44.3 us (24%)
  other arithmetic  41.5 us (23%)
  starting transfers between devices  23.3 us (13%)
  between operations  15.5 us (8%)
  matrix products  6.77 us (4%)
  waiting for transfers between devices  3.99 us (2%)
    pallas_call x1, Pallas kernels, rates_exchange(): pl.pallas_call(functools.partial(exchange_kernel, member_count), out_shap...  44.3 us
    ppermute x4, starting transfers between devices, extended_2(): lax.ppermute(lax.slice_in_dim(block, block.shape[dim] - width, None, axis...  14.1 us
    another operation x3, other arithmetic, solve_spd(): jnp.linalg.cholesky(gram_matrix + jnp.eye(gram_matrix.shape[0], dtype=jnp...  12.4 us
    another operation x2, other arithmetic, solve_spd(): lax.linalg.triangular_solve(factor, halfway, left_side=True, lower=True,...  10.5 us
    unnamed x69, local copies, waits for them, and re-layouts  10.1 us
    ppermute x4, starting transfers between devices, extended_2(): lax.ppermute(lax.slice_in_dim(block, 0, width, axis=dim), axis, backward)  9.12 us
    div x2, other arithmetic, jacobi(): return (baseline + flow_sum) / (storage_term + weight_sum)  4.11 us
    ppermute x4, waiting for transfers between devices, extended_2(): lax.ppermute(lax.slice_in_dim(block, 0, width, axis=dim), axis, backward)  3.94 us
  transfers between devices with their start and end apart: 9, of which 1 were waited for; matrix products, arithmetic and copies ran while one was open for 48% of the time, Pallas kernels for 24%

profile of v1, /device:TPU:1, one launch (start us, length us, event | category | flops | bytes accessed | tf_op | source)
XLA Modules:
  0.0 181.9 jit_solution(11417534057718187363)
XLA Ops:
  7.3 1.9 %copy.26 = f32[32,4,8,256]{3,0,2,1:T(8,128)S(1)} copy(f32[32,4,8,256]{3,2,1,0:T(8,128)} %param.14) | data formatting | bytes 2097152 | tf_op args[0]
  9.2 4.9 %collective-permute-start = (f32[32,4,1,256]{3,0,2,1:T(8,128)S(1)}, f32[32,4,1,256]{3,0,2,1:T(8,128)S(1)}, u32[]{:S(2)}, u32[]{:S(2)}) collective-permute-start(f32[32,4,1,256]{3,0,2,1:T(8,128)S(1)} %get-tuple-element.19), channel_id=1, source_target_pairs={{0,4},{4,8},{8,12},{12,16},{16,20},{20,24},{24,28},{28,32},{32,36}... | collective-permute-start | bytes 393224 | tf_op jit(solution)/shard_map/ppermute | solution.py:24
  14.2 1.9 %collective-permute-start.1 = (f32[32,4,1,256]{3,0,2,1:T(8,128)S(1)}, f32[32,4,1,256]{3,0,2,1:T(8,128)}, u32[]{:S(2)}, u32[]{:S(2)}) collective-permute-start(f32[32,4,1,256]{3,0,2,1:T(8,128)S(1)} %get-tuple-element.20), channel_id=1, source_target_pairs={{4,0},{8,4},{12,8},{16,12},{20,16},{24,20},{28,24},{32,28},{36,32}... | collective-permute-start | bytes 393224 | tf_op jit(solution)/shard_map/ppermute | solution.py:27
  16.1 3.6 %collective-permute-start.2 = (f32[2,4,1,256]{3,2,1,0:T(1,128)S(1)}, f32[2,4,1,256]{3,2,1,0:T(1,128)S(1)}, u32[]{:S(2)}, u32[]{:S(2)}) collective-permute-start(f32[2,4,1,256]{3,2,1,0:T(1,128)S(1)} %get-tuple-element.36), channel_id=1, source_target_pairs={{0,4},{4,8},{8,12},{12,16},{16,20},{20,24},{24,28},{28,32},{32,36}... | collective-permute-start | bytes 24584 | tf_op jit(solution)/shard_map/ppermute | solution.py:24
  19.8 2.1 %collective-permute-start.3 = (f32[2,4,1,256]{3,2,1,0:T(1,128)S(1)}, f32[2,4,1,256]{3,2,1,0:T(1,128)S(1)}, u32[]{:S(2)}, u32[]{:S(2)}) collective-permute-start(f32[2,4,1,256]{3,2,1,0:T(1,128)S(1)} %get-tuple-element.37), channel_id=1, source_target_pairs={{4,0},{8,4},{12,8},{16,12},{20,16},{24,20},{28,24},{32,28},{36,32}... | collective-permute-start | bytes 24584 | tf_op jit(solution)/shard_map/ppermute | solution.py:27
  36.8 2.0 %fusion.4 = f32[32,4,10,256]{3,0,2,1:T(8,128)S(1)} fusion(f32[32,3,10,256]{3,0,2,1:T(8,128)S(1)} %divide_multiply_fusion.1, f32[32,3,10,256]{3,0,2,1:T(8,128)S(1)} %broadcast_in_dim.122, f32[32,3,10,256]{3,0,2,1:T(8,128)S(1)} %broadcast_in_dim.121, f32[32,4,10,255]{3,0,2,1:T(8,128)S(1)} %broadcast_in_dim.120, f32[32,4,10,255]{3,0,2,1:T(8,128)S(1)} %broadcast_in_dim.119, ...), kind=kLoop, calls=%fused_computation.17 | loop fusion | flops 6225920 | bytes 11797504 | tf_op jit(solution)/shard_map/div | solution.py:77
  38.9 3.6 %collective-permute-start.4 = (f32[32,4,1,256]{3,0,2,1:T(8,128)S(1)}, f32[32,4,1,256]{3,0,2,1:T(8,128)S(1)}, u32[]{:S(2)}, u32[]{:S(2)}) collective-permute-start(f32[32,4,1,256]{3,0,2,1:T(8,128)S(1)} %get-tuple-element.17), channel_id=1, source_target_pairs={{0,4},{4,8},{8,12},{12,16},{16,20},{20,24},{24,28},{28,32},{32,36}... | collective-permute-start | bytes 393224 | tf_op jit(solution)/shard_map/ppermute | solution.py:24
  42.6 1.9 %collective-permute-start.5 = (f32[32,4,1,256]{3,0,2,1:T(8,128)S(1)}, f32[32,4,1,256]{3,0,2,1:T(8,128)S(1)}, u32[]{:S(2)}, u32[]{:S(2)}) collective-permute-start(f32[32,4,1,256]{3,0,2,1:T(8,128)S(1)} %get-tuple-element.18), channel_id=1, source_target_pairs={{4,0},{8,4},{12,8},{16,12},{20,16},{24,20},{28,24},{32,28},{36,32}... | collective-permute-start | bytes 393224 | tf_op jit(solution)/shard_map/ppermute | solution.py:27
  45.3 3.9 %collective-permute-done.5 = f32[32,4,1,256]{3,0,2,1:T(8,128)S(1)} collective-permute-done((f32[32,4,1,256]{3,0,2,1:T(8,128)S(1)}, f32[32,4,1,256]{3,0,2,1:T(8,128)S(1)}, u32[]{:S(2)}, u32[]{:S(2)}) %collective-permute-start.5) | collective-permute-done | bytes 131104 | tf_op jit(solution)/shard_map/ppermute | solution.py:27
  50.1 2.1 %fusion.8 = f32[32,4,10,256]{3,0,2,1:T(8,128)S(1)} fusion(f32[32,3,10,256]{3,0,2,1:T(8,128)S(1)} %divide_multiply_fusion.1, f32[32,4,1,256]{3,0,2,1:T(8,128)S(1)} %collective-permute-done.5, f32[32,4,8,256]{3,0,2,1:T(8,128)S(1)} %slice.245, f32[32,4,1,256]{3,0,2,1:T(8,128)S(1)} %collective-permute-done.4, f32[32,3,10,256]{3,0,2,1:T(8,128)S(1)} %get-tuple-element.16, ...), kind=kLoop, calls=%fused_computation.21 | loop fusion | flops 8847360 | bytes 10748928 | tf_op jit(solution)/shard_map/div | solution.py:77
  52.9 1.9 %collective-permute-start.6 = (f32[32,4,1,256]{3,0,2,1:T(8,128)}, f32[32,4,1,256]{3,0,2,1:T(8,128)}, u32[]{:S(2)}, u32[]{:S(2)}) collective-permute-start(f32[32,4,1,256]{3,0,2,1:T(8,128)} %get-tuple-element.11), channel_id=1, source_target_pairs={{0,4},{4,8},{8,12},{12,16},{16,20},{20,24},{24,28},{28,32},{32,36}... | collective-permute-start | bytes 393224 | tf_op jit(solution)/shard_map/ppermute | solution.py:24
  54.8 3.2 %collective-permute-start.7 = (f32[32,4,1,256]{3,0,2,1:T(8,128)}, f32[32,4,1,256]{3,0,2,1:T(8,128)}, u32[]{:S(2)}, u32[]{:S(2)}) collective-permute-start(f32[32,4,1,256]{3,0,2,1:T(8,128)} %get-tuple-element.12), channel_id=1, source_target_pairs={{4,0},{8,4},{12,8},{16,12},{20,16},{24,20},{28,24},{32,28},{36,32}... | collective-permute-start | bytes 393224 | tf_op jit(solution)/shard_map/ppermute | solution.py:27
  58.8 2.7 %copy.30 = f32[32,4,8,256]{0,3,2,1:T(8,128)} copy(f32[32,4,8,256]{3,0,2,1:T(8,128)S(1)} %slice.252) | data formatting | bytes 2097152 | tf_op jit(solution)/shard_map/slice | solution.py:109
  63.0 3.7 %gather_fusion.1 = f32[256,32]{1,0:T(8,128)} fusion(f32[32,8192]{0,1:T(8,128)} %bitcast.91, s32[1024]{0:T(1024)} %pad_clamp_fusion), kind=kCustom, calls=%fused_computation.1.clone | custom fusion | bytes 66560 | tf_op jit(solution)/shard_map/jit(_take)/gather | solution.py:252
  72.7 2.7 %copy.29 = f32[32,4,8,256]{0,3,2,1:T(8,128)} copy(f32[32,4,8,256]{3,0,2,1:T(8,128)S(1)} %get-tuple-element.9) | data formatting | bytes 2097152 | tf_op jit(solution)/shard_map/mul | solution.py:249
  75.4 3.0 %gather_fusion = f32[256,32]{1,0:T(8,128)S(1)} fusion(f32[32,8192]{0,1:T(8,128)} %bitcast.90, s32[1024]{0:T(1024)} %pad_clamp_fusion), kind=kCustom, calls=%fused_computation.clone | custom fusion | bytes 66560 | tf_op jit(solution)/shard_map/jit(_take)/gather | solution.py:251
  81.7 44.3 %shard_map.147 = f32[4,32,2,8,128]{4,3,2,1,0:T(8,128)} custom-call(f32[32,8,128]{2,1,0:T(8,128)} %reshape.115.part_ref, f32[8,128]{1,0:T(8,128)} %broadcast_in_dim.137.obs_ref, f32[8,128]{1,0:T(8,128)} %broadcast_in_dim.140.spr_ref, f32[8,128]{1,0:T(8,128)} %reshape.116.noise_ref), custom_call_target="tpu_custom_call" | custom-call | tf_op jit(solution)/shard_map/pallas_call | solution.py:196
  125.9 3.7 %reshape.117 = f32[4,32,2,32,32]{4,3,2,1,0:T(8,128)} reshape(f32[4,32,2,8,128]{4,3,2,1,0:T(8,128)} %shard_map.147) | data formatting | bytes 2097152 | tf_op jit(solution)/shard_map/reshape | solution.py:278
  129.7 1.9 %fusion = f32[32,32]{1,0:T(8,128)S(1)} fusion(f32[4,32,2,32,32]{4,3,2,1,0:T(8,128)} %reshape.117), kind=kLoop, calls=%fused_computation.5 | loop fusion | flops 130048 | bytes 528384 | tf_op jit(solution)/shard_map/reduce_sum | solution.py:285
  131.6 1.9 %subtract_divide_fusion = f32[4,32,32,32]{3,1,2,0:T(8,128)S(1)} fusion(f32[4,32,2,32,32]{4,3,2,1,0:T(8,128)} %reshape.117, f32[32,32]{1,0:T(8,128)S(1)} %div.65, f32[32,32]{1,0:T(8,128)S(1)} %broadcast_multiply_fusion), kind=kLoop, calls=%fused_computation.4 | loop fusion | flops 262144 | bytes 1056768 | tf_op jit(solution)/shard_map/div | solution.py:286
  138.4 11.7 %cholesky.17 = f32[128,128]{1,0:T(8,128)S(1)} custom-call(f32[128,128]{1,0:T(8,128)S(1)} %fusion.42), custom_call_target="Cholesky" | custom-call | tf_op jit(solution)/shard_map/jit(cholesky)/cholesky | solution.py:101
  151.5 9.8 %custom-call.8 = f32[1,128,128]{1,2,0:T(8,128)S(1)} custom-call(f32[1,128,128]{2,1,0:T(8,128)S(1)} %fusion.36), custom_call_target="InvertDiagBlocksLowerTriangular" | custom-call | tf_op jit(solution)/shard_map/triangular_solve | solution.py:103
  166.1 2.9 %copy.36 = f32[32,4,8,256]{3,2,1,0:T(8,128)} copy(f32[32,4,8,256]{3,0,2,1:T(8,128)} %get-tuple-element.10) | data formatting | bytes 2097152
  171.5 2.0 %fusion.47 = f32[32,8192]{1,0:T(8,128)S(1)} fusion(bf16[128,8192]{1,0:T(8,128)(2,1)} %all-gather.2.cloned.1.call-done, bf16[128,128]{0,1:T(8,128)(2,1)S(1)} %fusion.37, s32[]{:T(128)S(6)} %select_n.48), kind=kOutput, calls=%fused_computation.104 | convolution fusion | flops 67108864 | bytes 3153924 | tf_op jit(solution)/shard_map/dot_general | solution.py:299
  (153 shorter events, 42.9 us)
Async XLA Ops:
  7.2 19.1 %copy-start = (f32[32,1024]{1,0:T(8,128)S(1)}, f32[32,1024]{1,0:T(8,128)}, u32[]{:S(2)}) copy-start(f32[32,1024]{1,0:T(8,128)} %param.25) | copy-start | bytes 393220
  7.2 14.7 %copy-start.2 = (f32[32,4,8,256]{3,2,1,0:T(8,128)S(1)}, f32[32,4,8,256]{3,2,1,0:T(8,128)}, u32[]{:S(2)}) copy-start(f32[32,4,8,256]{3,2,1,0:T(8,128)} %param.14) | copy-start | bytes 3145732
  7.2 8.9 %copy-start.7 = (f32[4,8,256]{2,1,0:T(8,128)S(1)}, f32[4,8,256]{2,1,0:T(8,128)}, u32[]{:S(2)}) copy-start(f32[4,8,256]{2,1,0:T(8,128)} %param.15) | copy-start | bytes 98308
  7.2 8.9 %copy-start.17 = (f32[4,8,256]{2,1,0:T(8,128)S(1)}, f32[4,8,256]{2,1,0:T(8,128)}, u32[]{:S(2)}) copy-start(f32[4,8,256]{2,1,0:T(8,128)} %param.16) | copy-start | bytes 98308
  7.2 164.3 %all-gather.2.cloned.1.call-start = ((), (), s32[]{:S(2)}) async-start(), calls=%async_computation | async-start | bytes 2621440 | tf_op jit(solution)/shard_map/all_gather | solution.py:295
  9.2 23.3 %collective-permute-start = (f32[32,4,1,256]{3,0,2,1:T(8,128)S(1)}, f32[32,4,1,256]{3,0,2,1:T(8,128)S(1)}, u32[]{:S(2)}, u32[]{:S(2)}) collective-permute-start(f32[32,4,1,256]{3,0,2,1:T(8,128)S(1)} %get-tuple-element.19), channel_id=1, source_target_pairs={{0,4},{4,8},{8,12},{12,16},{16,20},{20,24},{24,28},{28,32},{32,36}... | collective-permute-start | bytes 393224 | tf_op jit(solution)/shard_map/ppermute | solution.py:24
  14.2 19.0 %collective-permute-start.1 = (f32[32,4,1,256]{3,0,2,1:T(8,128)S(1)}, f32[32,4,1,256]{3,0,2,1:T(8,128)}, u32[]{:S(2)}, u32[]{:S(2)}) collective-permute-start(f32[32,4,1,256]{3,0,2,1:T(8,128)S(1)} %get-tuple-element.20), channel_id=1, source_target_pairs={{4,0},{8,4},{12,8},{16,12},{20,16},{24,20},{28,24},{32,28},{36,32}... | collective-permute-start | bytes 393224 | tf_op jit(solution)/shard_map/ppermute | solution.py:27
  16.1 14.9 %collective-permute-start.2 = (f32[2,4,1,256]{3,2,1,0:T(1,128)S(1)}, f32[2,4,1,256]{3,2,1,0:T(1,128)S(1)}, u32[]{:S(2)}, u32[]{:S(2)}) collective-permute-start(f32[2,4,1,256]{3,2,1,0:T(1,128)S(1)} %get-tuple-element.36), channel_id=1, source_target_pairs={{0,4},{4,8},{8,12},{12,16},{16,20},{20,24},{24,28},{28,32},{32,36}... | collective-permute-start | bytes 24584 | tf_op jit(solution)/shard_map/ppermute | solution.py:24
  19.8 5.2 %copy-start.20 = (f32[1024]{0:T(1024)S(1)}, f32[1024]{0:T(1024)}, u32[]{:S(2)}) copy-start(f32[1024]{0:T(1024)} %param.24) | copy-start | bytes 12292
  19.8 5.2 %copy-start.16 = (f32[4,8,256]{2,1,0:T(8,128)S(1)}, f32[4,8,256]{2,1,0:T(8,128)}, u32[]{:S(2)}) copy-start(f32[4,8,256]{2,1,0:T(8,128)} %param.18) | copy-start | bytes 98308
  19.8 5.2 %copy-start.18 = (f32[4,8,256]{2,1,0:T(8,128)S(1)}, f32[4,8,256]{2,1,0:T(8,128)}, u32[]{:S(2)}) copy-start(f32[4,8,256]{2,1,0:T(8,128)} %param.17) | copy-start | bytes 98308
  19.8 5.2 %copy-start.28 = (f32[1024]{0:T(1024)S(1)}, f32[1024]{0:T(1024)}, u32[]{:S(2)}) copy-start(f32[1024]{0:T(1024)} %param.19) | copy-start | bytes 12292
  19.8 5.2 %copy-start.29 = (s32[256]{0:T(256)S(1)}, s32[256]{0:T(256)}, u32[]{:S(2)}) copy-start(s32[256]{0:T(256)} %param.21) | copy-start | bytes 3076
  19.8 11.2 %collective-permute-start.3 = (f32[2,4,1,256]{3,2,1,0:T(1,128)S(1)}, f32[2,4,1,256]{3,2,1,0:T(1,128)S(1)}, u32[]{:S(2)}, u32[]{:S(2)}) collective-permute-start(f32[2,4,1,256]{3,2,1,0:T(1,128)S(1)} %get-tuple-element.37), channel_id=1, source_target_pairs={{4,0},{8,4},{12,8},{16,12},{20,16},{24,20},{28,24},{32,28},{36,32}... | collective-permute-start | bytes 24584 | tf_op jit(solution)/shard_map/ppermute | solution.py:27
  38.9 6.4 %collective-permute-start.4 = (f32[32,4,1,256]{3,0,2,1:T(8,128)S(1)}, f32[32,4,1,256]{3,0,2,1:T(8,128)S(1)}, u32[]{:S(2)}, u32[]{:S(2)}) collective-permute-start(f32[32,4,1,256]{3,0,2,1:T(8,128)S(1)} %get-tuple-element.17), channel_id=1, source_target_pairs={{0,4},{4,8},{8,12},{12,16},{16,20},{20,24},{24,28},{28,32},{32,36}... | collective-permute-start | bytes 393224 | tf_op jit(solution)/shard_map/ppermute | solution.py:24
  42.6 6.7 %collective-permute-start.5 = (f32[32,4,1,256]{3,0,2,1:T(8,128)S(1)}, f32[32,4,1,256]{3,0,2,1:T(8,128)S(1)}, u32[]{:S(2)}, u32[]{:S(2)}) collective-permute-start(f32[32,4,1,256]{3,0,2,1:T(8,128)S(1)} %get-tuple-element.18), channel_id=1, source_target_pairs={{4,0},{8,4},{12,8},{16,12},{20,16},{24,20},{28,24},{32,28},{36,32}... | collective-permute-start | bytes 393224 | tf_op jit(solution)/shard_map/ppermute | solution.py:27
  52.9 13.8 %collective-permute-start.6 = (f32[32,4,1,256]{3,0,2,1:T(8,128)}, f32[32,4,1,256]{3,0,2,1:T(8,128)}, u32[]{:S(2)}, u32[]{:S(2)}) collective-permute-start(f32[32,4,1,256]{3,0,2,1:T(8,128)} %get-tuple-element.11), channel_id=1, source_target_pairs={{0,4},{4,8},{8,12},{12,16},{16,20},{20,24},{24,28},{28,32},{32,36}... | collective-permute-start | bytes 393224 | tf_op jit(solution)/shard_map/ppermute | solution.py:24
  54.8 11.9 %collective-permute-start.7 = (f32[32,4,1,256]{3,0,2,1:T(8,128)}, f32[32,4,1,256]{3,0,2,1:T(8,128)}, u32[]{:S(2)}, u32[]{:S(2)}) collective-permute-start(f32[32,4,1,256]{3,0,2,1:T(8,128)} %get-tuple-element.12), channel_id=1, source_target_pairs={{4,0},{8,4},{12,8},{16,12},{20,16},{24,20},{28,24},{32,28},{36,32}... | collective-permute-start | bytes 393224 | tf_op jit(solution)/shard_map/ppermute | solution.py:27
  72.7 5.8 %copy-start.19 = (f32[256,32]{1,0:T(8,128)S(1)}, f32[256,32]{1,0:T(8,128)}, u32[]{:S(2)}) copy-start(f32[256,32]{1,0:T(8,128)} %gather_fusion.1) | copy-start | bytes 98308
  72.7 5.8 %copy-start.26 = (f32[256]{0:T(256)S(1)}, f32[256]{0:T(256)}, u32[]{:S(2)}) copy-start(f32[256]{0:T(256)} %get-tuple-element.41) | copy-start | bytes 3076
  72.7 5.8 %copy-start.27 = (pred[256]{0:T(512)(128)(4,1)S(1)}, pred[256]{0:T(512)(128)(4,1)}, u32[]{:S(2)}) copy-start(pred[256]{0:T(512)(128)(4,1)} %get-tuple-element.40) | copy-start | bytes 772
  72.7 5.8 %copy-start.30 = (s32[256]{0:T(256)S(1)}, s32[256]{0:T(256)}, u32[]{:S(2)}) copy-start(s32[256]{0:T(256)} %param.21) | copy-start | bytes 3076
  72.7 5.8 %copy-start.31 = (f32[1,256]{1,0:T(1,128)S(1)}, f32[1,256]{1,0:T(1,128)}, u32[]{:S(2)}) copy-start(f32[1,256]{1,0:T(1,128)} %fusion.26) | copy-start | bytes 3076
  166.1 4.2 %copy-start.4 = (f32[128,1024]{1,0:T(8,128)S(1)}, f32[128,1024]{1,0:T(8,128)}, u32[]{:S(2)}) copy-start(f32[128,1024]{1,0:T(8,128)} %reshape.118) | copy-start | bytes 1572868
  (17 other events, 24.7 us)
Sparse Core Ops, SparseCore 0:
  23.3 33.5 all-gather.1

commit v2 on v1

--- a/solution.py
+++ b/solution.py
@@ -292,9 +292,23 @@
     )
     weights_low = solve_spd(gram_matrix, cross_matrix).astype(jnp.bfloat16)
     anomaly = (log_perm / member_root).astype(jnp.bfloat16).reshape(local_count, cell_count)
-    anomaly_all = lax.all_gather(anomaly, "member", axis=0, tiled=True)
+    anomaly_parts = [anomaly]
+    for shift in range(1, member_count):
+        pairs = [(i, (i + shift) % member_count) for i in range(member_count)]
+        anomaly_parts.append(lax.ppermute(anomaly, "member", pairs))
+    anomaly_all = jnp.concatenate(anomaly_parts, axis=0)
     first_member = member_rank * local_count
     own_cols = lax.dynamic_slice_in_dim(weights_low, first_member, local_count, 1)
+    own_cols = jnp.concatenate(
+        [
+            lax.dynamic_slice_in_dim(
+                own_cols, lax.rem(member_rank - shift + member_count, member_count) * local_count,
+                local_count, 0,
+            )
+            for shift in range(member_count)
+        ],
+        axis=0,
+    )
     contract = (((0,), (0,)), ((), ()))
     update_sum = lax.dot_general(own_cols, anomaly_all, contract, preferred_element_type=jnp.float32)
     new_log_perm = log_perm + update_sum.reshape(log_perm.shape)

time: 183 us -> 173 us (0.945)
  between operations: 15.5 us -> 2.09 us
  starting transfers between devices: 23.3 us -> 27.2 us
  Pallas kernels: 44.3 us -> 41.1 us
  waiting for transfers between devices: 3.99 us -> 6.21 us
    ppermute x0 -> x3, starting transfers between devices: none -> 5.21 us  [per_device(): anomaly_parts.append(lax.ppermute(anomaly, 'member', pairs))]
    unnamed x69 -> x67, local copies, waits for them, and re-layouts: 10.1 us -> 6.83 us
    pallas_call x1, Pallas kernels: 44.3 us -> 41.1 us  [rates_exchange(): pl.pallas_call(functools.partial(exchange_kernel, member_count), out_shap...]
    transpose x2, local copies, waits for them, and re-layouts: 3.05 us -> 6.1 us  [per_device(): innov_all = full[:, :, 1].transpose(0, 2, 1, 3).reshape(members, well_count)]
    ppermute x4, waiting for transfers between devices: 3.94 us -> 6.19 us  [extended_2(): lax.ppermute(lax.slice_in_dim(block, 0, width, axis=dim), axis, backward)]
  transfers between devices with their start and end apart: 9 -> 11, of which waited for: 1 -> 2; matrix products, arithmetic and copies ran while one was open for 48% -> 51% of each run, Pallas kernels for 24% -> 24%
where the time goes in v2:
time: 173 us; the launch traced here: 171 us
  local copies, waits for them, and re-layouts  46.5 us (27%)
  Pallas kernels  41.1 us (24%)
  other arithmetic  40.3 us (23%)
  starting transfers between devices  27.2 us (16%)
  matrix products  8.04 us (5%)
  waiting for transfers between devices  6.21 us (4%)
  between operations  2.09 us (1%)
    pallas_call x1, Pallas kernels, rates_exchange(): pl.pallas_call(functools.partial(exchange_kernel, member_count), out_shap...  41.1 us
    ppermute x4, starting transfers between devices, extended_2(): lax.ppermute(lax.slice_in_dim(block, block.shape[dim] - width, None, axis...  12.4 us
    another operation x3, other arithmetic, solve_spd(): jnp.linalg.cholesky(gram_matrix + jnp.eye(gram_matrix.shape[0], dtype=jnp...  12.4 us
    another operation x2, other arithmetic, solve_spd(): lax.linalg.triangular_solve(factor, halfway, left_side=True, lower=True,...  10.5 us
    ppermute x4, starting transfers between devices, extended_2(): lax.ppermute(lax.slice_in_dim(block, 0, width, axis=dim), axis, backward)  9.6 us
    unnamed x67, local copies, waits for them, and re-layouts  6.83 us
    ppermute x4, waiting for transfers between devices, extended_2(): lax.ppermute(lax.slice_in_dim(block, 0, width, axis=dim), axis, backward)  6.19 us
    transpose x2, local copies, waits for them, and re-layouts, per_device(): innov_all = full[:, :, 1].transpose(0, 2, 1, 3).reshape(members, well_count)  6.1 us
  transfers between devices with their start and end apart: 11, of which 2 were waited for; matrix products, arithmetic and copies ran while one was open for 51% of the time, Pallas kernels for 24%

profile of v2, /device:TPU:1, one launch (start us, length us, event | category | flops | bytes accessed | tf_op | source)
XLA Modules:
  0.0 171.5 jit_solution(5207608786786816991)
XLA Ops:
  3.2 3.6 %collective-permute-start.10 = (bf16[32,8192]{1,0:T(8,128)(2,1)}, bf16[32,8192]{1,0:T(8,128)(2,1)}, u32[]{:S(2)}, u32[]{:S(2)}) collective-permute-start(bf16[32,8192]{1,0:T(8,128)(2,1)} %bitcast.35), channel_id=1, source_target_pairs={{0,3},{1,0},{2,1},{3,2},{4,7},{5,4},{6,5},{7,6},{8,11},{9,8},{10,9... | collective-permute-start | bytes 1572872 | tf_op jit(solution)/shard_map/ppermute | solution.py:298
  8.4 4.9 %collective-permute-start.2 = (f32[2,4,1,256]{3,2,1,0:T(1,128)S(1)}, f32[2,4,1,256]{3,2,1,0:T(1,128)S(1)}, u32[]{:S(2)}, u32[]{:S(2)}) collective-permute-start(f32[2,4,1,256]{3,2,1,0:T(1,128)S(1)} %get-tuple-element.36), channel_id=1, source_target_pairs={{0,4},{4,8},{8,12},{12,16},{16,20},{20,24},{24,28},{28,32},{32,36}... | collective-permute-start | bytes 24584 | tf_op jit(solution)/shard_map/ppermute | solution.py:24
  13.5 2.1 %collective-permute-start.3 = (f32[2,4,1,256]{3,2,1,0:T(1,128)S(1)}, f32[2,4,1,256]{3,2,1,0:T(1,128)S(1)}, u32[]{:S(2)}, u32[]{:S(2)}) collective-permute-start(f32[2,4,1,256]{3,2,1,0:T(1,128)S(1)} %get-tuple-element.37), channel_id=1, source_target_pairs={{4,0},{8,4},{12,8},{16,12},{20,16},{24,20},{28,24},{32,28},{36,32}... | collective-permute-start | bytes 24584 | tf_op jit(solution)/shard_map/ppermute | solution.py:27
  24.0 3.6 %collective-permute-start = (f32[32,4,1,256]{3,0,2,1:T(8,128)S(1)}, f32[32,4,1,256]{3,0,2,1:T(8,128)S(1)}, u32[]{:S(2)}, u32[]{:S(2)}) collective-permute-start(f32[32,4,1,256]{3,0,2,1:T(8,128)S(1)} %get-tuple-element.19), channel_id=1, source_target_pairs={{0,4},{4,8},{8,12},{12,16},{16,20},{20,24},{24,28},{28,32},{32,36}... | collective-permute-start | bytes 393224 | tf_op jit(solution)/shard_map/ppermute | solution.py:24
  27.7 1.9 %collective-permute-start.1 = (f32[32,4,1,256]{3,0,2,1:T(8,128)S(1)}, f32[32,4,1,256]{3,0,2,1:T(8,128)S(1)}, u32[]{:S(2)}, u32[]{:S(2)}) collective-permute-start(f32[32,4,1,256]{3,0,2,1:T(8,128)S(1)} %get-tuple-element.20), channel_id=1, source_target_pairs={{4,0},{8,4},{12,8},{16,12},{20,16},{24,20},{28,24},{32,28},{36,32}... | collective-permute-start | bytes 393224 | tf_op jit(solution)/shard_map/ppermute | solution.py:27
  31.1 2.9 %collective-permute-done.1 = f32[32,4,1,256]{3,0,2,1:T(8,128)S(1)} collective-permute-done((f32[32,4,1,256]{3,0,2,1:T(8,128)S(1)}, f32[32,4,1,256]{3,0,2,1:T(8,128)S(1)}, u32[]{:S(2)}, u32[]{:S(2)}) %collective-permute-start.1) | collective-permute-done | bytes 131104 | tf_op jit(solution)/shard_map/ppermute | solution.py:27
  36.7 2.0 %fusion.12 = f32[32,4,10,256]{3,0,2,1:T(8,128)S(1)} fusion(f32[32,3,10,256]{3,0,2,1:T(8,128)S(1)} %divide_multiply_fusion.1, f32[32,3,10,256]{3,0,2,1:T(8,128)S(1)} %broadcast_in_dim.122, f32[32,3,10,256]{3,0,2,1:T(8,128)S(1)} %broadcast_in_dim.121, f32[32,4,10,255]{3,0,2,1:T(8,128)S(1)} %broadcast_in_dim.120, f32[32,4,10,255]{3,0,2,1:T(8,128)S(1)} %broadcast_in_dim.119, ...), kind=kLoop, calls=%fused_computation.25 | loop fusion | flops 6225920 | bytes 11797504 | tf_op jit(solution)/shard_map/div | solution.py:77
  38.8 1.9 %collective-permute-start.4 = (f32[32,4,1,256]{3,0,2,1:T(8,128)S(1)}, f32[32,4,1,256]{3,0,2,1:T(8,128)S(1)}, u32[]{:S(2)}, u32[]{:S(2)}) collective-permute-start(f32[32,4,1,256]{3,0,2,1:T(8,128)S(1)} %get-tuple-element.17), channel_id=1, source_target_pairs={{0,4},{4,8},{8,12},{12,16},{16,20},{20,24},{24,28},{28,32},{32,36}... | collective-permute-start | bytes 393224 | tf_op jit(solution)/shard_map/ppermute | solution.py:24
  40.8 2.4 %collective-permute-start.5 = (f32[32,4,1,256]{3,0,2,1:T(8,128)S(1)}, f32[32,4,1,256]{3,0,2,1:T(8,128)S(1)}, u32[]{:S(2)}, u32[]{:S(2)}) collective-permute-start(f32[32,4,1,256]{3,0,2,1:T(8,128)S(1)} %get-tuple-element.18), channel_id=1, source_target_pairs={{4,0},{8,4},{12,8},{16,12},{20,16},{24,20},{28,24},{32,28},{36,32}... | collective-permute-start | bytes 393224 | tf_op jit(solution)/shard_map/ppermute | solution.py:27
  44.0 3.3 %collective-permute-done.5 = f32[32,4,1,256]{3,0,2,1:T(8,128)S(1)} collective-permute-done((f32[32,4,1,256]{3,0,2,1:T(8,128)S(1)}, f32[32,4,1,256]{3,0,2,1:T(8,128)S(1)}, u32[]{:S(2)}, u32[]{:S(2)}) %collective-permute-start.5) | collective-permute-done | bytes 131104 | tf_op jit(solution)/shard_map/ppermute | solution.py:27
  48.2 2.1 %fusion.16 = f32[32,4,10,256]{3,0,2,1:T(8,128)S(1)} fusion(f32[32,3,10,256]{3,0,2,1:T(8,128)S(1)} %divide_multiply_fusion.1, f32[32,4,1,256]{3,0,2,1:T(8,128)S(1)} %collective-permute-done.5, f32[32,4,8,256]{3,0,2,1:T(8,128)S(1)} %slice.245, f32[32,4,1,256]{3,0,2,1:T(8,128)S(1)} %collective-permute-done.4, f32[32,3,10,256]{3,0,2,1:T(8,128)S(1)} %get-tuple-element.16, ...), kind=kLoop, calls=%fused_computation.29 | loop fusion | flops 8847360 | bytes 10748928 | tf_op jit(solution)/shard_map/div | solution.py:77
  51.0 1.9 %collective-permute-start.6 = (f32[32,4,1,256]{3,0,2,1:T(8,128)}, f32[32,4,1,256]{3,0,2,1:T(8,128)}, u32[]{:S(2)}, u32[]{:S(2)}) collective-permute-start(f32[32,4,1,256]{3,0,2,1:T(8,128)} %get-tuple-element.11), channel_id=1, source_target_pairs={{0,4},{4,8},{8,12},{12,16},{16,20},{20,24},{24,28},{28,32},{32,36}... | collective-permute-start | bytes 393224 | tf_op jit(solution)/shard_map/ppermute | solution.py:24
  52.9 3.2 %collective-permute-start.7 = (f32[32,4,1,256]{3,0,2,1:T(8,128)}, f32[32,4,1,256]{3,0,2,1:T(8,128)}, u32[]{:S(2)}, u32[]{:S(2)}) collective-permute-start(f32[32,4,1,256]{3,0,2,1:T(8,128)} %get-tuple-element.12), channel_id=1, source_target_pairs={{4,0},{8,4},{12,8},{16,12},{20,16},{24,20},{28,24},{32,28},{36,32}... | collective-permute-start | bytes 393224 | tf_op jit(solution)/shard_map/ppermute | solution.py:27
  56.9 2.7 %copy.30 = f32[32,4,8,256]{0,3,2,1:T(8,128)} copy(f32[32,4,8,256]{3,0,2,1:T(8,128)S(1)} %slice.252) | data formatting | bytes 2097152 | tf_op jit(solution)/shard_map/slice | solution.py:109
  61.1 3.7 %gather_fusion.1 = f32[256,32]{1,0:T(8,128)} fusion(f32[32,8192]{0,1:T(8,128)} %bitcast.90, s32[1024]{0:T(1024)} %pad_clamp_fusion), kind=kCustom, calls=%fused_computation.1.clone | custom fusion | bytes 66560 | tf_op jit(solution)/shard_map/jit(_take)/gather | solution.py:252
  70.8 2.7 %copy.29 = f32[32,4,8,256]{0,3,2,1:T(8,128)} copy(f32[32,4,8,256]{3,0,2,1:T(8,128)S(1)} %get-tuple-element.9) | data formatting | bytes 2097152 | tf_op jit(solution)/shard_map/mul | solution.py:249
  73.5 3.0 %gather_fusion = f32[256,32]{1,0:T(8,128)S(1)} fusion(f32[32,8192]{0,1:T(8,128)} %bitcast.89, s32[1024]{0:T(1024)} %pad_clamp_fusion), kind=kCustom, calls=%fused_computation.clone | custom fusion | bytes 66560 | tf_op jit(solution)/shard_map/jit(_take)/gather | solution.py:251
  79.7 41.1 %shard_map.147 = f32[4,32,2,8,128]{4,3,2,1,0:T(8,128)} custom-call(f32[32,8,128]{2,1,0:T(8,128)} %reshape.115.part_ref, f32[8,128]{1,0:T(8,128)} %broadcast_in_dim.137.obs_ref, f32[8,128]{1,0:T(8,128)} %broadcast_in_dim.140.spr_ref, f32[8,128]{1,0:T(8,128)} %reshape.116.noise_ref), custom_call_target="tpu_custom_call" | custom-call | tf_op jit(solution)/shard_map/pallas_call | solution.py:196
  120.8 3.7 %reshape.117 = f32[4,32,2,32,32]{4,3,2,1,0:T(8,128)} reshape(f32[4,32,2,8,128]{4,3,2,1,0:T(8,128)} %shard_map.147) | data formatting | bytes 2097152 | tf_op jit(solution)/shard_map/reshape | solution.py:278
  126.5 3.3 %slice_bitcast_fusion = f32[4,32,32,32]{3,1,2,0:T(8,128)} fusion(f32[4,32,2,32,32]{4,3,2,1,0:T(8,128)} %reshape.117), kind=kLoop, calls=%fused_computation.2 | loop fusion | bytes 1048576 | tf_op jit(solution)/shard_map/transpose | solution.py:280
  135.1 11.7 %cholesky.17 = f32[128,128]{1,0:T(8,128)S(1)} custom-call(f32[128,128]{1,0:T(8,128)S(1)} %fusion.49), custom_call_target="Cholesky" | custom-call | tf_op jit(solution)/shard_map/jit(cholesky)/cholesky | solution.py:101
  148.2 9.8 %custom-call.8 = f32[1,128,128]{1,2,0:T(8,128)S(1)} custom-call(f32[1,128,128]{2,1,0:T(8,128)S(1)} %fusion.44), custom_call_target="InvertDiagBlocksLowerTriangular" | custom-call | tf_op jit(solution)/shard_map/triangular_solve | solution.py:103
  158.0 2.8 %copy.34 = f32[4,32,32,32]{3,2,1,0:T(8,128)S(1)} copy(f32[4,32,32,32]{3,1,2,0:T(8,128)} %slice_bitcast_fusion) | data formatting | bytes 1048576 | tf_op jit(solution)/shard_map/transpose | solution.py:280
  168.0 2.0 %fusion = f32[32,8192]{1,0:T(8,128)S(1)} fusion(bf16[32,8192]{1,0:T(8,128)(2,1)} %collective-permute-done.10, bf16[32,8192]{1,0:T(8,128)(2,1)} %collective-permute-done.9, bf16[32,8192]{1,0:T(8,128)(2,1)} %collective-permute-done.8, bf16[32,8192]{1,0:T(8,128)(2,1)} %bitcast.35, bf16[32,32]{0,1:T(8,128)(2,1)S(1)} %get-tuple-element.39, ...), kind=kOutput, calls=%fused_computation.4 | convolution fusion | flops 75530240 | bytes 3153920 | tf_op jit(solution)/shard_map/dot_general | solution.py:313
  (155 shorter events, 47.1 us)
Async XLA Ops:
  0.6 18.7 %copy-start = (f32[32,1024]{1,0:T(8,128)S(1)}, f32[32,1024]{1,0:T(8,128)}, u32[]{:S(2)}) copy-start(f32[32,1024]{1,0:T(8,128)} %param.25) | copy-start | bytes 393220
  0.6 14.9 %copy-start.3 = (f32[32,4,8,256]{3,2,1,0:T(8,128)S(1)}, f32[32,4,8,256]{3,2,1,0:T(8,128)}, u32[]{:S(2)}) copy-start(f32[32,4,8,256]{3,2,1,0:T(8,128)} %param.14) | copy-start | bytes 3145732
  0.7 7.8 %copy-start.7 = (f32[4,8,256]{2,1,0:T(8,128)S(1)}, f32[4,8,256]{2,1,0:T(8,128)}, u32[]{:S(2)}) copy-start(f32[4,8,256]{2,1,0:T(8,128)} %param.15) | copy-start | bytes 98308
  0.7 7.8 %copy-start.16 = (f32[4,8,256]{2,1,0:T(8,128)S(1)}, f32[4,8,256]{2,1,0:T(8,128)}, u32[]{:S(2)}) copy-start(f32[4,8,256]{2,1,0:T(8,128)} %param.16) | copy-start | bytes 98308
  3.2 164.8 %collective-permute-start.10 = (bf16[32,8192]{1,0:T(8,128)(2,1)}, bf16[32,8192]{1,0:T(8,128)(2,1)}, u32[]{:S(2)}, u32[]{:S(2)}) collective-permute-start(bf16[32,8192]{1,0:T(8,128)(2,1)} %bitcast.35), channel_id=1, source_target_pairs={{0,3},{1,0},{2,1},{3,2},{4,7},{5,4},{6,5},{7,6},{8,11},{9,8},{10,9... | collective-permute-start | bytes 1572872 | tf_op jit(solution)/shard_map/ppermute | solution.py:298
  6.8 161.3 %collective-permute-start.8 = (bf16[32,8192]{1,0:T(8,128)(2,1)}, bf16[32,8192]{1,0:T(8,128)(2,1)}, u32[]{:S(2)}, u32[]{:S(2)}) collective-permute-start(bf16[32,8192]{1,0:T(8,128)(2,1)} %bitcast.35), channel_id=1, source_target_pairs={{0,1},{1,2},{2,3},{3,0},{4,5},{5,6},{6,7},{7,4},{8,9},{9,10},{10,1... | collective-permute-start | bytes 1572872 | tf_op jit(solution)/shard_map/ppermute | solution.py:298
  6.8 161.3 %collective-permute-start.9 = (bf16[32,8192]{1,0:T(8,128)(2,1)}, bf16[32,8192]{1,0:T(8,128)(2,1)}, u32[]{:S(2)}, u32[]{:S(2)}) collective-permute-start(bf16[32,8192]{1,0:T(8,128)(2,1)} %bitcast.35), channel_id=1, source_target_pairs={{0,2},{1,3},{2,0},{3,1},{4,6},{5,7},{6,4},{7,5},{8,10},{9,11},{10,... | collective-permute-start | bytes 1572872 | tf_op jit(solution)/shard_map/ppermute | solution.py:298
  8.4 15.6 %collective-permute-start.2 = (f32[2,4,1,256]{3,2,1,0:T(1,128)S(1)}, f32[2,4,1,256]{3,2,1,0:T(1,128)S(1)}, u32[]{:S(2)}, u32[]{:S(2)}) collective-permute-start(f32[2,4,1,256]{3,2,1,0:T(1,128)S(1)} %get-tuple-element.36), channel_id=1, source_target_pairs={{0,4},{4,8},{8,12},{12,16},{16,20},{20,24},{24,28},{28,32},{32,36}... | collective-permute-start | bytes 24584 | tf_op jit(solution)/shard_map/ppermute | solution.py:24
  13.4 4.6 %copy-start.19 = (f32[1024]{0:T(1024)S(1)}, f32[1024]{0:T(1024)}, u32[]{:S(2)}) copy-start(f32[1024]{0:T(1024)} %param.24) | copy-start | bytes 12292
  13.4 4.6 %copy-start.15 = (f32[4,8,256]{2,1,0:T(8,128)S(1)}, f32[4,8,256]{2,1,0:T(8,128)}, u32[]{:S(2)}) copy-start(f32[4,8,256]{2,1,0:T(8,128)} %param.18) | copy-start | bytes 98308
  13.4 4.6 %copy-start.27 = (f32[1024]{0:T(1024)S(1)}, f32[1024]{0:T(1024)}, u32[]{:S(2)}) copy-start(f32[1024]{0:T(1024)} %param.19) | copy-start | bytes 12292
  13.5 4.6 %copy-start.28 = (s32[256]{0:T(256)S(1)}, s32[256]{0:T(256)}, u32[]{:S(2)}) copy-start(s32[256]{0:T(256)} %param.21) | copy-start | bytes 3076
  13.5 14.2 %collective-permute-start.3 = (f32[2,4,1,256]{3,2,1,0:T(1,128)S(1)}, f32[2,4,1,256]{3,2,1,0:T(1,128)S(1)}, u32[]{:S(2)}, u32[]{:S(2)}) collective-permute-start(f32[2,4,1,256]{3,2,1,0:T(1,128)S(1)} %get-tuple-element.37), channel_id=1, source_target_pairs={{4,0},{8,4},{12,8},{16,12},{20,16},{24,20},{28,24},{32,28},{36,32}... | collective-permute-start | bytes 24584 | tf_op jit(solution)/shard_map/ppermute | solution.py:27
  24.0 7.1 %collective-permute-start = (f32[32,4,1,256]{3,0,2,1:T(8,128)S(1)}, f32[32,4,1,256]{3,0,2,1:T(8,128)S(1)}, u32[]{:S(2)}, u32[]{:S(2)}) collective-permute-start(f32[32,4,1,256]{3,0,2,1:T(8,128)S(1)} %get-tuple-element.19), channel_id=1, source_target_pairs={{0,4},{4,8},{8,12},{12,16},{16,20},{20,24},{24,28},{28,32},{32,36}... | collective-permute-start | bytes 393224 | tf_op jit(solution)/shard_map/ppermute | solution.py:24
  27.7 6.3 %collective-permute-start.1 = (f32[32,4,1,256]{3,0,2,1:T(8,128)S(1)}, f32[32,4,1,256]{3,0,2,1:T(8,128)S(1)}, u32[]{:S(2)}, u32[]{:S(2)}) collective-permute-start(f32[32,4,1,256]{3,0,2,1:T(8,128)S(1)} %get-tuple-element.20), channel_id=1, source_target_pairs={{4,0},{8,4},{12,8},{16,12},{20,16},{24,20},{28,24},{32,28},{36,32}... | collective-permute-start | bytes 393224 | tf_op jit(solution)/shard_map/ppermute | solution.py:27
  38.8 5.2 %collective-permute-start.4 = (f32[32,4,1,256]{3,0,2,1:T(8,128)S(1)}, f32[32,4,1,256]{3,0,2,1:T(8,128)S(1)}, u32[]{:S(2)}, u32[]{:S(2)}) collective-permute-start(f32[32,4,1,256]{3,0,2,1:T(8,128)S(1)} %get-tuple-element.17), channel_id=1, source_target_pairs={{0,4},{4,8},{8,12},{12,16},{16,20},{20,24},{24,28},{28,32},{32,36}... | collective-permute-start | bytes 393224 | tf_op jit(solution)/shard_map/ppermute | solution.py:24
  40.8 6.6 %collective-permute-start.5 = (f32[32,4,1,256]{3,0,2,1:T(8,128)S(1)}, f32[32,4,1,256]{3,0,2,1:T(8,128)S(1)}, u32[]{:S(2)}, u32[]{:S(2)}) collective-permute-start(f32[32,4,1,256]{3,0,2,1:T(8,128)S(1)} %get-tuple-element.18), channel_id=1, source_target_pairs={{4,0},{8,4},{12,8},{16,12},{20,16},{24,20},{28,24},{32,28},{36,32}... | collective-permute-start | bytes 393224 | tf_op jit(solution)/shard_map/ppermute | solution.py:27
  51.0 13.8 %collective-permute-start.6 = (f32[32,4,1,256]{3,0,2,1:T(8,128)}, f32[32,4,1,256]{3,0,2,1:T(8,128)}, u32[]{:S(2)}, u32[]{:S(2)}) collective-permute-start(f32[32,4,1,256]{3,0,2,1:T(8,128)} %get-tuple-element.11), channel_id=1, source_target_pairs={{0,4},{4,8},{8,12},{12,16},{16,20},{20,24},{24,28},{28,32},{32,36}... | collective-permute-start | bytes 393224 | tf_op jit(solution)/shard_map/ppermute | solution.py:24
  52.9 11.9 %collective-permute-start.7 = (f32[32,4,1,256]{3,0,2,1:T(8,128)}, f32[32,4,1,256]{3,0,2,1:T(8,128)}, u32[]{:S(2)}, u32[]{:S(2)}) collective-permute-start(f32[32,4,1,256]{3,0,2,1:T(8,128)} %get-tuple-element.12), channel_id=1, source_target_pairs={{4,0},{8,4},{12,8},{16,12},{20,16},{24,20},{28,24},{32,28},{36,32}... | collective-permute-start | bytes 393224 | tf_op jit(solution)/shard_map/ppermute | solution.py:27
  70.8 5.7 %copy-start.18 = (f32[256,32]{1,0:T(8,128)S(1)}, f32[256,32]{1,0:T(8,128)}, u32[]{:S(2)}) copy-start(f32[256,32]{1,0:T(8,128)} %gather_fusion.1) | copy-start | bytes 98308
  70.8 5.7 %copy-start.25 = (f32[256]{0:T(256)S(1)}, f32[256]{0:T(256)}, u32[]{:S(2)}) copy-start(f32[256]{0:T(256)} %get-tuple-element.45) | copy-start | bytes 3076
  70.8 5.7 %copy-start.26 = (pred[256]{0:T(512)(128)(4,1)S(1)}, pred[256]{0:T(512)(128)(4,1)}, u32[]{:S(2)}) copy-start(pred[256]{0:T(512)(128)(4,1)} %get-tuple-element.44) | copy-start | bytes 772
  70.8 5.7 %copy-start.29 = (s32[256]{0:T(256)S(1)}, s32[256]{0:T(256)}, u32[]{:S(2)}) copy-start(s32[256]{0:T(256)} %param.21) | copy-start | bytes 3076
  70.8 5.8 %copy-start.30 = (f32[1,256]{1,0:T(1,128)S(1)}, f32[1,256]{1,0:T(1,128)}, u32[]{:S(2)}) copy-start(f32[1,256]{1,0:T(1,128)} %fusion.34) | copy-start | bytes 3076
  (18 other events, 29.1 us)

commit v3 on v2

--- a/solution.py
+++ b/solution.py
@@ -109,27 +109,30 @@
     return values_in[:, :, rim_cut : values_in.shape[2] - rim_cut, :]
 
 
-def exchange_kernel(member_count, part_ref, obs_ref, spr_ref, noise_ref, full_ref,
-                    recv_a, mine, send_a, recv_a_sem, send_b, recv_b_sem):
+def exchange_kernel(member_count, part_ref, full_ref,
+                    recv_a, send_a, recv_a_sem, send_m, recv_m_sem, send_t, recv_t_sem):
     tile_count = part_ref.shape[0]
-    total = tile_count * member_count
     me_t = lax.axis_index("tile")
     me_m = lax.axis_index("member")
-    me = me_t * member_count + me_m
     mesh_ids = pl.DeviceIdType.MESH
 
     barrier = pltpu.get_barrier_semaphore()
 
-    def greet(k, carry):
-        peer = lax.rem(me + k, total)
+    def greet_tile(k, carry):
         pl.semaphore_signal(
-            barrier, 1, device_id=(peer // member_count, lax.rem(peer, member_count)),
-            device_id_type=mesh_ids,
-        )
-        return carry
-
-    lax.fori_loop(1, total, greet, 0)
-    pl.semaphore_wait(barrier, total - 1)
+            barrier, 1, device_id=(lax.rem(me_t + k, tile_count), me_m), device_id_type=mesh_ids
+        )
+        return carry
+
+    def greet_member(k, carry):
+        pl.semaphore_signal(
+            barrier, 1, device_id=(me_t, lax.rem(me_m + k, member_count)), device_id_type=mesh_ids
+        )
+        return carry
+
+    lax.fori_loop(1, tile_count, greet_tile, 0)
+    lax.fori_loop(1, member_count, greet_member, 0)
+    pl.semaphore_wait(barrier, tile_count + member_count - 2)
 
     def copy_a(dst_t, src_t):
         return pltpu.make_async_remote_copy(
@@ -157,57 +160,78 @@
 
     lax.fori_loop(1, tile_count, wait_a_send, 0)
 
-    innov = (obs_ref[...] - acc) / spr_ref[...] + noise_ref[...]
-    mine[0] = acc
-    mine[1] = innov
-    full_ref[me_m, me_t, 0] = acc
-    full_ref[me_m, me_t, 1] = innov
-
-    def copy_b(dst, src):
+    full_ref[me_t, me_m] = acc
+
+    def copy_m(dst_m, src_m):
         return pltpu.make_async_remote_copy(
-            src_ref=mine, dst_ref=full_ref.at[lax.rem(src, member_count), src // member_count],
-            send_sem=send_b.at[dst], recv_sem=recv_b_sem.at[src],
-            device_id=(dst // member_count, lax.rem(dst, member_count)), device_id_type=mesh_ids,
-        )
-
-    def start_b(k, carry):
-        copy_b(lax.rem(me + k, total), me).start()
-        return carry
-
-    lax.fori_loop(1, total, start_b, 0)
-
-    def wait_b(k, carry):
-        copy_b(me, lax.rem(me + k, total)).wait_recv()
-        return carry
-
-    lax.fori_loop(1, total, wait_b, 0)
-
-    def wait_b_send(k, carry):
-        copy_b(lax.rem(me + k, total), me).wait_send()
-        return carry
-
-    lax.fori_loop(1, total, wait_b_send, 0)
-
-
-def rates_exchange(pieces, obs_blk, spr_blk, noise_blk, member_count):
+            src_ref=full_ref.at[me_t, src_m], dst_ref=full_ref.at[me_t, src_m],
+            send_sem=send_m.at[dst_m], recv_sem=recv_m_sem.at[src_m],
+            device_id=(me_t, dst_m), device_id_type=mesh_ids,
+        )
+
+    def start_m(k, carry):
+        copy_m(lax.rem(me_m + k, member_count), me_m).start()
+        return carry
+
+    lax.fori_loop(1, member_count, start_m, 0)
+
+    def wait_m(k, carry):
+        copy_m(me_m, lax.rem(me_m + k, member_count)).wait_recv()
+        return carry
+
+    lax.fori_loop(1, member_count, wait_m, 0)
+
+    def wait_m_send(k, carry):
+        copy_m(lax.rem(me_m + k, member_count), me_m).wait_send()
+        return carry
+
+    lax.fori_loop(1, member_count, wait_m_send, 0)
+
+    def copy_t(dst_t, src_t):
+        return pltpu.make_async_remote_copy(
+            src_ref=full_ref.at[src_t], dst_ref=full_ref.at[src_t],
+            send_sem=send_t.at[dst_t], recv_sem=recv_t_sem.at[src_t],
+            device_id=(dst_t, me_m), device_id_type=mesh_ids,
+        )
+
+    def start_t(k, carry):
+        copy_t(lax.rem(me_t + k, tile_count), me_t).start()
+        return carry
+
+    lax.fori_loop(1, tile_count, start_t, 0)
+
+    def wait_t(k, carry):
+        copy_t(me_t, lax.rem(me_t + k, tile_count)).wait_recv()
+        return carry
+
+    lax.fori_loop(1, tile_count, wait_t, 0)
+
+    def wait_t_send(k, carry):
+        copy_t(lax.rem(me_t + k, tile_count), me_t).wait_send()
+        return carry
+
+    lax.fori_loop(1, tile_count, wait_t_send, 0)
+
+
+def rates_exchange(pieces, member_count):
     tile_count, rows, lanes = pieces.shape
-    total = tile_count * member_count
     vmem = pl.BlockSpec(memory_space=pltpu.VMEM)
     return pl.pallas_call(
         functools.partial(exchange_kernel, member_count),
-        out_shape=jax.ShapeDtypeStruct((member_count, tile_count, 2, rows, lanes), jnp.float32),
-        in_specs=[vmem] * 4,
+        out_shape=jax.ShapeDtypeStruct((tile_count, member_count, rows, lanes), jnp.float32),
+        in_specs=[vmem],
         out_specs=vmem,
         scratch_shapes=[
             pltpu.VMEM((tile_count, rows, lanes), jnp.float32),
-            pltpu.VMEM((2, rows, lanes), jnp.float32),
             pltpu.SemaphoreType.DMA((tile_count,)),
             pltpu.SemaphoreType.DMA((tile_count,)),
-            pltpu.SemaphoreType.DMA((total,)),
-            pltpu.SemaphoreType.DMA((total,)),
+            pltpu.SemaphoreType.DMA((member_count,)),
+            pltpu.SemaphoreType.DMA((member_count,)),
+            pltpu.SemaphoreType.DMA((tile_count,)),
+            pltpu.SemaphoreType.DMA((tile_count,)),
         ],
         compiler_params=pltpu.CompilerParams(collective_id=0, has_side_effects=True),
-    )(pieces, obs_blk, spr_blk, noise_blk)
+    )(pieces)
 
 
 def per_device(
@@ -264,31 +288,25 @@
     member_root = (members - 1) ** 0.5
     spread = jnp.sqrt(INFLATION * obs_var)
     member_count = lax.axis_size("member")
-    well_first = tile_rank * well_share
-    spread_part = lax.dynamic_slice_in_dim(spread, well_first, well_share, 0)
-    observed_part = lax.dynamic_slice_in_dim(observed, well_first, well_share, 0)
-    noise_part = lax.dynamic_slice_in_dim(obs_noise, well_first, well_share, 1)
     block_rows = local_count * well_share // 128
     pieces = partial_rates.reshape(local_count, tile_count, well_share).transpose(1, 0, 2)
     pieces = pieces.reshape(tile_count, block_rows, 128)
-    obs_blk = jnp.broadcast_to(observed_part[None, :], (local_count, well_share)).reshape(block_rows, 128)
-    spr_blk = jnp.broadcast_to(spread_part[None, :], (local_count, well_share)).reshape(block_rows, 128)
-    noise_blk = noise_part.reshape(block_rows, 128)
-    full = rates_exchange(pieces, obs_blk, spr_blk, noise_blk, member_count)
-    full = full.reshape(member_count, tile_count, 2, local_count, well_share)
-    rates_all = full[:, :, 0].transpose(0, 2, 1, 3).reshape(members, well_count)
-    innov_all = full[:, :, 1].transpose(0, 2, 1, 3).reshape(members, well_count)
-    own_block = lax.dynamic_index_in_dim(
-        lax.dynamic_index_in_dim(full, member_rank, 0, keepdims=False), tile_rank, 0, keepdims=False
-    )
-    well_rates = own_block[0]
+    full = rates_exchange(pieces, member_count)
+    full = full.reshape(tile_count, member_count, local_count, well_share)
+    rates_all = full.transpose(1, 2, 0, 3).reshape(members, well_count)
+    well_rates = lax.dynamic_index_in_dim(
+        lax.dynamic_index_in_dim(full, tile_rank, 0, keepdims=False), member_rank, 0, keepdims=False
+    )
+    rates_own = lax.dynamic_index_in_dim(full, member_rank, 1, keepdims=False)
+    rates_own = rates_own.transpose(1, 0, 2).reshape(local_count, well_count)
+    innov_own = (observed - rates_own) / spread + obs_noise
     mean_rate = jnp.sum(rates_all, 0) / members
     scaled_all = (rates_all - mean_rate) / (spread * member_root)
     gram_matrix = jnp.dot(
         scaled_all, scaled_all.T, precision=lax.Precision.HIGHEST, preferred_element_type=jnp.float32
     )
     cross_matrix = jnp.dot(
-        scaled_all, innov_all.T, precision=lax.Precision.HIGHEST, preferred_element_type=jnp.float32
+        scaled_all, innov_own.T, precision=lax.Precision.HIGHEST, preferred_element_type=jnp.float32
     )
     weights_low = solve_spd(gram_matrix, cross_matrix).astype(jnp.bfloat16)
     anomaly = (log_perm / member_root).astype(jnp.bfloat16).reshape(local_count, cell_count)
@@ -297,12 +315,10 @@
         pairs = [(i, (i + shift) % member_count) for i in range(member_count)]
         anomaly_parts.append(lax.ppermute(anomaly, "member", pairs))
     anomaly_all = jnp.concatenate(anomaly_parts, axis=0)
-    first_member = member_rank * local_count
-    own_cols = lax.dynamic_slice_in_dim(weights_low, first_member, local_count, 1)
     own_cols = jnp.concatenate(
         [
             lax.dynamic_slice_in_dim(
-                own_cols, lax.rem(member_rank - shift + member_count, member_count) * local_count,
+                weights_low, lax.rem(member_rank - shift + member_count, member_count) * local_count,
                 local_count, 0,
             )
             for shift in range(member_count)

time: 173 us -> 157 us (0.908)
  Pallas kernels: 41.1 us -> 31.2 us
  local copies, waits for them, and re-layouts: 46.5 us -> 41.5 us
    pallas_call x1, Pallas kernels: 41.1 us -> 31.2 us  [rates_exchange(): pl.pallas_call(functools.partial(exchange_kernel, member_count), out_shap...]
    transpose x2, local copies, waits for them, and re-layouts: 6.1 us -> 2.99 us  [per_device(): rates_own = rates_own.transpose(1, 0, 2).reshape(local_count, well_count)]
    broadcast_in_dim x6 -> x0, local copies, waits for them, and re-layouts: 2.4 us -> none  [the longest x3 1.2 us: per_device(): jnp.broadcast_to(observed_part[None, :], (local_count, well_share))]
    reshape x3 -> x4, local copies, waits for them, and re-layouts: 6.15 us -> 8.54 us  [the longest x2 4.16 us: per_device(): full = full.reshape(tile_count, member_count, local_count, well_share)]
    div x1, other arithmetic: 0.39 us -> 2.54 us  [per_device(): scaled_all = (rates_all - mean_rate) / (spread * member_root)]
    div x3 -> x2, local copies, waits for them, and re-layouts: 3.08 us -> 3.74 us  [per_device(): scaled_all = (rates_all - mean_rate) / (spread * member_root)]
    unnamed x67 -> x59, local copies, waits for them, and re-layouts: 6.83 us -> 7.42 us
  transfers between devices with their start and end apart: 11 -> 11, of which waited for: 2 -> 2; matrix products, arithmetic and copies ran while one was open for 51% -> 53% of each run, Pallas kernels for 24% -> 20%
where the time goes in v3:
time: 157 us; the launch traced here: 156 us
  local copies, waits for them, and re-layouts  41.5 us (26%)
  other arithmetic  41.3 us (26%)
  Pallas kernels  31.2 us (20%)
  starting transfers between devices  26.6 us (17%)
  waiting for transfers between devices  6.65 us (4%)
  matrix products  6.6 us (4%)
  between operations  2.05 us (1%)
    pallas_call x1, Pallas kernels, rates_exchange(): pl.pallas_call(functools.partial(exchange_kernel, member_count), out_shap...  31.2 us
    ppermute x4, starting transfers between devices, extended_2(): lax.ppermute(lax.slice_in_dim(block, block.shape[dim] - width, None, axis...  12.4 us
    another operation x3, other arithmetic, solve_spd(): jnp.linalg.cholesky(gram_matrix + jnp.eye(gram_matrix.shape[0], dtype=jnp...  12.4 us
    another operation x2, other arithmetic, solve_spd(): lax.linalg.triangular_solve(factor, halfway, left_side=True, lower=True,...  10.5 us
    ppermute x4, starting transfers between devices, extended_2(): lax.ppermute(lax.slice_in_dim(block, 0, width, axis=dim), axis, backward)  8.97 us
    unnamed x59, local copies, waits for them, and re-layouts  7.42 us
    ppermute x4, waiting for transfers between devices, extended_2(): lax.ppermute(lax.slice_in_dim(block, 0, width, axis=dim), axis, backward)  6.63 us
    ppermute x3, starting transfers between devices, per_device(): anomaly_parts.append(lax.ppermute(anomaly, 'member', pairs))  5.21 us
  transfers between devices with their start and end apart: 11, of which 2 were waited for; matrix products, arithmetic and copies ran while one was open for 53% of the time, Pallas kernels for 20%

profile of v3, /device:TPU:1, one launch (start us, length us, event | category | flops | bytes accessed | tf_op | source)
XLA Modules:
  0.0 156.0 jit_solution(4819088777694585518)
XLA Ops:
  3.2 3.6 %collective-permute-start.10 = (bf16[32,8192]{1,0:T(8,128)(2,1)}, bf16[32,8192]{1,0:T(8,128)(2,1)}, u32[]{:S(2)}, u32[]{:S(2)}) collective-permute-start(bf16[32,8192]{1,0:T(8,128)(2,1)} %bitcast.35), channel_id=1, source_target_pairs={{0,3},{1,0},{2,1},{3,2},{4,7},{5,4},{6,5},{7,6},{8,11},{9,8},{10,9... | collective-permute-start | bytes 1572872 | tf_op jit(solution)/shard_map/ppermute | solution.py:316
  8.4 4.9 %collective-permute-start.2 = (f32[2,4,1,256]{3,2,1,0:T(1,128)S(1)}, f32[2,4,1,256]{3,2,1,0:T(1,128)S(1)}, u32[]{:S(2)}, u32[]{:S(2)}) collective-permute-start(f32[2,4,1,256]{3,2,1,0:T(1,128)S(1)} %get-tuple-element.36), channel_id=1, source_target_pairs={{0,4},{4,8},{8,12},{12,16},{16,20},{20,24},{24,28},{28,32},{32,36}... | collective-permute-start | bytes 24584 | tf_op jit(solution)/shard_map/ppermute | solution.py:24
  13.5 2.1 %collective-permute-start.3 = (f32[2,4,1,256]{3,2,1,0:T(1,128)S(1)}, f32[2,4,1,256]{3,2,1,0:T(1,128)S(1)}, u32[]{:S(2)}, u32[]{:S(2)}) collective-permute-start(f32[2,4,1,256]{3,2,1,0:T(1,128)S(1)} %get-tuple-element.37), channel_id=1, source_target_pairs={{4,0},{8,4},{12,8},{16,12},{20,16},{24,20},{28,24},{32,28},{36,32}... | collective-permute-start | bytes 24584 | tf_op jit(solution)/shard_map/ppermute | solution.py:27
  20.0 3.6 %collective-permute-start = (f32[32,4,1,256]{3,0,2,1:T(8,128)S(1)}, f32[32,4,1,256]{3,0,2,1:T(8,128)S(1)}, u32[]{:S(2)}, u32[]{:S(2)}) collective-permute-start(f32[32,4,1,256]{3,0,2,1:T(8,128)S(1)} %get-tuple-element.19), channel_id=1, source_target_pairs={{0,4},{4,8},{8,12},{12,16},{16,20},{20,24},{24,28},{28,32},{32,36}... | collective-permute-start | bytes 393224 | tf_op jit(solution)/shard_map/ppermute | solution.py:24
  27.1 3.3 %collective-permute-done.1 = f32[32,4,1,256]{3,0,2,1:T(8,128)S(1)} collective-permute-done((f32[32,4,1,256]{3,0,2,1:T(8,128)S(1)}, f32[32,4,1,256]{3,0,2,1:T(8,128)S(1)}, u32[]{:S(2)}, u32[]{:S(2)}) %collective-permute-start.1) | collective-permute-done | bytes 131104 | tf_op jit(solution)/shard_map/ppermute | solution.py:27
  32.5 2.1 %fusion.11 = f32[32,4,10,256]{3,0,2,1:T(8,128)S(1)} fusion(f32[32,3,10,256]{3,0,2,1:T(8,128)S(1)} %divide_multiply_fusion.1, f32[32,3,10,256]{3,0,2,1:T(8,128)S(1)} %broadcast_in_dim.104, f32[32,3,10,256]{3,0,2,1:T(8,128)S(1)} %broadcast_in_dim.103, f32[32,4,10,255]{3,0,2,1:T(8,128)S(1)} %broadcast_in_dim.102, f32[32,4,10,255]{3,0,2,1:T(8,128)S(1)} %broadcast_in_dim.101, ...), kind=kLoop, calls=%fused_computation.23 | loop fusion | flops 6225920 | bytes 11797504 | tf_op jit(solution)/shard_map/div | solution.py:77
  36.6 2.4 %collective-permute-start.5 = (f32[32,4,1,256]{3,0,2,1:T(8,128)S(1)}, f32[32,4,1,256]{3,0,2,1:T(8,128)S(1)}, u32[]{:S(2)}, u32[]{:S(2)}) collective-permute-start(f32[32,4,1,256]{3,0,2,1:T(8,128)S(1)} %get-tuple-element.18), channel_id=1, source_target_pairs={{4,0},{8,4},{12,8},{16,12},{20,16},{24,20},{28,24},{32,28},{36,32}... | collective-permute-start | bytes 393224 | tf_op jit(solution)/shard_map/ppermute | solution.py:27
  39.8 3.3 %collective-permute-done.5 = f32[32,4,1,256]{3,0,2,1:T(8,128)S(1)} collective-permute-done((f32[32,4,1,256]{3,0,2,1:T(8,128)S(1)}, f32[32,4,1,256]{3,0,2,1:T(8,128)S(1)}, u32[]{:S(2)}, u32[]{:S(2)}) %collective-permute-start.5) | collective-permute-done | bytes 131104 | tf_op jit(solution)/shard_map/ppermute | solution.py:27
  44.0 2.1 %fusion.15 = f32[32,4,10,256]{3,0,2,1:T(8,128)S(1)} fusion(f32[32,3,10,256]{3,0,2,1:T(8,128)S(1)} %divide_multiply_fusion.1, f32[32,4,1,256]{3,0,2,1:T(8,128)S(1)} %collective-permute-done.5, f32[32,4,8,256]{3,0,2,1:T(8,128)S(1)} %slice.232, f32[32,4,1,256]{3,0,2,1:T(8,128)S(1)} %collective-permute-done.4, f32[32,3,10,256]{3,0,2,1:T(8,128)S(1)} %get-tuple-element.16, ...), kind=kLoop, calls=%fused_computation.27 | loop fusion | flops 8847360 | bytes 10748928 | tf_op jit(solution)/shard_map/div | solution.py:77
  48.8 2.6 %collective-permute-start.7 = (f32[32,4,1,256]{3,0,2,1:T(8,128)}, f32[32,4,1,256]{3,0,2,1:T(8,128)}, u32[]{:S(2)}, u32[]{:S(2)}) collective-permute-start(f32[32,4,1,256]{3,0,2,1:T(8,128)} %get-tuple-element.12), channel_id=1, source_target_pairs={{4,0},{8,4},{12,8},{16,12},{20,16},{24,20},{28,24},{32,28},{36,32}... | collective-permute-start | bytes 393224 | tf_op jit(solution)/shard_map/ppermute | solution.py:27
  52.1 2.7 %copy.37 = f32[32,4,8,256]{0,3,2,1:T(8,128)} copy(f32[32,4,8,256]{3,0,2,1:T(8,128)S(1)} %slice.239) | data formatting | bytes 2097152 | tf_op jit(solution)/shard_map/slice | solution.py:109
  56.4 3.5 %gather_fusion.1 = f32[256,32]{1,0:T(8,128)} fusion(f32[32,8192]{0,1:T(8,128)} %bitcast.91, s32[1024]{0:T(1024)S(1)} %pad_clamp_fusion), kind=kCustom, calls=%fused_computation.1.clone | custom fusion | bytes 66560 | tf_op jit(solution)/shard_map/jit(_take)/gather | solution.py:276
  65.8 2.7 %copy.36 = f32[32,4,8,256]{0,3,2,1:T(8,128)} copy(f32[32,4,8,256]{3,0,2,1:T(8,128)S(1)} %get-tuple-element.9) | data formatting | bytes 2097152 | tf_op jit(solution)/shard_map/mul | solution.py:273
  68.5 2.9 %gather_fusion = f32[256,32]{1,0:T(8,128)S(1)} fusion(f32[32,8192]{0,1:T(8,128)} %bitcast.90, s32[1024]{0:T(1024)S(1)} %pad_clamp_fusion), kind=kCustom, calls=%fused_computation.clone | custom fusion | bytes 66560 | tf_op jit(solution)/shard_map/jit(_take)/gather | solution.py:275
  73.4 31.2 %shard_map.147 = f32[32,4,8,128]{3,2,1,0:T(8,128)} custom-call(f32[32,8,128]{2,1,0:T(8,128)} %reshape.101.part_ref), custom_call_target="tpu_custom_call" | custom-call | tf_op jit(solution)/shard_map/pallas_call | solution.py:219
  107.5 2.6 %copy.54 = f32[32,4,32,32]{3,0,2,1:T(8,128)} copy(f32[32,4,32,32]{3,2,1,0:T(8,128)S(1)} %reshape.102) | data formatting | bytes 1048576 | tf_op jit(solution)/shard_map/reshape | solution.py:295
  111.0 2.5 %subtract_divide_fusion = f32[4,32,32,32]{3,2,1,0:T(8,128)} fusion(f32[32,32]{1,0:T(8,128)S(1)} %copy-done.13, f32[32,32]{1,0:T(8,128)S(1)} %broadcast_multiply_fusion, f32[32,4,32,32]{3,2,1,0:T(8,128)S(1)} %reshape.102), kind=kLoop, calls=%fused_computation.11 | loop fusion | flops 262144 | bytes 1056768 | tf_op jit(solution)/shard_map/div | solution.py:304
  113.5 3.1 %div.81 = f32[128,1024]{1,0:T(8,128)} reshape(f32[4,32,32,32]{3,2,1,0:T(8,128)} %subtract_divide_fusion) | data formatting | bytes 1048576 | tf_op jit(solution)/shard_map/div | solution.py:304
  118.5 11.7 %cholesky.17 = f32[128,128]{1,0:T(8,128)S(1)} custom-call(f32[128,128]{1,0:T(8,128)S(1)} %fusion.54), custom_call_target="Cholesky" | custom-call | tf_op jit(solution)/shard_map/jit(cholesky)/cholesky | solution.py:101
  131.5 9.8 %custom-call.8 = f32[1,128,128]{1,2,0:T(8,128)S(1)} custom-call(f32[1,128,128]{2,1,0:T(8,128)S(1)} %fusion.49), custom_call_target="InvertDiagBlocksLowerTriangular" | custom-call | tf_op jit(solution)/shard_map/triangular_solve | solution.py:103
  141.3 3.1 %reshape.103 = f32[128,1024]{1,0:T(8,128)} reshape(f32[4,32,32,32]{3,2,1,0:T(8,128)} %bitcast.89) | data formatting | bytes 1048576 | tf_op jit(solution)/shard_map/reshape | solution.py:296
  144.4 2.2 %copy.42 = f32[32,32,32]{2,1,0:T(8,128)} copy(f32[32,32,32]{2,0,1:T(8,128)} %dynamic-slice_bitcast_fusion) | data formatting | bytes 262144 | tf_op jit(solution)/shard_map/transpose | solution.py:301
  147.9 2.9 %copy.44 = f32[32,4,8,256]{3,2,1,0:T(8,128)} copy(f32[32,4,8,256]{3,0,2,1:T(8,128)} %get-tuple-element.10) | data formatting | bytes 2097152
  152.5 2.0 %fusion = f32[32,8192]{1,0:T(8,128)S(1)} fusion(bf16[32,8192]{1,0:T(8,128)(2,1)} %collective-permute-done.10, bf16[32,8192]{1,0:T(8,128)(2,1)} %collective-permute-done.9, bf16[32,8192]{1,0:T(8,128)(2,1)} %collective-permute-done.8, bf16[32,8192]{1,0:T(8,128)(2,1)} %bitcast.35, bf16[32,32]{0,1:T(8,128)(2,1)S(1)} %get-tuple-element.39, ...), kind=kOutput, calls=%fused_computation.2 | convolution fusion | flops 75530240 | bytes 3153920 | tf_op jit(solution)/shard_map/dot_general | solution.py:329
  (139 shorter events, 41.1 us)
Async XLA Ops:
  0.6 17.5 %copy-start = (f32[1024]{0:T(1024)S(1)}, f32[1024]{0:T(1024)}, u32[]{:S(2)}) copy-start(f32[1024]{0:T(1024)} %param.19) | copy-start | bytes 12292
  0.6 14.9 %copy-start.1 = (f32[32,4,8,256]{3,2,1,0:T(8,128)S(1)}, f32[32,4,8,256]{3,2,1,0:T(8,128)}, u32[]{:S(2)}) copy-start(f32[32,4,8,256]{3,2,1,0:T(8,128)} %param.14) | copy-start | bytes 3145732
  0.7 7.8 %copy-start.3 = (f32[4,8,256]{2,1,0:T(8,128)S(1)}, f32[4,8,256]{2,1,0:T(8,128)}, u32[]{:S(2)}) copy-start(f32[4,8,256]{2,1,0:T(8,128)} %param.15) | copy-start | bytes 98308
  0.7 7.8 %copy-start.12 = (f32[4,8,256]{2,1,0:T(8,128)S(1)}, f32[4,8,256]{2,1,0:T(8,128)}, u32[]{:S(2)}) copy-start(f32[4,8,256]{2,1,0:T(8,128)} %param.16) | copy-start | bytes 98308
  3.2 149.3 %collective-permute-start.10 = (bf16[32,8192]{1,0:T(8,128)(2,1)}, bf16[32,8192]{1,0:T(8,128)(2,1)}, u32[]{:S(2)}, u32[]{:S(2)}) collective-permute-start(bf16[32,8192]{1,0:T(8,128)(2,1)} %bitcast.35), channel_id=1, source_target_pairs={{0,3},{1,0},{2,1},{3,2},{4,7},{5,4},{6,5},{7,6},{8,11},{9,8},{10,9... | collective-permute-start | bytes 1572872 | tf_op jit(solution)/shard_map/ppermute | solution.py:316
  6.8 145.7 %collective-permute-start.8 = (bf16[32,8192]{1,0:T(8,128)(2,1)}, bf16[32,8192]{1,0:T(8,128)(2,1)}, u32[]{:S(2)}, u32[]{:S(2)}) collective-permute-start(bf16[32,8192]{1,0:T(8,128)(2,1)} %bitcast.35), channel_id=1, source_target_pairs={{0,1},{1,2},{2,3},{3,0},{4,5},{5,6},{6,7},{7,4},{8,9},{9,10},{10,1... | collective-permute-start | bytes 1572872 | tf_op jit(solution)/shard_map/ppermute | solution.py:316
  6.8 145.8 %collective-permute-start.9 = (bf16[32,8192]{1,0:T(8,128)(2,1)}, bf16[32,8192]{1,0:T(8,128)(2,1)}, u32[]{:S(2)}, u32[]{:S(2)}) collective-permute-start(bf16[32,8192]{1,0:T(8,128)(2,1)} %bitcast.35), channel_id=1, source_target_pairs={{0,2},{1,3},{2,0},{3,1},{4,6},{5,7},{6,4},{7,5},{8,10},{9,11},{10,... | collective-permute-start | bytes 1572872 | tf_op jit(solution)/shard_map/ppermute | solution.py:316
  8.4 11.6 %collective-permute-start.2 = (f32[2,4,1,256]{3,2,1,0:T(1,128)S(1)}, f32[2,4,1,256]{3,2,1,0:T(1,128)S(1)}, u32[]{:S(2)}, u32[]{:S(2)}) collective-permute-start(f32[2,4,1,256]{3,2,1,0:T(1,128)S(1)} %get-tuple-element.36), channel_id=1, source_target_pairs={{0,4},{4,8},{8,12},{12,16},{16,20},{20,24},{24,28},{28,32},{32,36}... | collective-permute-start | bytes 24584 | tf_op jit(solution)/shard_map/ppermute | solution.py:24
  13.4 4.6 %copy-start.16 = (f32[1024]{0:T(1024)S(1)}, f32[1024]{0:T(1024)}, u32[]{:S(2)}) copy-start(f32[1024]{0:T(1024)} %param.24) | copy-start | bytes 12292
  13.4 4.7 %copy-start.24 = (s32[256]{0:T(256)S(1)}, s32[256]{0:T(256)}, u32[]{:S(2)}) copy-start(s32[256]{0:T(256)} %param.21) | copy-start | bytes 3076
  13.5 10.2 %collective-permute-start.3 = (f32[2,4,1,256]{3,2,1,0:T(1,128)S(1)}, f32[2,4,1,256]{3,2,1,0:T(1,128)S(1)}, u32[]{:S(2)}, u32[]{:S(2)}) collective-permute-start(f32[2,4,1,256]{3,2,1,0:T(1,128)S(1)} %get-tuple-element.37), channel_id=1, source_target_pairs={{4,0},{8,4},{12,8},{16,12},{20,16},{24,20},{28,24},{32,28},{36,32}... | collective-permute-start | bytes 24584 | tf_op jit(solution)/shard_map/ppermute | solution.py:27
  20.0 7.0 %collective-permute-start = (f32[32,4,1,256]{3,0,2,1:T(8,128)S(1)}, f32[32,4,1,256]{3,0,2,1:T(8,128)S(1)}, u32[]{:S(2)}, u32[]{:S(2)}) collective-permute-start(f32[32,4,1,256]{3,0,2,1:T(8,128)S(1)} %get-tuple-element.19), channel_id=1, source_target_pairs={{0,4},{4,8},{8,12},{12,16},{16,20},{20,24},{24,28},{28,32},{32,36}... | collective-permute-start | bytes 393224 | tf_op jit(solution)/shard_map/ppermute | solution.py:24
  23.7 6.7 %collective-permute-start.1 = (f32[32,4,1,256]{3,0,2,1:T(8,128)S(1)}, f32[32,4,1,256]{3,0,2,1:T(8,128)S(1)}, u32[]{:S(2)}, u32[]{:S(2)}) collective-permute-start(f32[32,4,1,256]{3,0,2,1:T(8,128)S(1)} %get-tuple-element.20), channel_id=1, source_target_pairs={{4,0},{8,4},{12,8},{16,12},{20,16},{24,20},{28,24},{32,28},{36,32}... | collective-permute-start | bytes 393224 | tf_op jit(solution)/shard_map/ppermute | solution.py:27
  34.6 5.2 %collective-permute-start.4 = (f32[32,4,1,256]{3,0,2,1:T(8,128)S(1)}, f32[32,4,1,256]{3,0,2,1:T(8,128)S(1)}, u32[]{:S(2)}, u32[]{:S(2)}) collective-permute-start(f32[32,4,1,256]{3,0,2,1:T(8,128)S(1)} %get-tuple-element.17), channel_id=1, source_target_pairs={{0,4},{4,8},{8,12},{12,16},{16,20},{20,24},{24,28},{28,32},{32,36}... | collective-permute-start | bytes 393224 | tf_op jit(solution)/shard_map/ppermute | solution.py:24
  36.6 6.6 %collective-permute-start.5 = (f32[32,4,1,256]{3,0,2,1:T(8,128)S(1)}, f32[32,4,1,256]{3,0,2,1:T(8,128)S(1)}, u32[]{:S(2)}, u32[]{:S(2)}) collective-permute-start(f32[32,4,1,256]{3,0,2,1:T(8,128)S(1)} %get-tuple-element.18), channel_id=1, source_target_pairs={{4,0},{8,4},{12,8},{16,12},{20,16},{24,20},{28,24},{32,28},{36,32}... | collective-permute-start | bytes 393224 | tf_op jit(solution)/shard_map/ppermute | solution.py:27
  46.9 13.0 %collective-permute-start.6 = (f32[32,4,1,256]{3,0,2,1:T(8,128)}, f32[32,4,1,256]{3,0,2,1:T(8,128)S(1)}, u32[]{:S(2)}, u32[]{:S(2)}) collective-permute-start(f32[32,4,1,256]{3,0,2,1:T(8,128)} %get-tuple-element.11), channel_id=1, source_target_pairs={{0,4},{4,8},{8,12},{12,16},{16,20},{20,24},{24,28},{28,32},{32,36}... | collective-permute-start | bytes 393224 | tf_op jit(solution)/shard_map/ppermute | solution.py:24
  48.8 11.1 %collective-permute-start.7 = (f32[32,4,1,256]{3,0,2,1:T(8,128)}, f32[32,4,1,256]{3,0,2,1:T(8,128)}, u32[]{:S(2)}, u32[]{:S(2)}) collective-permute-start(f32[32,4,1,256]{3,0,2,1:T(8,128)} %get-tuple-element.12), channel_id=1, source_target_pairs={{4,0},{8,4},{12,8},{16,12},{20,16},{24,20},{28,24},{32,28},{36,32}... | collective-permute-start | bytes 393224 | tf_op jit(solution)/shard_map/ppermute | solution.py:27
  65.8 5.6 %copy-start.15 = (f32[256,32]{1,0:T(8,128)S(1)}, f32[256,32]{1,0:T(8,128)}, u32[]{:S(2)}) copy-start(f32[256,32]{1,0:T(8,128)} %gather_fusion.1) | copy-start | bytes 98308
  65.8 5.6 %copy-start.20 = (f32[256]{0:T(256)S(1)}, f32[256]{0:T(256)}, u32[]{:S(2)}) copy-start(f32[256]{0:T(256)} %get-tuple-element.45) | copy-start | bytes 3076
  65.8 5.6 %copy-start.21 = (pred[256]{0:T(512)(128)(4,1)S(1)}, pred[256]{0:T(512)(128)(4,1)}, u32[]{:S(2)}) copy-start(pred[256]{0:T(512)(128)(4,1)} %get-tuple-element.44) | copy-start | bytes 772
  65.8 5.6 %copy-start.25 = (s32[256]{0:T(256)S(1)}, s32[256]{0:T(256)}, u32[]{:S(2)}) copy-start(s32[256]{0:T(256)} %param.21) | copy-start | bytes 3076
  65.8 5.6 %copy-start.26 = (f32[1,256]{1,0:T(1,128)S(1)}, f32[1,256]{1,0:T(1,128)}, u32[]{:S(2)}) copy-start(f32[1,256]{1,0:T(1,128)} %fusion.33) | copy-start | bytes 3076
  146.6 4.8 %copy-start.22 = (f32[32,1024]{1,0:T(8,128)S(1)}, f32[32,1024]{1,0:T(8,128)}, u32[]{:S(2)}) copy-start(f32[32,1024]{1,0:T(8,128)} %param.25) | copy-start | bytes 393220
  146.6 4.8 %copy-start.23 = (f32[1024]{0:T(1024)S(1)}, f32[1024]{0:T(1024)}, u32[]{:S(2)}) copy-start(f32[1024]{0:T(1024)} %param.23) | copy-start | bytes 12292
  (14 other events, 28.1 us)

commit v4 on v3

--- a/solution.py
+++ b/solution.py
@@ -211,6 +211,43 @@
         return carry
 
     lax.fori_loop(1, tile_count, wait_t_send, 0)
+
+
+def halo_kernel(out_ref, in_ref, send_sem, recv_sem):
+    tile_count = lax.axis_size("tile")
+    me_t = lax.axis_index("tile")
+    me_m = lax.axis_index("member")
+    mesh_ids = pl.DeviceIdType.MESH
+    left = lax.rem(me_t + tile_count - 1, tile_count)
+    right = lax.rem(me_t + 1, tile_count)
+    barrier = pltpu.get_barrier_semaphore()
+    for peer in (left, right):
+        pl.semaphore_signal(barrier, 1, device_id=(peer, me_m), device_id_type=mesh_ids)
+    pl.semaphore_wait(barrier, 2)
+    to_right = pltpu.make_async_remote_copy(
+        src_ref=out_ref.at[1], dst_ref=in_ref.at[0], send_sem=send_sem.at[1],
+        recv_sem=recv_sem.at[0], device_id=(right, me_m), device_id_type=mesh_ids,
+    )
+    to_left = pltpu.make_async_remote_copy(
+        src_ref=out_ref.at[0], dst_ref=in_ref.at[1], send_sem=send_sem.at[0],
+        recv_sem=recv_sem.at[1], device_id=(left, me_m), device_id_type=mesh_ids,
+    )
+    to_right.start()
+    to_left.start()
+    to_right.wait()
+    to_left.wait()
+
+
+def halo_exchange(outgoing):
+    vmem = pl.BlockSpec(memory_space=pltpu.VMEM)
+    return pl.pallas_call(
+        halo_kernel,
+        out_shape=jax.ShapeDtypeStruct(outgoing.shape, outgoing.dtype),
+        in_specs=[vmem],
+        out_specs=vmem,
+        scratch_shapes=[pltpu.SemaphoreType.DMA((2,)), pltpu.SemaphoreType.DMA((2,))],
+        compiler_params=pltpu.CompilerParams(collective_id=1, has_side_effects=True),
+    )(outgoing)
 
 
 def rates_exchange(pieces, member_count):
@@ -255,20 +292,44 @@
     well_share = well_count // tile_count
     tile_rank = lax.axis_index("tile")
     member_rank = lax.axis_index("member")
-    permeab = jnp.exp(extended_2(log_perm, (("tile", 2),), 1))
-    shared = extended_2(jnp.stack([start_pressure, start_sat]), (("tile", 2),), 1)
-    column = tile_rank * strip_width - 1 + jnp.arange(strip_width + 2 * 1, dtype=jnp.int32)
-    face_sets = face_terms(
-        permeab, ((column >= 0) & (column < strip_width * tile_count)).astype(jnp.float32)
-    )
-    baseline = jnp.pad(source + storage * start_pressure, ((0, 0), (1, 1), (0, 0)))[None]
-    storage_term = jnp.pad(storage, ((0, 0), (1, 1), (0, 0)), constant_values=1.0)[None]
-    extended = jnp.broadcast_to(shared[0:1], (local_count,) + shared.shape[1:])
+    rim = SWEEPS + 1
+    fields = jnp.stack([start_pressure, start_sat, source, storage])
+    halo_rows = local_count * layers * rim + fields.shape[0] * layers * rim
+
+    def rim_rows(first):
+        return jnp.concatenate(
+            [
+                lax.slice_in_dim(log_perm, first, first + rim, axis=2).reshape(-1, strip_depth),
+                lax.slice_in_dim(fields, first, first + rim, axis=2).reshape(-1, strip_depth),
+            ]
+        )
+
+    outgoing = jnp.stack([rim_rows(0), rim_rows(strip_width - rim)])
+    incoming = halo_exchange(outgoing)
+    lp_count = local_count * layers * rim
+
+    def unpack(side):
+        lp_part = incoming[side, :lp_count].reshape(local_count, layers, rim, strip_depth)
+        field_part = incoming[side, lp_count:].reshape(fields.shape[0], layers, rim, strip_depth)
+        return lp_part, field_part
+
+    low_lp, low_fields = unpack(0)
+    high_lp, high_fields = unpack(1)
+    lp_ext = jnp.concatenate([low_lp, log_perm, high_lp], axis=2)
+    fields_ext = jnp.concatenate([low_fields, fields, high_fields], axis=2)
+    permeab = jnp.exp(lp_ext)
+    column = tile_rank * strip_width - rim + jnp.arange(strip_width + 2 * rim, dtype=jnp.int32)
+    inside = (column >= 0) & (column < strip_width * tile_count)
+    face_sets = face_terms(permeab, inside.astype(jnp.float32))
+    press_ext, sat_ext, source_ext, storage_ext = (fields_ext[i] for i in range(4))
+    baseline = (source_ext + storage_ext * press_ext)[None]
+    storage_term = jnp.where(inside[None, :, None], storage_ext, 1.0)[None]
+    pressure = jnp.broadcast_to(press_ext[None], (local_count,) + press_ext.shape)
     for sweep_idx in range(SWEEPS):
-        pressure = trim_rim(jacobi(extended, baseline, storage_term, face_sets), 1)
-        extended = extended_2(pressure, (("tile", 2),), 1)
-    saturation = trim_rim(transport(extended, shared[1:2], face_sets), 1)
-    permeab = trim_rim(permeab, 1)
+        pressure = jacobi(pressure, baseline, storage_term, face_sets)
+    saturation = trim_rim(transport(pressure, sat_ext[None], face_sets), rim)
+    pressure = trim_rim(pressure, rim)
+    permeab = trim_rim(permeab, rim)
     cell_count = layers * strip_width * strip_depth
     mobility = (permeab * water_frac(saturation)).reshape(local_count, cell_count)
     cell_press = pressure.reshape(local_count, cell_count)

time: 157 us -> 135 us (0.86)
  starting transfers between devices: 26.6 us -> 5.81 us
  Pallas kernels: 31.2 us -> 38.2 us
  waiting for transfers between devices: 6.65 us -> 0.01 us
  local copies, waits for them, and re-layouts: 41.5 us -> 36.5 us
  other arithmetic: 41.3 us -> 45.2 us
    ppermute x8 -> x0, starting transfers between devices: 21.4 us -> none  [the longest x4 12.4 us: extended_2(): lax.ppermute(lax.slice_in_dim(block, block.shape[dim] - width, None, axis...]
    pallas_call x0 -> x1, Pallas kernels: none -> 11.6 us  [halo_exchange(): pl.pallas_call(halo_kernel, out_shape=jax.ShapeDtypeStruct(outgoing.shape...]
    ppermute x8 -> x0, waiting for transfers between devices: 6.64 us -> none  [the longest x4 6.63 us: extended_2(): lax.ppermute(lax.slice_in_dim(block, 0, width, axis=dim), axis, backward)]
    unnamed x59 -> x32, local copies, waits for them, and re-layouts: 7.42 us -> 2.01 us
    pallas_call x1, Pallas kernels: 31.2 us -> 26.7 us  [rates_exchange(): pl.pallas_call(functools.partial(exchange_kernel, member_count), out_shap...]
    div x2, other arithmetic: 4.26 us -> 6.78 us  [jacobi(): return (baseline + flow_sum) / (storage_term + weight_sum)]
    broadcast_in_dim x3, local copies, waits for them, and re-layouts: 2.03 us -> 0.1 us  [transport(): carried = velocity * jnp.where(velocity > 0, lower_frac, upper_frac)]
    slice x5 -> x6, local copies, waits for them, and re-layouts: 0.82 us -> 2.66 us  [slide_by(): remain = lax.slice_in_dim(values_in, 0, extent - 1, axis=along_dim)]
  transfers between devices with their start and end apart: 11 -> 3, of which waited for: 2 -> 0; matrix products, arithmetic and copies ran while one was open for 53% -> 61% of each run, Pallas kernels for 20% -> 28%
where the time goes in v4:
time: 135 us
  other arithmetic  45.2 us (33%)
  Pallas kernels  38.2 us (28%)
  local copies, waits for them, and re-layouts  36.5 us (27%)
  matrix products  7.05 us (5%)
  starting transfers between devices  5.81 us (4%)
  between operations  1.95 us (1%)
    pallas_call x1, Pallas kernels, rates_exchange(): pl.pallas_call(functools.partial(exchange_kernel, member_count), out_shap...  26.7 us
    another operation x3, other arithmetic, solve_spd(): jnp.linalg.cholesky(gram_matrix + jnp.eye(gram_matrix.shape[0], dtype=jnp...  12.4 us
    pallas_call x1, Pallas kernels, halo_exchange(): pl.pallas_call(halo_kernel, out_shape=jax.ShapeDtypeStruct(outgoing.shape...  11.6 us
    another operation x2, other arithmetic, solve_spd(): lax.linalg.triangular_solve(factor, halfway, left_side=True, lower=True,...  10.5 us
    div x2, other arithmetic, jacobi(): return (baseline + flow_sum) / (storage_term + weight_sum)  6.78 us
    ppermute x3, starting transfers between devices, per_device(): anomaly_parts.append(lax.ppermute(anomaly, 'member', pairs))  5.81 us
    reshape x2, local copies, waits for them, and re-layouts, per_device(): full = full.reshape(tile_count, member_count, local_count, well_share)  4.15 us
    div x2, local copies, waits for them, and re-layouts, per_device(): scaled_all = (rates_all - mean_rate) / (spread * member_root)  3.13 us
  transfers between devices with their start and end apart: 3, of which 0 were waited for; matrix products, arithmetic and copies ran while one was open for 61% of the time, Pallas kernels for 28%

profile of v4, /device:TPU:1, one launch (start us, length us, event | category | flops | bytes accessed | tf_op | source)
XLA Modules:
  0.0 134.7 jit_solution(1909777948090040791)
XLA Ops:
  0.7 1.4 %multiply_convert_fusion = bf16[32,4,8,256]{3,2,1,0:T(8,128)(2,1)S(1)} fusion(f32[32,4,8,256]{3,2,1,0:T(8,128)} %param.14), kind=kLoop, calls=%fused_computation.54 | loop fusion | flops 524288 | bytes 1572864 | tf_op jit(solution)/shard_map/convert_element_type | solution.py:373
  3.2 2.1 %collective-permute-start = (bf16[32,8192]{1,0:T(8,128)(2,1)}, bf16[32,8192]{1,0:T(8,128)(2,1)}, u32[]{:S(2)}, u32[]{:S(2)}) collective-permute-start(bf16[32,8192]{1,0:T(8,128)(2,1)} %bitcast.41), channel_id=1, source_target_pairs={{0,1},{1,2},{2,3},{3,0},{4,5},{5,6},{6,7},{7,4},{8,9},{9,10},{10,1... | collective-permute-start | bytes 1572872 | tf_op jit(solution)/shard_map/ppermute | solution.py:377
  5.3 2.6 %collective-permute-start.1 = (bf16[32,8192]{1,0:T(8,128)(2,1)}, bf16[32,8192]{1,0:T(8,128)(2,1)}, u32[]{:S(2)}, u32[]{:S(2)}) collective-permute-start(bf16[32,8192]{1,0:T(8,128)(2,1)} %bitcast.41), channel_id=1, source_target_pairs={{0,2},{1,3},{2,0},{3,1},{4,6},{5,7},{6,4},{7,5},{8,10},{9,11},{10,... | collective-permute-start | bytes 1572872 | tf_op jit(solution)/shard_map/ppermute | solution.py:377
  10.9 11.6 %shard_map.147 = f32[2,432,256]{2,1,0:T(8,128)} custom-call(f32[2,432,256]{2,1,0:T(8,128)} %pad_maximum_fusion.out_ref), custom_call_target="tpu_custom_call" | custom-call | tf_op jit(solution)/shard_map/pallas_call | solution.py:243
  29.1 3.5 %fusion.3 = f32[32,4,14,256]{3,2,1,0:T(8,128)S(1)} fusion(f32[32,3,14,256]{3,2,1,0:T(8,128)S(1)} %divide_multiply_fusion.1, f32[32,3,14,256]{3,2,1,0:T(8,128)S(1)} %broadcast_in_dim.117, f32[32,3,14,256]{3,2,1,0:T(8,128)S(1)} %broadcast_in_dim.116, f32[32,4,14,255]{3,2,1,0:T(8,128)S(1)} %broadcast_in_dim.115, f32[32,4,14,255]{3,2,1,0:T(8,128)S(1)} %broadcast_in_dim.114, ...), kind=kLoop, calls=%fused_computation.11 | loop fusion | flops 8716288 | bytes 16673792 | tf_op jit(solution)/shard_map/div | solution.py:77
  35.0 3.3 %fusion.7 = f32[32,4,14,256]{3,2,1,0:T(8,128)S(1)} fusion(f32[32,3,14,256]{3,2,1,0:T(8,128)S(1)} %divide_multiply_fusion.1, f32[32,3,14,256]{3,2,1,0:T(8,128)S(1)} %get-tuple-element.12, f32[32,3,14,256]{3,2,1,0:T(8,128)S(1)} %get-tuple-element.11, f32[32,4,14,255]{3,2,1,0:T(8,128)S(1)} %get-tuple-element.10, f32[32,4,14,255]{3,2,1,0:T(8,128)S(1)} %get-tuple-element.9, ...), kind=kLoop, calls=%fused_computation.15 | loop fusion | flops 8716288 | bytes 16673792 | tf_op jit(solution)/shard_map/div | solution.py:77
  41.6 2.2 %fusion.20 = (f32[32,4,8,256]{3,2,1,0:T(8,128)S(1)}, f32[32,4,8,256]{3,2,1,0:T(8,128)}) fusion(f32[32,4,14,256]{3,2,1,0:T(8,128)S(1)} %maximum_exponential_fusion, f32[32,3,14,256]{3,2,1,0:T(8,128)S(1)} %select_multiply_fusion.2, f32[32,4,14,255]{3,2,1,0:T(8,128)S(1)} %select_multiply_fusion, f32[32,4,13,256]{3,2,1,0:T(8,128)S(1)} %select_multiply_fusion.1, ...), kind=kLoop, calls=%fused_computation.46 | loop fusion | flops 3670016 | bytes 8086528 | tf_op jit(solution)/shard_map/mul | solution.py:334
  43.9 2.7 %copy.26 = f32[32,4,8,256]{0,3,2,1:T(8,128)} copy(f32[32,4,8,256]{3,2,1,0:T(8,128)S(1)} %get-tuple-element.5) | data formatting | bytes 2097152 | tf_op jit(solution)/shard_map/mul | solution.py:334
  46.6 2.7 %copy.27 = f32[32,4,8,256]{0,3,2,1:T(8,128)} copy(f32[32,4,8,256]{3,2,1,0:T(8,128)S(1)} %slice.262) | data formatting | bytes 2097152 | tf_op jit(solution)/shard_map/slice | solution.py:109
  49.3 2.9 %gather_fusion = f32[256,32]{1,0:T(8,128)S(1)} fusion(f32[32,8192]{0,1:T(8,128)} %bitcast.100, s32[1024]{0:T(1024)S(1)} %pad_clamp_fusion), kind=kCustom, calls=%fused_computation.clone | custom fusion | bytes 66560 | tf_op jit(solution)/shard_map/jit(_take)/gather | solution.py:336
  52.2 2.9 %gather_fusion.1 = f32[256,32]{1,0:T(8,128)S(1)} fusion(f32[32,8192]{0,1:T(8,128)} %bitcast.101, s32[1024]{0:T(1024)S(1)} %pad_clamp_fusion), kind=kCustom, calls=%fused_computation.1.clone | custom fusion | bytes 66560 | tf_op jit(solution)/shard_map/jit(_take)/gather | solution.py:337
  58.4 26.7 %shard_map.148 = f32[32,4,8,128]{3,2,1,0:T(8,128)} custom-call(f32[32,8,128]{2,1,0:T(8,128)} %reshape.122.part_ref), custom_call_target="tpu_custom_call" | custom-call | tf_op jit(solution)/shard_map/pallas_call | solution.py:256
  85.0 1.6 %reshape.123 = f32[32,4,32,32]{3,2,1,0:T(8,128)S(1)} reshape(f32[32,4,8,128]{3,2,1,0:T(8,128)} %shard_map.148) | data formatting | bytes 1048576 | tf_op jit(solution)/shard_map/reshape | solution.py:356
  87.9 2.6 %copy.42 = f32[32,4,32,32]{3,0,2,1:T(8,128)} copy(f32[32,4,32,32]{3,2,1,0:T(8,128)S(1)} %reshape.123) | data formatting | bytes 1048576 | tf_op jit(solution)/shard_map/reshape | solution.py:356
  91.5 2.5 %subtract_divide_fusion = f32[4,32,32,32]{3,2,1,0:T(8,128)} fusion(f32[32,32]{1,0:T(8,128)S(1)} %div.78, f32[32,32]{1,0:T(8,128)S(1)} %broadcast_multiply_fusion, f32[32,4,32,32]{3,2,1,0:T(8,128)S(1)} %reshape.123), kind=kLoop, calls=%fused_computation.31 | loop fusion | flops 262144 | bytes 1056768 | tf_op jit(solution)/shard_map/div | solution.py:365
  94.0 3.1 %div.81 = f32[128,1024]{1,0:T(8,128)} reshape(f32[4,32,32,32]{3,2,1,0:T(8,128)} %subtract_divide_fusion) | data formatting | bytes 1048576 | tf_op jit(solution)/shard_map/div | solution.py:365
  97.1 1.8 %fusion.78 = f32[128,128]{1,0:T(8,128)S(1)} fusion(f32[128,1024]{1,0:T(8,128)} %div.81), kind=kOutput, calls=%fused_computation.148 | convolution fusion | flops 201326592 | bytes 589824 | tf_op jit(solution)/shard_map/dot_general | solution.py:366
  99.0 11.7 %cholesky.17 = f32[128,128]{1,0:T(8,128)S(1)} custom-call(f32[128,128]{1,0:T(8,128)S(1)} %fusion.50), custom_call_target="Cholesky" | custom-call | tf_op jit(solution)/shard_map/jit(cholesky)/cholesky | solution.py:101
  112.0 9.8 %custom-call.8 = f32[1,128,128]{1,2,0:T(8,128)S(1)} custom-call(f32[1,128,128]{2,1,0:T(8,128)S(1)} %fusion.44), custom_call_target="InvertDiagBlocksLowerTriangular" | custom-call | tf_op jit(solution)/shard_map/triangular_solve | solution.py:103
  121.9 3.1 %reshape.124 = f32[128,1024]{1,0:T(8,128)} reshape(f32[4,32,32,32]{3,2,1,0:T(8,128)} %bitcast.99) | data formatting | bytes 1048576 | tf_op jit(solution)/shard_map/reshape | solution.py:357
  125.0 2.1 %copy.32 = f32[32,32,32]{2,1,0:T(8,128)} copy(f32[32,32,32]{2,0,1:T(8,128)} %dynamic-slice_bitcast_fusion) | data formatting | bytes 262144 | tf_op jit(solution)/shard_map/transpose | solution.py:362
  127.1 1.3 reshape.125
  129.1 1.7 %fusion.32 = f32[128,32]{0,1:T(8,128)S(1)} fusion(f32[128,1024]{1,0:T(8,128)} %reshape.124, f32[1024]{0:T(1024)S(1)} %get-tuple-element.43, f32[1024]{0:T(1024)S(1)} %div.84, f32[32,1024]{1,0:T(8,128)S(1)} %copy-done.12, f32[32,1024]{1,0:T(8,128)S(1)} %reshape.125, f32[1024]{0:T(1024)S(1)} %get-tuple-element.42, f32[1024]{0:T(1024)S(1)} %copy-done.13), kind=kOutput, calls=%fused_computation.64 | convolution fusion | flops 50692096 | bytes 819200 | tf_op jit(solution)/shard_map/dot_general | solution.py:369
  131.3 2.0 %fusion.11 = f32[32,8192]{1,0:T(8,128)S(1)} fusion(bf16[32,8192]{1,0:T(8,128)(2,1)} %collective-permute-done.2, bf16[32,8192]{1,0:T(8,128)(2,1)} %collective-permute-done.1, bf16[32,8192]{1,0:T(8,128)(2,1)} %collective-permute-done, bf16[32,8192]{1,0:T(8,128)(2,1)} %bitcast.41, bf16[32,32]{0,1:T(8,128)(2,1)S(1)} %get-tuple-element.39, ...), kind=kOutput, calls=%fused_computation.22 | convolution fusion | flops 75530240 | bytes 3153920 | tf_op jit(solution)/shard_map/dot_general | solution.py:390
  (103 shorter events, 24.9 us)
Async XLA Ops:
  0.6 55.2 %copy-start = (f32[1024]{0:T(1024)S(1)}, f32[1024]{0:T(1024)}, u32[]{:S(2)}) copy-start(f32[1024]{0:T(1024)} %param.19) | copy-start | bytes 12292
  0.6 8.4 %copy-start.1 = (f32[32,4,8,256]{3,2,1,0:T(8,128)S(1)}, f32[32,4,8,256]{3,2,1,0:T(8,128)}, u32[]{:S(2)}) copy-start(f32[32,4,8,256]{3,2,1,0:T(8,128)} %param.14) | copy-start | bytes 3145732
  0.7 8.7 %copy-start.9 = (f32[4,8,256]{2,1,0:T(8,128)S(1)}, f32[4,8,256]{2,1,0:T(8,128)}, u32[]{:S(2)}) copy-start(f32[4,8,256]{2,1,0:T(8,128)} %param.15) | copy-start | bytes 98308
  0.7 8.7 %copy-start.8 = (f32[4,8,256]{2,1,0:T(8,128)S(1)}, f32[4,8,256]{2,1,0:T(8,128)}, u32[]{:S(2)}) copy-start(f32[4,8,256]{2,1,0:T(8,128)} %param.16) | copy-start | bytes 98308
  0.7 8.7 %copy-start.7 = (f32[4,8,256]{2,1,0:T(8,128)S(1)}, f32[4,8,256]{2,1,0:T(8,128)}, u32[]{:S(2)}) copy-start(f32[4,8,256]{2,1,0:T(8,128)} %param.17) | copy-start | bytes 98308
  0.7 8.7 %copy-start.6 = (f32[4,8,256]{2,1,0:T(8,128)S(1)}, f32[4,8,256]{2,1,0:T(8,128)}, u32[]{:S(2)}) copy-start(f32[4,8,256]{2,1,0:T(8,128)} %param.18) | copy-start | bytes 98308
  3.2 128.0 %collective-permute-start = (bf16[32,8192]{1,0:T(8,128)(2,1)}, bf16[32,8192]{1,0:T(8,128)(2,1)}, u32[]{:S(2)}, u32[]{:S(2)}) collective-permute-start(bf16[32,8192]{1,0:T(8,128)(2,1)} %bitcast.41), channel_id=1, source_target_pairs={{0,1},{1,2},{2,3},{3,0},{4,5},{5,6},{6,7},{7,4},{8,9},{9,10},{10,1... | collective-permute-start | bytes 1572872 | tf_op jit(solution)/shard_map/ppermute | solution.py:377
  5.3 125.9 %collective-permute-start.1 = (bf16[32,8192]{1,0:T(8,128)(2,1)}, bf16[32,8192]{1,0:T(8,128)(2,1)}, u32[]{:S(2)}, u32[]{:S(2)}) collective-permute-start(bf16[32,8192]{1,0:T(8,128)(2,1)} %bitcast.41), channel_id=1, source_target_pairs={{0,2},{1,3},{2,0},{3,1},{4,6},{5,7},{6,4},{7,5},{8,10},{9,11},{10,... | collective-permute-start | bytes 1572872 | tf_op jit(solution)/shard_map/ppermute | solution.py:377
  8.0 123.3 %collective-permute-start.2 = (bf16[32,8192]{1,0:T(8,128)(2,1)}, bf16[32,8192]{1,0:T(8,128)(2,1)}, u32[]{:S(2)}, u32[]{:S(2)}) collective-permute-start(bf16[32,8192]{1,0:T(8,128)(2,1)} %bitcast.41), channel_id=1, source_target_pairs={{0,3},{1,0},{2,1},{3,2},{4,7},{5,4},{6,5},{7,6},{8,11},{9,8},{10,9... | collective-permute-start | bytes 1572872 | tf_op jit(solution)/shard_map/ppermute | solution.py:377
  22.5 2.4 %copy-start.3 = (f32[2,432,256]{2,1,0:T(8,128)S(1)}, f32[2,432,256]{2,1,0:T(8,128)}, u32[]{:S(2)}) copy-start(f32[2,432,256]{2,1,0:T(8,128)} %shard_map.147) | copy-start | bytes 2654212
  26.9 0.8 copy-start.4
  34.1 0.8 copy-start.5
  38.5 8.1 %copy-start.2 = (f32[32,4,8,256]{3,2,1,0:T(8,128)}, f32[32,4,8,256]{3,2,1,0:T(8,128)S(1)}, u32[]{:S(2)}) copy-start(f32[32,4,8,256]{3,2,1,0:T(8,128)S(1)} %slice.262) | copy-start | bytes 3145732
  43.9 2.7 %copy-start.11 = (s32[256]{0:T(256)S(1)}, s32[256]{0:T(256)}, u32[]{:S(2)}) copy-start(s32[256]{0:T(256)} %param.20) | copy-start | bytes 3076
  46.6 9.2 %copy-start.14 = (s32[256]{0:T(256)S(1)}, s32[256]{0:T(256)}, u32[]{:S(2)}) copy-start(s32[256]{0:T(256)} %param.21) | copy-start | bytes 3076
  87.9 3.4 %copy-start.10 = (f32[1024]{0:T(1024)S(1)}, f32[1024]{0:T(1024)}, u32[]{:S(2)}) copy-start(f32[1024]{0:T(1024)} %param.24) | copy-start | bytes 12292
  121.8 7.2 %copy-start.12 = (f32[32,1024]{1,0:T(8,128)S(1)}, f32[32,1024]{1,0:T(8,128)}, u32[]{:S(2)}) copy-start(f32[32,1024]{1,0:T(8,128)} %param.25) | copy-start | bytes 393220
  121.9 7.2 %copy-start.13 = (f32[1024]{0:T(1024)S(1)}, f32[1024]{0:T(1024)}, u32[]{:S(2)}) copy-start(f32[1024]{0:T(1024)} %param.23) | copy-start | bytes 12292

commit v5 on v4

--- a/solution.py
+++ b/solution.py
@@ -331,10 +331,12 @@
     pressure = trim_rim(pressure, rim)
     permeab = trim_rim(permeab, rim)
     cell_count = layers * strip_width * strip_depth
-    mobility = (permeab * water_frac(saturation)).reshape(local_count, cell_count)
-    cell_press = pressure.reshape(local_count, cell_count)
-    perf_mob = jnp.take(mobility, perf_cell, axis=1)
-    perf_press = jnp.take(cell_press, perf_cell, axis=1)
+    mobility = permeab * water_frac(saturation)
+    cell_layer = perf_cell // (strip_width * strip_depth)
+    cell_row = lax.rem(perf_cell // strip_depth, strip_width)
+    cell_col = lax.rem(perf_cell, strip_depth)
+    perf_mob = mobility[:, cell_layer, cell_row, cell_col]
+    perf_press = pressure[:, cell_layer, cell_row, cell_col]
     selector = (perf_well[:, None] == jnp.arange(well_count, dtype=jnp.int32)[None, :]).astype(
         jnp.float32
     )
@@ -358,8 +360,7 @@
     well_rates = lax.dynamic_index_in_dim(
         lax.dynamic_index_in_dim(full, tile_rank, 0, keepdims=False), member_rank, 0, keepdims=False
     )
-    rates_own = lax.dynamic_index_in_dim(full, member_rank, 1, keepdims=False)
-    rates_own = rates_own.transpose(1, 0, 2).reshape(local_count, well_count)
+    rates_own = lax.dynamic_slice_in_dim(rates_all, member_rank * local_count, local_count, 0)
     innov_own = (observed - rates_own) / spread + obs_noise
     mean_rate = jnp.sum(rates_all, 0) / members
     scaled_all = (rates_all - mean_rate) / (spread * member_root)

time: 135 us -> 130 us (0.963)
  local copies, waits for them, and re-layouts: 36.5 us -> 31.1 us
    transpose x2 -> x0, local copies, waits for them, and re-layouts: 3 us -> none  [per_device(): rates_own = rates_own.transpose(1, 0, 2).reshape(local_count, well_count)]
  transfers between devices with their start and end apart: 3 -> 3, of which waited for: 0 -> 0; matrix products, arithmetic and copies ran while one was open for 61% -> 59% of each run, Pallas kernels for 28% -> 30%
where the time goes in v5:
time: 130 us; the launch traced here: 129 us
  other arithmetic  45.2 us (35%)
  Pallas kernels  38.2 us (29%)
  local copies, waits for them, and re-layouts  31.1 us (24%)
  matrix products  7.07 us (5%)
  starting transfers between devices  5.81 us (4%)
  between operations  1.9 us (1%)
    pallas_call x1, Pallas kernels, rates_exchange(): pl.pallas_call(functools.partial(exchange_kernel, member_count), out_shap...  26.7 us
    another operation x3, other arithmetic, solve_spd(): jnp.linalg.cholesky(gram_matrix + jnp.eye(gram_matrix.shape[0], dtype=jnp...  12.4 us
    pallas_call x1, Pallas kernels, halo_exchange(): pl.pallas_call(halo_kernel, out_shape=jax.ShapeDtypeStruct(outgoing.shape...  11.6 us
    another operation x2, other arithmetic, solve_spd(): lax.linalg.triangular_solve(factor, halfway, left_side=True, lower=True,...  10.5 us
    div x2, other arithmetic, jacobi(): return (baseline + flow_sum) / (storage_term + weight_sum)  6.78 us
    ppermute x3, starting transfers between devices, per_device(): anomaly_parts.append(lax.ppermute(anomaly, 'member', pairs))  5.81 us
    reshape x2, local copies, waits for them, and re-layouts, per_device(): full = full.reshape(tile_count, member_count, local_count, well_share)  4.16 us
    div x2, local copies, waits for them, and re-layouts, per_device(): scaled_all = (rates_all - mean_rate) / (spread * member_root)  3.14 us
  transfers between devices with their start and end apart: 3, of which 0 were waited for; matrix products, arithmetic and copies ran while one was open for 59% of the time, Pallas kernels for 30%

profile of v5, /device:TPU:1, one launch (start us, length us, event | category | flops | bytes accessed | tf_op | source)
XLA Modules:
  0.0 129.3 jit_solution(7761820910017809451)
XLA Ops:
  0.7 1.4 %multiply_convert_fusion = bf16[32,4,8,256]{3,2,1,0:T(8,128)(2,1)S(1)} fusion(f32[32,4,8,256]{3,2,1,0:T(8,128)} %param.12), kind=kLoop, calls=%fused_computation.54 | loop fusion | flops 524288 | bytes 1572864 | tf_op jit(solution)/shard_map/convert_element_type | solution.py:374
  3.2 2.1 %collective-permute-start = (bf16[32,8192]{1,0:T(8,128)(2,1)}, bf16[32,8192]{1,0:T(8,128)(2,1)}, u32[]{:S(2)}, u32[]{:S(2)}) collective-permute-start(bf16[32,8192]{1,0:T(8,128)(2,1)} %bitcast.32), channel_id=1, source_target_pairs={{0,1},{1,2},{2,3},{3,0},{4,5},{5,6},{6,7},{7,4},{8,9},{9,10},{10,1... | collective-permute-start | bytes 1572872 | tf_op jit(solution)/shard_map/ppermute | solution.py:378
  5.3 2.6 %collective-permute-start.1 = (bf16[32,8192]{1,0:T(8,128)(2,1)}, bf16[32,8192]{1,0:T(8,128)(2,1)}, u32[]{:S(2)}, u32[]{:S(2)}) collective-permute-start(bf16[32,8192]{1,0:T(8,128)(2,1)} %bitcast.32), channel_id=1, source_target_pairs={{0,2},{1,3},{2,0},{3,1},{4,6},{5,7},{6,4},{7,5},{8,10},{9,11},{10,... | collective-permute-start | bytes 1572872 | tf_op jit(solution)/shard_map/ppermute | solution.py:378
  10.9 11.6 %shard_map.147 = f32[2,432,256]{2,1,0:T(8,128)} custom-call(f32[2,432,256]{2,1,0:T(8,128)} %pad_maximum_fusion.out_ref), custom_call_target="tpu_custom_call" | custom-call | tf_op jit(solution)/shard_map/pallas_call | solution.py:243
  29.1 3.5 %fusion.3 = f32[32,4,14,256]{3,2,1,0:T(8,128)S(1)} fusion(f32[32,3,14,256]{3,2,1,0:T(8,128)S(1)} %divide_multiply_fusion.1, f32[32,3,14,256]{3,2,1,0:T(8,128)S(1)} %broadcast_in_dim.120, f32[32,3,14,256]{3,2,1,0:T(8,128)S(1)} %broadcast_in_dim.119, f32[32,4,14,255]{3,2,1,0:T(8,128)S(1)} %broadcast_in_dim.118, f32[32,4,14,255]{3,2,1,0:T(8,128)S(1)} %broadcast_in_dim.117, ...), kind=kLoop, calls=%fused_computation.11 | loop fusion | flops 8716288 | bytes 16673792 | tf_op jit(solution)/shard_map/div | solution.py:77
  35.0 3.3 %fusion.7 = f32[32,4,14,256]{3,2,1,0:T(8,128)S(1)} fusion(f32[32,3,14,256]{3,2,1,0:T(8,128)S(1)} %divide_multiply_fusion.1, f32[32,3,14,256]{3,2,1,0:T(8,128)S(1)} %get-tuple-element.27, f32[32,3,14,256]{3,2,1,0:T(8,128)S(1)} %get-tuple-element.26, f32[32,4,14,255]{3,2,1,0:T(8,128)S(1)} %get-tuple-element.25, f32[32,4,14,255]{3,2,1,0:T(8,128)S(1)} %get-tuple-element.24, ...), kind=kLoop, calls=%fused_computation.15 | loop fusion | flops 8716288 | bytes 16673792 | tf_op jit(solution)/shard_map/div | solution.py:77
  38.5 1.2 select_multiply_fusion.1
  41.6 2.2 %fusion.20 = (f32[32,4,8,256]{3,2,1,0:T(8,128)S(1)}, f32[32,4,8,256]{3,2,1,0:T(8,128)}) fusion(f32[32,4,14,256]{3,2,1,0:T(8,128)S(1)} %maximum_exponential_fusion, f32[32,3,14,256]{3,2,1,0:T(8,128)S(1)} %select_multiply_fusion.2, f32[32,4,14,255]{3,2,1,0:T(8,128)S(1)} %select_multiply_fusion, f32[32,4,13,256]{3,2,1,0:T(8,128)S(1)} %select_multiply_fusion.1, ...), kind=kLoop, calls=%fused_computation.46 | loop fusion | flops 3670016 | bytes 8086528 | tf_op jit(solution)/shard_map/mul | solution.py:334
  43.9 2.7 %copy.49 = f32[32,4,8,256]{0,3,2,1:T(8,128)} copy(f32[32,4,8,256]{3,2,1,0:T(8,128)S(1)} %get-tuple-element.20) | data formatting | bytes 2097152 | tf_op jit(solution)/shard_map/mul | solution.py:334
  46.6 2.7 %copy.50 = f32[32,4,8,256]{0,3,2,1:T(8,128)} copy(f32[32,4,8,256]{3,2,1,0:T(8,128)S(1)} %slice.264) | data formatting | bytes 2097152 | tf_op jit(solution)/shard_map/slice | solution.py:109
  49.3 2.4 %gather_fusion = f32[256,32]{1,0:T(8,128)S(1)} fusion(f32[32,4,8,256]{0,3,2,1:T(8,128)} %copy.49, s32[256]{0:T(256)S(1)} %fusion.65), kind=kCustom, calls=%fused_computation | custom fusion | bytes 68608 | tf_op jit(solution)/shard_map/gather | solution.py:338
  51.7 2.4 %gather_fusion.1 = f32[256,32]{1,0:T(8,128)S(1)} fusion(f32[32,4,8,256]{0,3,2,1:T(8,128)} %copy.50, s32[256]{0:T(256)S(1)} %fusion.65), kind=kCustom, calls=%fused_computation.1 | custom fusion | bytes 68608 | tf_op jit(solution)/shard_map/gather | solution.py:339
  57.3 26.7 %shard_map.148 = f32[32,4,8,128]{3,2,1,0:T(8,128)} custom-call(f32[32,8,128]{2,1,0:T(8,128)} %reshape.106.part_ref), custom_call_target="tpu_custom_call" | custom-call | tf_op jit(solution)/shard_map/pallas_call | solution.py:256
  84.0 1.6 %reshape.107 = f32[32,4,32,32]{3,2,1,0:T(8,128)S(1)} reshape(f32[32,4,8,128]{3,2,1,0:T(8,128)} %shard_map.148) | data formatting | bytes 1048576 | tf_op jit(solution)/shard_map/reshape | solution.py:358
  85.6 1.2 fusion.72
  86.9 2.6 %copy.62 = f32[32,4,32,32]{3,0,2,1:T(8,128)} copy(f32[32,4,32,32]{3,2,1,0:T(8,128)S(1)} %reshape.107) | data formatting | bytes 1048576 | tf_op jit(solution)/shard_map/reshape | solution.py:358
  89.6 2.5 %subtract_divide_fusion = f32[4,32,32,32]{3,2,1,0:T(8,128)} fusion(f32[32,32]{1,0:T(8,128)S(1)} %div.108, f32[32,32]{1,0:T(8,128)S(1)} %broadcast_multiply_fusion, f32[32,4,32,32]{3,2,1,0:T(8,128)S(1)} %reshape.107), kind=kLoop, calls=%fused_computation.31 | loop fusion | flops 262144 | bytes 1056768 | tf_op jit(solution)/shard_map/div | solution.py:366
  92.1 3.1 %div.111 = f32[128,1024]{1,0:T(8,128)} reshape(f32[4,32,32,32]{3,2,1,0:T(8,128)} %subtract_divide_fusion) | data formatting | bytes 1048576 | tf_op jit(solution)/shard_map/div | solution.py:366
  95.2 1.8 %fusion.83 = f32[128,128]{1,0:T(8,128)S(1)} fusion(f32[128,1024]{1,0:T(8,128)} %div.111), kind=kOutput, calls=%fused_computation.161 | convolution fusion | flops 201326592 | bytes 589824 | tf_op jit(solution)/shard_map/dot_general | solution.py:367
  97.1 11.7 %cholesky.17 = f32[128,128]{1,0:T(8,128)S(1)} custom-call(f32[128,128]{1,0:T(8,128)S(1)} %fusion.48), custom_call_target="Cholesky" | custom-call | tf_op jit(solution)/shard_map/jit(cholesky)/cholesky | solution.py:101
  110.2 9.8 %custom-call.8 = f32[1,128,128]{1,2,0:T(8,128)S(1)} custom-call(f32[1,128,128]{2,1,0:T(8,128)S(1)} %fusion.42), custom_call_target="InvertDiagBlocksLowerTriangular" | custom-call | tf_op jit(solution)/shard_map/triangular_solve | solution.py:103
  120.0 3.1 %reshape.108 = f32[128,1024]{1,0:T(8,128)} reshape(f32[4,32,32,32]{3,2,1,0:T(8,128)} %bitcast.79) | data formatting | bytes 1048576 | tf_op jit(solution)/shard_map/reshape | solution.py:359
  123.7 1.7 %fusion.32 = f32[128,32]{0,1:T(8,128)S(1)} fusion(f32[128,1024]{1,0:T(8,128)} %reshape.108, f32[1024]{0:T(1024)S(1)} %get-tuple-element.58, f32[1024]{0:T(1024)S(1)} %div.114, f32[32,1024]{1,0:T(8,128)S(1)} %copy-done.13, s32[]{:T(128)S(6)} %select_n.78, f32[1024]{0:T(1024)S(1)} %get-tuple-element.57, f32[1024]{0:T(1024)S(1)} %copy-done.14), kind=kOutput, calls=%fused_computation.63 | convolution fusion | flops 50692096 | bytes 819204 | tf_op jit(solution)/shard_map/dot_general | solution.py:370
  125.9 2.0 %fusion.11 = f32[32,8192]{1,0:T(8,128)S(1)} fusion(bf16[32,8192]{1,0:T(8,128)(2,1)} %collective-permute-done.2, bf16[32,8192]{1,0:T(8,128)(2,1)} %collective-permute-done.1, bf16[32,8192]{1,0:T(8,128)(2,1)} %collective-permute-done, bf16[32,8192]{1,0:T(8,128)(2,1)} %bitcast.32, bf16[32,32]{0,1:T(8,128)(2,1)S(1)} %get-tuple-element.54, ...), kind=kOutput, calls=%fused_computation.22 | convolution fusion | flops 75530240 | bytes 3153920 | tf_op jit(solution)/shard_map/dot_general | solution.py:391
  (99 shorter events, 21.6 us)
Async XLA Ops:
  0.6 54.1 %copy-start = (f32[1024]{0:T(1024)S(1)}, f32[1024]{0:T(1024)}, u32[]{:S(2)}) copy-start(f32[1024]{0:T(1024)} %param.17) | copy-start | bytes 12292
  0.6 8.4 %copy-start.1 = (f32[32,4,8,256]{3,2,1,0:T(8,128)S(1)}, f32[32,4,8,256]{3,2,1,0:T(8,128)}, u32[]{:S(2)}) copy-start(f32[32,4,8,256]{3,2,1,0:T(8,128)} %param.12) | copy-start | bytes 3145732
  0.7 8.7 %copy-start.9 = (f32[4,8,256]{2,1,0:T(8,128)S(1)}, f32[4,8,256]{2,1,0:T(8,128)}, u32[]{:S(2)}) copy-start(f32[4,8,256]{2,1,0:T(8,128)} %param.13) | copy-start | bytes 98308
  0.7 8.7 %copy-start.8 = (f32[4,8,256]{2,1,0:T(8,128)S(1)}, f32[4,8,256]{2,1,0:T(8,128)}, u32[]{:S(2)}) copy-start(f32[4,8,256]{2,1,0:T(8,128)} %param.14) | copy-start | bytes 98308
  0.7 8.7 %copy-start.7 = (f32[4,8,256]{2,1,0:T(8,128)S(1)}, f32[4,8,256]{2,1,0:T(8,128)}, u32[]{:S(2)}) copy-start(f32[4,8,256]{2,1,0:T(8,128)} %param.15) | copy-start | bytes 98308
  0.7 8.7 %copy-start.6 = (f32[4,8,256]{2,1,0:T(8,128)S(1)}, f32[4,8,256]{2,1,0:T(8,128)}, u32[]{:S(2)}) copy-start(f32[4,8,256]{2,1,0:T(8,128)} %param.16) | copy-start | bytes 98308
  3.2 122.7 %collective-permute-start = (bf16[32,8192]{1,0:T(8,128)(2,1)}, bf16[32,8192]{1,0:T(8,128)(2,1)}, u32[]{:S(2)}, u32[]{:S(2)}) collective-permute-start(bf16[32,8192]{1,0:T(8,128)(2,1)} %bitcast.32), channel_id=1, source_target_pairs={{0,1},{1,2},{2,3},{3,0},{4,5},{5,6},{6,7},{7,4},{8,9},{9,10},{10,1... | collective-permute-start | bytes 1572872 | tf_op jit(solution)/shard_map/ppermute | solution.py:378
  5.3 120.5 %collective-permute-start.1 = (bf16[32,8192]{1,0:T(8,128)(2,1)}, bf16[32,8192]{1,0:T(8,128)(2,1)}, u32[]{:S(2)}, u32[]{:S(2)}) collective-permute-start(bf16[32,8192]{1,0:T(8,128)(2,1)} %bitcast.32), channel_id=1, source_target_pairs={{0,2},{1,3},{2,0},{3,1},{4,6},{5,7},{6,4},{7,5},{8,10},{9,11},{10,... | collective-permute-start | bytes 1572872 | tf_op jit(solution)/shard_map/ppermute | solution.py:378
  8.0 117.9 %collective-permute-start.2 = (bf16[32,8192]{1,0:T(8,128)(2,1)}, bf16[32,8192]{1,0:T(8,128)(2,1)}, u32[]{:S(2)}, u32[]{:S(2)}) collective-permute-start(bf16[32,8192]{1,0:T(8,128)(2,1)} %bitcast.32), channel_id=1, source_target_pairs={{0,3},{1,0},{2,1},{3,2},{4,7},{5,4},{6,5},{7,6},{8,11},{9,8},{10,9... | collective-permute-start | bytes 1572872 | tf_op jit(solution)/shard_map/ppermute | solution.py:378
  22.5 2.4 %copy-start.3 = (f32[2,432,256]{2,1,0:T(8,128)S(1)}, f32[2,432,256]{2,1,0:T(8,128)}, u32[]{:S(2)}) copy-start(f32[2,432,256]{2,1,0:T(8,128)} %shard_map.147) | copy-start | bytes 2654212
  26.9 0.8 copy-start.4
  34.1 0.8 copy-start.5
  38.5 8.1 %copy-start.2 = (f32[32,4,8,256]{3,2,1,0:T(8,128)}, f32[32,4,8,256]{3,2,1,0:T(8,128)S(1)}, u32[]{:S(2)}) copy-start(f32[32,4,8,256]{3,2,1,0:T(8,128)S(1)} %slice.264) | copy-start | bytes 3145732
  43.9 2.7 %copy-start.12 = (s32[256]{0:T(256)S(1)}, s32[256]{0:T(256)}, u32[]{:S(2)}) copy-start(s32[256]{0:T(256)} %param.18) | copy-start | bytes 3076
  46.6 8.2 %copy-start.11 = (s32[256]{0:T(256)S(1)}, s32[256]{0:T(256)}, u32[]{:S(2)}) copy-start(s32[256]{0:T(256)} %param.19) | copy-start | bytes 3076
  86.8 2.6 %copy-start.10 = (f32[1024]{0:T(1024)S(1)}, f32[1024]{0:T(1024)}, u32[]{:S(2)}) copy-start(f32[1024]{0:T(1024)} %param.22) | copy-start | bytes 12292
  95.2 28.5 %copy-start.13 = (f32[32,1024]{1,0:T(8,128)S(1)}, f32[32,1024]{1,0:T(8,128)}, u32[]{:S(2)}) copy-start(f32[32,1024]{1,0:T(8,128)} %param.23) | copy-start | bytes 393220
  95.2 28.5 %copy-start.14 = (f32[1024]{0:T(1024)S(1)}, f32[1024]{0:T(1024)}, u32[]{:S(2)}) copy-start(f32[1024]{0:T(1024)} %param.21) | copy-start | bytes 12292

commit v6 on v5

--- a/solution.py
+++ b/solution.py
@@ -109,8 +109,9 @@
     return values_in[:, :, rim_cut : values_in.shape[2] - rim_cut, :]
 
 
-def exchange_kernel(member_count, part_ref, full_ref,
-                    recv_a, send_a, recv_a_sem, send_m, recv_m_sem, send_t, recv_t_sem):
+def exchange_kernel(member_count, part_ref, anom_ref, full_ref, anom_all_ref,
+                    recv_a, send_a, recv_a_sem, send_m, recv_m_sem, send_t, recv_t_sem,
+                    send_n, recv_n_sem):
     tile_count = part_ref.shape[0]
     me_t = lax.axis_index("tile")
     me_m = lax.axis_index("member")
@@ -133,6 +134,20 @@
     lax.fori_loop(1, tile_count, greet_tile, 0)
     lax.fori_loop(1, member_count, greet_member, 0)
     pl.semaphore_wait(barrier, tile_count + member_count - 2)
+
+    def copy_n(dst_m, src_m):
+        return pltpu.make_async_remote_copy(
+            src_ref=anom_ref, dst_ref=anom_all_ref.at[src_m],
+            send_sem=send_n.at[dst_m], recv_sem=recv_n_sem.at[src_m],
+            device_id=(me_t, dst_m), device_id_type=mesh_ids,
+        )
+
+    def start_n(k, carry):
+        copy_n(lax.rem(me_m + k, member_count), me_m).start()
+        return carry
+
+    lax.fori_loop(1, member_count, start_n, 0)
+    anom_all_ref[me_m] = anom_ref[...]
 
     def copy_a(dst_t, src_t):
         return pltpu.make_async_remote_copy(
@@ -211,6 +226,18 @@
         return carry
 
     lax.fori_loop(1, tile_count, wait_t_send, 0)
+
+    def wait_n(k, carry):
+        copy_n(me_m, lax.rem(me_m + k, member_count)).wait_recv()
+        return carry
+
+    lax.fori_loop(1, member_count, wait_n, 0)
+
+    def wait_n_send(k, carry):
+        copy_n(lax.rem(me_m + k, member_count), me_m).wait_send()
+        return carry
+
+    lax.fori_loop(1, member_count, wait_n_send, 0)
 
 
 def halo_kernel(out_ref, in_ref, send_sem, recv_sem):
@@ -250,14 +277,17 @@
     )(outgoing)
 
 
-def rates_exchange(pieces, member_count):
+def rates_exchange(pieces, anomaly, member_count):
     tile_count, rows, lanes = pieces.shape
     vmem = pl.BlockSpec(memory_space=pltpu.VMEM)
     return pl.pallas_call(
         functools.partial(exchange_kernel, member_count),
-        out_shape=jax.ShapeDtypeStruct((tile_count, member_count, rows, lanes), jnp.float32),
-        in_specs=[vmem],
-        out_specs=vmem,
+        out_shape=(
+            jax.ShapeDtypeStruct((tile_count, member_count, rows, lanes), jnp.float32),
+            jax.ShapeDtypeStruct((member_count,) + anomaly.shape, anomaly.dtype),
+        ),
+        in_specs=[vmem, vmem],
+        out_specs=(vmem, vmem),
         scratch_shapes=[
             pltpu.VMEM((tile_count, rows, lanes), jnp.float32),
             pltpu.SemaphoreType.DMA((tile_count,)),
@@ -266,9 +296,11 @@
             pltpu.SemaphoreType.DMA((member_count,)),
             pltpu.SemaphoreType.DMA((tile_count,)),
             pltpu.SemaphoreType.DMA((tile_count,)),
+            pltpu.SemaphoreType.DMA((member_count,)),
+            pltpu.SemaphoreType.DMA((member_count,)),
         ],
         compiler_params=pltpu.CompilerParams(collective_id=0, has_side_effects=True),
-    )(pieces)
+    )(pieces, anomaly)
 
 
 def per_device(
@@ -354,7 +386,8 @@
     block_rows = local_count * well_share // 128
     pieces = partial_rates.reshape(local_count, tile_count, well_share).transpose(1, 0, 2)
     pieces = pieces.reshape(tile_count, block_rows, 128)
-    full = rates_exchange(pieces, member_count)
+    anomaly = (log_perm / member_root).astype(jnp.bfloat16).reshape(local_count, cell_count)
+    full, anomaly_all = rates_exchange(pieces, anomaly, member_count)
     full = full.reshape(tile_count, member_count, local_count, well_share)
     rates_all = full.transpose(1, 2, 0, 3).reshape(members, well_count)
     well_rates = lax.dynamic_index_in_dim(
@@ -371,22 +404,8 @@
         scaled_all, innov_own.T, precision=lax.Precision.HIGHEST, preferred_element_type=jnp.float32
     )
     weights_low = solve_spd(gram_matrix, cross_matrix).astype(jnp.bfloat16)
-    anomaly = (log_perm / member_root).astype(jnp.bfloat16).reshape(local_count, cell_count)
-    anomaly_parts = [anomaly]
-    for shift in range(1, member_count):
-        pairs = [(i, (i + shift) % member_count) for i in range(member_count)]
-        anomaly_parts.append(lax.ppermute(anomaly, "member", pairs))
-    anomaly_all = jnp.concatenate(anomaly_parts, axis=0)
-    own_cols = jnp.concatenate(
-        [
-            lax.dynamic_slice_in_dim(
-                weights_low, lax.rem(member_rank - shift + member_count, member_count) * local_count,
-                local_count, 0,
-            )
-            for shift in range(member_count)
-        ],
-        axis=0,
-    )
+    anomaly_all = anomaly_all.reshape(members, cell_count)
+    own_cols = weights_low
     contract = (((0,), (0,)), ((), ()))
     update_sum = lax.dot_general(own_cols, anomaly_all, contract, preferred_element_type=jnp.float32)
     new_log_perm = log_perm + update_sum.reshape(log_perm.shape)

time: 130 us -> 163 us (1.25)
  Pallas kernels: 38.2 us -> 58.4 us
  local copies, waits for them, and re-layouts: 31.1 us -> 49.9 us
  starting transfers between devices: 5.81 us -> 0 us
    pallas_call x1, Pallas kernels: 26.7 us -> 46.9 us  [rates_exchange(): pl.pallas_call(functools.partial(exchange_kernel, member_count), out_shap...]
    ppermute x3 -> x0, starting transfers between devices: 5.81 us -> none  [per_device(): anomaly_parts.append(lax.ppermute(anomaly, 'member', pairs))]
    dot_general x0 -> x1, local copies, waits for them, and re-layouts: none -> 4.09 us  [per_device(): lax.dot_general(own_cols, anomaly_all, contract, preferred_element_type=j...]
    broadcast_in_dim x6, local copies, waits for them, and re-layouts: 1.39 us -> 5.4 us  [per_device(): jnp.broadcast_to(press_ext[None], (local_count,) + press_ext.shape)]
    another operation x2, local copies, waits for them, and re-layouts: 0.33 us -> 3.9 us  [unpack(): incoming[side, :lp_count].reshape(local_count, layers, rim, strip_depth)]
    unnamed x32 -> x36, local copies, waits for them, and re-layouts: 2.01 us -> 4.93 us
    slice x3, local copies, waits for them, and re-layouts: 2.93 us -> 4.75 us  [trim_rim(): return values_in[:, :, rim_cut:values_in.shape[2] - rim_cut, :]]
  transfers between devices with their start and end apart: 3 -> 0, of which waited for: 0 -> 0; matrix products, arithmetic and copies ran while one was open for 59% -> 0% of each run, Pallas kernels for 30% -> 0%
where the time goes in v6:
time: 163 us
  Pallas kernels  58.4 us (36%)
  local copies, waits for them, and re-layouts  49.9 us (31%)
  other arithmetic  44.8 us (27%)
  matrix products  7.63 us (5%)
  between operations  1.82 us (1%)
    pallas_call x1, Pallas kernels, rates_exchange(): pl.pallas_call(functools.partial(exchange_kernel, member_count), out_shap...  46.9 us
    another operation x3, other arithmetic, solve_spd(): jnp.linalg.cholesky(gram_matrix + jnp.eye(gram_matrix.shape[0], dtype=jnp...  12.4 us
    pallas_call x1, Pallas kernels, halo_exchange(): pl.pallas_call(halo_kernel, out_shape=jax.ShapeDtypeStruct(outgoing.shape...  11.4 us
    another operation x2, other arithmetic, solve_spd(): lax.linalg.triangular_solve(factor, halfway, left_side=True, lower=True,...  10.5 us
    div x2, other arithmetic, jacobi(): return (baseline + flow_sum) / (storage_term + weight_sum)  6.41 us
    broadcast_in_dim x6, local copies, waits for them, and re-layouts, per_device(): jnp.broadcast_to(press_ext[None], (local_count,) + press_ext.shape)  5.4 us
    unnamed x36, local copies, waits for them, and re-layouts  4.93 us
    slice x3, local copies, waits for them, and re-layouts, trim_rim(): return values_in[:, :, rim_cut:values_in.shape[2] - rim_cut, :]  4.75 us

profile of v6, /device:TPU:1, one launch (start us, length us, event | category | flops | bytes accessed | tf_op | source)
XLA Modules:
  0.0 162.5 jit_solution(1400258991262396137)
XLA Ops:
  1.6 1.8 %fusion.62 = (f32[32,4,3,256]{3,2,1,0:T(4,128)S(1)}, f32[32,4,3,256]{3,2,1,0:T(4,128)S(1)}) fusion(f32[32,4,8,256]{3,2,1,0:T(8,128)} %param.12), kind=kLoop, calls=%fused_computation.137 | loop fusion | bytes 1572864 | tf_op jit(solution)/shard_map/slice | solution.py:334
  4.9 11.4 %shard_map.147 = f32[2,432,256]{2,1,0:T(8,128)} custom-call(f32[2,432,256]{2,1,0:T(8,128)} %pad_maximum_fusion.out_ref), custom_call_target="tpu_custom_call" | custom-call | tf_op jit(solution)/shard_map/pallas_call | solution.py:270
  20.0 1.6 broadcast_in_dim.117
  24.1 2.0 %reshape_squeeze.12 = f32[32,4,3,256]{3,2,1,0:T(4,128)} reshape(f32[1,384,256]{2,1,0:T(8,128)} %get-tuple-element.40) | data formatting | bytes 786432 | tf_op jit(solution)/shard_map/reshape;squeeze | solution.py:344
  26.0 2.0 %reshape_squeeze.13 = f32[32,4,3,256]{3,2,1,0:T(4,128)} reshape(f32[1,384,256]{2,1,0:T(8,128)} %get-tuple-element.41) | data formatting | bytes 786432 | tf_op jit(solution)/shard_map/reshape;squeeze | solution.py:344
  28.0 1.7 %maximum_exponential_fusion = f32[32,4,14,256]{3,2,1,0:T(8,128)S(1)} fusion(f32[32,4,3,256]{3,2,1,0:T(4,128)} %reshape_squeeze.13, f32[32,4,8,256]{3,2,1,0:T(8,128)S(1)} %copy-done.1, f32[32,4,3,256]{3,2,1,0:T(4,128)} %reshape_squeeze.12), kind=kLoop, calls=%fused_computation.21 | loop fusion | flops 917504 | bytes 3670016 | tf_op jit(solution)/shard_map/exp | solution.py:352
  33.9 3.1 %fusion.3 = f32[32,4,14,256]{3,2,1,0:T(8,128)S(1)} fusion(f32[32,3,14,256]{3,2,1,0:T(8,128)S(1)} %divide_multiply_fusion.1, f32[32,3,14,256]{3,2,1,0:T(8,128)S(1)} %broadcast_in_dim.120, f32[32,3,14,256]{3,2,1,0:T(8,128)S(1)} %broadcast_in_dim.119, f32[32,4,14,255]{3,2,1,0:T(8,128)S(1)} %copy-done.4, f32[32,4,14,255]{3,2,1,0:T(8,128)S(1)} %copy-done.3, ...), kind=kLoop, calls=%fused_computation.11 | loop fusion | flops 8716288 | bytes 16673792 | tf_op jit(solution)/shard_map/div | solution.py:77
  38.8 3.3 %fusion.7 = f32[32,4,14,256]{3,2,1,0:T(8,128)S(1)} fusion(f32[32,3,14,256]{3,2,1,0:T(8,128)S(1)} %divide_multiply_fusion.1, f32[32,3,14,256]{3,2,1,0:T(8,128)S(1)} %get-tuple-element.35, f32[32,3,14,256]{3,2,1,0:T(8,128)S(1)} %get-tuple-element.34, f32[32,4,14,255]{3,2,1,0:T(8,128)S(1)} %get-tuple-element.33, f32[32,4,14,255]{3,2,1,0:T(8,128)S(1)} %get-tuple-element.32, ...), kind=kLoop, calls=%fused_computation.15 | loop fusion | flops 8716288 | bytes 16673792 | tf_op jit(solution)/shard_map/div | solution.py:77
  45.4 2.6 %fusion.13 = (f32[32,4,8,256]{3,2,1,0:T(8,128)}, f32[32,4,8,256]{3,2,1,0:T(8,128)}) fusion(f32[32,4,14,256]{3,2,1,0:T(8,128)S(1)} %maximum_exponential_fusion, f32[32,3,14,256]{3,2,1,0:T(8,128)S(1)} %select_multiply_fusion.2, f32[32,4,14,255]{3,2,1,0:T(8,128)S(1)} %select_multiply_fusion, f32[32,4,13,256]{3,2,1,0:T(8,128)S(1)} %select_multiply_fusion.1, ...), kind=kLoop, calls=%fused_computation.40 | loop fusion | flops 3670016 | bytes 8086528 | tf_op jit(solution)/shard_map/mul | solution.py:366
  47.9 3.6 %copy.61 = f32[32,4,8,256]{0,3,2,1:T(8,128)} copy(f32[32,4,8,256]{3,2,1,0:T(8,128)} %get-tuple-element.28) | data formatting | bytes 2097152 | tf_op jit(solution)/shard_map/mul | solution.py:366
  51.6 2.4 %gather_fusion = f32[256,32]{1,0:T(8,128)S(1)} fusion(f32[32,4,8,256]{0,3,2,1:T(8,128)} %copy.61, s32[256]{0:T(256)S(1)} %fusion.50), kind=kCustom, calls=%fused_computation | custom fusion | bytes 68608 | tf_op jit(solution)/shard_map/gather | solution.py:370
  55.1 3.6 %copy.62 = f32[32,4,8,256]{0,3,2,1:T(8,128)} copy(f32[32,4,8,256]{3,2,1,0:T(8,128)} %slice.264) | data formatting | bytes 2097152 | tf_op jit(solution)/shard_map/slice | solution.py:109
  58.7 2.4 %gather_fusion.1 = f32[256,32]{1,0:T(8,128)S(1)} fusion(f32[32,4,8,256]{0,3,2,1:T(8,128)} %copy.62, s32[256]{0:T(256)S(1)} %fusion.50), kind=kCustom, calls=%fused_computation.1 | custom fusion | bytes 68608 | tf_op jit(solution)/shard_map/gather | solution.py:371
  65.6 46.9 %shard_map.148 = (f32[32,4,8,128]{3,2,1,0:T(8,128)}, bf16[4,32,8192]{2,1,0:T(8,128)(2,1)}) custom-call(f32[32,8,128]{2,1,0:T(8,128)} %reshape.108.part_ref, bf16[32,8192]{1,0:T(8,128)(2,1)} %bitcast.89), custom_call_target="tpu_custom_call" | custom-call | tf_op jit(solution)/shard_map/pallas_call | solution.py:283
  115.5 2.5 %subtract_divide_fusion = f32[4,32,32,32]{3,2,1,0:T(8,128)} fusion(f32[32,32]{1,0:T(8,128)S(1)} %div.110, f32[32,32]{1,0:T(8,128)S(1)} %broadcast_multiply_fusion, f32[32,4,32,32]{3,2,1,0:T(8,128)S(1)} %reshape.110), kind=kLoop, calls=%fused_computation.23 | loop fusion | flops 262144 | bytes 1056768 | tf_op jit(solution)/shard_map/div | solution.py:399
  118.0 3.1 %div.113 = f32[128,1024]{1,0:T(8,128)} reshape(f32[4,32,32,32]{3,2,1,0:T(8,128)} %subtract_divide_fusion) | data formatting | bytes 1048576 | tf_op jit(solution)/shard_map/div | solution.py:399
  121.1 1.8 %fusion.68 = f32[128,128]{1,0:T(8,128)S(1)} fusion(f32[128,1024]{1,0:T(8,128)} %div.113), kind=kOutput, calls=%fused_computation.143 | convolution fusion | flops 201326592 | bytes 589824 | tf_op jit(solution)/shard_map/dot_general | solution.py:400
  123.0 11.7 %cholesky.17 = f32[128,128]{1,0:T(8,128)S(1)} custom-call(f32[128,128]{1,0:T(8,128)S(1)} %fusion.41), custom_call_target="Cholesky" | custom-call | tf_op jit(solution)/shard_map/jit(cholesky)/cholesky | solution.py:101
  136.1 9.8 %custom-call.8 = f32[1,128,128]{1,2,0:T(8,128)S(1)} custom-call(f32[1,128,128]{2,1,0:T(8,128)S(1)} %fusion.35), custom_call_target="InvertDiagBlocksLowerTriangular" | custom-call | tf_op jit(solution)/shard_map/triangular_solve | solution.py:103
  145.9 2.5 %copy.78 = f32[32,4,32,32]{3,0,2,1:T(8,128)} copy(f32[32,4,32,32]{3,2,1,0:T(8,128)S(1)} %reshape.110) | data formatting | bytes 1048576 | tf_op jit(solution)/shard_map/reshape | solution.py:391
  148.4 3.1 %reshape.111 = f32[128,1024]{1,0:T(8,128)} reshape(f32[4,32,32,32]{3,2,1,0:T(8,128)} %bitcast.86) | data formatting | bytes 1048576 | tf_op jit(solution)/shard_map/reshape | solution.py:392
  151.6 1.7 %fusion.25 = f32[128,32]{0,1:T(8,128)S(1)} fusion(f32[128,1024]{1,0:T(8,128)} %reshape.111, f32[1024]{0:T(1024)S(1)} %get-tuple-element.62, f32[1024]{0:T(1024)S(1)} %div.116, f32[32,1024]{1,0:T(8,128)S(1)} %copy-done.15, s32[]{:T(128)S(6)} %select_n.66, f32[1024]{0:T(1024)S(1)} %get-tuple-element.61, f32[1024]{0:T(1024)S(1)} %copy-done.16), kind=kOutput, calls=%fused_computation.57 | convolution fusion | flops 50692096 | bytes 819204 | tf_op jit(solution)/shard_map/dot_general | solution.py:403
  153.6 4.1 %copy.66 = bf16[8192,128]{1,0:T(8,128)(2,1)} copy(bf16[8192,128]{0,1:T(8,128)(2,1)} %bitcast.91) | data formatting | bytes 4194304 | tf_op jit(solution)/shard_map/dot_general | solution.py:410
  157.7 2.6 %convolution_add_fusion = f32[32,4,8,256]{3,0,2,1:T(8,128)S(1)} fusion(bf16[128,32,1,1]{0,1,3,2:T(8,128)(2,1)S(1)} %fusion.12, bf16[4,8,256,128]{3,2,1,0:T(8,128)(2,1)} %bitcast.87, f32[32,4,8,256]{3,2,1,0:T(8,128)S(1)} %copy-done.1), kind=kOutput, calls=%fused_computation.37 | convolution fusion | flops 67371008 | bytes 4202496 | tf_op jit(solution)/shard_map/dot_general | solution.py:410
  (96 shorter events, 29.4 us)
Async XLA Ops:
  0.6 61.2 %copy-start = (f32[1024]{0:T(1024)S(1)}, f32[1024]{0:T(1024)}, u32[]{:S(2)}) copy-start(f32[1024]{0:T(1024)} %param.17) | copy-start | bytes 12292
  3.9 13.3 %copy-start.8 = (f32[4,8,256]{2,1,0:T(8,128)S(1)}, f32[4,8,256]{2,1,0:T(8,128)}, u32[]{:S(2)}) copy-start(f32[4,8,256]{2,1,0:T(8,128)} %param.16) | copy-start | bytes 98308
  3.9 13.3 %copy-start.9 = (f32[4,8,256]{2,1,0:T(8,128)S(1)}, f32[4,8,256]{2,1,0:T(8,128)}, u32[]{:S(2)}) copy-start(f32[4,8,256]{2,1,0:T(8,128)} %param.15) | copy-start | bytes 98308
  3.9 13.3 %copy-start.10 = (f32[4,8,256]{2,1,0:T(8,128)S(1)}, f32[4,8,256]{2,1,0:T(8,128)}, u32[]{:S(2)}) copy-start(f32[4,8,256]{2,1,0:T(8,128)} %param.14) | copy-start | bytes 98308
  3.9 13.3 %copy-start.11 = (f32[4,8,256]{2,1,0:T(8,128)S(1)}, f32[4,8,256]{2,1,0:T(8,128)}, u32[]{:S(2)}) copy-start(f32[4,8,256]{2,1,0:T(8,128)} %param.13) | copy-start | bytes 98308
  20.0 3.2 %copy-start.5 = (f32[2,432,256]{2,1,0:T(8,128)S(1)}, f32[2,432,256]{2,1,0:T(8,128)}, u32[]{:S(2)}) copy-start(f32[2,432,256]{2,1,0:T(8,128)} %shard_map.147) | copy-start | bytes 2654212
  23.1 4.8 %copy-start.1 = (f32[32,4,8,256]{3,2,1,0:T(8,128)S(1)}, f32[32,4,8,256]{3,2,1,0:T(8,128)}, u32[]{:S(2)}) copy-start(f32[32,4,8,256]{3,2,1,0:T(8,128)} %param.12) | copy-start | bytes 3145732
  31.0 1.6 copy-start.3
  31.0 2.2 %copy-start.4 = (f32[32,4,14,255]{3,2,1,0:T(8,128)S(1)}, f32[32,4,14,255]{3,2,1,0:T(8,128)}, u32[]{:S(2)}) copy-start(f32[32,4,14,255]{3,2,1,0:T(8,128)} %broadcast_in_dim.118) | copy-start | bytes 5483524
  31.3 2.6 %copy-start.2 = (f32[32,4,13,256]{3,2,1,0:T(8,128)S(1)}, f32[32,4,13,256]{3,2,1,0:T(8,128)}, u32[]{:S(2)}) copy-start(f32[32,4,13,256]{3,2,1,0:T(8,128)} %broadcast_in_dim.116) | copy-start | bytes 5111812
  31.3 2.6 %copy-start.6 = (f32[4,14,256]{2,1,0:T(8,128)S(1)}, f32[4,14,256]{2,1,0:T(8,128)}, u32[]{:S(2)}) copy-start(f32[4,14,256]{2,1,0:T(8,128)} %get-tuple-element.46) | copy-start | bytes 172036
  44.5 0.8 copy-start.7
  47.9 3.6 %copy-start.14 = (s32[256]{0:T(256)S(1)}, s32[256]{0:T(256)}, u32[]{:S(2)}) copy-start(s32[256]{0:T(256)} %param.18) | copy-start | bytes 3076
  55.1 6.7 %copy-start.13 = (s32[256]{0:T(256)S(1)}, s32[256]{0:T(256)}, u32[]{:S(2)}) copy-start(s32[256]{0:T(256)} %param.19) | copy-start | bytes 3076
  112.5 2.9 %copy-start.12 = (f32[1024]{0:T(1024)S(1)}, f32[1024]{0:T(1024)}, u32[]{:S(2)}) copy-start(f32[1024]{0:T(1024)} %param.22) | copy-start | bytes 12292
  148.4 3.2 %copy-start.15 = (f32[32,1024]{1,0:T(8,128)S(1)}, f32[32,1024]{1,0:T(8,128)}, u32[]{:S(2)}) copy-start(f32[32,1024]{1,0:T(8,128)} %param.23) | copy-start | bytes 393220
  148.4 3.2 %copy-start.16 = (f32[1024]{0:T(1024)S(1)}, f32[1024]{0:T(1024)}, u32[]{:S(2)}) copy-start(f32[1024]{0:T(1024)} %param.21) | copy-start | bytes 12292

commit v7 on v5

--- a/solution.py
+++ b/solution.py
@@ -332,11 +332,23 @@
     permeab = trim_rim(permeab, rim)
     cell_count = layers * strip_width * strip_depth
     mobility = permeab * water_frac(saturation)
-    cell_layer = perf_cell // (strip_width * strip_depth)
-    cell_row = lax.rem(perf_cell // strip_depth, strip_width)
+    plane_rows = layers * strip_width
+    cell_row = perf_cell // strip_depth
     cell_col = lax.rem(perf_cell, strip_depth)
-    perf_mob = mobility[:, cell_layer, cell_row, cell_col]
-    perf_press = pressure[:, cell_layer, cell_row, cell_col]
+    col_pick = (jnp.arange(strip_depth, dtype=jnp.int32)[:, None] == cell_col[None, :]).astype(
+        jnp.float32
+    )
+    row_pick = jnp.arange(plane_rows, dtype=jnp.int32)[:, None] == cell_row[None, :]
+
+    def pick_cells(values_in):
+        by_col = jnp.dot(
+            values_in.reshape(local_count * plane_rows, strip_depth), col_pick,
+            precision=lax.Precision.HIGHEST, preferred_element_type=jnp.float32,
+        ).reshape(local_count, plane_rows, -1)
+        return jnp.sum(jnp.where(row_pick[None], by_col, 0.0), axis=1)
+
+    perf_mob = pick_cells(mobility)
+    perf_press = pick_cells(pressure)
     selector = (perf_well[:, None] == jnp.arange(well_count, dtype=jnp.int32)[None, :]).astype(
         jnp.float32
     )

time: 130 us -> 120 us (0.923)
  local copies, waits for them, and re-layouts: 31.1 us -> 20.9 us
  matrix products: 7.07 us -> 8.65 us
    gather x2 -> x0, local copies, waits for them, and re-layouts: 4.78 us -> none  [the longest x1 2.39 us: per_device(): perf_press = pressure[:, cell_layer, cell_row, cell_col]]
    slice x3 -> x2, local copies, waits for them, and re-layouts: 2.93 us -> 0.18 us  [trim_rim(): return values_in[:, :, rim_cut:values_in.shape[2] - rim_cut, :]]
    mul x1 -> x0, local copies, waits for them, and re-layouts: 2.65 us -> none  [per_device(): mobility = permeab * water_frac(saturation)]
    mul x1 -> x0, other arithmetic: 2.25 us -> none  [per_device(): mobility = permeab * water_frac(saturation)]
    dot_general x0 -> x2, matrix products: none -> 1.64 us  [pick_cells(): jnp.dot(values_in.reshape(local_count * plane_rows, strip_depth), col_pic...]
  transfers between devices with their start and end apart: 3 -> 3, of which waited for: 0 -> 0; matrix products, arithmetic and copies ran while one was open for 59% -> 56% of each run, Pallas kernels for 30% -> 32%
where the time goes in v7:
time: 120 us
  other arithmetic  44.4 us (37%)
  Pallas kernels  38.2 us (32%)
  local copies, waits for them, and re-layouts  20.9 us (17%)
  matrix products  8.65 us (7%)
  starting transfers between devices  5.81 us (5%)
  between operations  1.95 us (2%)
    pallas_call x1, Pallas kernels, rates_exchange(): pl.pallas_call(functools.partial(exchange_kernel, member_count), out_shap...  26.6 us
    another operation x3, other arithmetic, solve_spd(): jnp.linalg.cholesky(gram_matrix + jnp.eye(gram_matrix.shape[0], dtype=jnp...  12.4 us
    pallas_call x1, Pallas kernels, halo_exchange(): pl.pallas_call(halo_kernel, out_shape=jax.ShapeDtypeStruct(outgoing.shape...  11.5 us
    another operation x2, other arithmetic, solve_spd(): lax.linalg.triangular_solve(factor, halfway, left_side=True, lower=True,...  10.5 us
    div x2, other arithmetic, jacobi(): return (baseline + flow_sum) / (storage_term + weight_sum)  7.21 us
    ppermute x3, starting transfers between devices, per_device(): anomaly_parts.append(lax.ppermute(anomaly, 'member', pairs))  5.81 us
    reshape x2, local copies, waits for them, and re-layouts, per_device(): full = full.reshape(tile_count, member_count, local_count, well_share)  4.14 us
    div x2, local copies, waits for them, and re-layouts, per_device(): scaled_all = (rates_all - mean_rate) / (spread * member_root)  3.14 us
  transfers between devices with their start and end apart: 3, of which 0 were waited for; matrix products, arithmetic and copies ran while one was open for 56% of the time, Pallas kernels for 32%

profile of v7, /device:TPU:1, one launch (start us, length us, event | category | flops | bytes accessed | tf_op | source)
XLA Modules:
  0.0 119.9 jit_solution(8982229126513906552)
XLA Ops:
  0.7 1.4 %multiply_convert_fusion = bf16[32,4,8,256]{3,2,1,0:T(8,128)(2,1)S(1)} fusion(f32[32,4,8,256]{3,2,1,0:T(8,128)} %param.12), kind=kLoop, calls=%fused_computation.58 | loop fusion | flops 524288 | bytes 1572864 | tf_op jit(solution)/shard_map/convert_element_type | solution.py:386
  2.1 1.1 copy.25
  3.2 2.1 %collective-permute-start = (bf16[32,8192]{1,0:T(8,128)(2,1)}, bf16[32,8192]{1,0:T(8,128)(2,1)}, u32[]{:S(2)}, u32[]{:S(2)}) collective-permute-start(bf16[32,8192]{1,0:T(8,128)(2,1)} %bitcast.35), channel_id=1, source_target_pairs={{0,1},{1,2},{2,3},{3,0},{4,5},{5,6},{6,7},{7,4},{8,9},{9,10},{10,1... | collective-permute-start | bytes 1572872 | tf_op jit(solution)/shard_map/ppermute | solution.py:390
  5.3 2.6 %collective-permute-start.1 = (bf16[32,8192]{1,0:T(8,128)(2,1)}, bf16[32,8192]{1,0:T(8,128)(2,1)}, u32[]{:S(2)}, u32[]{:S(2)}) collective-permute-start(bf16[32,8192]{1,0:T(8,128)(2,1)} %bitcast.35), channel_id=1, source_target_pairs={{0,2},{1,3},{2,0},{3,1},{4,6},{5,7},{6,4},{7,5},{8,10},{9,11},{10,... | collective-permute-start | bytes 1572872 | tf_op jit(solution)/shard_map/ppermute | solution.py:390
  8.0 1.1 collective-permute-start.2
  10.9 11.5 %shard_map.147 = f32[2,432,256]{2,1,0:T(8,128)} custom-call(f32[2,432,256]{2,1,0:T(8,128)} %pad_maximum_fusion.out_ref), custom_call_target="tpu_custom_call" | custom-call | tf_op jit(solution)/shard_map/pallas_call | solution.py:243
  29.2 3.7 %fusion.3 = f32[32,4,14,256]{3,2,1,0:T(8,128)S(1)} fusion(f32[32,3,14,256]{3,2,1,0:T(8,128)S(1)} %divide_multiply_fusion.1, f32[32,3,14,256]{3,2,1,0:T(8,128)S(1)} %broadcast_in_dim.131, f32[32,3,14,256]{3,2,1,0:T(8,128)S(1)} %broadcast_in_dim.130, f32[32,4,14,255]{3,2,1,0:T(8,128)S(1)} %broadcast_in_dim.129, f32[32,4,14,255]{3,2,1,0:T(8,128)S(1)} %broadcast_in_dim.128, ...), kind=kLoop, calls=%fused_computation.9 | loop fusion | flops 8716288 | bytes 16673792 | tf_op jit(solution)/shard_map/div | solution.py:77
  35.3 3.5 %fusion.7 = f32[32,4,14,256]{3,2,1,0:T(8,128)S(1)} fusion(f32[32,3,14,256]{3,2,1,0:T(8,128)S(1)} %divide_multiply_fusion.1, f32[32,3,14,256]{3,2,1,0:T(8,128)S(1)} %get-tuple-element.9, f32[32,3,14,256]{3,2,1,0:T(8,128)S(1)} %get-tuple-element.8, f32[32,4,14,255]{3,2,1,0:T(8,128)S(1)} %get-tuple-element.7, f32[32,4,14,255]{3,2,1,0:T(8,128)S(1)} %get-tuple-element.6, ...), kind=kLoop, calls=%fused_computation.13 | loop fusion | flops 8716288 | bytes 16673792 | tf_op jit(solution)/shard_map/div | solution.py:77
  39.0 1.2 select_multiply_fusion
  41.0 1.1 select_multiply_fusion.1
  43.1 1.0 fusion.20
  47.9 26.6 %shard_map.148 = f32[32,4,8,128]{3,2,1,0:T(8,128)} custom-call(f32[32,8,128]{2,1,0:T(8,128)} %reshape.136.part_ref), custom_call_target="tpu_custom_call" | custom-call | tf_op jit(solution)/shard_map/pallas_call | solution.py:256
  74.6 1.6 %reshape.137 = f32[32,4,32,32]{3,2,1,0:T(8,128)S(1)} reshape(f32[32,4,8,128]{3,2,1,0:T(8,128)} %shard_map.148) | data formatting | bytes 1048576 | tf_op jit(solution)/shard_map/reshape | solution.py:370
  76.2 1.2 %fusion.77 = f32[32,32]{1,0:T(8,128)S(1)} fusion(f32[32,4,32,32]{3,2,1,0:T(8,128)S(1)} %reshape.137), kind=kLoop, calls=%fused_computation.148 | loop fusion | flops 130048 | bytes 528384 | tf_op jit(solution)/shard_map/reduce_sum | solution.py:377
  77.4 2.5 %copy.33 = f32[32,4,32,32]{3,0,2,1:T(8,128)} copy(f32[32,4,32,32]{3,2,1,0:T(8,128)S(1)} %reshape.137) | data formatting | bytes 1048576 | tf_op jit(solution)/shard_map/reshape | solution.py:370
  80.1 2.5 %subtract_divide_fusion = f32[4,32,32,32]{3,2,1,0:T(8,128)} fusion(f32[32,32]{1,0:T(8,128)S(1)} %div.94, f32[32,32]{1,0:T(8,128)S(1)} %broadcast_multiply_fusion, f32[32,4,32,32]{3,2,1,0:T(8,128)S(1)} %reshape.137), kind=kLoop, calls=%fused_computation.29 | loop fusion | flops 262144 | bytes 1056768 | tf_op jit(solution)/shard_map/div | solution.py:378
  82.7 3.1 %div.97 = f32[128,1024]{1,0:T(8,128)} reshape(f32[4,32,32,32]{3,2,1,0:T(8,128)} %subtract_divide_fusion) | data formatting | bytes 1048576 | tf_op jit(solution)/shard_map/div | solution.py:378
  85.7 1.8 %fusion.87 = f32[128,128]{1,0:T(8,128)S(1)} fusion(f32[128,1024]{1,0:T(8,128)} %div.97), kind=kOutput, calls=%fused_computation.158 | convolution fusion | flops 201326592 | bytes 589824 | tf_op jit(solution)/shard_map/dot_general | solution.py:379
  87.7 11.7 %cholesky.17 = f32[128,128]{1,0:T(8,128)S(1)} custom-call(f32[128,128]{1,0:T(8,128)S(1)} %fusion.57), custom_call_target="Cholesky" | custom-call | tf_op jit(solution)/shard_map/jit(cholesky)/cholesky | solution.py:101
  100.7 9.8 %custom-call.8 = f32[1,128,128]{1,2,0:T(8,128)S(1)} custom-call(f32[1,128,128]{2,1,0:T(8,128)S(1)} %fusion.51), custom_call_target="InvertDiagBlocksLowerTriangular" | custom-call | tf_op jit(solution)/shard_map/triangular_solve | solution.py:103
  110.5 3.1 %reshape.138 = f32[128,1024]{1,0:T(8,128)} reshape(f32[4,32,32,32]{3,2,1,0:T(8,128)} %bitcast.89) | data formatting | bytes 1048576 | tf_op jit(solution)/shard_map/reshape | solution.py:371
  114.2 1.7 %fusion.39 = f32[128,32]{0,1:T(8,128)S(1)} fusion(f32[128,1024]{1,0:T(8,128)} %reshape.138, f32[1024]{0:T(1024)S(1)} %get-tuple-element.40, f32[1024]{0:T(1024)S(1)} %div.100, f32[32,1024]{1,0:T(8,128)S(1)} %copy-done.13, s32[]{:T(128)S(6)} %select_n.68, f32[1024]{0:T(1024)S(1)} %get-tuple-element.39, f32[1024]{0:T(1024)S(1)} %copy-done.14), kind=kOutput, calls=%fused_computation.69 | convolution fusion | flops 50692096 | bytes 819204 | tf_op jit(solution)/shard_map/dot_general | solution.py:382
  116.4 2.0 %fusion.11 = f32[32,8192]{1,0:T(8,128)S(1)} fusion(bf16[32,8192]{1,0:T(8,128)(2,1)} %collective-permute-done.2, bf16[32,8192]{1,0:T(8,128)(2,1)} %collective-permute-done.1, bf16[32,8192]{1,0:T(8,128)(2,1)} %collective-permute-done, bf16[32,8192]{1,0:T(8,128)(2,1)} %bitcast.35, bf16[32,32]{0,1:T(8,128)(2,1)S(1)} %get-tuple-element.36, ...), kind=kOutput, calls=%fused_computation.20 | convolution fusion | flops 75530240 | bytes 3153920 | tf_op jit(solution)/shard_map/dot_general | solution.py:403
  118.8 1.1 add.294
  (100 shorter events, 18.8 us)
Async XLA Ops:
  0.6 44.8 %copy-start = (f32[1024]{0:T(1024)S(1)}, f32[1024]{0:T(1024)}, u32[]{:S(2)}) copy-start(f32[1024]{0:T(1024)} %param.17) | copy-start | bytes 12292
  0.6 8.4 %copy-start.1 = (f32[32,4,8,256]{3,2,1,0:T(8,128)S(1)}, f32[32,4,8,256]{3,2,1,0:T(8,128)}, u32[]{:S(2)}) copy-start(f32[32,4,8,256]{3,2,1,0:T(8,128)} %param.12) | copy-start | bytes 3145732
  0.7 8.7 %copy-start.10 = (f32[4,8,256]{2,1,0:T(8,128)S(1)}, f32[4,8,256]{2,1,0:T(8,128)}, u32[]{:S(2)}) copy-start(f32[4,8,256]{2,1,0:T(8,128)} %param.13) | copy-start | bytes 98308
  0.7 8.7 %copy-start.9 = (f32[4,8,256]{2,1,0:T(8,128)S(1)}, f32[4,8,256]{2,1,0:T(8,128)}, u32[]{:S(2)}) copy-start(f32[4,8,256]{2,1,0:T(8,128)} %param.14) | copy-start | bytes 98308
  0.7 8.7 %copy-start.8 = (f32[4,8,256]{2,1,0:T(8,128)S(1)}, f32[4,8,256]{2,1,0:T(8,128)}, u32[]{:S(2)}) copy-start(f32[4,8,256]{2,1,0:T(8,128)} %param.15) | copy-start | bytes 98308
  0.7 8.7 %copy-start.7 = (f32[4,8,256]{2,1,0:T(8,128)S(1)}, f32[4,8,256]{2,1,0:T(8,128)}, u32[]{:S(2)}) copy-start(f32[4,8,256]{2,1,0:T(8,128)} %param.16) | copy-start | bytes 98308
  3.2 113.2 %collective-permute-start = (bf16[32,8192]{1,0:T(8,128)(2,1)}, bf16[32,8192]{1,0:T(8,128)(2,1)}, u32[]{:S(2)}, u32[]{:S(2)}) collective-permute-start(bf16[32,8192]{1,0:T(8,128)(2,1)} %bitcast.35), channel_id=1, source_target_pairs={{0,1},{1,2},{2,3},{3,0},{4,5},{5,6},{6,7},{7,4},{8,9},{9,10},{10,1... | collective-permute-start | bytes 1572872 | tf_op jit(solution)/shard_map/ppermute | solution.py:390
  5.3 111.1 %collective-permute-start.1 = (bf16[32,8192]{1,0:T(8,128)(2,1)}, bf16[32,8192]{1,0:T(8,128)(2,1)}, u32[]{:S(2)}, u32[]{:S(2)}) collective-permute-start(bf16[32,8192]{1,0:T(8,128)(2,1)} %bitcast.35), channel_id=1, source_target_pairs={{0,2},{1,3},{2,0},{3,1},{4,6},{5,7},{6,4},{7,5},{8,10},{9,11},{10,... | collective-permute-start | bytes 1572872 | tf_op jit(solution)/shard_map/ppermute | solution.py:390
  8.0 108.5 %collective-permute-start.2 = (bf16[32,8192]{1,0:T(8,128)(2,1)}, bf16[32,8192]{1,0:T(8,128)(2,1)}, u32[]{:S(2)}, u32[]{:S(2)}) collective-permute-start(bf16[32,8192]{1,0:T(8,128)(2,1)} %bitcast.35), channel_id=1, source_target_pairs={{0,3},{1,0},{2,1},{3,2},{4,7},{5,4},{6,5},{7,6},{8,11},{9,8},{10,9... | collective-permute-start | bytes 1572872 | tf_op jit(solution)/shard_map/ppermute | solution.py:390
  22.5 2.4 %copy-start.3 = (f32[2,432,256]{2,1,0:T(8,128)S(1)}, f32[2,432,256]{2,1,0:T(8,128)}, u32[]{:S(2)}) copy-start(f32[2,432,256]{2,1,0:T(8,128)} %shard_map.147) | copy-start | bytes 2654212
  26.9 0.8 copy-start.5
  34.4 0.8 copy-start.6
  34.4 0.8 copy-start.12
  39.0 5.1 %copy-start.2 = (f32[32,4,8,256]{3,2,1,0:T(8,128)}, f32[32,4,8,256]{3,2,1,0:T(8,128)S(1)}, u32[]{:S(2)}) copy-start(f32[32,4,8,256]{3,2,1,0:T(8,128)S(1)} %slice.258) | copy-start | bytes 3145732
  43.0 1.0 copy-start.4
  43.1 2.4 %copy-start.15 = (s32[256]{0:T(256)S(1)}, s32[256]{0:T(256)}, u32[]{:S(2)}) copy-start(s32[256]{0:T(256)} %param.19) | copy-start | bytes 3076
  77.4 2.6 %copy-start.11 = (f32[1024]{0:T(1024)S(1)}, f32[1024]{0:T(1024)}, u32[]{:S(2)}) copy-start(f32[1024]{0:T(1024)} %param.22) | copy-start | bytes 12292
  85.7 28.5 %copy-start.13 = (f32[32,1024]{1,0:T(8,128)S(1)}, f32[32,1024]{1,0:T(8,128)}, u32[]{:S(2)}) copy-start(f32[32,1024]{1,0:T(8,128)} %param.23) | copy-start | bytes 393220
  85.7 28.5 %copy-start.14 = (f32[1024]{0:T(1024)S(1)}, f32[1024]{0:T(1024)}, u32[]{:S(2)}) copy-start(f32[1024]{0:T(1024)} %param.21) | copy-start | bytes 12292

commit v8 on v7

--- a/solution.py
+++ b/solution.py
@@ -98,7 +98,9 @@
 
 
 def solve_spd(gram_matrix, cross_matrix):
-    factor = jnp.linalg.cholesky(gram_matrix + jnp.eye(gram_matrix.shape[0], dtype=jnp.float32))
+    factor = lax.linalg.cholesky(
+        gram_matrix + jnp.eye(gram_matrix.shape[0], dtype=jnp.float32), symmetrize_input=False
+    )
     halfway = lax.linalg.triangular_solve(factor, cross_matrix, left_side=True, lower=True)
     return lax.linalg.triangular_solve(
         factor, halfway, left_side=True, lower=True, transpose_a=True
@@ -306,6 +308,7 @@
 
     outgoing = jnp.stack([rim_rows(0), rim_rows(strip_width - rim)])
     incoming = halo_exchange(outgoing)
+    incoming, log_perm_after = lax.optimization_barrier((incoming, log_perm))
     lp_count = local_count * layers * rim
 
     def unpack(side):
@@ -383,7 +386,7 @@
         scaled_all, innov_own.T, precision=lax.Precision.HIGHEST, preferred_element_type=jnp.float32
     )
     weights_low = solve_spd(gram_matrix, cross_matrix).astype(jnp.bfloat16)
-    anomaly = (log_perm / member_root).astype(jnp.bfloat16).reshape(local_count, cell_count)
+    anomaly = (log_perm_after / member_root).astype(jnp.bfloat16).reshape(local_count, cell_count)
     anomaly_parts = [anomaly]
     for shift in range(1, member_count):
         pairs = [(i, (i + shift) % member_count) for i in range(member_count)]

time: 120 us -> 120 us (level)
    slice x1, local copies, waits for them, and re-layouts: 0.27 us -> 1.79 us  [rim_rows(): lax.slice_in_dim(log_perm, first, first + rim, axis=2)]
    convert_element_type x1, other arithmetic: 1.42 us -> 0.13 us  [per_device(): (log_perm_after / member_root).astype(jnp.bfloat16)]
  transfers between devices with their start and end apart: 3 -> 3, of which waited for: 0 -> 0; matrix products, arithmetic and copies ran while one was open for 56% -> 54% of each run, Pallas kernels for 32% -> 23%
where the time goes in v8:
time: 120 us
  other arithmetic  43.8 us (36%)
  Pallas kernels  39.1 us (33%)
  local copies, waits for them, and re-layouts  21.4 us (18%)
  matrix products  8.66 us (7%)
  starting transfers between devices  4.99 us (4%)
  between operations  1.9 us (2%)
    pallas_call x1, Pallas kernels, rates_exchange(): pl.pallas_call(functools.partial(exchange_kernel, member_count), out_shap...  27.6 us
    another operation x3, other arithmetic, solve_spd(): lax.linalg.cholesky(gram_matrix + jnp.eye(gram_matrix.shape[0], dtype=jnp...  12.4 us
    pallas_call x1, Pallas kernels, halo_exchange(): pl.pallas_call(halo_kernel, out_shape=jax.ShapeDtypeStruct(outgoing.shape...  11.5 us
    another operation x2, other arithmetic, solve_spd(): lax.linalg.triangular_solve(factor, halfway, left_side=True, lower=True,...  10.5 us
    div x2, other arithmetic, jacobi(): return (baseline + flow_sum) / (storage_term + weight_sum)  7.21 us
    ppermute x3, starting transfers between devices, per_device(): anomaly_parts.append(lax.ppermute(anomaly, 'member', pairs))  4.99 us
    reshape x2, local copies, waits for them, and re-layouts, per_device(): full = full.reshape(tile_count, member_count, local_count, well_share)  4.14 us
    div x2, local copies, waits for them, and re-layouts, per_device(): scaled_all = (rates_all - mean_rate) / (spread * member_root)  3.14 us
  transfers between devices with their start and end apart: 3, of which 0 were waited for; matrix products, arithmetic and copies ran while one was open for 54% of the time, Pallas kernels for 23%

profile of v8, /device:TPU:1, one launch (start us, length us, event | category | flops | bytes accessed | tf_op | source)
XLA Modules:
  0.0 119.9 jit_solution(16601077140723509500)
XLA Ops:
  1.6 1.8 %fusion.79 = (f32[32,4,3,256]{3,2,1,0:T(4,128)S(1)}, f32[32,4,3,256]{3,2,1,0:T(4,128)S(1)}) fusion(f32[32,4,8,256]{3,2,1,0:T(8,128)} %param.12), kind=kLoop, calls=%fused_computation.149 | loop fusion | bytes 1572864 | tf_op jit(solution)/shard_map/slice | solution.py:304
  4.8 11.5 %shard_map.147 = f32[2,432,256]{2,1,0:T(8,128)} custom-call(f32[2,432,256]{2,1,0:T(8,128)} %pad_maximum_fusion.out_ref), custom_call_target="tpu_custom_call" | custom-call | tf_op jit(solution)/shard_map/pallas_call | solution.py:245
  16.5 1.1 copy.22
  17.6 1.3 %collective-permute-start = (bf16[32,8192]{1,0:T(8,128)(2,1)}, bf16[32,8192]{1,0:T(8,128)(2,1)}, u32[]{:S(2)}, u32[]{:S(2)}) collective-permute-start(bf16[32,8192]{1,0:T(8,128)(2,1)} %bitcast.34), channel_id=1, source_target_pairs={{0,1},{1,2},{2,3},{3,0},{4,5},{5,6},{6,7},{7,4},{8,9},{9,10},{10,1... | collective-permute-start | bytes 1572872 | tf_op jit(solution)/shard_map/ppermute | solution.py:393
  18.9 2.6 %collective-permute-start.1 = (bf16[32,8192]{1,0:T(8,128)(2,1)}, bf16[32,8192]{1,0:T(8,128)(2,1)}, u32[]{:S(2)}, u32[]{:S(2)}) collective-permute-start(bf16[32,8192]{1,0:T(8,128)(2,1)} %bitcast.34), channel_id=1, source_target_pairs={{0,2},{1,3},{2,0},{3,1},{4,6},{5,7},{6,4},{7,5},{8,10},{9,11},{10,... | collective-permute-start | bytes 1572872 | tf_op jit(solution)/shard_map/ppermute | solution.py:393
  21.5 1.1 collective-permute-start.2
  28.4 3.7 %fusion.3 = f32[32,4,14,256]{3,2,1,0:T(8,128)S(1)} fusion(f32[32,3,14,256]{3,2,1,0:T(8,128)S(1)} %divide_multiply_fusion.1, f32[32,3,14,256]{3,2,1,0:T(8,128)S(1)} %broadcast_in_dim.130, f32[32,3,14,256]{3,2,1,0:T(8,128)S(1)} %broadcast_in_dim.129, f32[32,4,14,255]{3,2,1,0:T(8,128)S(1)} %broadcast_in_dim.128, f32[32,4,14,255]{3,2,1,0:T(8,128)S(1)} %broadcast_in_dim.127, ...), kind=kLoop, calls=%fused_computation.9 | loop fusion | flops 8716288 | bytes 16673792 | tf_op jit(solution)/shard_map/div | solution.py:77
  34.5 3.5 %fusion.7 = f32[32,4,14,256]{3,2,1,0:T(8,128)S(1)} fusion(f32[32,3,14,256]{3,2,1,0:T(8,128)S(1)} %divide_multiply_fusion.1, f32[32,3,14,256]{3,2,1,0:T(8,128)S(1)} %get-tuple-element.13, f32[32,3,14,256]{3,2,1,0:T(8,128)S(1)} %get-tuple-element.12, f32[32,4,14,255]{3,2,1,0:T(8,128)S(1)} %get-tuple-element.11, f32[32,4,14,255]{3,2,1,0:T(8,128)S(1)} %get-tuple-element.10, ...), kind=kLoop, calls=%fused_computation.13 | loop fusion | flops 8716288 | bytes 16673792 | tf_op jit(solution)/shard_map/div | solution.py:77
  38.2 1.2 select_multiply_fusion
  40.2 1.1 select_multiply_fusion.1
  42.3 1.0 fusion.20
  47.1 27.6 %shard_map.148 = f32[32,4,8,128]{3,2,1,0:T(8,128)} custom-call(f32[32,8,128]{2,1,0:T(8,128)} %reshape.135.part_ref), custom_call_target="tpu_custom_call" | custom-call | tf_op jit(solution)/shard_map/pallas_call | solution.py:258
  74.8 1.6 %reshape.136 = f32[32,4,32,32]{3,2,1,0:T(8,128)S(1)} reshape(f32[32,4,8,128]{3,2,1,0:T(8,128)} %shard_map.148) | data formatting | bytes 1048576 | tf_op jit(solution)/shard_map/reshape | solution.py:373
  76.4 1.2 %fusion.75 = f32[32,32]{1,0:T(8,128)S(1)} fusion(f32[32,4,32,32]{3,2,1,0:T(8,128)S(1)} %reshape.136), kind=kLoop, calls=%fused_computation.145 | loop fusion | flops 130048 | bytes 528384 | tf_op jit(solution)/shard_map/reduce_sum | solution.py:380
  77.6 2.5 %copy.30 = f32[32,4,32,32]{3,0,2,1:T(8,128)} copy(f32[32,4,32,32]{3,2,1,0:T(8,128)S(1)} %reshape.136) | data formatting | bytes 1048576 | tf_op jit(solution)/shard_map/reshape | solution.py:373
  80.3 2.5 %subtract_divide_fusion = f32[4,32,32,32]{3,2,1,0:T(8,128)} fusion(f32[32,32]{1,0:T(8,128)S(1)} %div.86, f32[32,32]{1,0:T(8,128)S(1)} %broadcast_multiply_fusion, f32[32,4,32,32]{3,2,1,0:T(8,128)S(1)} %reshape.136), kind=kLoop, calls=%fused_computation.29 | loop fusion | flops 262144 | bytes 1056768 | tf_op jit(solution)/shard_map/div | solution.py:381
  82.8 3.1 %div.89 = f32[128,1024]{1,0:T(8,128)} reshape(f32[4,32,32,32]{3,2,1,0:T(8,128)} %subtract_divide_fusion) | data formatting | bytes 1048576 | tf_op jit(solution)/shard_map/div | solution.py:381
  85.9 1.8 %convolution_add_fusion = f32[128,128]{1,0:T(8,128)S(1)} fusion(f32[128,1024]{1,0:T(8,128)} %div.89), kind=kOutput, calls=%fused_computation.47 | convolution fusion | flops 201375744 | bytes 589824 | tf_op jit(solution)/shard_map/dot_general | solution.py:382
  87.7 11.7 %cholesky.17 = f32[128,128]{1,0:T(8,128)S(1)} custom-call(f32[128,128]{1,0:T(8,128)S(1)} %convolution_add_fusion), custom_call_target="Cholesky" | custom-call | tf_op jit(solution)/shard_map/cholesky | solution.py:101
  100.8 9.8 %custom-call.7 = f32[1,128,128]{1,2,0:T(8,128)S(1)} custom-call(f32[1,128,128]{2,1,0:T(8,128)S(1)} %fusion.51), custom_call_target="InvertDiagBlocksLowerTriangular" | custom-call | tf_op jit(solution)/shard_map/triangular_solve | solution.py:105
  110.6 3.1 %reshape.137 = f32[128,1024]{1,0:T(8,128)} reshape(f32[4,32,32,32]{3,2,1,0:T(8,128)} %bitcast.83) | data formatting | bytes 1048576 | tf_op jit(solution)/shard_map/reshape | solution.py:374
  114.3 1.7 %fusion.39 = f32[128,32]{0,1:T(8,128)S(1)} fusion(f32[128,1024]{1,0:T(8,128)} %reshape.137, f32[1024]{0:T(1024)S(1)} %get-tuple-element.44, f32[1024]{0:T(1024)S(1)} %div.90, f32[32,1024]{1,0:T(8,128)S(1)} %copy-done.13, s32[]{:T(128)S(6)} %select_n.67, f32[1024]{0:T(1024)S(1)} %get-tuple-element.43, f32[1024]{0:T(1024)S(1)} %copy-done.14), kind=kOutput, calls=%fused_computation.70 | convolution fusion | flops 50692096 | bytes 819204 | tf_op jit(solution)/shard_map/dot_general | solution.py:385
  116.5 2.0 %fusion.11 = f32[32,8192]{1,0:T(8,128)S(1)} fusion(bf16[32,8192]{1,0:T(8,128)(2,1)} %collective-permute-done.2, bf16[32,8192]{1,0:T(8,128)(2,1)} %collective-permute-done.1, bf16[32,8192]{1,0:T(8,128)(2,1)} %collective-permute-done, bf16[32,8192]{1,0:T(8,128)(2,1)} %bitcast.34, bf16[32,32]{0,1:T(8,128)(2,1)S(1)} %get-tuple-element.40, ...), kind=kOutput, calls=%fused_computation.20 | convolution fusion | flops 75530240 | bytes 3153920 | tf_op jit(solution)/shard_map/dot_general | solution.py:406
  118.8 1.1 add.284
  (98 shorter events, 18.4 us)
Async XLA Ops:
  0.6 44.0 %copy-start = (f32[1024]{0:T(1024)S(1)}, f32[1024]{0:T(1024)}, u32[]{:S(2)}) copy-start(f32[1024]{0:T(1024)} %param.17) | copy-start | bytes 12292
  3.8 12.5 %copy-start.1 = (f32[32,4,8,256]{3,2,1,0:T(8,128)S(1)}, f32[32,4,8,256]{3,2,1,0:T(8,128)}, u32[]{:S(2)}) copy-start(f32[32,4,8,256]{3,2,1,0:T(8,128)} %param.12) | copy-start | bytes 3145732
  4.8 17.8 %copy-start.7 = (f32[4,8,256]{2,1,0:T(8,128)S(1)}, f32[4,8,256]{2,1,0:T(8,128)}, u32[]{:S(2)}) copy-start(f32[4,8,256]{2,1,0:T(8,128)} %param.16) | copy-start | bytes 98308
  4.8 17.9 %copy-start.8 = (f32[4,8,256]{2,1,0:T(8,128)S(1)}, f32[4,8,256]{2,1,0:T(8,128)}, u32[]{:S(2)}) copy-start(f32[4,8,256]{2,1,0:T(8,128)} %param.15) | copy-start | bytes 98308
  4.8 17.9 %copy-start.9 = (f32[4,8,256]{2,1,0:T(8,128)S(1)}, f32[4,8,256]{2,1,0:T(8,128)}, u32[]{:S(2)}) copy-start(f32[4,8,256]{2,1,0:T(8,128)} %param.14) | copy-start | bytes 98308
  4.8 17.9 %copy-start.10 = (f32[4,8,256]{2,1,0:T(8,128)S(1)}, f32[4,8,256]{2,1,0:T(8,128)}, u32[]{:S(2)}) copy-start(f32[4,8,256]{2,1,0:T(8,128)} %param.13) | copy-start | bytes 98308
  16.4 6.2 %copy-start.3 = (f32[2,432,256]{2,1,0:T(8,128)S(1)}, f32[2,432,256]{2,1,0:T(8,128)}, u32[]{:S(2)}) copy-start(f32[2,432,256]{2,1,0:T(8,128)} %shard_map.147) | copy-start | bytes 2654212
  17.6 98.9 %collective-permute-start = (bf16[32,8192]{1,0:T(8,128)(2,1)}, bf16[32,8192]{1,0:T(8,128)(2,1)}, u32[]{:S(2)}, u32[]{:S(2)}) collective-permute-start(bf16[32,8192]{1,0:T(8,128)(2,1)} %bitcast.34), channel_id=1, source_target_pairs={{0,1},{1,2},{2,3},{3,0},{4,5},{5,6},{6,7},{7,4},{8,9},{9,10},{10,1... | collective-permute-start | bytes 1572872 | tf_op jit(solution)/shard_map/ppermute | solution.py:393
  18.9 97.6 %collective-permute-start.1 = (bf16[32,8192]{1,0:T(8,128)(2,1)}, bf16[32,8192]{1,0:T(8,128)(2,1)}, u32[]{:S(2)}, u32[]{:S(2)}) collective-permute-start(bf16[32,8192]{1,0:T(8,128)(2,1)} %bitcast.34), channel_id=1, source_target_pairs={{0,2},{1,3},{2,0},{3,1},{4,6},{5,7},{6,4},{7,5},{8,10},{9,11},{10,... | collective-permute-start | bytes 1572872 | tf_op jit(solution)/shard_map/ppermute | solution.py:393
  21.5 95.0 %collective-permute-start.2 = (bf16[32,8192]{1,0:T(8,128)(2,1)}, bf16[32,8192]{1,0:T(8,128)(2,1)}, u32[]{:S(2)}, u32[]{:S(2)}) collective-permute-start(bf16[32,8192]{1,0:T(8,128)(2,1)} %bitcast.34), channel_id=1, source_target_pairs={{0,3},{1,0},{2,1},{3,2},{4,7},{5,4},{6,5},{7,6},{8,11},{9,8},{10,9... | collective-permute-start | bytes 1572872 | tf_op jit(solution)/shard_map/ppermute | solution.py:393
  26.1 0.8 copy-start.5
  33.6 0.8 copy-start.6
  33.6 0.8 copy-start.12
  38.2 5.1 %copy-start.2 = (f32[32,4,8,256]{3,2,1,0:T(8,128)}, f32[32,4,8,256]{3,2,1,0:T(8,128)S(1)}, u32[]{:S(2)}) copy-start(f32[32,4,8,256]{3,2,1,0:T(8,128)S(1)} %slice.256) | copy-start | bytes 3145732
  42.3 1.0 copy-start.4
  42.3 2.4 %copy-start.15 = (s32[256]{0:T(256)S(1)}, s32[256]{0:T(256)}, u32[]{:S(2)}) copy-start(s32[256]{0:T(256)} %param.19) | copy-start | bytes 3076
  77.6 2.6 %copy-start.11 = (f32[1024]{0:T(1024)S(1)}, f32[1024]{0:T(1024)}, u32[]{:S(2)}) copy-start(f32[1024]{0:T(1024)} %param.22) | copy-start | bytes 12292
  85.9 28.4 %copy-start.13 = (f32[32,1024]{1,0:T(8,128)S(1)}, f32[32,1024]{1,0:T(8,128)}, u32[]{:S(2)}) copy-start(f32[32,1024]{1,0:T(8,128)} %param.23) | copy-start | bytes 393220
  85.9 28.4 %copy-start.14 = (f32[1024]{0:T(1024)S(1)}, f32[1024]{0:T(1024)}, u32[]{:S(2)}) copy-start(f32[1024]{0:T(1024)} %param.21) | copy-start | bytes 12292

commit v9 on v8

--- a/solution.py
+++ b/solution.py
@@ -370,20 +370,24 @@
     pieces = partial_rates.reshape(local_count, tile_count, well_share).transpose(1, 0, 2)
     pieces = pieces.reshape(tile_count, block_rows, 128)
     full = rates_exchange(pieces, member_count)
-    full = full.reshape(tile_count, member_count, local_count, well_share)
-    rates_all = full.transpose(1, 2, 0, 3).reshape(members, well_count)
+    lane_groups = 128 // well_share
     well_rates = lax.dynamic_index_in_dim(
         lax.dynamic_index_in_dim(full, tile_rank, 0, keepdims=False), member_rank, 0, keepdims=False
-    )
-    rates_own = lax.dynamic_slice_in_dim(rates_all, member_rank * local_count, local_count, 0)
-    innov_own = (observed - rates_own) / spread + obs_noise
-    mean_rate = jnp.sum(rates_all, 0) / members
-    scaled_all = (rates_all - mean_rate) / (spread * member_root)
-    gram_matrix = jnp.dot(
-        scaled_all, scaled_all.T, precision=lax.Precision.HIGHEST, preferred_element_type=jnp.float32
-    )
-    cross_matrix = jnp.dot(
-        scaled_all, innov_own.T, precision=lax.Precision.HIGHEST, preferred_element_type=jnp.float32
+    ).reshape(local_count, well_share)
+    rates_t = full.reshape(tile_count, member_count, block_rows, lane_groups, well_share)
+    rates_t = rates_t.transpose(0, 4, 1, 2, 3).reshape(well_count, members)
+    mean_rate = jnp.sum(rates_t, 1) / members
+    scaled_t = (rates_t - mean_rate[:, None]) / (spread * member_root)[:, None]
+    rates_own_t = lax.dynamic_slice_in_dim(rates_t, member_rank * local_count, local_count, 1)
+    innov_own_t = (observed[:, None] - rates_own_t) / spread[:, None] + obs_noise.T
+    contract_wells = (((0,), (0,)), ((), ()))
+    gram_matrix = lax.dot_general(
+        scaled_t, scaled_t, contract_wells, precision=lax.Precision.HIGHEST,
+        preferred_element_type=jnp.float32,
+    )
+    cross_matrix = lax.dot_general(
+        scaled_t, innov_own_t, contract_wells, precision=lax.Precision.HIGHEST,
+        preferred_element_type=jnp.float32,
     )
     weights_low = solve_spd(gram_matrix, cross_matrix).astype(jnp.bfloat16)
     anomaly = (log_perm_after / member_root).astype(jnp.bfloat16).reshape(local_count, cell_count)

time: 120 us -> 121 us (level)
    reshape x3 -> x4, local copies, waits for them, and re-layouts: 7.2 us -> 7.09 us  [the longest x2 4.64 us: per_device(): full.reshape(tile_count, member_count, block_rows, lane_groups, well_share)]
where the time goes in v9:
time: 121 us; the launch traced here: 120 us
  other arithmetic  43.9 us (36%)
  Pallas kernels  39.1 us (32%)
  local copies, waits for them, and re-layouts  21.5 us (18%)
  matrix products  8.74 us (7%)
  starting transfers between devices  4.99 us (4%)
  between operations  1.91 us (2%)
    pallas_call x1, Pallas kernels, rates_exchange(): pl.pallas_call(functools.partial(exchange_kernel, member_count), out_shap...  27.6 us
    another operation x3, other arithmetic, solve_spd(): lax.linalg.cholesky(gram_matrix + jnp.eye(gram_matrix.shape[0], dtype=jnp...  12.4 us
    pallas_call x1, Pallas kernels, halo_exchange(): pl.pallas_call(halo_kernel, out_shape=jax.ShapeDtypeStruct(outgoing.shape...  11.5 us
    another operation x2, other arithmetic, solve_spd(): lax.linalg.triangular_solve(factor, halfway, left_side=True, lower=True,...  10.5 us
    div x2, other arithmetic, jacobi(): return (baseline + flow_sum) / (storage_term + weight_sum)  7.21 us
    ppermute x3, starting transfers between devices, per_device(): anomaly_parts.append(lax.ppermute(anomaly, 'member', pairs))  4.99 us
    reshape x2, local copies, waits for them, and re-layouts, per_device(): full.reshape(tile_count, member_count, block_rows, lane_groups, well_share)  4.64 us
    div x2, local copies, waits for them, and re-layouts, per_device(): scaled_t = (rates_t - mean_rate[:, None]) / (spread * member_root)[:, None]  3.29 us
  transfers between devices with their start and end apart: 3, of which 0 were waited for; matrix products, arithmetic and copies ran while one was open for 54% of the time, Pallas kernels for 23%

profile of v9, /device:TPU:1, one launch (start us, length us, event | category | flops | bytes accessed | tf_op | source)
XLA Modules:
  0.0 120.2 jit_solution(16561798028678285799)
XLA Ops:
  1.6 1.8 %fusion.78 = (f32[32,4,3,256]{3,2,1,0:T(4,128)S(1)}, f32[32,4,3,256]{3,2,1,0:T(4,128)S(1)}) fusion(f32[32,4,8,256]{3,2,1,0:T(8,128)} %param.12), kind=kLoop, calls=%fused_computation.149 | loop fusion | bytes 1572864 | tf_op jit(solution)/shard_map/slice | solution.py:304
  4.8 11.5 %shard_map.147 = f32[2,432,256]{2,1,0:T(8,128)} custom-call(f32[2,432,256]{2,1,0:T(8,128)} %pad_maximum_fusion.out_ref), custom_call_target="tpu_custom_call" | custom-call | tf_op jit(solution)/shard_map/pallas_call | solution.py:245
  16.5 1.1 copy.22
  17.6 1.3 %collective-permute-start = (bf16[32,8192]{1,0:T(8,128)(2,1)}, bf16[32,8192]{1,0:T(8,128)(2,1)}, u32[]{:S(2)}, u32[]{:S(2)}) collective-permute-start(bf16[32,8192]{1,0:T(8,128)(2,1)} %bitcast.36), channel_id=1, source_target_pairs={{0,1},{1,2},{2,3},{3,0},{4,5},{5,6},{6,7},{7,4},{8,9},{9,10},{10,1... | collective-permute-start | bytes 1572872 | tf_op jit(solution)/shard_map/ppermute | solution.py:397
  18.9 2.6 %collective-permute-start.1 = (bf16[32,8192]{1,0:T(8,128)(2,1)}, bf16[32,8192]{1,0:T(8,128)(2,1)}, u32[]{:S(2)}, u32[]{:S(2)}) collective-permute-start(bf16[32,8192]{1,0:T(8,128)(2,1)} %bitcast.36), channel_id=1, source_target_pairs={{0,2},{1,3},{2,0},{3,1},{4,6},{5,7},{6,4},{7,5},{8,10},{9,11},{10,... | collective-permute-start | bytes 1572872 | tf_op jit(solution)/shard_map/ppermute | solution.py:397
  21.5 1.1 collective-permute-start.2
  28.4 3.7 %fusion.3 = f32[32,4,14,256]{3,2,1,0:T(8,128)S(1)} fusion(f32[32,3,14,256]{3,2,1,0:T(8,128)S(1)} %divide_multiply_fusion.1, f32[32,3,14,256]{3,2,1,0:T(8,128)S(1)} %broadcast_in_dim.130, f32[32,3,14,256]{3,2,1,0:T(8,128)S(1)} %broadcast_in_dim.129, f32[32,4,14,255]{3,2,1,0:T(8,128)S(1)} %broadcast_in_dim.128, f32[32,4,14,255]{3,2,1,0:T(8,128)S(1)} %broadcast_in_dim.127, ...), kind=kLoop, calls=%fused_computation.9 | loop fusion | flops 8716288 | bytes 16673792 | tf_op jit(solution)/shard_map/div | solution.py:77
  34.5 3.5 %fusion.7 = f32[32,4,14,256]{3,2,1,0:T(8,128)S(1)} fusion(f32[32,3,14,256]{3,2,1,0:T(8,128)S(1)} %divide_multiply_fusion.1, f32[32,3,14,256]{3,2,1,0:T(8,128)S(1)} %get-tuple-element.13, f32[32,3,14,256]{3,2,1,0:T(8,128)S(1)} %get-tuple-element.12, f32[32,4,14,255]{3,2,1,0:T(8,128)S(1)} %get-tuple-element.11, f32[32,4,14,255]{3,2,1,0:T(8,128)S(1)} %get-tuple-element.10, ...), kind=kLoop, calls=%fused_computation.13 | loop fusion | flops 8716288 | bytes 16673792 | tf_op jit(solution)/shard_map/div | solution.py:77
  38.2 1.2 select_multiply_fusion
  40.2 1.1 select_multiply_fusion.1
  42.3 1.0 fusion.20
  47.1 27.6 %shard_map.148 = f32[32,4,8,128]{3,2,1,0:T(8,128)} custom-call(f32[32,8,128]{2,1,0:T(8,128)} %reshape.139.part_ref), custom_call_target="tpu_custom_call" | custom-call | tf_op jit(solution)/shard_map/pallas_call | solution.py:258
  74.8 2.1 %reshape.140 = f32[32,4,8,4,32]{4,3,2,1,0:T(4,128)S(1)} reshape(f32[32,4,8,128]{3,2,1,0:T(8,128)} %shard_map.148) | data formatting | bytes 1048576 | tf_op jit(solution)/shard_map/reshape | solution.py:377
  76.8 1.3 %fusion.74 = f32[32,32]{1,0:T(8,128)S(1)} fusion(f32[32,4,8,4,32]{4,3,2,1,0:T(4,128)S(1)} %reshape.140), kind=kLoop, calls=%fused_computation.145 | loop fusion | flops 130048 | bytes 528384 | tf_op jit(solution)/shard_map/reduce_sum | solution.py:379
  78.1 2.6 %copy.30 = f32[32,4,8,4,32]{4,0,3,2,1:T(8,128)} copy(f32[32,4,8,4,32]{4,3,2,1,0:T(4,128)S(1)} %reshape.140) | data formatting | bytes 1048576 | tf_op jit(solution)/shard_map/reshape | solution.py:377
  80.8 2.5 %subtract_divide_fusion = f32[32,32,4,8,4]{1,0,4,3,2:T(8,128)} fusion(f32[32,32]{1,0:T(8,128)S(1)} %div.86, f32[32,32]{1,0:T(8,128)S(1)} %broadcast_multiply_fusion, f32[32,4,8,4,32]{4,3,2,1,0:T(4,128)S(1)} %reshape.140), kind=kLoop, calls=%fused_computation.29 | loop fusion | flops 262144 | bytes 1056768 | tf_op jit(solution)/shard_map/div | solution.py:380
  83.4 3.2 %div.89 = f32[1024,128]{0,1:T(8,128)} reshape(f32[32,32,4,8,4]{1,0,4,3,2:T(8,128)} %subtract_divide_fusion) | data formatting | bytes 1048576 | tf_op jit(solution)/shard_map/div | solution.py:380
  86.6 1.9 %convolution_add_fusion = f32[128,128]{1,0:T(8,128)S(1)} fusion(f32[1024,128]{0,1:T(8,128)} %div.89), kind=kOutput, calls=%fused_computation.47 | convolution fusion | flops 201375744 | bytes 589824 | tf_op jit(solution)/shard_map/dot_general | solution.py:384
  88.5 11.7 %cholesky.17 = f32[128,128]{1,0:T(8,128)S(1)} custom-call(f32[128,128]{1,0:T(8,128)S(1)} %convolution_add_fusion), custom_call_target="Cholesky" | custom-call | tf_op jit(solution)/shard_map/cholesky | solution.py:101
  101.5 9.8 %custom-call.7 = f32[1,128,128]{1,2,0:T(8,128)S(1)} custom-call(f32[1,128,128]{2,1,0:T(8,128)S(1)} %fusion.50), custom_call_target="InvertDiagBlocksLowerTriangular" | custom-call | tf_op jit(solution)/shard_map/triangular_solve | solution.py:105
  111.4 1.8 %reshape.141 = f32[1024,128]{0,1:T(8,128)} reshape(f32[32,32,4,8,4]{1,0,4,3,2:T(8,128)S(1)} %bitcast.90) | data formatting | bytes 1048576 | tf_op jit(solution)/shard_map/reshape | solution.py:378
  114.5 1.7 %fusion.39 = f32[128,32]{0,1:T(8,128)S(1)} fusion(f32[1024,128]{0,1:T(8,128)} %reshape.141, f32[1024]{0:T(1024)S(1)} %get-tuple-element.44, f32[1024]{0:T(1024)S(1)} %div.90, f32[32,1024]{1,0:T(8,128)S(1)} %copy-done.14, s32[]{:T(128)S(6)} %select_n.67, f32[1024]{0:T(1024)S(1)} %get-tuple-element.43, f32[1024]{0:T(1024)S(1)} %copy-done.15), kind=kOutput, calls=%fused_computation.70 | convolution fusion | flops 50692096 | bytes 819204 | tf_op jit(solution)/shard_map/dot_general | solution.py:388
  116.7 2.0 %fusion.11 = f32[32,8192]{1,0:T(8,128)S(1)} fusion(bf16[32,8192]{1,0:T(8,128)(2,1)} %collective-permute-done.2, bf16[32,8192]{1,0:T(8,128)(2,1)} %collective-permute-done.1, bf16[32,8192]{1,0:T(8,128)(2,1)} %collective-permute-done, bf16[32,8192]{1,0:T(8,128)(2,1)} %bitcast.36, bf16[32,32]{0,1:T(8,128)(2,1)S(1)} %get-tuple-element.40, ...), kind=kOutput, calls=%fused_computation.20 | convolution fusion | flops 75530240 | bytes 3153920 | tf_op jit(solution)/shard_map/dot_general | solution.py:410
  119.0 1.1 add.284
  (101 shorter events, 19.2 us)
Async XLA Ops:
  0.6 44.0 %copy-start = (f32[1024]{0:T(1024)S(1)}, f32[1024]{0:T(1024)}, u32[]{:S(2)}) copy-start(f32[1024]{0:T(1024)} %param.17) | copy-start | bytes 12292
  3.8 12.5 %copy-start.1 = (f32[32,4,8,256]{3,2,1,0:T(8,128)S(1)}, f32[32,4,8,256]{3,2,1,0:T(8,128)}, u32[]{:S(2)}) copy-start(f32[32,4,8,256]{3,2,1,0:T(8,128)} %param.12) | copy-start | bytes 3145732
  4.8 17.9 %copy-start.8 = (f32[4,8,256]{2,1,0:T(8,128)S(1)}, f32[4,8,256]{2,1,0:T(8,128)}, u32[]{:S(2)}) copy-start(f32[4,8,256]{2,1,0:T(8,128)} %param.16) | copy-start | bytes 98308
  4.8 17.9 %copy-start.9 = (f32[4,8,256]{2,1,0:T(8,128)S(1)}, f32[4,8,256]{2,1,0:T(8,128)}, u32[]{:S(2)}) copy-start(f32[4,8,256]{2,1,0:T(8,128)} %param.15) | copy-start | bytes 98308
  4.8 17.9 %copy-start.10 = (f32[4,8,256]{2,1,0:T(8,128)S(1)}, f32[4,8,256]{2,1,0:T(8,128)}, u32[]{:S(2)}) copy-start(f32[4,8,256]{2,1,0:T(8,128)} %param.14) | copy-start | bytes 98308
  4.8 17.9 %copy-start.11 = (f32[4,8,256]{2,1,0:T(8,128)S(1)}, f32[4,8,256]{2,1,0:T(8,128)}, u32[]{:S(2)}) copy-start(f32[4,8,256]{2,1,0:T(8,128)} %param.13) | copy-start | bytes 98308
  16.4 6.2 %copy-start.4 = (f32[2,432,256]{2,1,0:T(8,128)S(1)}, f32[2,432,256]{2,1,0:T(8,128)}, u32[]{:S(2)}) copy-start(f32[2,432,256]{2,1,0:T(8,128)} %shard_map.147) | copy-start | bytes 2654212
  17.6 99.1 %collective-permute-start = (bf16[32,8192]{1,0:T(8,128)(2,1)}, bf16[32,8192]{1,0:T(8,128)(2,1)}, u32[]{:S(2)}, u32[]{:S(2)}) collective-permute-start(bf16[32,8192]{1,0:T(8,128)(2,1)} %bitcast.36), channel_id=1, source_target_pairs={{0,1},{1,2},{2,3},{3,0},{4,5},{5,6},{6,7},{7,4},{8,9},{9,10},{10,1... | collective-permute-start | bytes 1572872 | tf_op jit(solution)/shard_map/ppermute | solution.py:397
  18.9 97.8 %collective-permute-start.1 = (bf16[32,8192]{1,0:T(8,128)(2,1)}, bf16[32,8192]{1,0:T(8,128)(2,1)}, u32[]{:S(2)}, u32[]{:S(2)}) collective-permute-start(bf16[32,8192]{1,0:T(8,128)(2,1)} %bitcast.36), channel_id=1, source_target_pairs={{0,2},{1,3},{2,0},{3,1},{4,6},{5,7},{6,4},{7,5},{8,10},{9,11},{10,... | collective-permute-start | bytes 1572872 | tf_op jit(solution)/shard_map/ppermute | solution.py:397
  21.5 95.2 %collective-permute-start.2 = (bf16[32,8192]{1,0:T(8,128)(2,1)}, bf16[32,8192]{1,0:T(8,128)(2,1)}, u32[]{:S(2)}, u32[]{:S(2)}) collective-permute-start(bf16[32,8192]{1,0:T(8,128)(2,1)} %bitcast.36), channel_id=1, source_target_pairs={{0,3},{1,0},{2,1},{3,2},{4,7},{5,4},{6,5},{7,6},{8,11},{9,8},{10,9... | collective-permute-start | bytes 1572872 | tf_op jit(solution)/shard_map/ppermute | solution.py:397
  26.1 0.8 copy-start.6
  33.6 0.8 copy-start.7
  33.6 0.8 copy-start.13
  38.2 5.1 %copy-start.3 = (f32[32,4,8,256]{3,2,1,0:T(8,128)}, f32[32,4,8,256]{3,2,1,0:T(8,128)S(1)}, u32[]{:S(2)}) copy-start(f32[32,4,8,256]{3,2,1,0:T(8,128)S(1)} %slice.256) | copy-start | bytes 3145732
  42.3 1.0 copy-start.5
  42.3 2.4 %copy-start.16 = (s32[256]{0:T(256)S(1)}, s32[256]{0:T(256)}, u32[]{:S(2)}) copy-start(s32[256]{0:T(256)} %param.19) | copy-start | bytes 3076
  78.1 2.6 %copy-start.12 = (f32[1024]{0:T(1024)S(1)}, f32[1024]{0:T(1024)}, u32[]{:S(2)}) copy-start(f32[1024]{0:T(1024)} %param.22) | copy-start | bytes 12292
  83.4 28.0 %copy-start.2 = (f32[32,4,8,4,32]{4,0,3,2,1:T(8,128)S(1)}, f32[32,4,8,4,32]{4,0,3,2,1:T(8,128)}, u32[]{:S(2)}) copy-start(f32[32,4,8,4,32]{4,0,3,2,1:T(8,128)} %copy.30) | copy-start | bytes 1572868
  86.6 27.9 %copy-start.14 = (f32[32,1024]{1,0:T(8,128)S(1)}, f32[32,1024]{1,0:T(8,128)}, u32[]{:S(2)}) copy-start(f32[32,1024]{1,0:T(8,128)} %param.23) | copy-start | bytes 393220
  86.6 27.9 %copy-start.15 = (f32[1024]{0:T(1024)S(1)}, f32[1024]{0:T(1024)}, u32[]{:S(2)}) copy-start(f32[1024]{0:T(1024)} %param.21) | copy-start | bytes 12292

commit v10 on v9

--- a/solution.py
+++ b/solution.py
@@ -213,6 +213,44 @@
         return carry
 
     lax.fori_loop(1, tile_count, wait_t_send, 0)
+
+
+def stencil_kernel(rim, lp_ref, fields_ref, inside_ref, press_ref, sat_ref, mob_ref):
+    inside = inside_ref[...]
+    permeab = jnp.exp(lp_ref[...])
+    face_sets = face_terms(permeab, inside)
+    press_ext = fields_ref[0]
+    sat_ext = fields_ref[1]
+    source_ext = fields_ref[2]
+    storage_ext = fields_ref[3]
+    baseline = (source_ext + storage_ext * press_ext)[None]
+    storage_term = jnp.where(inside[None, :, None] > 0.0, storage_ext, 1.0)[None]
+    pressure = jnp.broadcast_to(press_ext[None], permeab.shape)
+    for sweep_idx in range(SWEEPS):
+        pressure = jacobi(pressure, baseline, storage_term, face_sets)
+    saturation = trim_rim(transport(pressure, sat_ext[None], face_sets), rim)
+    press_ref[...] = trim_rim(pressure, rim)
+    sat_ref[...] = saturation
+    mob_ref[...] = trim_rim(permeab, rim) * water_frac(saturation)
+
+
+def stencil(lp_ext, fields_ext, inside, rim):
+    members, layers, rows, depth = lp_ext.shape
+    block = 4
+    out_rows = rows - 2 * rim
+    out_spec = pl.BlockSpec((block, layers, out_rows, depth), lambda i: (i, 0, 0, 0))
+    out_shape = jax.ShapeDtypeStruct((members, layers, out_rows, depth), jnp.float32)
+    return pl.pallas_call(
+        functools.partial(stencil_kernel, rim),
+        grid=(members // block,),
+        in_specs=[
+            pl.BlockSpec((block, layers, rows, depth), lambda i: (i, 0, 0, 0)),
+            pl.BlockSpec(fields_ext.shape, lambda i: (0, 0, 0, 0)),
+            pl.BlockSpec(inside.shape, lambda i: (0,)),
+        ],
+        out_specs=[out_spec, out_spec, out_spec],
+        out_shape=[out_shape, out_shape, out_shape],
+    )(lp_ext, fields_ext, inside)
 
 
 def halo_kernel(out_ref, in_ref, send_sem, recv_sem):
@@ -320,21 +358,10 @@
     high_lp, high_fields = unpack(1)
     lp_ext = jnp.concatenate([low_lp, log_perm, high_lp], axis=2)
     fields_ext = jnp.concatenate([low_fields, fields, high_fields], axis=2)
-    permeab = jnp.exp(lp_ext)
     column = tile_rank * strip_width - rim + jnp.arange(strip_width + 2 * rim, dtype=jnp.int32)
-    inside = (column >= 0) & (column < strip_width * tile_count)
-    face_sets = face_terms(permeab, inside.astype(jnp.float32))
-    press_ext, sat_ext, source_ext, storage_ext = (fields_ext[i] for i in range(4))
-    baseline = (source_ext + storage_ext * press_ext)[None]
-    storage_term = jnp.where(inside[None, :, None], storage_ext, 1.0)[None]
-    pressure = jnp.broadcast_to(press_ext[None], (local_count,) + press_ext.shape)
-    for sweep_idx in range(SWEEPS):
-        pressure = jacobi(pressure, baseline, storage_term, face_sets)
-    saturation = trim_rim(transport(pressure, sat_ext[None], face_sets), rim)
-    pressure = trim_rim(pressure, rim)
-    permeab = trim_rim(permeab, rim)
+    inside = ((column >= 0) & (column < strip_width * tile_count)).astype(jnp.float32)
+    pressure, saturation, mobility = stencil(lp_ext, fields_ext, inside, rim)
     cell_count = layers * strip_width * strip_depth
-    mobility = permeab * water_frac(saturation)
     plane_rows = layers * strip_width
     cell_row = perf_cell // strip_depth
     cell_col = lax.rem(perf_cell, strip_depth)

time: 121 us -> 117 us (0.967)
  other arithmetic: 43.9 us -> 32.8 us
  Pallas kernels: 39.1 us -> 48.9 us
  local copies, waits for them, and re-layouts: 21.5 us -> 16.7 us
  matrix products: 8.74 us -> 10.8 us
    pallas_call x0 -> x1, Pallas kernels: none -> 9.88 us  [stencil(): pl.pallas_call(functools.partial(stencil_kernel, rim), grid=(members // b...]
    div x3 -> x0, other arithmetic: 7.85 us -> none  [the longest x2 7.21 us: jacobi(): return (baseline + flow_sum) / (storage_term + weight_sum)]
    mul x6 -> x0, other arithmetic: 4.12 us -> none  [the longest x3 3.1 us: transport(): carried = velocity * jnp.where(velocity > 0, lower_frac, upper_frac)]
    slice x8 -> x0, local copies, waits for them, and re-layouts: 2.84 us -> none  [the longest x6 2.66 us: slide_by(): remain = lax.slice_in_dim(values_in, 0, extent - 1, axis=along_dim)]
    dot_general x2, matrix products: 1.64 us -> 3.73 us  [pick_cells(): jnp.dot(values_in.reshape(local_count * plane_rows, strip_depth), col_pic...]
    concatenate x0 -> x1, other arithmetic: none -> 1.77 us  [per_device(): lp_ext = jnp.concatenate([low_lp, log_perm, high_lp], axis=2)]
    add x2 -> x0, other arithmetic: 1.57 us -> none  [transport(): return saturation + STEP_COEF * change]
    broadcast_in_dim x9 -> x0, local copies, waits for them, and re-layouts: 1.49 us -> none  [the longest x6 1.39 us: per_device(): jnp.broadcast_to(press_ext[None], (local_count,) + press_ext.shape)]
  transfers between devices with their start and end apart: 3 -> 3, of which waited for: 0 -> 0; matrix products, arithmetic and copies ran while one was open for 54% -> 44% of each run, Pallas kernels for 23% -> 32%
where the time goes in v10:
time: 117 us; the launch traced here: 116 us
  Pallas kernels  48.9 us (42%)
  other arithmetic  32.8 us (28%)
  local copies, waits for them, and re-layouts  16.7 us (14%)
  matrix products  10.8 us (9%)
  starting transfers between devices  5.05 us (4%)
  between operations  1.67 us (1%)
    pallas_call x1, Pallas kernels, rates_exchange(): pl.pallas_call(functools.partial(exchange_kernel, member_count), out_shap...  27.6 us
    another operation x3, other arithmetic, solve_spd(): lax.linalg.cholesky(gram_matrix + jnp.eye(gram_matrix.shape[0], dtype=jnp...  12.4 us
    pallas_call x1, Pallas kernels, halo_exchange(): pl.pallas_call(halo_kernel, out_shape=jax.ShapeDtypeStruct(outgoing.shape...  11.4 us
    another operation x2, other arithmetic, solve_spd(): lax.linalg.triangular_solve(factor, halfway, left_side=True, lower=True,...  10.5 us
    pallas_call x1, Pallas kernels, stencil(): pl.pallas_call(functools.partial(stencil_kernel, rim), grid=(members // b...  9.88 us
    ppermute x3, starting transfers between devices, per_device(): anomaly_parts.append(lax.ppermute(anomaly, 'member', pairs))  5.05 us
    reshape x2, local copies, waits for them, and re-layouts, per_device(): full.reshape(tile_count, member_count, block_rows, lane_groups, well_share)  4.64 us
    dot_general x2, matrix products, pick_cells(): jnp.dot(values_in.reshape(local_count * plane_rows, strip_depth), col_pic...  3.73 us
  transfers between devices with their start and end apart: 3, of which 0 were waited for; matrix products, arithmetic and copies ran while one was open for 44% of the time, Pallas kernels for 32%

profile of v10, /device:TPU:1, one launch (start us, length us, event | category | flops | bytes accessed | tf_op | source)
XLA Modules:
  0.0 116.0 jit_solution(17057009140218728293)
XLA Ops:
  1.6 1.8 %fusion.48 = (f32[32,4,3,256]{3,2,1,0:T(4,128)S(1)}, f32[32,4,3,256]{3,2,1,0:T(4,128)S(1)}) fusion(f32[32,4,8,256]{3,2,1,0:T(8,128)} %param.12), kind=kLoop, calls=%fused_computation.85 | loop fusion | bytes 1572864 | tf_op jit(solution)/shard_map/slice | solution.py:342
  3.9 1.0 pad_maximum_fusion.1.out_ref
  4.9 11.4 %shard_map.147 = f32[2,432,256]{2,1,0:T(8,128)} custom-call(f32[2,432,256]{2,1,0:T(8,128)} %pad_maximum_fusion.1.out_ref), custom_call_target="tpu_custom_call" | custom-call | tf_op jit(solution)/shard_map/pallas_call | solution.py:283
  16.5 1.1 copy.22
  17.6 1.4 %collective-permute-start = (bf16[32,8192]{1,0:T(8,128)(2,1)}, bf16[32,8192]{1,0:T(8,128)(2,1)}, u32[]{:S(2)}, u32[]{:S(2)}) collective-permute-start(bf16[32,8192]{1,0:T(8,128)(2,1)} %bitcast.24), channel_id=1, source_target_pairs={{0,1},{1,2},{2,3},{3,0},{4,5},{5,6},{6,7},{7,4},{8,9},{9,10},{10,1... | collective-permute-start | bytes 1572872 | tf_op jit(solution)/shard_map/ppermute | solution.py:424
  18.9 2.6 %collective-permute-start.1 = (bf16[32,8192]{1,0:T(8,128)(2,1)}, bf16[32,8192]{1,0:T(8,128)(2,1)}, u32[]{:S(2)}, u32[]{:S(2)}) collective-permute-start(bf16[32,8192]{1,0:T(8,128)(2,1)} %bitcast.24), channel_id=1, source_target_pairs={{0,2},{1,3},{2,0},{3,1},{4,6},{5,7},{6,4},{7,5},{8,10},{9,11},{10,... | collective-permute-start | bytes 1572872 | tf_op jit(solution)/shard_map/ppermute | solution.py:424
  21.6 1.1 collective-permute-start.2
  24.5 1.8 %pad_maximum_fusion.lp_ref = f32[32,4,14,256]{3,2,1,0:T(8,128)} fusion(f32[32,4,3,256]{3,2,1,0:T(4,128)S(1)} %reshape_squeeze.13, f32[32,4,8,256]{3,2,1,0:T(8,128)S(1)} %copy-done.1, f32[32,4,3,256]{3,2,1,0:T(4,128)S(1)} %reshape_squeeze.12), kind=kLoop, calls=%fused_computation | loop fusion | flops 917504 | bytes 3670016 | tf_op jit(solution)/shard_map/concatenate | solution.py:359
  26.2 9.9 %shard_map.148 = (f32[32,4,8,256]{3,2,1,0:T(8,128)}, f32[32,4,8,256]{3,2,1,0:T(8,128)}, f32[32,4,8,256]{3,2,1,0:T(8,128)}) custom-call(f32[32,4,14,256]{3,2,1,0:T(8,128)} %pad_maximum_fusion.lp_ref, f32[4,4,14,256]{3,2,1,0:T(8,128)} %pad_maximum_fusion.2.fields_ref, f32[14]{0:T(128)} %and_convert_fusion.inside_ref), custom_call_target="tpu_custom_call" | custom-call | tf_op jit(solution)/shard_map/pallas_call | solution.py:243
  36.1 1.9 %fusion.9 = f32[32,256]{1,0:T(8,128)S(1)} fusion(f32[32,4,8,256]{3,2,1,0:T(8,128)} %get-tuple-element.6, pred[32,256]{1,0:T(8,128)(4,1)S(1)} %iota_compare_fusion.6, s32[256]{0:T(256)S(1)} %get-tuple-element.28), kind=kOutput, calls=%fused_computation.14 | convolution fusion | flops 805888000 | bytes 1090560 | tf_op jit(solution)/shard_map/dot_general | solution.py:374
  38.0 1.9 %fusion.8 = f32[32,256]{1,0:T(8,128)S(1)} fusion(f32[32,4,8,256]{3,2,1,0:T(8,128)} %get-tuple-element.10, pred[32,256]{1,0:T(8,128)(4,1)S(1)} %iota_compare_fusion.6, s32[256]{0:T(256)S(1)} %get-tuple-element.28), kind=kOutput, calls=%fused_computation.13 | convolution fusion | flops 805888000 | bytes 1090560 | tf_op jit(solution)/shard_map/dot_general | solution.py:374
  43.0 27.6 %shard_map.149 = f32[32,4,8,128]{3,2,1,0:T(8,128)} custom-call(f32[32,8,128]{2,1,0:T(8,128)} %reshape.129.part_ref), custom_call_target="tpu_custom_call" | custom-call | tf_op jit(solution)/shard_map/pallas_call | solution.py:296
  70.6 2.1 %reshape.130 = f32[32,4,8,4,32]{4,3,2,1,0:T(4,128)S(1)} reshape(f32[32,4,8,128]{3,2,1,0:T(8,128)} %shard_map.149) | data formatting | bytes 1048576 | tf_op jit(solution)/shard_map/reshape | solution.py:404
  72.7 1.3 %fusion.47 = f32[32,32]{1,0:T(8,128)S(1)} fusion(f32[32,4,8,4,32]{4,3,2,1,0:T(4,128)S(1)} %reshape.130), kind=kLoop, calls=%fused_computation.84 | loop fusion | flops 130048 | bytes 528384 | tf_op jit(solution)/shard_map/reduce_sum | solution.py:406
  74.0 2.6 %copy.30 = f32[32,4,8,4,32]{4,0,3,2,1:T(8,128)} copy(f32[32,4,8,4,32]{4,3,2,1,0:T(4,128)S(1)} %reshape.130) | data formatting | bytes 1048576 | tf_op jit(solution)/shard_map/reshape | solution.py:404
  76.7 2.5 %subtract_divide_fusion = f32[32,32,4,8,4]{1,0,4,3,2:T(8,128)} fusion(f32[32,32]{1,0:T(8,128)S(1)} %div.58, f32[32,32]{1,0:T(8,128)S(1)} %broadcast_multiply_fusion, f32[32,4,8,4,32]{4,3,2,1,0:T(4,128)S(1)} %reshape.130), kind=kLoop, calls=%fused_computation.10 | loop fusion | flops 262144 | bytes 1056768 | tf_op jit(solution)/shard_map/div | solution.py:407
  79.3 3.2 %div.61 = f32[1024,128]{0,1:T(8,128)} reshape(f32[32,32,4,8,4]{1,0,4,3,2:T(8,128)} %subtract_divide_fusion) | data formatting | bytes 1048576 | tf_op jit(solution)/shard_map/div | solution.py:407
  82.5 1.8 %convolution_add_fusion = f32[128,128]{1,0:T(8,128)S(1)} fusion(f32[1024,128]{0,1:T(8,128)} %div.61), kind=kOutput, calls=%fused_computation.15 | convolution fusion | flops 201375744 | bytes 589824 | tf_op jit(solution)/shard_map/dot_general | solution.py:411
  84.3 11.7 %cholesky.17 = f32[128,128]{1,0:T(8,128)S(1)} custom-call(f32[128,128]{1,0:T(8,128)S(1)} %convolution_add_fusion), custom_call_target="Cholesky" | custom-call | tf_op jit(solution)/shard_map/cholesky | solution.py:101
  97.4 9.8 %custom-call.7 = f32[1,128,128]{1,2,0:T(8,128)S(1)} custom-call(f32[1,128,128]{2,1,0:T(8,128)S(1)} %fusion.27), custom_call_target="InvertDiagBlocksLowerTriangular" | custom-call | tf_op jit(solution)/shard_map/triangular_solve | solution.py:105
  107.2 1.8 %reshape.131 = f32[1024,128]{0,1:T(8,128)} reshape(f32[32,32,4,8,4]{1,0,4,3,2:T(8,128)S(1)} %bitcast.66) | data formatting | bytes 1048576 | tf_op jit(solution)/shard_map/reshape | solution.py:405
  110.3 1.7 %fusion.16 = f32[128,32]{0,1:T(8,128)S(1)} fusion(f32[1024,128]{0,1:T(8,128)} %reshape.131, f32[1024]{0:T(1024)S(1)} %get-tuple-element.27, f32[1024]{0:T(1024)S(1)} %div.62, f32[32,1024]{1,0:T(8,128)S(1)} %copy-done.10, s32[]{:T(128)S(6)} %select_n.46, f32[1024]{0:T(1024)S(1)} %get-tuple-element.26, f32[1024]{0:T(1024)S(1)} %copy-done.11), kind=kOutput, calls=%fused_computation.28 | convolution fusion | flops 50692096 | bytes 819204 | tf_op jit(solution)/shard_map/dot_general | solution.py:415
  112.5 2.0 %fusion = f32[32,8192]{1,0:T(8,128)S(1)} fusion(bf16[32,8192]{1,0:T(8,128)(2,1)} %collective-permute-done.2, bf16[32,8192]{1,0:T(8,128)(2,1)} %collective-permute-done.1, bf16[32,8192]{1,0:T(8,128)(2,1)} %collective-permute-done, bf16[32,8192]{1,0:T(8,128)(2,1)} %bitcast.24, bf16[32,32]{0,1:T(8,128)(2,1)S(1)} %get-tuple-element.23, ...), kind=kOutput, calls=%fused_computation.1 | convolution fusion | flops 75530240 | bytes 3153920 | tf_op jit(solution)/shard_map/dot_general | solution.py:437
  114.9 1.1 add.84
  (66 shorter events, 9.4 us)
Async XLA Ops:
  0.6 39.9 %copy-start = (f32[1024]{0:T(1024)S(1)}, f32[1024]{0:T(1024)}, u32[]{:S(2)}) copy-start(f32[1024]{0:T(1024)} %param.17) | copy-start | bytes 12292
  3.9 12.4 %copy-start.1 = (f32[32,4,8,256]{3,2,1,0:T(8,128)S(1)}, f32[32,4,8,256]{3,2,1,0:T(8,128)}, u32[]{:S(2)}) copy-start(f32[32,4,8,256]{3,2,1,0:T(8,128)} %param.12) | copy-start | bytes 3145732
  16.3 6.3 %copy-start.3 = (f32[2,432,256]{2,1,0:T(8,128)S(1)}, f32[2,432,256]{2,1,0:T(8,128)}, u32[]{:S(2)}) copy-start(f32[2,432,256]{2,1,0:T(8,128)} %shard_map.147) | copy-start | bytes 2654212
  17.6 6.1 %copy-start.9 = (s32[256]{0:T(256)S(1)}, s32[256]{0:T(256)}, u32[]{:S(2)}) copy-start(s32[256]{0:T(256)} %param.18) | copy-start | bytes 3076
  17.6 6.1 %copy-start.4 = (f32[4,8,256]{2,1,0:T(8,128)S(1)}, f32[4,8,256]{2,1,0:T(8,128)}, u32[]{:S(2)}) copy-start(f32[4,8,256]{2,1,0:T(8,128)} %param.16) | copy-start | bytes 98308
  17.6 6.1 %copy-start.5 = (f32[4,8,256]{2,1,0:T(8,128)S(1)}, f32[4,8,256]{2,1,0:T(8,128)}, u32[]{:S(2)}) copy-start(f32[4,8,256]{2,1,0:T(8,128)} %param.15) | copy-start | bytes 98308
  17.6 6.1 %copy-start.6 = (f32[4,8,256]{2,1,0:T(8,128)S(1)}, f32[4,8,256]{2,1,0:T(8,128)}, u32[]{:S(2)}) copy-start(f32[4,8,256]{2,1,0:T(8,128)} %param.14) | copy-start | bytes 98308
  17.6 6.1 %copy-start.7 = (f32[4,8,256]{2,1,0:T(8,128)S(1)}, f32[4,8,256]{2,1,0:T(8,128)}, u32[]{:S(2)}) copy-start(f32[4,8,256]{2,1,0:T(8,128)} %param.13) | copy-start | bytes 98308
  17.6 94.9 %collective-permute-start = (bf16[32,8192]{1,0:T(8,128)(2,1)}, bf16[32,8192]{1,0:T(8,128)(2,1)}, u32[]{:S(2)}, u32[]{:S(2)}) collective-permute-start(bf16[32,8192]{1,0:T(8,128)(2,1)} %bitcast.24), channel_id=1, source_target_pairs={{0,1},{1,2},{2,3},{3,0},{4,5},{5,6},{6,7},{7,4},{8,9},{9,10},{10,1... | collective-permute-start | bytes 1572872 | tf_op jit(solution)/shard_map/ppermute | solution.py:424
  18.9 93.6 %collective-permute-start.1 = (bf16[32,8192]{1,0:T(8,128)(2,1)}, bf16[32,8192]{1,0:T(8,128)(2,1)}, u32[]{:S(2)}, u32[]{:S(2)}) collective-permute-start(bf16[32,8192]{1,0:T(8,128)(2,1)} %bitcast.24), channel_id=1, source_target_pairs={{0,2},{1,3},{2,0},{3,1},{4,6},{5,7},{6,4},{7,5},{8,10},{9,11},{10,... | collective-permute-start | bytes 1572872 | tf_op jit(solution)/shard_map/ppermute | solution.py:424
  21.6 91.0 %collective-permute-start.2 = (bf16[32,8192]{1,0:T(8,128)(2,1)}, bf16[32,8192]{1,0:T(8,128)(2,1)}, u32[]{:S(2)}, u32[]{:S(2)}) collective-permute-start(bf16[32,8192]{1,0:T(8,128)(2,1)} %bitcast.24), channel_id=1, source_target_pairs={{0,3},{1,0},{2,1},{3,2},{4,7},{5,4},{6,5},{7,6},{8,11},{9,8},{10,9... | collective-permute-start | bytes 1572872 | tf_op jit(solution)/shard_map/ppermute | solution.py:424
  26.2 14.3 %copy-start.12 = (s32[256]{0:T(256)S(1)}, s32[256]{0:T(256)}, u32[]{:S(2)}) copy-start(s32[256]{0:T(256)} %param.19) | copy-start | bytes 3076
  74.0 2.6 %copy-start.8 = (f32[1024]{0:T(1024)S(1)}, f32[1024]{0:T(1024)}, u32[]{:S(2)}) copy-start(f32[1024]{0:T(1024)} %param.22) | copy-start | bytes 12292
  79.3 27.9 %copy-start.2 = (f32[32,4,8,4,32]{4,0,3,2,1:T(8,128)S(1)}, f32[32,4,8,4,32]{4,0,3,2,1:T(8,128)}, u32[]{:S(2)}) copy-start(f32[32,4,8,4,32]{4,0,3,2,1:T(8,128)} %copy.30) | copy-start | bytes 1572868
  82.5 27.8 %copy-start.10 = (f32[32,1024]{1,0:T(8,128)S(1)}, f32[32,1024]{1,0:T(8,128)}, u32[]{:S(2)}) copy-start(f32[32,1024]{1,0:T(8,128)} %param.23) | copy-start | bytes 393220
  82.5 27.8 %copy-start.11 = (f32[1024]{0:T(1024)S(1)}, f32[1024]{0:T(1024)}, u32[]{:S(2)}) copy-start(f32[1024]{0:T(1024)} %param.21) | copy-start | bytes 12292

commit v11 on v10

--- a/solution.py
+++ b/solution.py
@@ -112,7 +112,7 @@
 
 
 def exchange_kernel(member_count, part_ref, full_ref,
-                    recv_a, send_a, recv_a_sem, send_m, recv_m_sem, send_t, recv_t_sem):
+                    recv_a, own_blk, recv_m, send_a, recv_a_sem, send_m, recv_m_sem, send_t, recv_t_sem):
     tile_count = part_ref.shape[0]
     me_t = lax.axis_index("tile")
     me_m = lax.axis_index("member")
@@ -162,11 +162,11 @@
 
     lax.fori_loop(1, tile_count, wait_a_send, 0)
 
-    full_ref[me_t, me_m] = acc
+    own_blk[...] = acc
 
     def copy_m(dst_m, src_m):
         return pltpu.make_async_remote_copy(
-            src_ref=full_ref.at[me_t, src_m], dst_ref=full_ref.at[me_t, src_m],
+            src_ref=own_blk, dst_ref=recv_m.at[src_m],
             send_sem=send_m.at[dst_m], recv_sem=recv_m_sem.at[src_m],
             device_id=(me_t, dst_m), device_id_type=mesh_ids,
         )
@@ -177,11 +177,12 @@
 
     lax.fori_loop(1, member_count, start_m, 0)
 
-    def wait_m(k, carry):
-        copy_m(me_m, lax.rem(me_m + k, member_count)).wait_recv()
-        return carry
-
-    lax.fori_loop(1, member_count, wait_m, 0)
+    def wait_m(k, total):
+        src_m = lax.rem(me_m + k, member_count)
+        copy_m(me_m, src_m).wait_recv()
+        return total + recv_m[src_m]
+
+    full_ref[me_t] = lax.fori_loop(1, member_count, wait_m, acc)
 
     def wait_m_send(k, carry):
         copy_m(lax.rem(me_m + k, member_count), me_m).wait_send()
@@ -295,11 +296,13 @@
     vmem = pl.BlockSpec(memory_space=pltpu.VMEM)
     return pl.pallas_call(
         functools.partial(exchange_kernel, member_count),
-        out_shape=jax.ShapeDtypeStruct((tile_count, member_count, rows, lanes), jnp.float32),
+        out_shape=jax.ShapeDtypeStruct((tile_count, rows, lanes), jnp.float32),
         in_specs=[vmem],
         out_specs=vmem,
         scratch_shapes=[
             pltpu.VMEM((tile_count, rows, lanes), jnp.float32),
+            pltpu.VMEM((rows, lanes), jnp.float32),
+            pltpu.VMEM((member_count, rows, lanes), jnp.float32),
             pltpu.SemaphoreType.DMA((tile_count,)),
             pltpu.SemaphoreType.DMA((tile_count,)),
             pltpu.SemaphoreType.DMA((member_count,)),
@@ -387,22 +390,22 @@
         jnp.float32
     )
     perf_terms = perf_mob * (perf_press - perf_bhp[None]) * live_mask[None]
-    partial_rates = jnp.dot(
-        perf_terms, selector, precision=lax.Precision.HIGHEST, preferred_element_type=jnp.float32
-    )
     member_root = (members - 1) ** 0.5
     spread = jnp.sqrt(INFLATION * obs_var)
     member_count = lax.axis_size("member")
-    block_rows = local_count * well_share // 128
-    pieces = partial_rates.reshape(local_count, tile_count, well_share).transpose(1, 0, 2)
-    pieces = pieces.reshape(tile_count, block_rows, 128)
+    lane_group = jnp.arange(members, dtype=jnp.int32) // local_count
+    terms_wide = jnp.where(
+        (lane_group == member_rank)[:, None], jnp.tile(perf_terms, (member_count, 1)), 0.0
+    )
+    contract_slots = (((0,), (1,)), ((), ()))
+    pieces = lax.dot_general(
+        selector, terms_wide, contract_slots, precision=lax.Precision.HIGHEST,
+        preferred_element_type=jnp.float32,
+    ).reshape(tile_count, well_share, members)
     full = rates_exchange(pieces, member_count)
-    lane_groups = 128 // well_share
-    well_rates = lax.dynamic_index_in_dim(
-        lax.dynamic_index_in_dim(full, tile_rank, 0, keepdims=False), member_rank, 0, keepdims=False
-    ).reshape(local_count, well_share)
-    rates_t = full.reshape(tile_count, member_count, block_rows, lane_groups, well_share)
-    rates_t = rates_t.transpose(0, 4, 1, 2, 3).reshape(well_count, members)
+    own_block = lax.dynamic_index_in_dim(full, tile_rank, 0, keepdims=False)
+    well_rates = lax.dynamic_slice_in_dim(own_block, member_rank * local_count, local_count, 1).T
+    rates_t = full.reshape(well_count, members)
     mean_rate = jnp.sum(rates_t, 1) / members
     scaled_t = (rates_t - mean_rate[:, None]) / (spread * member_root)[:, None]
     rates_own_t = lax.dynamic_slice_in_dim(rates_t, member_rank * local_count, local_count, 1)

time: 117 us -> 109 us (0.932)
  local copies, waits for them, and re-layouts: 16.7 us -> 5.08 us
  Pallas kernels: 48.9 us -> 53.6 us
  other arithmetic: 32.8 us -> 30.5 us
  matrix products: 10.8 us -> 12.3 us
    reshape x7 -> x0, local copies, waits for them, and re-layouts: 8.38 us -> none  [the longest x2 4.64 us: per_device(): full.reshape(tile_count, member_count, block_rows, lane_groups, well_share)]
    pallas_call x1, Pallas kernels: 27.6 us -> 32.3 us  [rates_exchange(): pl.pallas_call(functools.partial(exchange_kernel, member_count), out_shap...]
    div x2 -> x1, local copies, waits for them, and re-layouts: 3.29 us -> 0.07 us  [per_device(): scaled_t = (rates_t - mean_rate[:, None]) / (spread * member_root)[:, None]]
    div x1, other arithmetic: 2.55 us -> 0.01 us  [per_device(): lane_group = jnp.arange(members, dtype=jnp.int32) // local_count]
  transfers between devices with their start and end apart: 3 -> 3, of which waited for: 0 -> 0; matrix products, arithmetic and copies ran while one was open for 44% -> 37% of each run, Pallas kernels for 32% -> 39%
where the time goes in v11:
time: 109 us; the launch traced here: 108 us
  Pallas kernels  53.6 us (49%)
  other arithmetic  30.5 us (28%)
  matrix products  12.3 us (11%)
  local copies, waits for them, and re-layouts  5.08 us (5%)
  starting transfers between devices  5.05 us (5%)
  between operations  1.76 us (2%)
    pallas_call x1, Pallas kernels, rates_exchange(): pl.pallas_call(functools.partial(exchange_kernel, member_count), out_shap...  32.3 us
    another operation x3, other arithmetic, solve_spd(): lax.linalg.cholesky(gram_matrix + jnp.eye(gram_matrix.shape[0], dtype=jnp...  12.4 us
    pallas_call x1, Pallas kernels, halo_exchange(): pl.pallas_call(halo_kernel, out_shape=jax.ShapeDtypeStruct(outgoing.shape...  11.4 us
    another operation x2, other arithmetic, solve_spd(): lax.linalg.triangular_solve(factor, halfway, left_side=True, lower=True,...  10.5 us
    pallas_call x1, Pallas kernels, stencil(): pl.pallas_call(functools.partial(stencil_kernel, rim), grid=(members // b...  9.88 us
    ppermute x3, starting transfers between devices, per_device(): anomaly_parts.append(lax.ppermute(anomaly, 'member', pairs))  5.05 us
    dot_general x2, matrix products, pick_cells(): jnp.dot(values_in.reshape(local_count * plane_rows, strip_depth), col_pic...  3.74 us
    dot_general x1, matrix products, per_device(): lax.dot_general(scaled_t, scaled_t, contract_wells, precision=lax.Precisi...  2.86 us
  transfers between devices with their start and end apart: 3, of which 0 were waited for; matrix products, arithmetic and copies ran while one was open for 37% of the time, Pallas kernels for 39%

profile of v11, /device:TPU:1, one launch (start us, length us, event | category | flops | bytes accessed | tf_op | source)
XLA Modules:
  0.0 108.3 jit_solution(2567066702157285)
XLA Ops:
  0.6 0.8 pad_maximum_fusion.3
  1.6 1.9 %fusion.51 = (f32[32,4,3,256]{3,2,1,0:T(4,128)S(1)}, f32[32,4,3,256]{3,2,1,0:T(4,128)S(1)}) fusion(f32[32,4,8,256]{3,2,1,0:T(8,128)} %param.12), kind=kLoop, calls=%fused_computation.93 | loop fusion | bytes 1572864 | tf_op jit(solution)/shard_map/slice | solution.py:345
  4.0 1.0 pad_maximum_fusion.1.out_ref
  5.0 11.4 %shard_map.147 = f32[2,432,256]{2,1,0:T(8,128)} custom-call(f32[2,432,256]{2,1,0:T(8,128)} %pad_maximum_fusion.1.out_ref), custom_call_target="tpu_custom_call" | custom-call | tf_op jit(solution)/shard_map/pallas_call | solution.py:284
  16.9 1.4 %collective-permute-start = (bf16[32,8192]{1,0:T(8,128)(2,1)S(1)}, bf16[32,8192]{1,0:T(8,128)(2,1)}, u32[]{:S(2)}, u32[]{:S(2)}) collective-permute-start(bf16[32,8192]{1,0:T(8,128)(2,1)S(1)} %bitcast.61), channel_id=1, source_target_pairs={{0,1},{1,2},{2,3},{3,0},{4,5},{5,6},{6,7},{7,4},{8,9},{9,10},{10,1... | collective-permute-start | bytes 1572872 | tf_op jit(solution)/shard_map/ppermute | solution.py:427
  18.3 2.6 %collective-permute-start.1 = (bf16[32,8192]{1,0:T(8,128)(2,1)S(1)}, bf16[32,8192]{1,0:T(8,128)(2,1)}, u32[]{:S(2)}, u32[]{:S(2)}) collective-permute-start(bf16[32,8192]{1,0:T(8,128)(2,1)S(1)} %bitcast.62), channel_id=1, source_target_pairs={{0,2},{1,3},{2,0},{3,1},{4,6},{5,7},{6,4},{7,5},{8,10},{9,11},{10,... | collective-permute-start | bytes 1572872 | tf_op jit(solution)/shard_map/ppermute | solution.py:427
  20.9 1.1 collective-permute-start.2
  23.1 0.8 pad_maximum_fusion.2.fields_ref
  23.9 1.8 %pad_maximum_fusion.lp_ref = f32[32,4,14,256]{3,2,1,0:T(8,128)} fusion(f32[32,4,3,256]{3,2,1,0:T(4,128)S(1)} %reshape_squeeze.13, f32[32,4,8,256]{3,2,1,0:T(8,128)S(1)} %copy-done.1, f32[32,4,3,256]{3,2,1,0:T(4,128)S(1)} %reshape_squeeze.12), kind=kLoop, calls=%fused_computation | loop fusion | flops 917504 | bytes 3670016 | tf_op jit(solution)/shard_map/concatenate | solution.py:362
  25.7 9.9 %shard_map.148 = (f32[32,4,8,256]{3,2,1,0:T(8,128)}, f32[32,4,8,256]{3,2,1,0:T(8,128)}, f32[32,4,8,256]{3,2,1,0:T(8,128)}) custom-call(f32[32,4,14,256]{3,2,1,0:T(8,128)} %pad_maximum_fusion.lp_ref, f32[4,4,14,256]{3,2,1,0:T(8,128)} %pad_maximum_fusion.2.fields_ref, f32[14]{0:T(128)} %and_convert_fusion.inside_ref), custom_call_target="tpu_custom_call" | custom-call | tf_op jit(solution)/shard_map/pallas_call | solution.py:244
  35.6 1.9 %fusion.9 = f32[32,256]{1,0:T(8,128)S(1)} fusion(f32[32,4,8,256]{3,2,1,0:T(8,128)} %get-tuple-element.15, pred[32,256]{1,0:T(8,128)(4,1)S(1)} %iota_compare_fusion.5, s32[256]{0:T(256)S(1)} %get-tuple-element.32), kind=kOutput, calls=%fused_computation.12 | convolution fusion | flops 805888000 | bytes 1090560 | tf_op jit(solution)/shard_map/dot_general | solution.py:377
  37.4 1.9 %fusion.8 = f32[32,256]{1,0:T(8,128)S(1)} fusion(f32[32,4,8,256]{3,2,1,0:T(8,128)} %get-tuple-element.10, pred[32,256]{1,0:T(8,128)(4,1)S(1)} %iota_compare_fusion.5, s32[256]{0:T(256)S(1)} %get-tuple-element.32), kind=kOutput, calls=%fused_computation.11 | convolution fusion | flops 805888000 | bytes 1090560 | tf_op jit(solution)/shard_map/dot_general | solution.py:377
  40.9 1.4 %fusion.13.part_ref = f32[32,32,128]{2,1,0:T(8,128)} fusion(s32[32,32]{1,0:T(8,128)S(1)} %multiply_add_fusion, s32[256]{0:T(256)S(1)} %copy-done.9, f32[128,256]{1,0:T(8,128)S(1)} %bitcast_select_fusion), kind=kOutput, calls=%fused_computation.20 | convolution fusion | flops 402915328 | bytes 660480 | tf_op jit(solution)/shard_map/dot_general | solution.py:401
  42.3 32.3 %shard_map.149 = f32[32,32,128]{2,1,0:T(8,128)} custom-call(f32[32,32,128]{2,1,0:T(8,128)} %fusion.13.part_ref), custom_call_target="tpu_custom_call" | custom-call | tf_op jit(solution)/shard_map/pallas_call | solution.py:297
  74.6 1.3 %reduce_sum.29 = f32[32,32]{1,0:T(8,128)S(1)} reduce(f32[32,32,128]{2,1,0:T(8,128)} %shard_map.149, f32[]{:T(128)} %constant.127.clone.1), dimensions={2}, to_apply=%region_2.3 | reduce | flops 130048 | bytes 528388 | tf_op jit(solution)/shard_map/reduce_sum | solution.py:409
  76.1 2.9 %fusion.10 = f32[128,128]{1,0:T(8,128)S(1)} fusion(f32[32,32,128]{2,1,0:T(8,128)} %shard_map.149, f32[32,32]{1,0:T(8,128)S(1)} %div.69, f32[32,32]{1,0:T(8,128)S(1)} %broadcast_multiply_fusion), kind=kOutput, calls=%fused_computation.14 | convolution fusion | flops 201637888 | bytes 598016 | tf_op jit(solution)/shard_map/dot_general | solution.py:414
  79.0 11.7 %cholesky.17 = f32[128,128]{1,0:T(8,128)S(1)} custom-call(f32[128,128]{1,0:T(8,128)S(1)} %fusion.10), custom_call_target="Cholesky" | custom-call | tf_op jit(solution)/shard_map/cholesky | solution.py:101
  90.8 0.6 compare_reduce_fusion
  91.4 0.7 fusion.34
  92.1 9.8 %custom-call.7 = f32[1,128,128]{1,2,0:T(8,128)S(1)} custom-call(f32[1,128,128]{2,1,0:T(8,128)S(1)} %fusion.34), custom_call_target="InvertDiagBlocksLowerTriangular" | custom-call | tf_op jit(solution)/shard_map/triangular_solve | solution.py:105
  102.3 0.7 copy.18
  103.0 1.3 %fusion.21 = f32[128,32]{1,0:T(8,128)S(1)} fusion(f32[1024,128]{1,0:T(8,128)S(1)} %bitcast.57, f32[1024]{0:T(1024)S(1)} %get-tuple-element.31, f32[1024]{0:T(1024)S(1)} %div.72, f32[32,1024]{1,0:T(8,128)S(1)} %copy-done.11, f32[1024,32]{0,1:T(8,128)S(1)} %copy.19, f32[1024]{0:T(1024)S(1)} %get-tuple-element.30, f32[1024]{0:T(1024)S(1)} %copy-done.12), kind=kOutput, calls=%fused_computation.30 | convolution fusion | flops 50692096 | bytes 819200 | tf_op jit(solution)/shard_map/dot_general | solution.py:418
  105.0 1.8 %fusion = f32[32,8192]{1,0:T(8,128)S(1)} fusion(bf16[32,8192]{1,0:T(8,128)(2,1)} %collective-permute-done.2, bf16[32,8192]{1,0:T(8,128)(2,1)} %collective-permute-done.1, bf16[32,8192]{1,0:T(8,128)(2,1)} %collective-permute-done, bf16[32,8192]{1,0:T(8,128)(2,1)S(1)} %bitcast.64, bf16[32,32]{0,1:T(8,128)(2,1)S(1)} %get-tuple-element.27, ...), kind=kOutput, calls=%fused_computation.1 | convolution fusion | flops 75530240 | bytes 3153920 | tf_op jit(solution)/shard_map/dot_general | solution.py:440
  107.2 1.1 %add.97 = f32[32,4,8,256]{3,2,1,0:T(8,128)} add(f32[32,4,8,256]{3,2,1,0:T(8,128)S(1)} %copy-done.1, f32[32,4,8,256]{3,2,1,0:T(8,128)S(1)} %bitcast.58) | non-fusion elementwise | flops 262144 | bytes 3145728 | tf_op jit(solution)/shard_map/add | solution.py:441
  (68 shorter events, 4.6 us)
Async XLA Ops:
  0.6 39.5 %copy-start = (f32[1024]{0:T(1024)S(1)}, f32[1024]{0:T(1024)}, u32[]{:S(2)}) copy-start(f32[1024]{0:T(1024)} %param.17) | copy-start | bytes 12292
  4.0 12.4 %copy-start.1 = (f32[32,4,8,256]{3,2,1,0:T(8,128)S(1)}, f32[32,4,8,256]{3,2,1,0:T(8,128)}, u32[]{:S(2)}) copy-start(f32[32,4,8,256]{3,2,1,0:T(8,128)} %param.12) | copy-start | bytes 3145732
  16.4 5.6 %copy-start.3 = (f32[2,432,256]{2,1,0:T(8,128)S(1)}, f32[2,432,256]{2,1,0:T(8,128)}, u32[]{:S(2)}) copy-start(f32[2,432,256]{2,1,0:T(8,128)} %shard_map.147) | copy-start | bytes 2654212
  16.9 6.2 %copy-start.10 = (s32[256]{0:T(256)S(1)}, s32[256]{0:T(256)}, u32[]{:S(2)}) copy-start(s32[256]{0:T(256)} %param.18) | copy-start | bytes 3076
  16.9 6.2 %copy-start.4 = (f32[4,8,256]{2,1,0:T(8,128)S(1)}, f32[4,8,256]{2,1,0:T(8,128)}, u32[]{:S(2)}) copy-start(f32[4,8,256]{2,1,0:T(8,128)} %param.16) | copy-start | bytes 98308
  16.9 6.2 %copy-start.5 = (f32[4,8,256]{2,1,0:T(8,128)S(1)}, f32[4,8,256]{2,1,0:T(8,128)}, u32[]{:S(2)}) copy-start(f32[4,8,256]{2,1,0:T(8,128)} %param.15) | copy-start | bytes 98308
  16.9 6.2 %copy-start.6 = (f32[4,8,256]{2,1,0:T(8,128)S(1)}, f32[4,8,256]{2,1,0:T(8,128)}, u32[]{:S(2)}) copy-start(f32[4,8,256]{2,1,0:T(8,128)} %param.14) | copy-start | bytes 98308
  16.9 6.2 %copy-start.7 = (f32[4,8,256]{2,1,0:T(8,128)S(1)}, f32[4,8,256]{2,1,0:T(8,128)}, u32[]{:S(2)}) copy-start(f32[4,8,256]{2,1,0:T(8,128)} %param.13) | copy-start | bytes 98308
  16.9 88.0 %collective-permute-start = (bf16[32,8192]{1,0:T(8,128)(2,1)S(1)}, bf16[32,8192]{1,0:T(8,128)(2,1)}, u32[]{:S(2)}, u32[]{:S(2)}) collective-permute-start(bf16[32,8192]{1,0:T(8,128)(2,1)S(1)} %bitcast.61), channel_id=1, source_target_pairs={{0,1},{1,2},{2,3},{3,0},{4,5},{5,6},{6,7},{7,4},{8,9},{9,10},{10,1... | collective-permute-start | bytes 1572872 | tf_op jit(solution)/shard_map/ppermute | solution.py:427
  18.3 86.7 %collective-permute-start.1 = (bf16[32,8192]{1,0:T(8,128)(2,1)S(1)}, bf16[32,8192]{1,0:T(8,128)(2,1)}, u32[]{:S(2)}, u32[]{:S(2)}) collective-permute-start(bf16[32,8192]{1,0:T(8,128)(2,1)S(1)} %bitcast.62), channel_id=1, source_target_pairs={{0,2},{1,3},{2,0},{3,1},{4,6},{5,7},{6,4},{7,5},{8,10},{9,11},{10,... | collective-permute-start | bytes 1572872 | tf_op jit(solution)/shard_map/ppermute | solution.py:427
  20.9 84.1 %collective-permute-start.2 = (bf16[32,8192]{1,0:T(8,128)(2,1)S(1)}, bf16[32,8192]{1,0:T(8,128)(2,1)}, u32[]{:S(2)}, u32[]{:S(2)}) collective-permute-start(bf16[32,8192]{1,0:T(8,128)(2,1)S(1)} %bitcast.63), channel_id=1, source_target_pairs={{0,3},{1,0},{2,1},{3,2},{4,7},{5,4},{6,5},{7,6},{8,11},{9,8},{10,9... | collective-permute-start | bytes 1572872 | tf_op jit(solution)/shard_map/ppermute | solution.py:427
  25.7 14.5 %copy-start.9 = (s32[256]{0:T(256)S(1)}, s32[256]{0:T(256)}, u32[]{:S(2)}) copy-start(s32[256]{0:T(256)} %param.19) | copy-start | bytes 3076
  37.4 38.5 %copy-start.8 = (f32[1024]{0:T(1024)S(1)}, f32[1024]{0:T(1024)}, u32[]{:S(2)}) copy-start(f32[1024]{0:T(1024)} %param.22) | copy-start | bytes 12292
  74.6 27.2 %copy-start.2 = (f32[32,32,128]{2,1,0:T(8,128)S(1)}, f32[32,32,128]{2,1,0:T(8,128)}, u32[]{:S(2)}) copy-start(f32[32,32,128]{2,1,0:T(8,128)} %shard_map.149) | copy-start | bytes 1572868
  76.1 26.9 %copy-start.11 = (f32[32,1024]{1,0:T(8,128)S(1)}, f32[32,1024]{1,0:T(8,128)}, u32[]{:S(2)}) copy-start(f32[32,1024]{1,0:T(8,128)} %param.23) | copy-start | bytes 393220
  76.1 26.9 %copy-start.12 = (f32[1024]{0:T(1024)S(1)}, f32[1024]{0:T(1024)}, u32[]{:S(2)}) copy-start(f32[1024]{0:T(1024)} %param.21) | copy-start | bytes 12292

commit v12 on v11

--- a/solution.py
+++ b/solution.py
@@ -162,7 +162,14 @@
 
     lax.fori_loop(1, tile_count, wait_a_send, 0)
 
-    own_blk[...] = acc
+    groups = part_ref.shape[2] // member_count
+    lane_ids = lax.broadcasted_iota(jnp.int32, acc.shape, 1)
+    for q in range(member_count):
+        moved = pltpu.roll(acc, lax.rem((me_m - q + member_count) * groups, part_ref.shape[2]), 1)
+        own_blk[pl.ds(q, acc.shape[0], stride=member_count), :] = jnp.where(
+            lane_ids // groups == me_m, moved, 0.0
+        )
+    acc = own_blk[...]
 
     def copy_m(dst_m, src_m):
         return pltpu.make_async_remote_copy(
@@ -296,13 +303,13 @@
     vmem = pl.BlockSpec(memory_space=pltpu.VMEM)
     return pl.pallas_call(
         functools.partial(exchange_kernel, member_count),
-        out_shape=jax.ShapeDtypeStruct((tile_count, rows, lanes), jnp.float32),
+        out_shape=jax.ShapeDtypeStruct((tile_count, rows * member_count, lanes), jnp.float32),
         in_specs=[vmem],
         out_specs=vmem,
         scratch_shapes=[
             pltpu.VMEM((tile_count, rows, lanes), jnp.float32),
-            pltpu.VMEM((rows, lanes), jnp.float32),
-            pltpu.VMEM((member_count, rows, lanes), jnp.float32),
+            pltpu.VMEM((rows * member_count, lanes), jnp.float32),
+            pltpu.VMEM((member_count, rows * member_count, lanes), jnp.float32),
             pltpu.SemaphoreType.DMA((tile_count,)),
             pltpu.SemaphoreType.DMA((tile_count,)),
             pltpu.SemaphoreType.DMA((member_count,)),
@@ -393,15 +400,11 @@
     member_root = (members - 1) ** 0.5
     spread = jnp.sqrt(INFLATION * obs_var)
     member_count = lax.axis_size("member")
-    lane_group = jnp.arange(members, dtype=jnp.int32) // local_count
-    terms_wide = jnp.where(
-        (lane_group == member_rank)[:, None], jnp.tile(perf_terms, (member_count, 1)), 0.0
-    )
     contract_slots = (((0,), (1,)), ((), ()))
     pieces = lax.dot_general(
-        selector, terms_wide, contract_slots, precision=lax.Precision.HIGHEST,
+        selector, perf_terms, contract_slots, precision=lax.Precision.HIGHEST,
         preferred_element_type=jnp.float32,
-    ).reshape(tile_count, well_share, members)
+    ).reshape(tile_count, well_share * local_count // 128, 128)
     full = rates_exchange(pieces, member_count)
     own_block = lax.dynamic_index_in_dim(full, tile_rank, 0, keepdims=False)
     well_rates = lax.dynamic_slice_in_dim(own_block, member_rank * local_count, local_count, 1).T

time: 109 us -> 104 us (0.954)
  Pallas kernels: 53.6 us -> 49.3 us
  matrix products: 12.3 us -> 10.8 us
    pallas_call x1, Pallas kernels: 32.3 us -> 28 us  [rates_exchange(): pl.pallas_call(functools.partial(exchange_kernel, member_count), out_shap...]
  transfers between devices with their start and end apart: 3 -> 3, of which waited for: 0 -> 0; matrix products, arithmetic and copies ran while one was open for 37% -> 38% of each run, Pallas kernels for 39% -> 37%
where the time goes in v12:
time: 104 us; the launch traced here: 103 us
  Pallas kernels  49.3 us (47%)
  other arithmetic  30.3 us (29%)
  matrix products  10.8 us (10%)
  local copies, waits for them, and re-layouts  5.76 us (6%)
  starting transfers between devices  5.05 us (5%)
  between operations  1.73 us (2%)
    pallas_call x1, Pallas kernels, rates_exchange(): pl.pallas_call(functools.partial(exchange_kernel, member_count), out_shap...  28 us
    another operation x3, other arithmetic, solve_spd(): lax.linalg.cholesky(gram_matrix + jnp.eye(gram_matrix.shape[0], dtype=jnp...  12.4 us
    pallas_call x1, Pallas kernels, halo_exchange(): pl.pallas_call(halo_kernel, out_shape=jax.ShapeDtypeStruct(outgoing.shape...  11.4 us
    another operation x2, other arithmetic, solve_spd(): lax.linalg.triangular_solve(factor, halfway, left_side=True, lower=True,...  10.5 us
    pallas_call x1, Pallas kernels, stencil(): pl.pallas_call(functools.partial(stencil_kernel, rim), grid=(members // b...  9.88 us
    ppermute x3, starting transfers between devices, per_device(): anomaly_parts.append(lax.ppermute(anomaly, 'member', pairs))  5.05 us
    dot_general x2, matrix products, pick_cells(): jnp.dot(values_in.reshape(local_count * plane_rows, strip_depth), col_pic...  3.74 us
    dot_general x1, matrix products, per_device(): lax.dot_general(scaled_t, scaled_t, contract_wells, precision=lax.Precisi...  2.86 us
  transfers between devices with their start and end apart: 3, of which 0 were waited for; matrix products, arithmetic and copies ran while one was open for 38% of the time, Pallas kernels for 37%

profile of v12, /device:TPU:1, one launch (start us, length us, event | category | flops | bytes accessed | tf_op | source)
XLA Modules:
  0.0 103.0 jit_solution(17796586354552909929)
XLA Ops:
  0.6 0.8 pad_maximum_fusion.3
  1.6 1.9 %fusion.52 = (f32[32,4,3,256]{3,2,1,0:T(4,128)S(1)}, f32[32,4,3,256]{3,2,1,0:T(4,128)S(1)}) fusion(f32[32,4,8,256]{3,2,1,0:T(8,128)} %param.12), kind=kLoop, calls=%fused_computation.86 | loop fusion | bytes 1572864 | tf_op jit(solution)/shard_map/slice | solution.py:352
  4.0 1.0 pad_maximum_fusion.1.out_ref
  5.0 11.4 %shard_map.147 = f32[2,432,256]{2,1,0:T(8,128)} custom-call(f32[2,432,256]{2,1,0:T(8,128)} %pad_maximum_fusion.1.out_ref), custom_call_target="tpu_custom_call" | custom-call | tf_op jit(solution)/shard_map/pallas_call | solution.py:291
  16.9 1.4 %collective-permute-start = (bf16[32,8192]{1,0:T(8,128)(2,1)S(1)}, bf16[32,8192]{1,0:T(8,128)(2,1)}, u32[]{:S(2)}, u32[]{:S(2)}) collective-permute-start(bf16[32,8192]{1,0:T(8,128)(2,1)S(1)} %bitcast.56), channel_id=1, source_target_pairs={{0,1},{1,2},{2,3},{3,0},{4,5},{5,6},{6,7},{7,4},{8,9},{9,10},{10,1... | collective-permute-start | bytes 1572872 | tf_op jit(solution)/shard_map/ppermute | solution.py:430
  18.3 2.6 %collective-permute-start.1 = (bf16[32,8192]{1,0:T(8,128)(2,1)S(1)}, bf16[32,8192]{1,0:T(8,128)(2,1)}, u32[]{:S(2)}, u32[]{:S(2)}) collective-permute-start(bf16[32,8192]{1,0:T(8,128)(2,1)S(1)} %bitcast.57), channel_id=1, source_target_pairs={{0,2},{1,3},{2,0},{3,1},{4,6},{5,7},{6,4},{7,5},{8,10},{9,11},{10,... | collective-permute-start | bytes 1572872 | tf_op jit(solution)/shard_map/ppermute | solution.py:430
  20.9 1.1 %collective-permute-start.2 = (bf16[32,8192]{1,0:T(8,128)(2,1)S(1)}, bf16[32,8192]{1,0:T(8,128)(2,1)}, u32[]{:S(2)}, u32[]{:S(2)}) collective-permute-start(bf16[32,8192]{1,0:T(8,128)(2,1)S(1)} %bitcast.58), channel_id=1, source_target_pairs={{0,3},{1,0},{2,1},{3,2},{4,7},{5,4},{6,5},{7,6},{8,11},{9,8},{10,9... | collective-permute-start | bytes 1572872 | tf_op jit(solution)/shard_map/ppermute | solution.py:430
  23.1 0.8 pad_maximum_fusion.2.fields_ref
  23.9 1.8 %pad_maximum_fusion.lp_ref = f32[32,4,14,256]{3,2,1,0:T(8,128)} fusion(f32[32,4,3,256]{3,2,1,0:T(4,128)S(1)} %reshape_squeeze.13, f32[32,4,8,256]{3,2,1,0:T(8,128)S(1)} %copy-done.1, f32[32,4,3,256]{3,2,1,0:T(4,128)S(1)} %reshape_squeeze.12), kind=kLoop, calls=%fused_computation | loop fusion | flops 917504 | bytes 3670016 | tf_op jit(solution)/shard_map/concatenate | solution.py:369
  25.6 9.9 %shard_map.148 = (f32[32,4,8,256]{3,2,1,0:T(8,128)}, f32[32,4,8,256]{3,2,1,0:T(8,128)}, f32[32,4,8,256]{3,2,1,0:T(8,128)}) custom-call(f32[32,4,14,256]{3,2,1,0:T(8,128)} %pad_maximum_fusion.lp_ref, f32[4,4,14,256]{3,2,1,0:T(8,128)} %pad_maximum_fusion.2.fields_ref, f32[14]{0:T(128)} %and_convert_fusion.inside_ref), custom_call_target="tpu_custom_call" | custom-call | tf_op jit(solution)/shard_map/pallas_call | solution.py:251
  35.5 1.9 %fusion.9 = f32[32,256]{1,0:T(8,128)S(1)} fusion(f32[32,4,8,256]{3,2,1,0:T(8,128)} %get-tuple-element.19, pred[32,256]{1,0:T(8,128)(4,1)S(1)} %iota_compare_fusion.5, s32[256]{0:T(256)S(1)} %get-tuple-element.36), kind=kOutput, calls=%fused_computation.12 | convolution fusion | flops 805888000 | bytes 1090560 | tf_op jit(solution)/shard_map/dot_general | solution.py:384
  37.4 1.9 %fusion.8 = f32[32,256]{1,0:T(8,128)S(1)} fusion(f32[32,4,8,256]{3,2,1,0:T(8,128)} %get-tuple-element.10, pred[32,256]{1,0:T(8,128)(4,1)S(1)} %iota_compare_fusion.5, s32[256]{0:T(256)S(1)} %get-tuple-element.36), kind=kOutput, calls=%fused_computation.11 | convolution fusion | flops 805888000 | bytes 1090560 | tf_op jit(solution)/shard_map/dot_general | solution.py:384
  40.6 0.8 fusion.15
  41.4 0.8 reshape.117.part_ref
  42.2 28.0 %shard_map.149 = f32[32,32,128]{2,1,0:T(8,128)} custom-call(f32[32,8,128]{2,1,0:T(8,128)} %reshape.117.part_ref), custom_call_target="tpu_custom_call" | custom-call | tf_op jit(solution)/shard_map/pallas_call | solution.py:304
  70.2 1.3 %reduce_sum.29 = f32[32,32]{1,0:T(8,128)S(1)} reduce(f32[32,32,128]{2,1,0:T(8,128)} %shard_map.149, f32[]{:T(128)} %constant.107.clone.1), dimensions={2}, to_apply=%region_2.3 | reduce | flops 130048 | bytes 528388 | tf_op jit(solution)/shard_map/reduce_sum | solution.py:412
  71.7 2.9 %fusion.10 = f32[128,128]{1,0:T(8,128)S(1)} fusion(f32[32,32,128]{2,1,0:T(8,128)} %shard_map.149, f32[32,32]{1,0:T(8,128)S(1)} %div.56, f32[32,32]{1,0:T(8,128)S(1)} %broadcast_multiply_fusion), kind=kOutput, calls=%fused_computation.14 | convolution fusion | flops 201637888 | bytes 598016 | tf_op jit(solution)/shard_map/dot_general | solution.py:417
  74.6 11.7 %cholesky.17 = f32[128,128]{1,0:T(8,128)S(1)} custom-call(f32[128,128]{1,0:T(8,128)S(1)} %fusion.10), custom_call_target="Cholesky" | custom-call | tf_op jit(solution)/shard_map/cholesky | solution.py:101
  86.3 0.6 compare_reduce_fusion
  86.9 0.7 fusion.33
  87.6 9.8 %custom-call.7 = f32[1,128,128]{1,2,0:T(8,128)S(1)} custom-call(f32[1,128,128]{2,1,0:T(8,128)S(1)} %fusion.33), custom_call_target="InvertDiagBlocksLowerTriangular" | custom-call | tf_op jit(solution)/shard_map/triangular_solve | solution.py:105
  97.9 0.7 copy.23
  99.7 1.8 %fusion = f32[32,8192]{1,0:T(8,128)S(1)} fusion(bf16[32,8192]{1,0:T(8,128)(2,1)} %collective-permute-done.2, bf16[32,8192]{1,0:T(8,128)(2,1)} %collective-permute-done.1, bf16[32,8192]{1,0:T(8,128)(2,1)} %collective-permute-done, bf16[32,8192]{1,0:T(8,128)(2,1)S(1)} %bitcast.59, bf16[32,32]{0,1:T(8,128)(2,1)S(1)} %get-tuple-element.31, ...), kind=kOutput, calls=%fused_computation.1 | convolution fusion | flops 75530240 | bytes 3153920 | tf_op jit(solution)/shard_map/dot_general | solution.py:443
  101.9 1.1 %add.82 = f32[32,4,8,256]{3,2,1,0:T(8,128)} add(f32[32,4,8,256]{3,2,1,0:T(8,128)S(1)} %copy-done.1, f32[32,4,8,256]{3,2,1,0:T(8,128)S(1)} %bitcast.53) | non-fusion elementwise | flops 262144 | bytes 3145728 | tf_op jit(solution)/shard_map/add | solution.py:444
  (61 shorter events, 4.7 us)
Async XLA Ops:
  0.6 39.3 %copy-start = (f32[1024]{0:T(1024)S(1)}, f32[1024]{0:T(1024)}, u32[]{:S(2)}) copy-start(f32[1024]{0:T(1024)} %param.17) | copy-start | bytes 12292
  4.0 12.4 %copy-start.1 = (f32[32,4,8,256]{3,2,1,0:T(8,128)S(1)}, f32[32,4,8,256]{3,2,1,0:T(8,128)}, u32[]{:S(2)}) copy-start(f32[32,4,8,256]{3,2,1,0:T(8,128)} %param.12) | copy-start | bytes 3145732
  16.4 5.6 %copy-start.3 = (f32[2,432,256]{2,1,0:T(8,128)S(1)}, f32[2,432,256]{2,1,0:T(8,128)}, u32[]{:S(2)}) copy-start(f32[2,432,256]{2,1,0:T(8,128)} %shard_map.147) | copy-start | bytes 2654212
  16.9 6.1 %copy-start.10 = (s32[256]{0:T(256)S(1)}, s32[256]{0:T(256)}, u32[]{:S(2)}) copy-start(s32[256]{0:T(256)} %param.18) | copy-start | bytes 3076
  16.9 6.2 %copy-start.4 = (f32[4,8,256]{2,1,0:T(8,128)S(1)}, f32[4,8,256]{2,1,0:T(8,128)}, u32[]{:S(2)}) copy-start(f32[4,8,256]{2,1,0:T(8,128)} %param.16) | copy-start | bytes 98308
  16.9 6.2 %copy-start.5 = (f32[4,8,256]{2,1,0:T(8,128)S(1)}, f32[4,8,256]{2,1,0:T(8,128)}, u32[]{:S(2)}) copy-start(f32[4,8,256]{2,1,0:T(8,128)} %param.15) | copy-start | bytes 98308
  16.9 6.2 %copy-start.6 = (f32[4,8,256]{2,1,0:T(8,128)S(1)}, f32[4,8,256]{2,1,0:T(8,128)}, u32[]{:S(2)}) copy-start(f32[4,8,256]{2,1,0:T(8,128)} %param.14) | copy-start | bytes 98308
  16.9 6.2 %copy-start.7 = (f32[4,8,256]{2,1,0:T(8,128)S(1)}, f32[4,8,256]{2,1,0:T(8,128)}, u32[]{:S(2)}) copy-start(f32[4,8,256]{2,1,0:T(8,128)} %param.13) | copy-start | bytes 98308
  16.9 82.8 %collective-permute-start = (bf16[32,8192]{1,0:T(8,128)(2,1)S(1)}, bf16[32,8192]{1,0:T(8,128)(2,1)}, u32[]{:S(2)}, u32[]{:S(2)}) collective-permute-start(bf16[32,8192]{1,0:T(8,128)(2,1)S(1)} %bitcast.56), channel_id=1, source_target_pairs={{0,1},{1,2},{2,3},{3,0},{4,5},{5,6},{6,7},{7,4},{8,9},{9,10},{10,1... | collective-permute-start | bytes 1572872 | tf_op jit(solution)/shard_map/ppermute | solution.py:430
  18.3 81.4 %collective-permute-start.1 = (bf16[32,8192]{1,0:T(8,128)(2,1)S(1)}, bf16[32,8192]{1,0:T(8,128)(2,1)}, u32[]{:S(2)}, u32[]{:S(2)}) collective-permute-start(bf16[32,8192]{1,0:T(8,128)(2,1)S(1)} %bitcast.57), channel_id=1, source_target_pairs={{0,2},{1,3},{2,0},{3,1},{4,6},{5,7},{6,4},{7,5},{8,10},{9,11},{10,... | collective-permute-start | bytes 1572872 | tf_op jit(solution)/shard_map/ppermute | solution.py:430
  20.9 78.8 %collective-permute-start.2 = (bf16[32,8192]{1,0:T(8,128)(2,1)S(1)}, bf16[32,8192]{1,0:T(8,128)(2,1)}, u32[]{:S(2)}, u32[]{:S(2)}) collective-permute-start(bf16[32,8192]{1,0:T(8,128)(2,1)S(1)} %bitcast.58), channel_id=1, source_target_pairs={{0,3},{1,0},{2,1},{3,2},{4,7},{5,4},{6,5},{7,6},{8,11},{9,8},{10,9... | collective-permute-start | bytes 1572872 | tf_op jit(solution)/shard_map/ppermute | solution.py:430
  25.6 14.3 %copy-start.9 = (s32[256]{0:T(256)S(1)}, s32[256]{0:T(256)}, u32[]{:S(2)}) copy-start(s32[256]{0:T(256)} %param.19) | copy-start | bytes 3076
  37.4 34.1 %copy-start.8 = (f32[1024]{0:T(1024)S(1)}, f32[1024]{0:T(1024)}, u32[]{:S(2)}) copy-start(f32[1024]{0:T(1024)} %param.22) | copy-start | bytes 12292
  70.2 27.2 %copy-start.2 = (f32[32,32,128]{2,1,0:T(8,128)S(1)}, f32[32,32,128]{2,1,0:T(8,128)}, u32[]{:S(2)}) copy-start(f32[32,32,128]{2,1,0:T(8,128)} %shard_map.149) | copy-start | bytes 1572868
  71.7 26.9 %copy-start.11 = (f32[32,1024]{1,0:T(8,128)S(1)}, f32[32,1024]{1,0:T(8,128)}, u32[]{:S(2)}) copy-start(f32[32,1024]{1,0:T(8,128)} %param.23) | copy-start | bytes 393220
  71.7 26.9 %copy-start.12 = (f32[1024]{0:T(1024)S(1)}, f32[1024]{0:T(1024)}, u32[]{:S(2)}) copy-start(f32[1024]{0:T(1024)} %param.21) | copy-start | bytes 12292

commit v13 on v12

--- a/solution.py
+++ b/solution.py
@@ -244,7 +244,7 @@
 
 def stencil(lp_ext, fields_ext, inside, rim):
     members, layers, rows, depth = lp_ext.shape
-    block = 4
+    block = 8
     out_rows = rows - 2 * rim
     out_spec = pl.BlockSpec((block, layers, out_rows, depth), lambda i: (i, 0, 0, 0))
     out_shape = jax.ShapeDtypeStruct((members, layers, out_rows, depth), jnp.float32)

time: 104 us -> 103 us (level)
  no operation moved by 1% of the time
where the time goes in v13:
time: 103 us
  Pallas kernels  49.1 us (48%)
  other arithmetic  30.3 us (29%)
  matrix products  10.8 us (10%)
  local copies, waits for them, and re-layouts  5.76 us (6%)
  starting transfers between devices  5.05 us (5%)
  between operations  1.73 us (2%)
    pallas_call x1, Pallas kernels, rates_exchange(): pl.pallas_call(functools.partial(exchange_kernel, member_count), out_shap...  28 us
    another operation x3, other arithmetic, solve_spd(): lax.linalg.cholesky(gram_matrix + jnp.eye(gram_matrix.shape[0], dtype=jnp...  12.4 us
    pallas_call x1, Pallas kernels, halo_exchange(): pl.pallas_call(halo_kernel, out_shape=jax.ShapeDtypeStruct(outgoing.shape...  11.4 us
    another operation x2, other arithmetic, solve_spd(): lax.linalg.triangular_solve(factor, halfway, left_side=True, lower=True,...  10.5 us
    pallas_call x1, Pallas kernels, stencil(): pl.pallas_call(functools.partial(stencil_kernel, rim), grid=(members // b...  9.69 us
    ppermute x3, starting transfers between devices, per_device(): anomaly_parts.append(lax.ppermute(anomaly, 'member', pairs))  5.05 us
    dot_general x2, matrix products, pick_cells(): jnp.dot(values_in.reshape(local_count * plane_rows, strip_depth), col_pic...  3.74 us
    dot_general x1, matrix products, per_device(): lax.dot_general(scaled_t, scaled_t, contract_wells, precision=lax.Precisi...  2.86 us
  transfers between devices with their start and end apart: 3, of which 0 were waited for; matrix products, arithmetic and copies ran while one was open for 38% of the time, Pallas kernels for 37%

profile of v13, /device:TPU:1, one launch (start us, length us, event | category | flops | bytes accessed | tf_op | source)
XLA Modules:
  0.0 102.8 jit_solution(4036622450859734866)
XLA Ops:
  0.6 0.8 pad_maximum_fusion.3
  1.6 1.9 %fusion.52 = (f32[32,4,3,256]{3,2,1,0:T(4,128)S(1)}, f32[32,4,3,256]{3,2,1,0:T(4,128)S(1)}) fusion(f32[32,4,8,256]{3,2,1,0:T(8,128)} %param.12), kind=kLoop, calls=%fused_computation.86 | loop fusion | bytes 1572864 | tf_op jit(solution)/shard_map/slice | solution.py:352
  4.0 1.0 pad_maximum_fusion.1.out_ref
  5.0 11.4 %shard_map.147 = f32[2,432,256]{2,1,0:T(8,128)} custom-call(f32[2,432,256]{2,1,0:T(8,128)} %pad_maximum_fusion.1.out_ref), custom_call_target="tpu_custom_call" | custom-call | tf_op jit(solution)/shard_map/pallas_call | solution.py:291
  16.9 1.4 %collective-permute-start = (bf16[32,8192]{1,0:T(8,128)(2,1)S(1)}, bf16[32,8192]{1,0:T(8,128)(2,1)}, u32[]{:S(2)}, u32[]{:S(2)}) collective-permute-start(bf16[32,8192]{1,0:T(8,128)(2,1)S(1)} %bitcast.56), channel_id=1, source_target_pairs={{0,1},{1,2},{2,3},{3,0},{4,5},{5,6},{6,7},{7,4},{8,9},{9,10},{10,1... | collective-permute-start | bytes 1572872 | tf_op jit(solution)/shard_map/ppermute | solution.py:430
  18.3 2.6 %collective-permute-start.1 = (bf16[32,8192]{1,0:T(8,128)(2,1)S(1)}, bf16[32,8192]{1,0:T(8,128)(2,1)}, u32[]{:S(2)}, u32[]{:S(2)}) collective-permute-start(bf16[32,8192]{1,0:T(8,128)(2,1)S(1)} %bitcast.57), channel_id=1, source_target_pairs={{0,2},{1,3},{2,0},{3,1},{4,6},{5,7},{6,4},{7,5},{8,10},{9,11},{10,... | collective-permute-start | bytes 1572872 | tf_op jit(solution)/shard_map/ppermute | solution.py:430
  20.9 1.1 %collective-permute-start.2 = (bf16[32,8192]{1,0:T(8,128)(2,1)S(1)}, bf16[32,8192]{1,0:T(8,128)(2,1)}, u32[]{:S(2)}, u32[]{:S(2)}) collective-permute-start(bf16[32,8192]{1,0:T(8,128)(2,1)S(1)} %bitcast.58), channel_id=1, source_target_pairs={{0,3},{1,0},{2,1},{3,2},{4,7},{5,4},{6,5},{7,6},{8,11},{9,8},{10,9... | collective-permute-start | bytes 1572872 | tf_op jit(solution)/shard_map/ppermute | solution.py:430
  23.1 0.8 pad_maximum_fusion.2.fields_ref
  23.9 1.8 %pad_maximum_fusion.lp_ref = f32[32,4,14,256]{3,2,1,0:T(8,128)} fusion(f32[32,4,3,256]{3,2,1,0:T(4,128)S(1)} %reshape_squeeze.13, f32[32,4,8,256]{3,2,1,0:T(8,128)S(1)} %copy-done.1, f32[32,4,3,256]{3,2,1,0:T(4,128)S(1)} %reshape_squeeze.12), kind=kLoop, calls=%fused_computation | loop fusion | flops 917504 | bytes 3670016 | tf_op jit(solution)/shard_map/concatenate | solution.py:369
  25.6 9.7 %shard_map.148 = (f32[32,4,8,256]{3,2,1,0:T(8,128)}, f32[32,4,8,256]{3,2,1,0:T(8,128)}, f32[32,4,8,256]{3,2,1,0:T(8,128)}) custom-call(f32[32,4,14,256]{3,2,1,0:T(8,128)} %pad_maximum_fusion.lp_ref, f32[4,4,14,256]{3,2,1,0:T(8,128)} %pad_maximum_fusion.2.fields_ref, f32[14]{0:T(128)} %and_convert_fusion.inside_ref), custom_call_target="tpu_custom_call" | custom-call | tf_op jit(solution)/shard_map/pallas_call | solution.py:251
  35.3 1.9 %fusion.9 = f32[32,256]{1,0:T(8,128)S(1)} fusion(f32[32,4,8,256]{3,2,1,0:T(8,128)} %get-tuple-element.19, pred[32,256]{1,0:T(8,128)(4,1)S(1)} %iota_compare_fusion.5, s32[256]{0:T(256)S(1)} %get-tuple-element.36), kind=kOutput, calls=%fused_computation.12 | convolution fusion | flops 805888000 | bytes 1090560 | tf_op jit(solution)/shard_map/dot_general | solution.py:384
  37.2 1.9 %fusion.8 = f32[32,256]{1,0:T(8,128)S(1)} fusion(f32[32,4,8,256]{3,2,1,0:T(8,128)} %get-tuple-element.10, pred[32,256]{1,0:T(8,128)(4,1)S(1)} %iota_compare_fusion.5, s32[256]{0:T(256)S(1)} %get-tuple-element.36), kind=kOutput, calls=%fused_computation.11 | convolution fusion | flops 805888000 | bytes 1090560 | tf_op jit(solution)/shard_map/dot_general | solution.py:384
  40.4 0.8 fusion.15
  41.2 0.8 reshape.117.part_ref
  42.0 28.0 %shard_map.149 = f32[32,32,128]{2,1,0:T(8,128)} custom-call(f32[32,8,128]{2,1,0:T(8,128)} %reshape.117.part_ref), custom_call_target="tpu_custom_call" | custom-call | tf_op jit(solution)/shard_map/pallas_call | solution.py:304
  70.0 1.3 %reduce_sum.29 = f32[32,32]{1,0:T(8,128)S(1)} reduce(f32[32,32,128]{2,1,0:T(8,128)} %shard_map.149, f32[]{:T(128)} %constant.107.clone.1), dimensions={2}, to_apply=%region_2.3 | reduce | flops 130048 | bytes 528388 | tf_op jit(solution)/shard_map/reduce_sum | solution.py:412
  71.5 2.9 %fusion.10 = f32[128,128]{1,0:T(8,128)S(1)} fusion(f32[32,32,128]{2,1,0:T(8,128)} %shard_map.149, f32[32,32]{1,0:T(8,128)S(1)} %div.56, f32[32,32]{1,0:T(8,128)S(1)} %broadcast_multiply_fusion), kind=kOutput, calls=%fused_computation.14 | convolution fusion | flops 201637888 | bytes 598016 | tf_op jit(solution)/shard_map/dot_general | solution.py:417
  74.4 11.7 %cholesky.17 = f32[128,128]{1,0:T(8,128)S(1)} custom-call(f32[128,128]{1,0:T(8,128)S(1)} %fusion.10), custom_call_target="Cholesky" | custom-call | tf_op jit(solution)/shard_map/cholesky | solution.py:101
  86.1 0.6 compare_reduce_fusion
  86.8 0.7 fusion.33
  87.4 9.8 %custom-call.7 = f32[1,128,128]{1,2,0:T(8,128)S(1)} custom-call(f32[1,128,128]{2,1,0:T(8,128)S(1)} %fusion.33), custom_call_target="InvertDiagBlocksLowerTriangular" | custom-call | tf_op jit(solution)/shard_map/triangular_solve | solution.py:105
  97.7 0.7 copy.23
  99.6 1.8 %fusion = f32[32,8192]{1,0:T(8,128)S(1)} fusion(bf16[32,8192]{1,0:T(8,128)(2,1)} %collective-permute-done.2, bf16[32,8192]{1,0:T(8,128)(2,1)} %collective-permute-done.1, bf16[32,8192]{1,0:T(8,128)(2,1)} %collective-permute-done, bf16[32,8192]{1,0:T(8,128)(2,1)S(1)} %bitcast.59, bf16[32,32]{0,1:T(8,128)(2,1)S(1)} %get-tuple-element.31, ...), kind=kOutput, calls=%fused_computation.1 | convolution fusion | flops 75530240 | bytes 3153920 | tf_op jit(solution)/shard_map/dot_general | solution.py:443
  101.7 1.1 %add.82 = f32[32,4,8,256]{3,2,1,0:T(8,128)} add(f32[32,4,8,256]{3,2,1,0:T(8,128)S(1)} %copy-done.1, f32[32,4,8,256]{3,2,1,0:T(8,128)S(1)} %bitcast.53) | non-fusion elementwise | flops 262144 | bytes 3145728 | tf_op jit(solution)/shard_map/add | solution.py:444
  (61 shorter events, 4.7 us)
Async XLA Ops:
  0.6 39.1 %copy-start = (f32[1024]{0:T(1024)S(1)}, f32[1024]{0:T(1024)}, u32[]{:S(2)}) copy-start(f32[1024]{0:T(1024)} %param.17) | copy-start | bytes 12292
  4.0 12.4 %copy-start.1 = (f32[32,4,8,256]{3,2,1,0:T(8,128)S(1)}, f32[32,4,8,256]{3,2,1,0:T(8,128)}, u32[]{:S(2)}) copy-start(f32[32,4,8,256]{3,2,1,0:T(8,128)} %param.12) | copy-start | bytes 3145732
  16.4 5.6 %copy-start.3 = (f32[2,432,256]{2,1,0:T(8,128)S(1)}, f32[2,432,256]{2,1,0:T(8,128)}, u32[]{:S(2)}) copy-start(f32[2,432,256]{2,1,0:T(8,128)} %shard_map.147) | copy-start | bytes 2654212
  16.9 6.1 %copy-start.10 = (s32[256]{0:T(256)S(1)}, s32[256]{0:T(256)}, u32[]{:S(2)}) copy-start(s32[256]{0:T(256)} %param.18) | copy-start | bytes 3076
  16.9 6.2 %copy-start.4 = (f32[4,8,256]{2,1,0:T(8,128)S(1)}, f32[4,8,256]{2,1,0:T(8,128)}, u32[]{:S(2)}) copy-start(f32[4,8,256]{2,1,0:T(8,128)} %param.16) | copy-start | bytes 98308
  16.9 6.2 %copy-start.5 = (f32[4,8,256]{2,1,0:T(8,128)S(1)}, f32[4,8,256]{2,1,0:T(8,128)}, u32[]{:S(2)}) copy-start(f32[4,8,256]{2,1,0:T(8,128)} %param.15) | copy-start | bytes 98308
  16.9 6.2 %copy-start.6 = (f32[4,8,256]{2,1,0:T(8,128)S(1)}, f32[4,8,256]{2,1,0:T(8,128)}, u32[]{:S(2)}) copy-start(f32[4,8,256]{2,1,0:T(8,128)} %param.14) | copy-start | bytes 98308
  16.9 6.2 %copy-start.7 = (f32[4,8,256]{2,1,0:T(8,128)S(1)}, f32[4,8,256]{2,1,0:T(8,128)}, u32[]{:S(2)}) copy-start(f32[4,8,256]{2,1,0:T(8,128)} %param.13) | copy-start | bytes 98308
  16.9 82.6 %collective-permute-start = (bf16[32,8192]{1,0:T(8,128)(2,1)S(1)}, bf16[32,8192]{1,0:T(8,128)(2,1)}, u32[]{:S(2)}, u32[]{:S(2)}) collective-permute-start(bf16[32,8192]{1,0:T(8,128)(2,1)S(1)} %bitcast.56), channel_id=1, source_target_pairs={{0,1},{1,2},{2,3},{3,0},{4,5},{5,6},{6,7},{7,4},{8,9},{9,10},{10,1... | collective-permute-start | bytes 1572872 | tf_op jit(solution)/shard_map/ppermute | solution.py:430
  18.3 81.2 %collective-permute-start.1 = (bf16[32,8192]{1,0:T(8,128)(2,1)S(1)}, bf16[32,8192]{1,0:T(8,128)(2,1)}, u32[]{:S(2)}, u32[]{:S(2)}) collective-permute-start(bf16[32,8192]{1,0:T(8,128)(2,1)S(1)} %bitcast.57), channel_id=1, source_target_pairs={{0,2},{1,3},{2,0},{3,1},{4,6},{5,7},{6,4},{7,5},{8,10},{9,11},{10,... | collective-permute-start | bytes 1572872 | tf_op jit(solution)/shard_map/ppermute | solution.py:430
  20.9 78.6 %collective-permute-start.2 = (bf16[32,8192]{1,0:T(8,128)(2,1)S(1)}, bf16[32,8192]{1,0:T(8,128)(2,1)}, u32[]{:S(2)}, u32[]{:S(2)}) collective-permute-start(bf16[32,8192]{1,0:T(8,128)(2,1)S(1)} %bitcast.58), channel_id=1, source_target_pairs={{0,3},{1,0},{2,1},{3,2},{4,7},{5,4},{6,5},{7,6},{8,11},{9,8},{10,9... | collective-permute-start | bytes 1572872 | tf_op jit(solution)/shard_map/ppermute | solution.py:430
  25.6 14.1 %copy-start.9 = (s32[256]{0:T(256)S(1)}, s32[256]{0:T(256)}, u32[]{:S(2)}) copy-start(s32[256]{0:T(256)} %param.19) | copy-start | bytes 3076
  37.2 34.1 %copy-start.8 = (f32[1024]{0:T(1024)S(1)}, f32[1024]{0:T(1024)}, u32[]{:S(2)}) copy-start(f32[1024]{0:T(1024)} %param.22) | copy-start | bytes 12292
  70.0 27.2 %copy-start.2 = (f32[32,32,128]{2,1,0:T(8,128)S(1)}, f32[32,32,128]{2,1,0:T(8,128)}, u32[]{:S(2)}) copy-start(f32[32,32,128]{2,1,0:T(8,128)} %shard_map.149) | copy-start | bytes 1572868
  71.5 26.9 %copy-start.11 = (f32[32,1024]{1,0:T(8,128)S(1)}, f32[32,1024]{1,0:T(8,128)}, u32[]{:S(2)}) copy-start(f32[32,1024]{1,0:T(8,128)} %param.23) | copy-start | bytes 393220
  71.5 26.9 %copy-start.12 = (f32[1024]{0:T(1024)S(1)}, f32[1024]{0:T(1024)}, u32[]{:S(2)}) copy-start(f32[1024]{0:T(1024)} %param.21) | copy-start | bytes 12292

commit v14 on v12

--- a/solution.py
+++ b/solution.py
@@ -380,11 +380,18 @@
     )
     row_pick = jnp.arange(plane_rows, dtype=jnp.int32)[:, None] == cell_row[None, :]
 
+    col_pick_low = col_pick.astype(jnp.bfloat16)
+
     def pick_cells(values_in):
-        by_col = jnp.dot(
-            values_in.reshape(local_count * plane_rows, strip_depth), col_pick,
-            precision=lax.Precision.HIGHEST, preferred_element_type=jnp.float32,
-        ).reshape(local_count, plane_rows, -1)
+        flat = values_in.reshape(local_count * plane_rows, strip_depth)
+        high = lax.reduce_precision(flat, exponent_bits=8, mantissa_bits=7)
+        rest = flat - high
+        middle = lax.reduce_precision(rest, exponent_bits=8, mantissa_bits=7)
+        low = rest - middle
+        split = jnp.concatenate([high, middle, low]).astype(jnp.bfloat16)
+        parts = jnp.dot(split, col_pick_low, preferred_element_type=jnp.float32)
+        parts = parts.reshape(3, local_count, plane_rows, -1)
+        by_col = parts[0] + parts[1] + parts[2]
         return jnp.sum(jnp.where(row_pick[None], by_col, 0.0), axis=1)
 
     perf_mob = pick_cells(mobility)

time: 104 us -> 106 us (1.019)
  other arithmetic: 30.3 us -> 33.1 us
  matrix products: 10.8 us -> 9.19 us
  local copies, waits for them, and re-layouts: 5.76 us -> 7.37 us
    dot_general x2, matrix products: 3.74 us -> 1.16 us  [pick_cells(): parts = jnp.dot(split, col_pick_low, preferred_element_type=jnp.float32)]
    another operation x0 -> x2, other arithmetic: none -> 1.82 us
    unnamed x30 -> x32, local copies, waits for them, and re-layouts: 1.56 us -> 2.36 us
  transfers between devices with their start and end apart: 3 -> 3, of which waited for: 0 -> 0; matrix products, arithmetic and copies ran while one was open for 38% -> 38% of each run, Pallas kernels for 37% -> 36%
where the time goes in v14:
time: 106 us
  Pallas kernels  49.3 us (47%)
  other arithmetic  33.1 us (31%)
  matrix products  9.19 us (9%)
  local copies, waits for them, and re-layouts  7.37 us (7%)
  starting transfers between devices  4.99 us (5%)
  between operations  1.73 us (2%)
    pallas_call x1, Pallas kernels, rates_exchange(): pl.pallas_call(functools.partial(exchange_kernel, member_count), out_shap...  28 us
    another operation x3, other arithmetic, solve_spd(): lax.linalg.cholesky(gram_matrix + jnp.eye(gram_matrix.shape[0], dtype=jnp...  12.4 us
    pallas_call x1, Pallas kernels, halo_exchange(): pl.pallas_call(halo_kernel, out_shape=jax.ShapeDtypeStruct(outgoing.shape...  11.4 us
    another operation x2, other arithmetic, solve_spd(): lax.linalg.triangular_solve(factor, halfway, left_side=True, lower=True,...  10.5 us
    pallas_call x1, Pallas kernels, stencil(): pl.pallas_call(functools.partial(stencil_kernel, rim), grid=(members // b...  9.88 us
    ppermute x3, starting transfers between devices, per_device(): anomaly_parts.append(lax.ppermute(anomaly, 'member', pairs))  4.99 us
    dot_general x1, matrix products, per_device(): lax.dot_general(scaled_t, scaled_t, contract_wells, precision=lax.Precisi...  2.82 us
    unnamed x32, local copies, waits for them, and re-layouts  2.36 us
  transfers between devices with their start and end apart: 3, of which 0 were waited for; matrix products, arithmetic and copies ran while one was open for 38% of the time, Pallas kernels for 36%

profile of v14, /device:TPU:1, one launch (start us, length us, event | category | flops | bytes accessed | tf_op | source)
XLA Modules:
  0.0 105.6 jit_solution(5117072892090826860)
XLA Ops:
  0.6 0.8 pad_maximum_fusion.3
  1.6 1.9 %fusion.61 = (f32[32,4,3,256]{3,2,1,0:T(4,128)S(1)}, f32[32,4,3,256]{3,2,1,0:T(4,128)S(1)}) fusion(f32[32,4,8,256]{3,2,1,0:T(8,128)} %param.12), kind=kLoop, calls=%fused_computation.110 | loop fusion | bytes 1572864 | tf_op jit(solution)/shard_map/slice | solution.py:352
  4.0 1.0 pad_maximum_fusion.1.out_ref
  5.0 11.4 %shard_map.147 = f32[2,432,256]{2,1,0:T(8,128)} custom-call(f32[2,432,256]{2,1,0:T(8,128)} %pad_maximum_fusion.1.out_ref), custom_call_target="tpu_custom_call" | custom-call | tf_op jit(solution)/shard_map/pallas_call | solution.py:291
  16.6 1.1 %copy.23 = bf16[4,8,32,256]{3,1,2,0:T(8,128)(2,1)} copy(bf16[4,8,32,256]{3,2,1,0:T(8,128)(2,1)S(1)} %bitcast.62) | data formatting | bytes 1048576
  17.7 1.3 %collective-permute-start = (bf16[32,8192]{1,0:T(8,128)(2,1)}, bf16[32,8192]{1,0:T(8,128)(2,1)}, u32[]{:S(2)}, u32[]{:S(2)}) collective-permute-start(bf16[32,8192]{1,0:T(8,128)(2,1)} %bitcast.23), channel_id=1, source_target_pairs={{0,1},{1,2},{2,3},{3,0},{4,5},{5,6},{6,7},{7,4},{8,9},{9,10},{10,1... | collective-permute-start | bytes 1572872 | tf_op jit(solution)/shard_map/ppermute | solution.py:437
  19.0 2.6 %collective-permute-start.1 = (bf16[32,8192]{1,0:T(8,128)(2,1)}, bf16[32,8192]{1,0:T(8,128)(2,1)}, u32[]{:S(2)}, u32[]{:S(2)}) collective-permute-start(bf16[32,8192]{1,0:T(8,128)(2,1)} %bitcast.23), channel_id=1, source_target_pairs={{0,2},{1,3},{2,0},{3,1},{4,6},{5,7},{6,4},{7,5},{8,10},{9,11},{10,... | collective-permute-start | bytes 1572872 | tf_op jit(solution)/shard_map/ppermute | solution.py:437
  21.6 1.1 %collective-permute-start.2 = (bf16[32,8192]{1,0:T(8,128)(2,1)}, bf16[32,8192]{1,0:T(8,128)(2,1)}, u32[]{:S(2)}, u32[]{:S(2)}) collective-permute-start(bf16[32,8192]{1,0:T(8,128)(2,1)} %bitcast.23), channel_id=1, source_target_pairs={{0,3},{1,0},{2,1},{3,2},{4,7},{5,4},{6,5},{7,6},{8,11},{9,8},{10,9... | collective-permute-start | bytes 1572872 | tf_op jit(solution)/shard_map/ppermute | solution.py:437
  22.7 0.8 fusion.62
  24.5 0.8 pad_maximum_fusion.2.fields_ref
  25.3 1.8 %pad_maximum_fusion.lp_ref = f32[32,4,14,256]{3,2,1,0:T(8,128)} fusion(f32[32,4,3,256]{3,2,1,0:T(4,128)S(1)} %reshape_squeeze.13, f32[32,4,8,256]{3,2,1,0:T(8,128)S(1)} %copy-done.1, f32[32,4,3,256]{3,2,1,0:T(4,128)S(1)} %reshape_squeeze.12), kind=kLoop, calls=%fused_computation | loop fusion | flops 917504 | bytes 3670016 | tf_op jit(solution)/shard_map/concatenate | solution.py:369
  27.1 9.9 %shard_map.148 = (f32[32,4,8,256]{3,2,1,0:T(8,128)}, f32[32,4,8,256]{3,2,1,0:T(8,128)}, f32[32,4,8,256]{3,2,1,0:T(8,128)}) custom-call(f32[32,4,14,256]{3,2,1,0:T(8,128)} %pad_maximum_fusion.lp_ref, f32[4,4,14,256]{3,2,1,0:T(8,128)} %pad_maximum_fusion.2.fields_ref, f32[14]{0:T(128)} %and_convert_fusion.inside_ref), custom_call_target="tpu_custom_call" | custom-call | tf_op jit(solution)/shard_map/pallas_call | solution.py:251
  37.0 1.6 %reduce-precision_convert_fusion.3 = (bf16[1024,256]{1,0:T(8,128)(2,1)S(1)}, bf16[1024,256]{1,0:T(8,128)(2,1)S(1)}, bf16[1024,256]{1,0:T(8,128)(2,1)S(1)}) fusion(f32[32,4,8,256]{3,2,1,0:T(8,128)} %get-tuple-element.10), kind=kLoop, calls=%fused_computation.28 | loop fusion | flops 1835008 | bytes 2621440 | tf_op jit(solution)/shard_map/convert.3
  41.3 0.9 select_reduce_fusion
  42.3 0.8 fusion.25
  43.0 0.8 reshape.135.part_ref
  43.9 28.0 %shard_map.149 = f32[32,32,128]{2,1,0:T(8,128)} custom-call(f32[32,8,128]{2,1,0:T(8,128)} %reshape.135.part_ref), custom_call_target="tpu_custom_call" | custom-call | tf_op jit(solution)/shard_map/pallas_call | solution.py:304
  71.9 1.3 %reduce_sum.29 = f32[32,32]{1,0:T(8,128)S(1)} reduce(f32[32,32,128]{2,1,0:T(8,128)} %shard_map.149, f32[]{:T(128)} %constant.107.clone.1), dimensions={2}, to_apply=%region_2.3 | reduce | flops 130048 | bytes 528388 | tf_op jit(solution)/shard_map/reduce_sum | solution.py:419
  73.4 2.8 %fusion.20 = f32[128,128]{1,0:T(8,128)S(1)} fusion(f32[32,32,128]{2,1,0:T(8,128)} %shard_map.149, f32[32,32]{1,0:T(8,128)S(1)} %div.56, f32[32,32]{1,0:T(8,128)S(1)} %broadcast_multiply_fusion), kind=kOutput, calls=%fused_computation.30 | convolution fusion | flops 201637888 | bytes 598016 | tf_op jit(solution)/shard_map/dot_general | solution.py:424
  76.2 11.7 %cholesky.17 = f32[128,128]{1,0:T(8,128)S(1)} custom-call(f32[128,128]{1,0:T(8,128)S(1)} %fusion.20), custom_call_target="Cholesky" | custom-call | tf_op jit(solution)/shard_map/cholesky | solution.py:101
  89.3 9.8 %custom-call.7 = f32[1,128,128]{1,2,0:T(8,128)S(1)} custom-call(f32[1,128,128]{2,1,0:T(8,128)S(1)} %fusion.40), custom_call_target="InvertDiagBlocksLowerTriangular" | custom-call | tf_op jit(solution)/shard_map/triangular_solve | solution.py:105
  100.2 1.3 %fusion.31 = f32[128,32]{1,0:T(8,128)S(1)} fusion(f32[1024,128]{1,0:T(8,128)S(1)} %bitcast.60, f32[1024]{0:T(1024)S(1)} %get-tuple-element.39, f32[1024]{0:T(1024)S(1)} %div.59, f32[32,1024]{1,0:T(8,128)S(1)} %copy-done.12, f32[1024,32]{0,1:T(8,128)S(1)} %copy.22, f32[1024]{0:T(1024)S(1)} %get-tuple-element.38, f32[1024]{0:T(1024)S(1)} %copy-done.13), kind=kOutput, calls=%fused_computation.51 | convolution fusion | flops 50692096 | bytes 819200 | tf_op jit(solution)/shard_map/dot_general | solution.py:428
  102.2 2.0 %fusion = f32[32,8192]{1,0:T(8,128)S(1)} fusion(bf16[32,8192]{1,0:T(8,128)(2,1)} %collective-permute-done.2, bf16[32,8192]{1,0:T(8,128)(2,1)} %collective-permute-done.1, bf16[32,8192]{1,0:T(8,128)(2,1)} %collective-permute-done, bf16[32,8192]{1,0:T(8,128)(2,1)} %bitcast.23, bf16[32,32]{0,1:T(8,128)(2,1)S(1)} %get-tuple-element.35, ...), kind=kOutput, calls=%fused_computation.1 | convolution fusion | flops 75530240 | bytes 3153920 | tf_op jit(solution)/shard_map/dot_general | solution.py:450
  104.5 1.1 %add.108 = f32[32,4,8,256]{3,2,1,0:T(8,128)} add(f32[32,4,8,256]{3,2,1,0:T(8,128)S(1)} %copy-done.1, f32[32,4,8,256]{3,2,1,0:T(8,128)S(1)} %bitcast.61) | non-fusion elementwise | flops 262144 | bytes 3145728 | tf_op jit(solution)/shard_map/add | solution.py:451
  (66 shorter events, 7.4 us)
Async XLA Ops:
  0.6 38.9 %copy-start = (f32[1024]{0:T(1024)S(1)}, f32[1024]{0:T(1024)}, u32[]{:S(2)}) copy-start(f32[1024]{0:T(1024)} %param.17) | copy-start | bytes 12292
  3.7 12.7 %copy-start.1 = (f32[32,4,8,256]{3,2,1,0:T(8,128)S(1)}, f32[32,4,8,256]{3,2,1,0:T(8,128)}, u32[]{:S(2)}) copy-start(f32[32,4,8,256]{3,2,1,0:T(8,128)} %param.12) | copy-start | bytes 3145732
  16.4 7.1 %copy-start.3 = (f32[2,432,256]{2,1,0:T(8,128)S(1)}, f32[2,432,256]{2,1,0:T(8,128)}, u32[]{:S(2)}) copy-start(f32[2,432,256]{2,1,0:T(8,128)} %shard_map.147) | copy-start | bytes 2654212
  16.4 8.1 %copy-start.5 = (f32[4,8,256]{2,1,0:T(8,128)S(1)}, f32[4,8,256]{2,1,0:T(8,128)}, u32[]{:S(2)}) copy-start(f32[4,8,256]{2,1,0:T(8,128)} %param.16) | copy-start | bytes 98308
  16.4 8.1 %copy-start.6 = (f32[4,8,256]{2,1,0:T(8,128)S(1)}, f32[4,8,256]{2,1,0:T(8,128)}, u32[]{:S(2)}) copy-start(f32[4,8,256]{2,1,0:T(8,128)} %param.15) | copy-start | bytes 98308
  16.5 8.1 %copy-start.7 = (f32[4,8,256]{2,1,0:T(8,128)S(1)}, f32[4,8,256]{2,1,0:T(8,128)}, u32[]{:S(2)}) copy-start(f32[4,8,256]{2,1,0:T(8,128)} %param.14) | copy-start | bytes 98308
  16.5 8.1 %copy-start.8 = (f32[4,8,256]{2,1,0:T(8,128)S(1)}, f32[4,8,256]{2,1,0:T(8,128)}, u32[]{:S(2)}) copy-start(f32[4,8,256]{2,1,0:T(8,128)} %param.13) | copy-start | bytes 98308
  17.7 84.5 %collective-permute-start = (bf16[32,8192]{1,0:T(8,128)(2,1)}, bf16[32,8192]{1,0:T(8,128)(2,1)}, u32[]{:S(2)}, u32[]{:S(2)}) collective-permute-start(bf16[32,8192]{1,0:T(8,128)(2,1)} %bitcast.23), channel_id=1, source_target_pairs={{0,1},{1,2},{2,3},{3,0},{4,5},{5,6},{6,7},{7,4},{8,9},{9,10},{10,1... | collective-permute-start | bytes 1572872 | tf_op jit(solution)/shard_map/ppermute | solution.py:437
  19.0 83.2 %collective-permute-start.1 = (bf16[32,8192]{1,0:T(8,128)(2,1)}, bf16[32,8192]{1,0:T(8,128)(2,1)}, u32[]{:S(2)}, u32[]{:S(2)}) collective-permute-start(bf16[32,8192]{1,0:T(8,128)(2,1)} %bitcast.23), channel_id=1, source_target_pairs={{0,2},{1,3},{2,0},{3,1},{4,6},{5,7},{6,4},{7,5},{8,10},{9,11},{10,... | collective-permute-start | bytes 1572872 | tf_op jit(solution)/shard_map/ppermute | solution.py:437
  21.6 80.6 %collective-permute-start.2 = (bf16[32,8192]{1,0:T(8,128)(2,1)}, bf16[32,8192]{1,0:T(8,128)(2,1)}, u32[]{:S(2)}, u32[]{:S(2)}) collective-permute-start(bf16[32,8192]{1,0:T(8,128)(2,1)} %bitcast.23), channel_id=1, source_target_pairs={{0,3},{1,0},{2,1},{3,2},{4,7},{5,4},{6,5},{7,6},{8,11},{9,8},{10,9... | collective-permute-start | bytes 1572872 | tf_op jit(solution)/shard_map/ppermute | solution.py:437
  27.1 11.4 %copy-start.11 = (s32[256]{0:T(256)S(1)}, s32[256]{0:T(256)}, u32[]{:S(2)}) copy-start(s32[256]{0:T(256)} %param.18) | copy-start | bytes 3076
  37.0 1.6 %copy-start.4 = (f32[32,4,8,256]{3,2,1,0:T(8,128)S(1)}, f32[32,4,8,256]{3,2,1,0:T(8,128)}, u32[]{:S(2)}) copy-start(f32[32,4,8,256]{3,2,1,0:T(8,128)} %get-tuple-element.15) | copy-start | bytes 3145732
  37.0 2.6 %copy-start.10 = (s32[256]{0:T(256)S(1)}, s32[256]{0:T(256)}, u32[]{:S(2)}) copy-start(s32[256]{0:T(256)} %param.19) | copy-start | bytes 3076
  41.3 31.9 %copy-start.9 = (f32[1024]{0:T(1024)S(1)}, f32[1024]{0:T(1024)}, u32[]{:S(2)}) copy-start(f32[1024]{0:T(1024)} %param.22) | copy-start | bytes 12292
  43.0 57.2 %copy-start.12 = (f32[32,1024]{1,0:T(8,128)S(1)}, f32[32,1024]{1,0:T(8,128)}, u32[]{:S(2)}) copy-start(f32[32,1024]{1,0:T(8,128)} %param.23) | copy-start | bytes 393220
  43.0 57.2 %copy-start.13 = (f32[1024]{0:T(1024)S(1)}, f32[1024]{0:T(1024)}, u32[]{:S(2)}) copy-start(f32[1024]{0:T(1024)} %param.21) | copy-start | bytes 12292
  71.9 27.2 %copy-start.2 = (f32[32,32,128]{2,1,0:T(8,128)S(1)}, f32[32,32,128]{2,1,0:T(8,128)}, u32[]{:S(2)}) copy-start(f32[32,32,128]{2,1,0:T(8,128)} %shard_map.149) | copy-start | bytes 1572868

commit v15 on v12

--- a/solution.py
+++ b/solution.py
@@ -223,14 +223,16 @@
     lax.fori_loop(1, tile_count, wait_t_send, 0)
 
 
-def stencil_kernel(rim, lp_ref, fields_ref, inside_ref, press_ref, sat_ref, mob_ref):
+def stencil_kernel(rim, lp_low, lp_mid, lp_high, f_low, f_mid, f_high, inside_ref,
+                   press_ref, sat_ref, mob_ref):
     inside = inside_ref[...]
-    permeab = jnp.exp(lp_ref[...])
+    permeab = jnp.exp(jnp.concatenate([lp_low[...], lp_mid[...], lp_high[...]], axis=2))
     face_sets = face_terms(permeab, inside)
-    press_ext = fields_ref[0]
-    sat_ext = fields_ref[1]
-    source_ext = fields_ref[2]
-    storage_ext = fields_ref[3]
+    fields = jnp.concatenate([f_low[...], f_mid[...], f_high[...]], axis=2)
+    press_ext = fields[0]
+    sat_ext = fields[1]
+    source_ext = fields[2]
+    storage_ext = fields[3]
     baseline = (source_ext + storage_ext * press_ext)[None]
     storage_term = jnp.where(inside[None, :, None] > 0.0, storage_ext, 1.0)[None]
     pressure = jnp.broadcast_to(press_ext[None], permeab.shape)
@@ -242,23 +244,27 @@
     mob_ref[...] = trim_rim(permeab, rim) * water_frac(saturation)
 
 
-def stencil(lp_ext, fields_ext, inside, rim):
-    members, layers, rows, depth = lp_ext.shape
+def stencil(lp_parts, field_parts, inside, rim):
+    members, layers, out_rows, depth = lp_parts[1].shape
     block = 4
-    out_rows = rows - 2 * rim
+
+    def member_block(part):
+        return pl.BlockSpec((block,) + part.shape[1:], lambda i: (i, 0, 0, 0))
+
+    def whole(part):
+        return pl.BlockSpec(part.shape, lambda i: (0, 0, 0, 0))
+
     out_spec = pl.BlockSpec((block, layers, out_rows, depth), lambda i: (i, 0, 0, 0))
     out_shape = jax.ShapeDtypeStruct((members, layers, out_rows, depth), jnp.float32)
     return pl.pallas_call(
         functools.partial(stencil_kernel, rim),
         grid=(members // block,),
-        in_specs=[
-            pl.BlockSpec((block, layers, rows, depth), lambda i: (i, 0, 0, 0)),
-            pl.BlockSpec(fields_ext.shape, lambda i: (0, 0, 0, 0)),
-            pl.BlockSpec(inside.shape, lambda i: (0,)),
-        ],
+        in_specs=[member_block(p) for p in lp_parts]
+        + [whole(p) for p in field_parts]
+        + [pl.BlockSpec(inside.shape, lambda i: (0,))],
         out_specs=[out_spec, out_spec, out_spec],
         out_shape=[out_shape, out_shape, out_shape],
-    )(lp_ext, fields_ext, inside)
+    )(*lp_parts, *field_parts, inside)
 
 
 def halo_kernel(out_ref, in_ref, send_sem, recv_sem):
@@ -366,11 +372,11 @@
 
     low_lp, low_fields = unpack(0)
     high_lp, high_fields = unpack(1)
-    lp_ext = jnp.concatenate([low_lp, log_perm, high_lp], axis=2)
-    fields_ext = jnp.concatenate([low_fields, fields, high_fields], axis=2)
     column = tile_rank * strip_width - rim + jnp.arange(strip_width + 2 * rim, dtype=jnp.int32)
     inside = ((column >= 0) & (column < strip_width * tile_count)).astype(jnp.float32)
-    pressure, saturation, mobility = stencil(lp_ext, fields_ext, inside, rim)
+    pressure, saturation, mobility = stencil(
+        (low_lp, log_perm, high_lp), (low_fields, fields, high_fields), inside, rim
+    )
     cell_count = layers * strip_width * strip_depth
     plane_rows = layers * strip_width
     cell_row = perf_cell // strip_depth

time: 104 us -> 103 us (level)
  local copies, waits for them, and re-layouts: 5.76 us -> 9.31 us
  other arithmetic: 30.3 us -> 27.8 us
  matrix products: 10.8 us -> 8.38 us
    concatenate x2 -> x0, other arithmetic: 2.53 us -> none  [the longest x1 1.77 us: per_device(): lp_ext = jnp.concatenate([low_lp, log_perm, high_lp], axis=2)]
    another operation x2, local copies, waits for them, and re-layouts: 0.33 us -> 1.91 us  [unpack(): incoming[side, :lp_count].reshape(local_count, layers, rim, strip_depth)]
    dot_general x1, matrix products: 1.83 us -> 0.48 us  [per_device(): lax.dot_general(own_cols, anomaly_all, contract, preferred_element_type=j...]
    another operation x2, local copies, waits for them, and re-layouts: 0.05 us -> 1.28 us  [unpack(): incoming[side, lp_count:].reshape(fields.shape[0], layers, rim, strip_depth)]
    dot_general x2, matrix products: 3.74 us -> 2.61 us  [pick_cells(): jnp.dot(values_in.reshape(local_count * plane_rows, strip_depth), col_pic...]
    unnamed x30 -> x28, local copies, waits for them, and re-layouts: 1.56 us -> 2.43 us
  transfers between devices with their start and end apart: 3 -> 3, of which waited for: 0 -> 0; matrix products, arithmetic and copies ran while one was open for 38% -> 37% of each run, Pallas kernels for 37% -> 38%
where the time goes in v15:
time: 103 us; the launch traced here: 102 us
  Pallas kernels  49.8 us (48%)
  other arithmetic  27.8 us (27%)
  local copies, waits for them, and re-layouts  9.31 us (9%)
  matrix products  8.38 us (8%)
  starting transfers between devices  5.05 us (5%)
  between operations  1.68 us (2%)
    pallas_call x1, Pallas kernels, rates_exchange(): pl.pallas_call(functools.partial(exchange_kernel, member_count), out_shap...  28 us
    another operation x3, other arithmetic, solve_spd(): lax.linalg.cholesky(gram_matrix + jnp.eye(gram_matrix.shape[0], dtype=jnp...  12.4 us
    pallas_call x1, Pallas kernels, halo_exchange(): pl.pallas_call(halo_kernel, out_shape=jax.ShapeDtypeStruct(outgoing.shape...  11.5 us
    another operation x2, other arithmetic, solve_spd(): lax.linalg.triangular_solve(factor, halfway, left_side=True, lower=True,...  10.5 us
    pallas_call x1, Pallas kernels, stencil(): pl.pallas_call(functools.partial(stencil_kernel, rim), grid=(members // b...  10.3 us
    ppermute x3, starting transfers between devices, per_device(): anomaly_parts.append(lax.ppermute(anomaly, 'member', pairs))  5.05 us
    dot_general x1, matrix products, per_device(): lax.dot_general(scaled_t, scaled_t, contract_wells, precision=lax.Precisi...  2.88 us
    dot_general x2, matrix products, pick_cells(): jnp.dot(values_in.reshape(local_count * plane_rows, strip_depth), col_pic...  2.61 us
  transfers between devices with their start and end apart: 3, of which 0 were waited for; matrix products, arithmetic and copies ran while one was open for 37% of the time, Pallas kernels for 38%

profile of v15, /device:TPU:1, one launch (start us, length us, event | category | flops | bytes accessed | tf_op | source)
XLA Modules:
  0.0 102.0 jit_solution(1824462679807087755)
XLA Ops:
  0.6 0.8 pad_maximum_fusion.1.f_mid
  1.6 1.8 %fusion.52 = (f32[32,4,3,256]{3,2,1,0:T(4,128)S(1)}, f32[32,4,3,256]{3,2,1,0:T(4,128)S(1)}) fusion(f32[32,4,8,256]{3,2,1,0:T(8,128)} %lp_mid.1), kind=kLoop, calls=%fused_computation.84 | loop fusion | bytes 1572864 | tf_op jit(solution)/shard_map/slice | solution.py:358
  3.9 1.0 pad_maximum_fusion.out_ref
  4.9 11.5 %shard_map.147 = f32[2,432,256]{2,1,0:T(8,128)} custom-call(f32[2,432,256]{2,1,0:T(8,128)} %pad_maximum_fusion.out_ref), custom_call_target="tpu_custom_call" | custom-call | tf_op jit(solution)/shard_map/pallas_call | solution.py:297
  16.9 1.4 %collective-permute-start = (bf16[32,8192]{1,0:T(8,128)(2,1)S(1)}, bf16[32,8192]{1,0:T(8,128)(2,1)S(1)}, u32[]{:S(2)}, u32[]{:S(2)}) collective-permute-start(bf16[32,8192]{1,0:T(8,128)(2,1)S(1)} %bitcast.56), channel_id=1, source_target_pairs={{0,1},{1,2},{2,3},{3,0},{4,5},{5,6},{6,7},{7,4},{8,9},{9,10},{10,1... | collective-permute-start | bytes 1572872 | tf_op jit(solution)/shard_map/ppermute | solution.py:436
  18.2 2.6 %collective-permute-start.1 = (bf16[32,8192]{1,0:T(8,128)(2,1)S(1)}, bf16[32,8192]{1,0:T(8,128)(2,1)S(1)}, u32[]{:S(2)}, u32[]{:S(2)}) collective-permute-start(bf16[32,8192]{1,0:T(8,128)(2,1)S(1)} %bitcast.57), channel_id=1, source_target_pairs={{0,2},{1,3},{2,0},{3,1},{4,6},{5,7},{6,4},{7,5},{8,10},{9,11},{10,... | collective-permute-start | bytes 1572872 | tf_op jit(solution)/shard_map/ppermute | solution.py:436
  20.8 1.1 %collective-permute-start.2 = (bf16[32,8192]{1,0:T(8,128)(2,1)S(1)}, bf16[32,8192]{1,0:T(8,128)(2,1)S(1)}, u32[]{:S(2)}, u32[]{:S(2)}) collective-permute-start(bf16[32,8192]{1,0:T(8,128)(2,1)S(1)} %bitcast.58), channel_id=1, source_target_pairs={{0,3},{1,0},{2,1},{3,2},{4,7},{5,4},{6,5},{7,6},{8,11},{9,8},{10,9... | collective-permute-start | bytes 1572872 | tf_op jit(solution)/shard_map/ppermute | solution.py:436
  22.0 1.0 reshape_squeeze.12.lp_low
  23.0 0.9 reshape_squeeze.13.lp_high
  25.8 10.3 %shard_map.148 = (f32[32,4,8,256]{3,2,1,0:T(8,128)}, f32[32,4,8,256]{3,2,1,0:T(8,128)}, f32[32,4,8,256]{3,2,1,0:T(8,128)}) custom-call(f32[32,4,3,256]{3,2,1,0:T(4,128)} %reshape_squeeze.12.lp_low, f32[32,4,8,256]{3,2,1,0:T(8,128)} %lp_mid.1, f32[32,4,3,256]{3,2,1,0:T(4,128)} %reshape_squeeze.13.lp_high, f32[4,4,3,256]{3,2,1,0:T(4,128)} %reshape_squeeze.14.f_low, ...), custom_call_target="tpu_custom_call" | custom-call | tf_op jit(solution)/shard_map/pallas_call | solution.py:259
  36.1 2.0 %fusion.9 = f32[32,256]{1,0:T(8,128)S(1)} fusion(f32[32,4,8,256]{3,2,1,0:T(8,128)} %get-tuple-element.19, pred[32,256]{1,0:T(8,128)(4,1)S(1)} %iota_compare_fusion.5, s32[256]{0:T(256)S(1)} %get-tuple-element.36), kind=kOutput, calls=%fused_computation.11 | convolution fusion | flops 805888000 | bytes 1090560 | tf_op jit(solution)/shard_map/dot_general | solution.py:390
  38.1 0.7 fusion.8
  40.0 0.8 fusion.15
  40.8 0.8 reshape.117.part_ref
  41.7 28.0 %shard_map.149 = f32[32,32,128]{2,1,0:T(8,128)} custom-call(f32[32,8,128]{2,1,0:T(8,128)} %reshape.117.part_ref), custom_call_target="tpu_custom_call" | custom-call | tf_op jit(solution)/shard_map/pallas_call | solution.py:310
  69.7 1.2 %reduce_sum.29 = f32[32,32]{1,0:T(8,128)S(1)} reduce(f32[32,32,128]{2,1,0:T(8,128)} %shard_map.149, f32[]{:T(128)} %constant.107.clone.1), dimensions={2}, to_apply=%region_2.3 | reduce | flops 130048 | bytes 528388 | tf_op jit(solution)/shard_map/reduce_sum | solution.py:418
  71.1 2.9 %fusion.10 = f32[128,128]{1,0:T(8,128)S(1)} fusion(f32[32,32,128]{2,1,0:T(8,128)} %shard_map.149, f32[32,32]{1,0:T(8,128)S(1)} %div.56, f32[32,32]{1,0:T(8,128)S(1)} %broadcast_multiply_fusion), kind=kOutput, calls=%fused_computation.13 | convolution fusion | flops 201637888 | bytes 598016 | tf_op jit(solution)/shard_map/dot_general | solution.py:423
  74.0 11.7 %cholesky.17 = f32[128,128]{1,0:T(8,128)S(1)} custom-call(f32[128,128]{1,0:T(8,128)S(1)} %fusion.10), custom_call_target="Cholesky" | custom-call | tf_op jit(solution)/shard_map/cholesky | solution.py:101
  85.7 0.6 compare_reduce_fusion
  86.4 0.7 fusion.33
  87.1 9.8 %custom-call.7 = f32[1,128,128]{1,2,0:T(8,128)S(1)} custom-call(f32[1,128,128]{2,1,0:T(8,128)S(1)} %fusion.33), custom_call_target="InvertDiagBlocksLowerTriangular" | custom-call | tf_op jit(solution)/shard_map/triangular_solve | solution.py:105
  97.3 0.7 copy.23
  100.0 0.9 copy-done.2
  100.9 1.1 %add.82 = f32[32,4,8,256]{3,2,1,0:T(8,128)} add(f32[32,4,8,256]{3,2,1,0:T(8,128)S(1)} %copy-done.2, f32[32,4,8,256]{3,2,1,0:T(8,128)S(1)} %bitcast.53) | non-fusion elementwise | flops 262144 | bytes 3145728 | tf_op jit(solution)/shard_map/add | solution.py:450
  (57 shorter events, 6.1 us)
Async XLA Ops:
  0.6 38.8 %copy-start = (f32[1024]{0:T(1024)S(1)}, f32[1024]{0:T(1024)}, u32[]{:S(2)}) copy-start(f32[1024]{0:T(1024)} %param.17) | copy-start | bytes 12292
  1.5 1.9 %copy-start.5 = (f32[4,4,8,256]{3,2,1,0:T(8,128)}, f32[4,4,8,256]{3,2,1,0:T(8,128)S(1)}, u32[]{:S(2)}) copy-start(f32[4,4,8,256]{3,2,1,0:T(8,128)S(1)} %pad_maximum_fusion.1.f_mid) | copy-start | bytes 393220
  4.9 11.5 %copy-start.1 = (f32[32,4,8,256]{3,2,1,0:T(8,128)S(1)}, f32[32,4,8,256]{3,2,1,0:T(8,128)}, u32[]{:S(2)}) copy-start(f32[32,4,8,256]{3,2,1,0:T(8,128)} %lp_mid.1) | copy-start | bytes 3145732
  16.4 5.5 %copy-start.4 = (f32[2,432,256]{2,1,0:T(8,128)S(1)}, f32[2,432,256]{2,1,0:T(8,128)}, u32[]{:S(2)}) copy-start(f32[2,432,256]{2,1,0:T(8,128)} %shard_map.147) | copy-start | bytes 2654212
  16.9 82.3 %collective-permute-start = (bf16[32,8192]{1,0:T(8,128)(2,1)S(1)}, bf16[32,8192]{1,0:T(8,128)(2,1)S(1)}, u32[]{:S(2)}, u32[]{:S(2)}) collective-permute-start(bf16[32,8192]{1,0:T(8,128)(2,1)S(1)} %bitcast.56), channel_id=1, source_target_pairs={{0,1},{1,2},{2,3},{3,0},{4,5},{5,6},{6,7},{7,4},{8,9},{9,10},{10,1... | collective-permute-start | bytes 1572872 | tf_op jit(solution)/shard_map/ppermute | solution.py:436
  18.2 81.0 %collective-permute-start.1 = (bf16[32,8192]{1,0:T(8,128)(2,1)S(1)}, bf16[32,8192]{1,0:T(8,128)(2,1)S(1)}, u32[]{:S(2)}, u32[]{:S(2)}) collective-permute-start(bf16[32,8192]{1,0:T(8,128)(2,1)S(1)} %bitcast.57), channel_id=1, source_target_pairs={{0,2},{1,3},{2,0},{3,1},{4,6},{5,7},{6,4},{7,5},{8,10},{9,11},{10,... | collective-permute-start | bytes 1572872 | tf_op jit(solution)/shard_map/ppermute | solution.py:436
  20.8 78.3 %collective-permute-start.2 = (bf16[32,8192]{1,0:T(8,128)(2,1)S(1)}, bf16[32,8192]{1,0:T(8,128)(2,1)S(1)}, u32[]{:S(2)}, u32[]{:S(2)}) collective-permute-start(bf16[32,8192]{1,0:T(8,128)(2,1)S(1)} %bitcast.58), channel_id=1, source_target_pairs={{0,3},{1,0},{2,1},{3,2},{4,7},{5,4},{6,5},{7,6},{8,11},{9,8},{10,9... | collective-permute-start | bytes 1572872 | tf_op jit(solution)/shard_map/ppermute | solution.py:436
  22.0 3.7 %copy-start.9 = (s32[256]{0:T(256)S(1)}, s32[256]{0:T(256)}, u32[]{:S(2)}) copy-start(s32[256]{0:T(256)} %param.18) | copy-start | bytes 3076
  36.1 2.0 %copy-start.6 = (f32[32,4,8,256]{3,2,1,0:T(8,128)S(1)}, f32[32,4,8,256]{3,2,1,0:T(8,128)}, u32[]{:S(2)}) copy-start(f32[32,4,8,256]{3,2,1,0:T(8,128)} %get-tuple-element.10) | copy-start | bytes 3145732
  36.1 3.3 %copy-start.8 = (s32[256]{0:T(256)S(1)}, s32[256]{0:T(256)}, u32[]{:S(2)}) copy-start(s32[256]{0:T(256)} %param.19) | copy-start | bytes 3076
  40.8 30.1 %copy-start.7 = (f32[1024]{0:T(1024)S(1)}, f32[1024]{0:T(1024)}, u32[]{:S(2)}) copy-start(f32[1024]{0:T(1024)} %param.22) | copy-start | bytes 12292
  71.1 25.8 %copy-start.3 = (f32[32,32,128]{2,1,0:T(8,128)S(1)}, f32[32,32,128]{2,1,0:T(8,128)}, u32[]{:S(2)}) copy-start(f32[32,32,128]{2,1,0:T(8,128)} %shard_map.149) | copy-start | bytes 1572868
  74.0 24.0 %copy-start.10 = (f32[32,1024]{1,0:T(8,128)S(1)}, f32[32,1024]{1,0:T(8,128)}, u32[]{:S(2)}) copy-start(f32[32,1024]{1,0:T(8,128)} %param.23) | copy-start | bytes 393220
  74.0 24.0 %copy-start.11 = (f32[1024]{0:T(1024)S(1)}, f32[1024]{0:T(1024)}, u32[]{:S(2)}) copy-start(f32[1024]{0:T(1024)} %param.21) | copy-start | bytes 12292
  99.7 1.2 %copy-start.2 = (f32[32,4,8,256]{3,2,1,0:T(8,128)S(1)}, f32[32,4,8,256]{3,2,1,0:T(8,128)}, u32[]{:S(2)}) copy-start(f32[32,4,8,256]{3,2,1,0:T(8,128)} %lp_mid.1) | copy-start | bytes 3145732

commit v16 on v15

--- a/solution.py
+++ b/solution.py
@@ -362,7 +362,6 @@
 
     outgoing = jnp.stack([rim_rows(0), rim_rows(strip_width - rim)])
     incoming = halo_exchange(outgoing)
-    incoming, log_perm_after = lax.optimization_barrier((incoming, log_perm))
     lp_count = local_count * layers * rim
 
     def unpack(side):
@@ -378,6 +377,7 @@
         (low_lp, log_perm, high_lp), (low_fields, fields, high_fields), inside, rim
     )
     cell_count = layers * strip_width * strip_depth
+    mobility, log_perm_after = lax.optimization_barrier((mobility, log_perm))
     plane_rows = layers * strip_width
     cell_row = perf_cell // strip_depth
     cell_col = lax.rem(perf_cell, strip_depth)

time: 103 us -> 112 us (1.087)
  Pallas kernels: 49.8 us -> 58 us
  local copies, waits for them, and re-layouts: 9.31 us -> 11.9 us
  starting transfers between devices: 5.05 us -> 3.77 us
    pallas_call x1, Pallas kernels: 28 us -> 36.2 us  [rates_exchange(): pl.pallas_call(functools.partial(exchange_kernel, member_count), out_shap...]
    dot_general x1, matrix products: 0.48 us -> 1.98 us  [per_device(): lax.dot_general(own_cols, anomaly_all, contract, preferred_element_type=j...]
    dot_general x2, matrix products: 2.61 us -> 1.31 us  [pick_cells(): jnp.dot(values_in.reshape(local_count * plane_rows, strip_depth), col_pic...]
    ppermute x3, starting transfers between devices: 5.05 us -> 3.77 us  [per_device(): anomaly_parts.append(lax.ppermute(anomaly, 'member', pairs))]
    unnamed x28 -> x26, local copies, waits for them, and re-layouts: 2.43 us -> 2.34 us
  transfers between devices with their start and end apart: 3 -> 3, of which waited for: 0 -> 0; matrix products, arithmetic and copies ran while one was open for 37% -> 30% of each run, Pallas kernels for 38% -> 32%
where the time goes in v16:
time: 112 us
  Pallas kernels  58 us (52%)
  other arithmetic  27.7 us (25%)
  local copies, waits for them, and re-layouts  11.9 us (11%)
  matrix products  8.58 us (8%)
  starting transfers between devices  3.77 us (3%)
  between operations  1.68 us (2%)
    pallas_call x1, Pallas kernels, rates_exchange(): pl.pallas_call(functools.partial(exchange_kernel, member_count), out_shap...  36.2 us
    another operation x3, other arithmetic, solve_spd(): lax.linalg.cholesky(gram_matrix + jnp.eye(gram_matrix.shape[0], dtype=jnp...  12.4 us
    pallas_call x1, Pallas kernels, halo_exchange(): pl.pallas_call(halo_kernel, out_shape=jax.ShapeDtypeStruct(outgoing.shape...  11.4 us
    another operation x2, other arithmetic, solve_spd(): lax.linalg.triangular_solve(factor, halfway, left_side=True, lower=True,...  10.5 us
    pallas_call x1, Pallas kernels, stencil(): pl.pallas_call(functools.partial(stencil_kernel, rim), grid=(members // b...  10.4 us
    ppermute x3, starting transfers between devices, per_device(): anomaly_parts.append(lax.ppermute(anomaly, 'member', pairs))  3.77 us
    dot_general x1, matrix products, per_device(): lax.dot_general(scaled_t, scaled_t, contract_wells, precision=lax.Precisi...  2.88 us
    unnamed x26, local copies, waits for them, and re-layouts  2.34 us
  transfers between devices with their start and end apart: 3, of which 0 were waited for; matrix products, arithmetic and copies ran while one was open for 30% of the time, Pallas kernels for 32%

profile of v16, /device:TPU:1, one launch (start us, length us, event | category | flops | bytes accessed | tf_op | source)
XLA Modules:
  0.0 111.7 jit_solution(17602606848009121515)
XLA Ops:
  0.7 0.8 pad_maximum_fusion.1.f_mid
  1.6 1.8 %fusion.52 = (f32[32,4,3,256]{3,2,1,0:T(4,128)S(1)}, f32[32,4,3,256]{3,2,1,0:T(4,128)S(1)}) fusion(f32[32,4,8,256]{3,2,1,0:T(8,128)} %lp_mid.1), kind=kLoop, calls=%fused_computation.84 | loop fusion | bytes 1572864 | tf_op jit(solution)/shard_map/slice | solution.py:358
  3.9 1.0 pad_maximum_fusion.out_ref
  4.8 11.4 %shard_map.147 = f32[2,432,256]{2,1,0:T(8,128)} custom-call(f32[2,432,256]{2,1,0:T(8,128)} %pad_maximum_fusion.out_ref), custom_call_target="tpu_custom_call" | custom-call | tf_op jit(solution)/shard_map/pallas_call | solution.py:297
  16.3 0.8 fusion.53
  17.1 1.2 %fusion.54 = (f32[1,384,256]{2,1,0:T(8,128)S(1)}, f32[1,384,256]{2,1,0:T(8,128)S(1)}) fusion(f32[2,432,256]{2,1,0:T(8,128)} %shard_map.147), kind=kLoop, calls=%fused_computation.86 | loop fusion | bytes 1572864 | tf_op jit(solution)/shard_map/slice | solution.py:368
  20.1 1.0 reshape_squeeze.13.lp_high
  21.1 1.0 reshape_squeeze.12.lp_low
  22.0 10.4 %shard_map.148 = (f32[32,4,8,256]{3,2,1,0:T(8,128)}, f32[32,4,8,256]{3,2,1,0:T(8,128)}, f32[32,4,8,256]{3,2,1,0:T(8,128)}) custom-call(f32[32,4,3,256]{3,2,1,0:T(4,128)} %reshape_squeeze.12.lp_low, f32[32,4,8,256]{3,2,1,0:T(8,128)} %lp_mid.1, f32[32,4,3,256]{3,2,1,0:T(4,128)} %reshape_squeeze.13.lp_high, f32[4,4,3,256]{3,2,1,0:T(4,128)} %reshape_squeeze.14.f_low, ...), custom_call_target="tpu_custom_call" | custom-call | tf_op jit(solution)/shard_map/pallas_call | solution.py:259
  32.6 1.1 copy.26
  33.7 2.7 %collective-permute-start.2 = (bf16[32,8192]{1,0:T(8,128)(2,1)}, bf16[32,8192]{1,0:T(8,128)(2,1)}, u32[]{:S(2)}, u32[]{:S(2)}) collective-permute-start(bf16[32,8192]{1,0:T(8,128)(2,1)} %bitcast.22), channel_id=1, source_target_pairs={{0,3},{1,0},{2,1},{3,2},{4,7},{5,4},{6,5},{7,6},{8,11},{9,8},{10,9... | collective-permute-start | bytes 1572872 | tf_op jit(solution)/shard_map/ppermute | solution.py:436
  36.8 0.7 collective-permute-start
  40.3 0.8 fusion.15
  41.1 0.8 reshape.117.part_ref
  41.9 36.2 %shard_map.149 = f32[32,32,128]{2,1,0:T(8,128)} custom-call(f32[32,8,128]{2,1,0:T(8,128)} %reshape.117.part_ref), custom_call_target="tpu_custom_call" | custom-call | tf_op jit(solution)/shard_map/pallas_call | solution.py:310
  78.1 0.8 dynamic-slice_bitcast_fusion
  78.9 0.7 copy.23
  79.5 1.2 %reduce_sum.29 = f32[32,32]{1,0:T(8,128)S(1)} reduce(f32[32,32,128]{2,1,0:T(8,128)} %shard_map.149, f32[]{:T(128)} %constant.107.clone.1), dimensions={2}, to_apply=%region_2.3 | reduce | flops 130048 | bytes 528388 | tf_op jit(solution)/shard_map/reduce_sum | solution.py:418
  80.9 2.9 %fusion.10 = f32[128,128]{1,0:T(8,128)S(1)} fusion(f32[32,32,128]{2,1,0:T(8,128)} %shard_map.149, f32[32,32]{1,0:T(8,128)S(1)} %div.56, f32[32,32]{1,0:T(8,128)S(1)} %broadcast_multiply_fusion), kind=kOutput, calls=%fused_computation.13 | convolution fusion | flops 201637888 | bytes 598016 | tf_op jit(solution)/shard_map/dot_general | solution.py:423
  83.8 11.7 %cholesky.17 = f32[128,128]{1,0:T(8,128)S(1)} custom-call(f32[128,128]{1,0:T(8,128)S(1)} %fusion.10), custom_call_target="Cholesky" | custom-call | tf_op jit(solution)/shard_map/cholesky | solution.py:101
  96.2 0.7 fusion.33
  96.8 9.8 %custom-call.7 = f32[1,128,128]{1,2,0:T(8,128)S(1)} custom-call(f32[1,128,128]{2,1,0:T(8,128)S(1)} %fusion.33), custom_call_target="InvertDiagBlocksLowerTriangular" | custom-call | tf_op jit(solution)/shard_map/triangular_solve | solution.py:105
  108.2 2.0 %fusion = f32[32,8192]{1,0:T(8,128)S(1)} fusion(bf16[32,8192]{1,0:T(8,128)(2,1)} %collective-permute-done.2, bf16[32,8192]{1,0:T(8,128)(2,1)} %collective-permute-done.1, bf16[32,8192]{1,0:T(8,128)(2,1)} %collective-permute-done, bf16[32,8192]{1,0:T(8,128)(2,1)} %bitcast.22, bf16[32,32]{0,1:T(8,128)(2,1)S(1)} %get-tuple-element.31, ...), kind=kOutput, calls=%fused_computation | convolution fusion | flops 75530240 | bytes 3153920 | tf_op jit(solution)/shard_map/dot_general | solution.py:449
  110.6 1.1 %add.82 = f32[32,4,8,256]{3,2,1,0:T(8,128)} add(f32[32,4,8,256]{3,2,1,0:T(8,128)S(1)} %copy-done.1, f32[32,4,8,256]{3,2,1,0:T(8,128)S(1)} %bitcast.53) | non-fusion elementwise | flops 262144 | bytes 3145728 | tf_op jit(solution)/shard_map/add | solution.py:450
  (55 shorter events, 7.5 us)
Async XLA Ops:
  0.6 39.0 %copy-start = (f32[1024]{0:T(1024)S(1)}, f32[1024]{0:T(1024)}, u32[]{:S(2)}) copy-start(f32[1024]{0:T(1024)} %param.17) | copy-start | bytes 12292
  1.5 1.9 %copy-start.3 = (f32[4,4,8,256]{3,2,1,0:T(8,128)}, f32[4,4,8,256]{3,2,1,0:T(8,128)S(1)}, u32[]{:S(2)}) copy-start(f32[4,4,8,256]{3,2,1,0:T(8,128)S(1)} %pad_maximum_fusion.1.f_mid) | copy-start | bytes 393220
  22.0 10.4 %copy-start.1 = (f32[32,4,8,256]{3,2,1,0:T(8,128)S(1)}, f32[32,4,8,256]{3,2,1,0:T(8,128)}, u32[]{:S(2)}) copy-start(f32[32,4,8,256]{3,2,1,0:T(8,128)} %lp_mid.1) | copy-start | bytes 3145732
  32.4 5.7 %copy-start.8 = (s32[256]{0:T(256)S(1)}, s32[256]{0:T(256)}, u32[]{:S(2)}) copy-start(s32[256]{0:T(256)} %param.18) | copy-start | bytes 3076
  32.4 5.8 %copy-start.6 = (f32[1024]{0:T(1024)S(1)}, f32[1024]{0:T(1024)}, u32[]{:S(2)}) copy-start(f32[1024]{0:T(1024)} %param.22) | copy-start | bytes 12292
  32.5 5.8 %copy-start.5 = (f32[32,4,8,256]{3,2,1,0:T(8,128)S(1)}, f32[32,4,8,256]{3,2,1,0:T(8,128)}, u32[]{:S(2)}) copy-start(f32[32,4,8,256]{3,2,1,0:T(8,128)} %get-tuple-element.10) | copy-start | bytes 3145732
  32.6 6.4 %copy-start.4 = (f32[32,4,8,256]{3,2,1,0:T(8,128)S(1)}, f32[32,4,8,256]{3,2,1,0:T(8,128)}, u32[]{:S(2)}) copy-start(f32[32,4,8,256]{3,2,1,0:T(8,128)} %get-tuple-element.19) | copy-start | bytes 3145732
  33.7 74.5 %collective-permute-start.2 = (bf16[32,8192]{1,0:T(8,128)(2,1)}, bf16[32,8192]{1,0:T(8,128)(2,1)}, u32[]{:S(2)}, u32[]{:S(2)}) collective-permute-start(bf16[32,8192]{1,0:T(8,128)(2,1)} %bitcast.22), channel_id=1, source_target_pairs={{0,3},{1,0},{2,1},{3,2},{4,7},{5,4},{6,5},{7,6},{8,11},{9,8},{10,9... | collective-permute-start | bytes 1572872 | tf_op jit(solution)/shard_map/ppermute | solution.py:436
  36.4 71.8 %collective-permute-start.1 = (bf16[32,8192]{1,0:T(8,128)(2,1)}, bf16[32,8192]{1,0:T(8,128)(2,1)}, u32[]{:S(2)}, u32[]{:S(2)}) collective-permute-start(bf16[32,8192]{1,0:T(8,128)(2,1)} %bitcast.22), channel_id=1, source_target_pairs={{0,2},{1,3},{2,0},{3,1},{4,6},{5,7},{6,4},{7,5},{8,10},{9,11},{10,... | collective-permute-start | bytes 1572872 | tf_op jit(solution)/shard_map/ppermute | solution.py:436
  36.8 71.4 %collective-permute-start = (bf16[32,8192]{1,0:T(8,128)(2,1)}, bf16[32,8192]{1,0:T(8,128)(2,1)}, u32[]{:S(2)}, u32[]{:S(2)}) collective-permute-start(bf16[32,8192]{1,0:T(8,128)(2,1)} %bitcast.22), channel_id=1, source_target_pairs={{0,1},{1,2},{2,3},{3,0},{4,5},{5,6},{6,7},{7,4},{8,9},{9,10},{10,1... | collective-permute-start | bytes 1572872 | tf_op jit(solution)/shard_map/ppermute | solution.py:436
  38.3 1.3 %copy-start.7 = (s32[256]{0:T(256)S(1)}, s32[256]{0:T(256)}, u32[]{:S(2)}) copy-start(s32[256]{0:T(256)} %param.19) | copy-start | bytes 3076
  80.9 25.8 %copy-start.2 = (f32[32,32,128]{2,1,0:T(8,128)S(1)}, f32[32,32,128]{2,1,0:T(8,128)}, u32[]{:S(2)}) copy-start(f32[32,32,128]{2,1,0:T(8,128)} %shard_map.149) | copy-start | bytes 1572868
  83.8 23.3 %copy-start.9 = (f32[32,1024]{1,0:T(8,128)S(1)}, f32[32,1024]{1,0:T(8,128)}, u32[]{:S(2)}) copy-start(f32[32,1024]{1,0:T(8,128)} %param.23) | copy-start | bytes 393220
  83.8 23.3 %copy-start.10 = (f32[1024]{0:T(1024)S(1)}, f32[1024]{0:T(1024)}, u32[]{:S(2)}) copy-start(f32[1024]{0:T(1024)} %param.21) | copy-start | bytes 12292

commit v17 on v15

--- a/solution.py
+++ b/solution.py
@@ -224,7 +224,7 @@
 
 
 def stencil_kernel(rim, lp_low, lp_mid, lp_high, f_low, f_mid, f_high, inside_ref,
-                   press_ref, sat_ref, mob_ref):
+                   col_ref, row_ref, press_ref, sat_ref, pmob_ref, ppress_ref):
     inside = inside_ref[...]
     permeab = jnp.exp(jnp.concatenate([lp_low[...], lp_mid[...], lp_high[...]], axis=2))
     face_sets = face_terms(permeab, inside)
@@ -239,12 +239,21 @@
     for sweep_idx in range(SWEEPS):
         pressure = jacobi(pressure, baseline, storage_term, face_sets)
     saturation = trim_rim(transport(pressure, sat_ext[None], face_sets), rim)
-    press_ref[...] = trim_rim(pressure, rim)
+    pressure = trim_rim(pressure, rim)
+    press_ref[...] = pressure
     sat_ref[...] = saturation
-    mob_ref[...] = trim_rim(permeab, rim) * water_frac(saturation)
-
-
-def stencil(lp_parts, field_parts, inside, rim):
+    mobility = trim_rim(permeab, rim) * water_frac(saturation)
+    block, layers, rows, depth = pressure.shape
+    row_pick = row_ref[...] > 0.0
+    for values_in, out_ref in ((mobility, pmob_ref), (pressure, ppress_ref)):
+        by_col = jnp.dot(
+            values_in.reshape(block * layers * rows, depth), col_ref[...],
+            precision=lax.Precision.HIGHEST, preferred_element_type=jnp.float32,
+        ).reshape(block, layers * rows, -1)
+        out_ref[0] = jnp.sum(jnp.where(row_pick[None], by_col, 0.0), axis=1)
+
+
+def stencil(lp_parts, field_parts, inside, col_pick, row_pick, rim):
     members, layers, out_rows, depth = lp_parts[1].shape
     block = 4
 
@@ -256,15 +265,22 @@
 
     out_spec = pl.BlockSpec((block, layers, out_rows, depth), lambda i: (i, 0, 0, 0))
     out_shape = jax.ShapeDtypeStruct((members, layers, out_rows, depth), jnp.float32)
+    slots = col_pick.shape[1]
+    pick_spec = pl.BlockSpec((1, block, slots), lambda i: (i, 0, 0))
+    pick_shape = jax.ShapeDtypeStruct((members // block, block, slots), jnp.float32)
     return pl.pallas_call(
         functools.partial(stencil_kernel, rim),
         grid=(members // block,),
         in_specs=[member_block(p) for p in lp_parts]
         + [whole(p) for p in field_parts]
-        + [pl.BlockSpec(inside.shape, lambda i: (0,))],
-        out_specs=[out_spec, out_spec, out_spec],
-        out_shape=[out_shape, out_shape, out_shape],
-    )(*lp_parts, *field_parts, inside)
+        + [
+            pl.BlockSpec(inside.shape, lambda i: (0,)),
+            pl.BlockSpec(col_pick.shape, lambda i: (0, 0)),
+            pl.BlockSpec(row_pick.shape, lambda i: (0, 0)),
+        ],
+        out_specs=[out_spec, out_spec, pick_spec, pick_spec],
+        out_shape=[out_shape, out_shape, pick_shape, pick_shape],
+    )(*lp_parts, *field_parts, inside, col_pick, row_pick)
 
 
 def halo_kernel(out_ref, in_ref, send_sem, recv_sem):
@@ -374,27 +390,21 @@
     high_lp, high_fields = unpack(1)
     column = tile_rank * strip_width - rim + jnp.arange(strip_width + 2 * rim, dtype=jnp.int32)
     inside = ((column >= 0) & (column < strip_width * tile_count)).astype(jnp.float32)
-    pressure, saturation, mobility = stencil(
-        (low_lp, log_perm, high_lp), (low_fields, fields, high_fields), inside, rim
-    )
-    cell_count = layers * strip_width * strip_depth
     plane_rows = layers * strip_width
     cell_row = perf_cell // strip_depth
     cell_col = lax.rem(perf_cell, strip_depth)
     col_pick = (jnp.arange(strip_depth, dtype=jnp.int32)[:, None] == cell_col[None, :]).astype(
         jnp.float32
     )
-    row_pick = jnp.arange(plane_rows, dtype=jnp.int32)[:, None] == cell_row[None, :]
-
-    def pick_cells(values_in):
-        by_col = jnp.dot(
-            values_in.reshape(local_count * plane_rows, strip_depth), col_pick,
-            precision=lax.Precision.HIGHEST, preferred_element_type=jnp.float32,
-        ).reshape(local_count, plane_rows, -1)
-        return jnp.sum(jnp.where(row_pick[None], by_col, 0.0), axis=1)
-
-    perf_mob = pick_cells(mobility)
-    perf_press = pick_cells(pressure)
+    row_pick = (jnp.arange(plane_rows, dtype=jnp.int32)[:, None] == cell_row[None, :]).astype(
+        jnp.float32
+    )
+    pressure, saturation, perf_mob, perf_press = stencil(
+        (low_lp, log_perm, high_lp), (low_fields, fields, high_fields), inside, col_pick, row_pick, rim
+    )
+    cell_count = layers * strip_width * strip_depth
+    perf_mob = perf_mob.reshape(local_count, -1)
+    perf_press = perf_press.reshape(local_count, -1)
     selector = (perf_well[:, None] == jnp.arange(well_count, dtype=jnp.int32)[None, :]).astype(
         jnp.float32
     )

time: 103 us -> 107 us (1.039)
  Pallas kernels: 49.8 us -> 53.4 us
  matrix products: 8.38 us -> 6.6 us
  local copies, waits for them, and re-layouts: 9.31 us -> 10.9 us
  other arithmetic: 27.8 us -> 29.1 us
    pallas_call x1, Pallas kernels: 10.3 us -> 13.9 us  [stencil(): pl.pallas_call(functools.partial(stencil_kernel, rim), grid=(members // b...]
    dot_general x2 -> x0, matrix products: 2.61 us -> none  [pick_cells(): jnp.dot(values_in.reshape(local_count * plane_rows, strip_depth), col_pic...]
    reshape x0 -> x2, local copies, waits for them, and re-layouts: none -> 1.55 us  [the longest x1 0.77 us: per_device(): perf_press = perf_press.reshape(local_count, -1)]
    convert_element_type x0 -> x2, other arithmetic: none -> 1.36 us  [the longest x1 0.74 us: per_device(): (jnp.arange(strip_depth, dtype=jnp.int32)[:, None] == cell_col[None, :])....]
    unnamed x28 -> x26, local copies, waits for them, and re-layouts: 2.43 us -> 2.43 us
  transfers between devices with their start and end apart: 3 -> 3, of which waited for: 0 -> 0; matrix products, arithmetic and copies ran while one was open for 37% -> 37% of each run, Pallas kernels for 38% -> 39%
where the time goes in v17:
time: 107 us
  Pallas kernels  53.4 us (50%)
  other arithmetic  29.1 us (27%)
  local copies, waits for them, and re-layouts  10.9 us (10%)
  matrix products  6.6 us (6%)
  starting transfers between devices  5.05 us (5%)
  between operations  1.65 us (2%)
    pallas_call x1, Pallas kernels, rates_exchange(): pl.pallas_call(functools.partial(exchange_kernel, member_count), out_shap...  28 us
    pallas_call x1, Pallas kernels, stencil(): pl.pallas_call(functools.partial(stencil_kernel, rim), grid=(members // b...  13.9 us
    another operation x3, other arithmetic, solve_spd(): lax.linalg.cholesky(gram_matrix + jnp.eye(gram_matrix.shape[0], dtype=jnp...  12.4 us
    pallas_call x1, Pallas kernels, halo_exchange(): pl.pallas_call(halo_kernel, out_shape=jax.ShapeDtypeStruct(outgoing.shape...  11.5 us
    another operation x2, other arithmetic, solve_spd(): lax.linalg.triangular_solve(factor, halfway, left_side=True, lower=True,...  10.5 us
    ppermute x3, starting transfers between devices, per_device(): anomaly_parts.append(lax.ppermute(anomaly, 'member', pairs))  5.05 us
    dot_general x1, matrix products, per_device(): lax.dot_general(scaled_t, scaled_t, contract_wells, precision=lax.Precisi...  2.88 us
    unnamed x26, local copies, waits for them, and re-layouts  2.43 us
  transfers between devices with their start and end apart: 3, of which 0 were waited for; matrix products, arithmetic and copies ran while one was open for 37% of the time, Pallas kernels for 39%

profile of v17, /device:TPU:1, one launch (start us, length us, event | category | flops | bytes accessed | tf_op | source)
XLA Modules:
  0.0 106.7 jit_solution(13925068212930125818)
XLA Ops:
  0.6 0.8 pad_maximum_fusion.1.f_mid
  1.6 1.8 %fusion.45 = (f32[32,4,3,256]{3,2,1,0:T(4,128)S(1)}, f32[32,4,3,256]{3,2,1,0:T(4,128)S(1)}) fusion(f32[32,4,8,256]{3,2,1,0:T(8,128)} %lp_mid.1), kind=kLoop, calls=%fused_computation.77 | loop fusion | bytes 1572864 | tf_op jit(solution)/shard_map/slice | solution.py:374
  3.9 1.0 pad_maximum_fusion.out_ref
  4.9 11.5 %shard_map.147 = f32[2,432,256]{2,1,0:T(8,128)} custom-call(f32[2,432,256]{2,1,0:T(8,128)} %pad_maximum_fusion.out_ref), custom_call_target="tpu_custom_call" | custom-call | tf_op jit(solution)/shard_map/pallas_call | solution.py:313
  16.8 1.4 %collective-permute-start = (bf16[32,8192]{1,0:T(8,128)(2,1)S(1)}, bf16[32,8192]{1,0:T(8,128)(2,1)S(1)}, u32[]{:S(2)}, u32[]{:S(2)}) collective-permute-start(bf16[32,8192]{1,0:T(8,128)(2,1)S(1)} %bitcast.46), channel_id=1, source_target_pairs={{0,1},{1,2},{2,3},{3,0},{4,5},{5,6},{6,7},{7,4},{8,9},{9,10},{10,1... | collective-permute-start | bytes 1572872 | tf_op jit(solution)/shard_map/ppermute | solution.py:446
  18.2 2.6 %collective-permute-start.1 = (bf16[32,8192]{1,0:T(8,128)(2,1)S(1)}, bf16[32,8192]{1,0:T(8,128)(2,1)S(1)}, u32[]{:S(2)}, u32[]{:S(2)}) collective-permute-start(bf16[32,8192]{1,0:T(8,128)(2,1)S(1)} %bitcast.47), channel_id=1, source_target_pairs={{0,2},{1,3},{2,0},{3,1},{4,6},{5,7},{6,4},{7,5},{8,10},{9,11},{10,... | collective-permute-start | bytes 1572872 | tf_op jit(solution)/shard_map/ppermute | solution.py:446
  20.8 1.1 %collective-permute-start.2 = (bf16[32,8192]{1,0:T(8,128)(2,1)S(1)}, bf16[32,8192]{1,0:T(8,128)(2,1)S(1)}, u32[]{:S(2)}, u32[]{:S(2)}) collective-permute-start(bf16[32,8192]{1,0:T(8,128)(2,1)S(1)} %bitcast.48), channel_id=1, source_target_pairs={{0,3},{1,0},{2,1},{3,2},{4,7},{5,4},{6,5},{7,6},{8,11},{9,8},{10,9... | collective-permute-start | bytes 1572872 | tf_op jit(solution)/shard_map/ppermute | solution.py:446
  22.0 1.0 reshape_squeeze.12.lp_low
  23.0 1.0 reshape_squeeze.13.lp_high
  25.7 0.7 fusion.22.col_ref
  27.1 13.9 %shard_map.148 = (f32[32,4,8,256]{3,2,1,0:T(8,128)}, f32[32,4,8,256]{3,2,1,0:T(8,128)}, f32[8,4,256]{2,1,0:T(4,128)}, f32[8,4,256]{2,1,0:T(4,128)}) custom-call(f32[32,4,3,256]{3,2,1,0:T(4,128)} %reshape_squeeze.12.lp_low, f32[32,4,8,256]{3,2,1,0:T(8,128)} %lp_mid.1, f32[32,4,3,256]{3,2,1,0:T(4,128)} %reshape_squeeze.13.lp_high, ...), custom_call_target="tpu_custom_call" | custom-call | tf_op jit(solution)/shard_map/pallas_call | solution.py:271
  41.0 0.8 reshape.95
  41.8 0.8 reshape.96
  43.9 0.8 fusion.11
  44.7 0.8 reshape.97.part_ref
  45.5 28.0 %shard_map.149 = f32[32,32,128]{2,1,0:T(8,128)} custom-call(f32[32,8,128]{2,1,0:T(8,128)} %reshape.97.part_ref), custom_call_target="tpu_custom_call" | custom-call | tf_op jit(solution)/shard_map/pallas_call | solution.py:326
  73.5 1.2 %reduce_sum.9 = f32[32,32]{1,0:T(8,128)S(1)} reduce(f32[32,32,128]{2,1,0:T(8,128)} %shard_map.149, f32[]{:T(128)} %constant.107.clone.1), dimensions={2}, to_apply=%region_0.1 | reduce | flops 130048 | bytes 528388 | tf_op jit(solution)/shard_map/reduce_sum | solution.py:428
  74.9 2.9 %fusion.8 = f32[128,128]{1,0:T(8,128)S(1)} fusion(f32[32,32,128]{2,1,0:T(8,128)} %shard_map.149, f32[32,32]{1,0:T(8,128)S(1)} %div.56, f32[32,32]{1,0:T(8,128)S(1)} %broadcast_multiply_fusion), kind=kOutput, calls=%fused_computation.9 | convolution fusion | flops 201637888 | bytes 598016 | tf_op jit(solution)/shard_map/dot_general | solution.py:433
  77.8 11.7 %cholesky.17 = f32[128,128]{1,0:T(8,128)S(1)} custom-call(f32[128,128]{1,0:T(8,128)S(1)} %fusion.8), custom_call_target="Cholesky" | custom-call | tf_op jit(solution)/shard_map/cholesky | solution.py:101
  90.9 9.8 %custom-call.7 = f32[1,128,128]{1,2,0:T(8,128)S(1)} custom-call(f32[1,128,128]{2,1,0:T(8,128)S(1)} %fusion.25), custom_call_target="InvertDiagBlocksLowerTriangular" | custom-call | tf_op jit(solution)/shard_map/triangular_solve | solution.py:105
  101.2 0.7 copy.20
  101.8 1.3 %fusion.17 = f32[128,32]{1,0:T(8,128)S(1)} fusion(f32[1024,128]{1,0:T(8,128)S(1)} %bitcast.42, f32[1024]{0:T(1024)S(1)} %get-tuple-element.33, f32[1024]{0:T(1024)S(1)} %div.59, f32[32,1024]{1,0:T(8,128)S(1)} %copy-done.9, f32[1024,32]{0,1:T(8,128)S(1)} %copy.22, f32[1024]{0:T(1024)S(1)} %get-tuple-element.32, f32[1024]{0:T(1024)S(1)} %copy-done.10), kind=kOutput, calls=%fused_computation.22 | convolution fusion | flops 50692096 | bytes 819200 | tf_op jit(solution)/shard_map/dot_general | solution.py:437
  104.6 0.9 copy-done.2
  105.5 1.1 %add.82 = f32[32,4,8,256]{3,2,1,0:T(8,128)} add(f32[32,4,8,256]{3,2,1,0:T(8,128)S(1)} %copy-done.2, f32[32,4,8,256]{3,2,1,0:T(8,128)S(1)} %bitcast.43) | non-fusion elementwise | flops 262144 | bytes 3145728 | tf_op jit(solution)/shard_map/add | solution.py:460
  (56 shorter events, 7.5 us)
Async XLA Ops:
  0.6 42.6 %copy-start = (f32[1024]{0:T(1024)S(1)}, f32[1024]{0:T(1024)}, u32[]{:S(2)}) copy-start(f32[1024]{0:T(1024)} %param.17) | copy-start | bytes 12292
  1.5 1.9 %copy-start.5 = (f32[4,4,8,256]{3,2,1,0:T(8,128)}, f32[4,4,8,256]{3,2,1,0:T(8,128)S(1)}, u32[]{:S(2)}) copy-start(f32[4,4,8,256]{3,2,1,0:T(8,128)S(1)} %pad_maximum_fusion.1.f_mid) | copy-start | bytes 393220
  4.9 11.5 %copy-start.1 = (f32[32,4,8,256]{3,2,1,0:T(8,128)S(1)}, f32[32,4,8,256]{3,2,1,0:T(8,128)}, u32[]{:S(2)}) copy-start(f32[32,4,8,256]{3,2,1,0:T(8,128)} %lp_mid.1) | copy-start | bytes 3145732
  16.4 5.5 %copy-start.4 = (f32[2,432,256]{2,1,0:T(8,128)S(1)}, f32[2,432,256]{2,1,0:T(8,128)}, u32[]{:S(2)}) copy-start(f32[2,432,256]{2,1,0:T(8,128)} %shard_map.147) | copy-start | bytes 2654212
  16.8 87.0 %collective-permute-start = (bf16[32,8192]{1,0:T(8,128)(2,1)S(1)}, bf16[32,8192]{1,0:T(8,128)(2,1)S(1)}, u32[]{:S(2)}, u32[]{:S(2)}) collective-permute-start(bf16[32,8192]{1,0:T(8,128)(2,1)S(1)} %bitcast.46), channel_id=1, source_target_pairs={{0,1},{1,2},{2,3},{3,0},{4,5},{5,6},{6,7},{7,4},{8,9},{9,10},{10,1... | collective-permute-start | bytes 1572872 | tf_op jit(solution)/shard_map/ppermute | solution.py:446
  18.2 85.6 %collective-permute-start.1 = (bf16[32,8192]{1,0:T(8,128)(2,1)S(1)}, bf16[32,8192]{1,0:T(8,128)(2,1)S(1)}, u32[]{:S(2)}, u32[]{:S(2)}) collective-permute-start(bf16[32,8192]{1,0:T(8,128)(2,1)S(1)} %bitcast.47), channel_id=1, source_target_pairs={{0,2},{1,3},{2,0},{3,1},{4,6},{5,7},{6,4},{7,5},{8,10},{9,11},{10,... | collective-permute-start | bytes 1572872 | tf_op jit(solution)/shard_map/ppermute | solution.py:446
  20.8 83.0 %collective-permute-start.2 = (bf16[32,8192]{1,0:T(8,128)(2,1)S(1)}, bf16[32,8192]{1,0:T(8,128)(2,1)S(1)}, u32[]{:S(2)}, u32[]{:S(2)}) collective-permute-start(bf16[32,8192]{1,0:T(8,128)(2,1)S(1)} %bitcast.48), channel_id=1, source_target_pairs={{0,3},{1,0},{2,1},{3,2},{4,7},{5,4},{6,5},{7,6},{8,11},{9,8},{10,9... | collective-permute-start | bytes 1572872 | tf_op jit(solution)/shard_map/ppermute | solution.py:446
  22.0 3.7 %copy-start.8 = (s32[256]{0:T(256)S(1)}, s32[256]{0:T(256)}, u32[]{:S(2)}) copy-start(s32[256]{0:T(256)} %param.18) | copy-start | bytes 3076
  27.1 16.1 %copy-start.7 = (s32[256]{0:T(256)S(1)}, s32[256]{0:T(256)}, u32[]{:S(2)}) copy-start(s32[256]{0:T(256)} %param.19) | copy-start | bytes 3076
  44.6 30.1 %copy-start.6 = (f32[1024]{0:T(1024)S(1)}, f32[1024]{0:T(1024)}, u32[]{:S(2)}) copy-start(f32[1024]{0:T(1024)} %param.22) | copy-start | bytes 12292
  74.9 25.8 %copy-start.3 = (f32[32,32,128]{2,1,0:T(8,128)S(1)}, f32[32,32,128]{2,1,0:T(8,128)}, u32[]{:S(2)}) copy-start(f32[32,32,128]{2,1,0:T(8,128)} %shard_map.149) | copy-start | bytes 1572868
  77.8 24.0 %copy-start.9 = (f32[32,1024]{1,0:T(8,128)S(1)}, f32[32,1024]{1,0:T(8,128)}, u32[]{:S(2)}) copy-start(f32[32,1024]{1,0:T(8,128)} %param.23) | copy-start | bytes 393220
  77.8 24.0 %copy-start.10 = (f32[1024]{0:T(1024)S(1)}, f32[1024]{0:T(1024)}, u32[]{:S(2)}) copy-start(f32[1024]{0:T(1024)} %param.21) | copy-start | bytes 12292
  104.3 1.2 %copy-start.2 = (f32[32,4,8,256]{3,2,1,0:T(8,128)S(1)}, f32[32,4,8,256]{3,2,1,0:T(8,128)}, u32[]{:S(2)}) copy-start(f32[32,4,8,256]{3,2,1,0:T(8,128)} %lp_mid.1) | copy-start | bytes 3145732

commit v18 on v15

--- a/solution.py
+++ b/solution.py
@@ -429,12 +429,12 @@
         preferred_element_type=jnp.float32,
     )
     weights_low = solve_spd(gram_matrix, cross_matrix).astype(jnp.bfloat16)
-    anomaly = (log_perm_after / member_root).astype(jnp.bfloat16).reshape(local_count, cell_count)
+    anomaly = (log_perm_after / member_root).astype(jnp.bfloat16).transpose(1, 2, 0, 3)
     anomaly_parts = [anomaly]
     for shift in range(1, member_count):
         pairs = [(i, (i + shift) % member_count) for i in range(member_count)]
         anomaly_parts.append(lax.ppermute(anomaly, "member", pairs))
-    anomaly_all = jnp.concatenate(anomaly_parts, axis=0)
+    anomaly_all = jnp.concatenate(anomaly_parts, axis=2)
     own_cols = jnp.concatenate(
         [
             lax.dynamic_slice_in_dim(
@@ -445,9 +445,9 @@
         ],
         axis=0,
     )
-    contract = (((0,), (0,)), ((), ()))
+    contract = (((0,), (2,)), ((), ()))
     update_sum = lax.dot_general(own_cols, anomaly_all, contract, preferred_element_type=jnp.float32)
-    new_log_perm = log_perm + update_sum.reshape(log_perm.shape)
+    new_log_perm = log_perm + update_sum
     return (new_log_perm, pressure, saturation, well_rates)
 
 

time: 103 us -> 102 us (level)
    add x1 -> x0, other arithmetic: 1.13 us -> none  [per_device(): new_log_perm = log_perm + update_sum.reshape(log_perm.shape)]
    unnamed x28 -> x27, local copies, waits for them, and re-layouts: 2.43 us -> 2.56 us
where the time goes in v18:
time: 102 us
  Pallas kernels  49.8 us (49%)
  other arithmetic  27.1 us (27%)
  local copies, waits for them, and re-layouts  9.44 us (9%)
  matrix products  8.82 us (9%)
  starting transfers between devices  5.05 us (5%)
  between operations  1.66 us (2%)
    pallas_call x1, Pallas kernels, rates_exchange(): pl.pallas_call(functools.partial(exchange_kernel, member_count), out_shap...  28 us
    another operation x3, other arithmetic, solve_spd(): lax.linalg.cholesky(gram_matrix + jnp.eye(gram_matrix.shape[0], dtype=jnp...  12.4 us
    pallas_call x1, Pallas kernels, halo_exchange(): pl.pallas_call(halo_kernel, out_shape=jax.ShapeDtypeStruct(outgoing.shape...  11.5 us
    another operation x2, other arithmetic, solve_spd(): lax.linalg.triangular_solve(factor, halfway, left_side=True, lower=True,...  10.5 us
    pallas_call x1, Pallas kernels, stencil(): pl.pallas_call(functools.partial(stencil_kernel, rim), grid=(members // b...  10.3 us
    ppermute x3, starting transfers between devices, per_device(): anomaly_parts.append(lax.ppermute(anomaly, 'member', pairs))  5.05 us
    dot_general x1, matrix products, per_device(): lax.dot_general(scaled_t, scaled_t, contract_wells, precision=lax.Precisi...  2.88 us
    dot_general x2, matrix products, pick_cells(): jnp.dot(values_in.reshape(local_count * plane_rows, strip_depth), col_pic...  2.61 us
  transfers between devices with their start and end apart: 3, of which 0 were waited for; matrix products, arithmetic and copies ran while one was open for 37% of the time, Pallas kernels for 38%

profile of v18, /device:TPU:1, one launch (start us, length us, event | category | flops | bytes accessed | tf_op | source)
XLA Modules:
  0.0 102.0 jit_solution(5248743397500561777)
XLA Ops:
  0.6 0.8 pad_maximum_fusion.1.f_mid
  1.6 1.8 %fusion.56 = (f32[32,4,3,256]{3,2,1,0:T(4,128)S(1)}, f32[32,4,3,256]{3,2,1,0:T(4,128)S(1)}) fusion(f32[32,4,8,256]{3,2,1,0:T(8,128)} %lp_mid.1), kind=kLoop, calls=%fused_computation.87 | loop fusion | bytes 1572864 | tf_op jit(solution)/shard_map/slice | solution.py:358
  3.9 1.0 pad_maximum_fusion.out_ref
  4.9 11.5 %shard_map.147 = f32[2,432,256]{2,1,0:T(8,128)} custom-call(f32[2,432,256]{2,1,0:T(8,128)} %pad_maximum_fusion.out_ref), custom_call_target="tpu_custom_call" | custom-call | tf_op jit(solution)/shard_map/pallas_call | solution.py:297
  17.0 1.4 %collective-permute-start = (bf16[4,8,32,256]{3,2,1,0:T(8,128)(2,1)S(1)}, bf16[4,8,32,256]{3,2,1,0:T(8,128)(2,1)S(1)}, u32[]{:S(2)}, u32[]{:S(2)}) collective-permute-start(bf16[4,8,32,256]{3,2,1,0:T(8,128)(2,1)S(1)} %fusion.21), channel_id=1, source_target_pairs={{0,1},{1,2},{2,3},{3,0},{4,5},{5,6},{6,7},{7,4},{8,9},{9,10},{10,1... | collective-permute-start | bytes 1572872 | tf_op jit(solution)/shard_map/ppermute | solution.py:436
  18.4 2.6 %collective-permute-start.1 = (bf16[4,8,32,256]{3,2,1,0:T(8,128)(2,1)S(1)}, bf16[4,8,32,256]{3,2,1,0:T(8,128)(2,1)S(1)}, u32[]{:S(2)}, u32[]{:S(2)}) collective-permute-start(bf16[4,8,32,256]{3,2,1,0:T(8,128)(2,1)S(1)} %fusion.21), channel_id=1, source_target_pairs={{0,2},{1,3},{2,0},{3,1},{4,6},{5,7},{6,4},{7,5},{8,10},{9,11},{10,... | collective-permute-start | bytes 1572872 | tf_op jit(solution)/shard_map/ppermute | solution.py:436
  21.0 1.1 %collective-permute-start.2 = (bf16[4,8,32,256]{3,2,1,0:T(8,128)(2,1)S(1)}, bf16[4,8,32,256]{3,2,1,0:T(8,128)(2,1)S(1)}, u32[]{:S(2)}, u32[]{:S(2)}) collective-permute-start(bf16[4,8,32,256]{3,2,1,0:T(8,128)(2,1)S(1)} %fusion.21), channel_id=1, source_target_pairs={{0,3},{1,0},{2,1},{3,2},{4,7},{5,4},{6,5},{7,6},{8,11},{9,8},{10,9... | collective-permute-start | bytes 1572872 | tf_op jit(solution)/shard_map/ppermute | solution.py:436
  22.2 1.0 reshape_squeeze.12.lp_low
  23.2 0.9 reshape_squeeze.13.lp_high
  25.9 10.3 %shard_map.148 = (f32[32,4,8,256]{3,2,1,0:T(8,128)}, f32[32,4,8,256]{3,2,1,0:T(8,128)}, f32[32,4,8,256]{3,2,1,0:T(8,128)}) custom-call(f32[32,4,3,256]{3,2,1,0:T(4,128)} %reshape_squeeze.12.lp_low, f32[32,4,8,256]{3,2,1,0:T(8,128)} %lp_mid.1, f32[32,4,3,256]{3,2,1,0:T(4,128)} %reshape_squeeze.13.lp_high, f32[4,4,3,256]{3,2,1,0:T(4,128)} %reshape_squeeze.14.f_low, ...), custom_call_target="tpu_custom_call" | custom-call | tf_op jit(solution)/shard_map/pallas_call | solution.py:259
  36.3 2.0 %fusion.12 = f32[32,256]{1,0:T(8,128)S(1)} fusion(f32[32,4,8,256]{3,2,1,0:T(8,128)} %get-tuple-element.23, pred[32,256]{1,0:T(8,128)(4,1)S(1)} %iota_compare_fusion.5, s32[256]{0:T(256)S(1)} %get-tuple-element.40), kind=kOutput, calls=%fused_computation.12 | convolution fusion | flops 805888000 | bytes 1090560 | tf_op jit(solution)/shard_map/dot_general | solution.py:390
  38.3 0.7 fusion.11
  40.2 0.8 fusion.19
  41.0 0.8 reshape.111.part_ref
  41.8 28.0 %shard_map.149 = f32[32,32,128]{2,1,0:T(8,128)} custom-call(f32[32,8,128]{2,1,0:T(8,128)} %reshape.111.part_ref), custom_call_target="tpu_custom_call" | custom-call | tf_op jit(solution)/shard_map/pallas_call | solution.py:310
  69.8 1.2 %reduce_sum.29 = f32[32,32]{1,0:T(8,128)S(1)} reduce(f32[32,32,128]{2,1,0:T(8,128)} %shard_map.149, f32[]{:T(128)} %constant.107.clone.1), dimensions={2}, to_apply=%region_2.3 | reduce | flops 130048 | bytes 528388 | tf_op jit(solution)/shard_map/reduce_sum | solution.py:418
  71.3 2.9 %fusion.13 = f32[128,128]{1,0:T(8,128)S(1)} fusion(f32[32,32,128]{2,1,0:T(8,128)} %shard_map.149, f32[32,32]{1,0:T(8,128)S(1)} %div.56, f32[32,32]{1,0:T(8,128)S(1)} %broadcast_multiply_fusion), kind=kOutput, calls=%fused_computation.14 | convolution fusion | flops 201637888 | bytes 598016 | tf_op jit(solution)/shard_map/dot_general | solution.py:423
  74.2 11.7 %cholesky.17 = f32[128,128]{1,0:T(8,128)S(1)} custom-call(f32[128,128]{1,0:T(8,128)S(1)} %fusion.13), custom_call_target="Cholesky" | custom-call | tf_op jit(solution)/shard_map/cholesky | solution.py:101
  85.9 0.6 compare_reduce_fusion
  86.6 0.7 fusion.38
  87.2 9.8 %custom-call.7 = f32[1,128,128]{1,2,0:T(8,128)S(1)} custom-call(f32[1,128,128]{2,1,0:T(8,128)S(1)} %fusion.38), custom_call_target="InvertDiagBlocksLowerTriangular" | custom-call | tf_op jit(solution)/shard_map/triangular_solve | solution.py:105
  97.5 0.7 copy.32
  99.4 0.9 fusion.8
  100.4 1.6 %copy.31 = f32[32,4,8,256]{3,2,1,0:T(8,128)} copy(f32[32,4,8,256]{3,0,2,1:T(8,128)S(1)} %fusion.8) | data formatting | bytes 2097152
  (55 shorter events, 5.5 us)
Async XLA Ops:
  0.6 38.9 %copy-start = (f32[1024]{0:T(1024)S(1)}, f32[1024]{0:T(1024)}, u32[]{:S(2)}) copy-start(f32[1024]{0:T(1024)} %param.17) | copy-start | bytes 12292
  1.5 1.9 %copy-start.5 = (f32[4,4,8,256]{3,2,1,0:T(8,128)}, f32[4,4,8,256]{3,2,1,0:T(8,128)S(1)}, u32[]{:S(2)}) copy-start(f32[4,4,8,256]{3,2,1,0:T(8,128)S(1)} %pad_maximum_fusion.1.f_mid) | copy-start | bytes 393220
  4.9 11.5 %copy-start.1 = (f32[32,4,8,256]{3,2,1,0:T(8,128)S(1)}, f32[32,4,8,256]{3,2,1,0:T(8,128)}, u32[]{:S(2)}) copy-start(f32[32,4,8,256]{3,2,1,0:T(8,128)} %lp_mid.1) | copy-start | bytes 3145732
  16.4 5.7 %copy-start.4 = (f32[2,432,256]{2,1,0:T(8,128)S(1)}, f32[2,432,256]{2,1,0:T(8,128)}, u32[]{:S(2)}) copy-start(f32[2,432,256]{2,1,0:T(8,128)} %shard_map.147) | copy-start | bytes 2654212
  17.0 82.3 %collective-permute-start = (bf16[4,8,32,256]{3,2,1,0:T(8,128)(2,1)S(1)}, bf16[4,8,32,256]{3,2,1,0:T(8,128)(2,1)S(1)}, u32[]{:S(2)}, u32[]{:S(2)}) collective-permute-start(bf16[4,8,32,256]{3,2,1,0:T(8,128)(2,1)S(1)} %fusion.21), channel_id=1, source_target_pairs={{0,1},{1,2},{2,3},{3,0},{4,5},{5,6},{6,7},{7,4},{8,9},{9,10},{10,1... | collective-permute-start | bytes 1572872 | tf_op jit(solution)/shard_map/ppermute | solution.py:436
  18.4 81.0 %collective-permute-start.1 = (bf16[4,8,32,256]{3,2,1,0:T(8,128)(2,1)S(1)}, bf16[4,8,32,256]{3,2,1,0:T(8,128)(2,1)S(1)}, u32[]{:S(2)}, u32[]{:S(2)}) collective-permute-start(bf16[4,8,32,256]{3,2,1,0:T(8,128)(2,1)S(1)} %fusion.21), channel_id=1, source_target_pairs={{0,2},{1,3},{2,0},{3,1},{4,6},{5,7},{6,4},{7,5},{8,10},{9,11},{10,... | collective-permute-start | bytes 1572872 | tf_op jit(solution)/shard_map/ppermute | solution.py:436
  21.0 78.3 %collective-permute-start.2 = (bf16[4,8,32,256]{3,2,1,0:T(8,128)(2,1)S(1)}, bf16[4,8,32,256]{3,2,1,0:T(8,128)(2,1)S(1)}, u32[]{:S(2)}, u32[]{:S(2)}) collective-permute-start(bf16[4,8,32,256]{3,2,1,0:T(8,128)(2,1)S(1)} %fusion.21), channel_id=1, source_target_pairs={{0,3},{1,0},{2,1},{3,2},{4,7},{5,4},{6,5},{7,6},{8,11},{9,8},{10,9... | collective-permute-start | bytes 1572872 | tf_op jit(solution)/shard_map/ppermute | solution.py:436
  22.2 3.7 %copy-start.9 = (s32[256]{0:T(256)S(1)}, s32[256]{0:T(256)}, u32[]{:S(2)}) copy-start(s32[256]{0:T(256)} %param.18) | copy-start | bytes 3076
  36.3 2.0 %copy-start.6 = (f32[32,4,8,256]{3,2,1,0:T(8,128)S(1)}, f32[32,4,8,256]{3,2,1,0:T(8,128)}, u32[]{:S(2)}) copy-start(f32[32,4,8,256]{3,2,1,0:T(8,128)} %get-tuple-element.10) | copy-start | bytes 3145732
  36.3 3.3 %copy-start.8 = (s32[256]{0:T(256)S(1)}, s32[256]{0:T(256)}, u32[]{:S(2)}) copy-start(s32[256]{0:T(256)} %param.19) | copy-start | bytes 3076
  41.0 30.1 %copy-start.7 = (f32[1024]{0:T(1024)S(1)}, f32[1024]{0:T(1024)}, u32[]{:S(2)}) copy-start(f32[1024]{0:T(1024)} %param.22) | copy-start | bytes 12292
  71.3 25.8 %copy-start.3 = (f32[32,32,128]{2,1,0:T(8,128)S(1)}, f32[32,32,128]{2,1,0:T(8,128)}, u32[]{:S(2)}) copy-start(f32[32,32,128]{2,1,0:T(8,128)} %shard_map.149) | copy-start | bytes 1572868
  74.2 24.0 %copy-start.10 = (f32[32,1024]{1,0:T(8,128)S(1)}, f32[32,1024]{1,0:T(8,128)}, u32[]{:S(2)}) copy-start(f32[32,1024]{1,0:T(8,128)} %param.23) | copy-start | bytes 393220
  74.2 24.0 %copy-start.11 = (f32[1024]{0:T(1024)S(1)}, f32[1024]{0:T(1024)}, u32[]{:S(2)}) copy-start(f32[1024]{0:T(1024)} %param.21) | copy-start | bytes 12292
  98.2 1.2 %copy-start.2 = (f32[32,4,8,256]{3,2,1,0:T(8,128)S(1)}, f32[32,4,8,256]{3,2,1,0:T(8,128)}, u32[]{:S(2)}) copy-start(f32[32,4,8,256]{3,2,1,0:T(8,128)} %lp_mid.1) | copy-start | bytes 3145732

commit v19 on v18

--- a/solution.py
+++ b/solution.py
@@ -223,12 +223,26 @@
     lax.fori_loop(1, tile_count, wait_t_send, 0)
 
 
-def stencil_kernel(rim, lp_low, lp_mid, lp_high, f_low, f_mid, f_high, inside_ref,
-                   press_ref, sat_ref, mob_ref):
+def stencil_kernel(rim, halo_ref, lp_mid, f_mid, inside_ref, press_ref, sat_ref, mob_ref):
     inside = inside_ref[...]
-    permeab = jnp.exp(jnp.concatenate([lp_low[...], lp_mid[...], lp_high[...]], axis=2))
+    block, layers = lp_mid.shape[0], lp_mid.shape[1]
+    field_count = f_mid.shape[0]
+    lp_rows = pl.ds(pl.multiple_of(pl.program_id(0) * block * layers, block * layers), block * layers)
+    field_first = halo_ref.shape[2] - field_count * layers
+
+    def halo_piece(side, rows, shape):
+        return [halo_ref[side, r, rows, :].reshape(shape) for r in range(rim)]
+
+    lp_shape = (block, layers, 1, lp_mid.shape[3])
+    f_shape = (field_count, layers, 1, f_mid.shape[3])
+    f_rows = pl.ds(field_first, field_count * layers)
+    permeab = jnp.exp(jnp.concatenate(
+        halo_piece(0, lp_rows, lp_shape) + [lp_mid[...]] + halo_piece(1, lp_rows, lp_shape), axis=2
+    ))
     face_sets = face_terms(permeab, inside)
-    fields = jnp.concatenate([f_low[...], f_mid[...], f_high[...]], axis=2)
+    fields = jnp.concatenate(
+        halo_piece(0, f_rows, f_shape) + [f_mid[...]] + halo_piece(1, f_rows, f_shape), axis=2
+    )
     press_ext = fields[0]
     sat_ext = fields[1]
     source_ext = fields[2]
@@ -244,27 +258,27 @@
     mob_ref[...] = trim_rim(permeab, rim) * water_frac(saturation)
 
 
-def stencil(lp_parts, field_parts, inside, rim):
-    members, layers, out_rows, depth = lp_parts[1].shape
+def stencil(halo, log_perm, fields, inside, rim):
+    members, layers, out_rows, depth = log_perm.shape
     block = 4
 
-    def member_block(part):
-        return pl.BlockSpec((block,) + part.shape[1:], lambda i: (i, 0, 0, 0))
-
     def whole(part):
-        return pl.BlockSpec(part.shape, lambda i: (0, 0, 0, 0))
+        return pl.BlockSpec(part.shape, lambda i: (0,) * part.ndim)
 
     out_spec = pl.BlockSpec((block, layers, out_rows, depth), lambda i: (i, 0, 0, 0))
     out_shape = jax.ShapeDtypeStruct((members, layers, out_rows, depth), jnp.float32)
     return pl.pallas_call(
         functools.partial(stencil_kernel, rim),
         grid=(members // block,),
-        in_specs=[member_block(p) for p in lp_parts]
-        + [whole(p) for p in field_parts]
-        + [pl.BlockSpec(inside.shape, lambda i: (0,))],
+        in_specs=[
+            whole(halo),
+            pl.BlockSpec((block, layers, out_rows, depth), lambda i: (i, 0, 0, 0)),
+            whole(fields),
+            whole(inside),
+        ],
         out_specs=[out_spec, out_spec, out_spec],
         out_shape=[out_shape, out_shape, out_shape],
-    )(*lp_parts, *field_parts, inside)
+    )(halo, log_perm, fields, inside)
 
 
 def halo_kernel(out_ref, in_ref, send_sem, recv_sem):
@@ -355,28 +369,19 @@
     def rim_rows(first):
         return jnp.concatenate(
             [
-                lax.slice_in_dim(log_perm, first, first + rim, axis=2).reshape(-1, strip_depth),
-                lax.slice_in_dim(fields, first, first + rim, axis=2).reshape(-1, strip_depth),
-            ]
-        )
+                lax.slice_in_dim(log_perm, first, first + rim, axis=2).transpose(2, 0, 1, 3),
+                lax.slice_in_dim(fields, first, first + rim, axis=2).transpose(2, 0, 1, 3),
+            ],
+            axis=1,
+        ).reshape(-1, strip_depth)
 
     outgoing = jnp.stack([rim_rows(0), rim_rows(strip_width - rim)])
     incoming = halo_exchange(outgoing)
     incoming, log_perm_after = lax.optimization_barrier((incoming, log_perm))
-    lp_count = local_count * layers * rim
-
-    def unpack(side):
-        lp_part = incoming[side, :lp_count].reshape(local_count, layers, rim, strip_depth)
-        field_part = incoming[side, lp_count:].reshape(fields.shape[0], layers, rim, strip_depth)
-        return lp_part, field_part
-
-    low_lp, low_fields = unpack(0)
-    high_lp, high_fields = unpack(1)
+    halo = incoming.reshape(2, rim, -1, strip_depth)
     column = tile_rank * strip_width - rim + jnp.arange(strip_width + 2 * rim, dtype=jnp.int32)
     inside = ((column >= 0) & (column < strip_width * tile_count)).astype(jnp.float32)
-    pressure, saturation, mobility = stencil(
-        (low_lp, log_perm, high_lp), (low_fields, fields, high_fields), inside, rim
-    )
+    pressure, saturation, mobility = stencil(halo, log_perm, fields, inside, rim)
     cell_count = layers * strip_width * strip_depth
     plane_rows = layers * strip_width
     cell_row = perf_cell // strip_depth

time: 102 us -> 100 us (0.980)
  local copies, waits for them, and re-layouts: 9.44 us -> 6.28 us
    another operation x4 -> x2, local copies, waits for them, and re-layouts: 3.19 us -> 0.31 us  [per_device(): outgoing = jnp.stack([rim_rows(0), rim_rows(strip_width - rim)])]
    slice x4 -> x0, local copies, waits for them, and re-layouts: 1.89 us -> none  [the longest x1 1.81 us: rim_rows(): lax.slice_in_dim(log_perm, first, first + rim, axis=2)]
    transpose x0 -> x2, local copies, waits for them, and re-layouts: none -> 1.83 us  [the longest x1 1.81 us: rim_rows(): lax.slice_in_dim(log_perm, first, first + rim, axis=2).transpose(2, 0, 1, 3)]
    unnamed x27 -> x25, local copies, waits for them, and re-layouts: 2.56 us -> 2.55 us
  transfers between devices with their start and end apart: 3 -> 3, of which waited for: 0 -> 0; matrix products, arithmetic and copies ran while one was open for 37% -> 35% of each run, Pallas kernels for 38% -> 39%
where the time goes in v19:
time: 100 us; the launch traced here: 99.9 us
  Pallas kernels  50.8 us (51%)
  other arithmetic  27.4 us (27%)
  matrix products  8.82 us (9%)
  local copies, waits for them, and re-layouts  6.28 us (6%)
  starting transfers between devices  5.05 us (5%)
  between operations  1.6 us (2%)
    pallas_call x1, Pallas kernels, rates_exchange(): pl.pallas_call(functools.partial(exchange_kernel, member_count), out_shap...  28 us
    another operation x3, other arithmetic, solve_spd(): lax.linalg.cholesky(gram_matrix + jnp.eye(gram_matrix.shape[0], dtype=jnp...  12.4 us
    pallas_call x1, Pallas kernels, halo_exchange(): pl.pallas_call(halo_kernel, out_shape=jax.ShapeDtypeStruct(outgoing.shape...  11.5 us
    pallas_call x1, Pallas kernels, stencil(): pl.pallas_call(functools.partial(stencil_kernel, rim), grid=(members // b...  11.3 us
    another operation x2, other arithmetic, solve_spd(): lax.linalg.triangular_solve(factor, halfway, left_side=True, lower=True,...  10.5 us
    ppermute x3, starting transfers between devices, per_device(): anomaly_parts.append(lax.ppermute(anomaly, 'member', pairs))  5.05 us
    dot_general x1, matrix products, per_device(): lax.dot_general(scaled_t, scaled_t, contract_wells, precision=lax.Precisi...  2.88 us
    dot_general x2, matrix products, pick_cells(): jnp.dot(values_in.reshape(local_count * plane_rows, strip_depth), col_pic...  2.61 us
  transfers between devices with their start and end apart: 3, of which 0 were waited for; matrix products, arithmetic and copies ran while one was open for 35% of the time, Pallas kernels for 39%

profile of v19, /device:TPU:1, one launch (start us, length us, event | category | flops | bytes accessed | tf_op | source)
XLA Modules:
  0.0 99.9 jit_solution(15190943643494390590)
XLA Ops:
  0.6 0.8 pad_maximum_fusion.3.f_mid
  1.5 1.8 %slice_bitcast_fusion.1 = (f32[3,32,4,256]{3,0,2,1:T(4,128)S(1)}, f32[3,32,4,256]{3,0,2,1:T(4,128)S(1)}) fusion(f32[32,4,8,256]{3,2,1,0:T(8,128)} %lp_mid.1), kind=kLoop, calls=%fused_computation.32 | loop fusion | bytes 1572864 | tf_op jit(solution)/shard_map/transpose | solution.py:372
  4.2 1.0 pad_maximum_fusion.out_ref
  5.2 11.5 %shard_map.147 = f32[2,432,256]{2,1,0:T(8,128)} custom-call(f32[2,432,256]{2,1,0:T(8,128)} %pad_maximum_fusion.out_ref), custom_call_target="tpu_custom_call" | custom-call | tf_op jit(solution)/shard_map/pallas_call | solution.py:311
  17.4 1.4 %collective-permute-start = (bf16[4,8,32,256]{3,2,1,0:T(8,128)(2,1)S(1)}, bf16[4,8,32,256]{3,2,1,0:T(8,128)(2,1)S(1)}, u32[]{:S(2)}, u32[]{:S(2)}) collective-permute-start(bf16[4,8,32,256]{3,2,1,0:T(8,128)(2,1)S(1)} %fusion.21), channel_id=1, source_target_pairs={{0,1},{1,2},{2,3},{3,0},{4,5},{5,6},{6,7},{7,4},{8,9},{9,10},{10,1... | collective-permute-start | bytes 1572872 | tf_op jit(solution)/shard_map/ppermute | solution.py:441
  18.7 2.6 %collective-permute-start.1 = (bf16[4,8,32,256]{3,2,1,0:T(8,128)(2,1)S(1)}, bf16[4,8,32,256]{3,2,1,0:T(8,128)(2,1)S(1)}, u32[]{:S(2)}, u32[]{:S(2)}) collective-permute-start(bf16[4,8,32,256]{3,2,1,0:T(8,128)(2,1)S(1)} %fusion.21), channel_id=1, source_target_pairs={{0,2},{1,3},{2,0},{3,1},{4,6},{5,7},{6,4},{7,5},{8,10},{9,11},{10,... | collective-permute-start | bytes 1572872 | tf_op jit(solution)/shard_map/ppermute | solution.py:441
  21.3 1.1 %collective-permute-start.2 = (bf16[4,8,32,256]{3,2,1,0:T(8,128)(2,1)S(1)}, bf16[4,8,32,256]{3,2,1,0:T(8,128)(2,1)S(1)}, u32[]{:S(2)}, u32[]{:S(2)}) collective-permute-start(bf16[4,8,32,256]{3,2,1,0:T(8,128)(2,1)S(1)} %fusion.21), channel_id=1, source_target_pairs={{0,3},{1,0},{2,1},{3,2},{4,7},{5,4},{6,5},{7,6},{8,11},{9,8},{10,9... | collective-permute-start | bytes 1572872 | tf_op jit(solution)/shard_map/ppermute | solution.py:441
  23.0 11.3 %shard_map.148 = (f32[32,4,8,256]{3,2,1,0:T(8,128)}, f32[32,4,8,256]{3,2,1,0:T(8,128)}, f32[32,4,8,256]{3,2,1,0:T(8,128)}) custom-call(f32[2,3,144,256]{3,2,1,0:T(8,128)} %bitcast.59, f32[32,4,8,256]{3,2,1,0:T(8,128)} %lp_mid.1, f32[4,4,8,256]{3,2,1,0:T(8,128)} %copy-done.4, f32[14]{0:T(128)} %and_convert_fusion.inside_ref), custom_call_target="tpu_custom_call" | custom-call | tf_op jit(solution)/shard_map/pallas_call | solution.py:270
  34.3 2.0 %fusion.12 = f32[32,256]{1,0:T(8,128)S(1)} fusion(f32[32,4,8,256]{3,2,1,0:T(8,128)} %get-tuple-element.23, pred[32,256]{1,0:T(8,128)(4,1)S(1)} %iota_compare_fusion.5, s32[256]{0:T(256)S(1)} %get-tuple-element.36), kind=kOutput, calls=%fused_computation.12 | convolution fusion | flops 805888000 | bytes 1090560 | tf_op jit(solution)/shard_map/dot_general | solution.py:395
  36.2 0.7 fusion.11
  37.6 0.6 fusion.18
  38.2 0.8 fusion.19
  39.0 0.8 reshape.99.part_ref
  39.8 28.0 %shard_map.149 = f32[32,32,128]{2,1,0:T(8,128)} custom-call(f32[32,8,128]{2,1,0:T(8,128)} %reshape.99.part_ref), custom_call_target="tpu_custom_call" | custom-call | tf_op jit(solution)/shard_map/pallas_call | solution.py:324
  67.8 1.2 %reduce_sum.29 = f32[32,32]{1,0:T(8,128)S(1)} reduce(f32[32,32,128]{2,1,0:T(8,128)} %shard_map.149, f32[]{:T(128)} %constant.107.clone.1), dimensions={2}, to_apply=%region_2.3 | reduce | flops 130048 | bytes 528388 | tf_op jit(solution)/shard_map/reduce_sum | solution.py:423
  69.3 2.9 %fusion.13 = f32[128,128]{1,0:T(8,128)S(1)} fusion(f32[32,32,128]{2,1,0:T(8,128)} %shard_map.149, f32[32,32]{1,0:T(8,128)S(1)} %div.56, f32[32,32]{1,0:T(8,128)S(1)} %broadcast_multiply_fusion), kind=kOutput, calls=%fused_computation.14 | convolution fusion | flops 201637888 | bytes 598016 | tf_op jit(solution)/shard_map/dot_general | solution.py:428
  72.2 11.7 %cholesky.17 = f32[128,128]{1,0:T(8,128)S(1)} custom-call(f32[128,128]{1,0:T(8,128)S(1)} %fusion.13), custom_call_target="Cholesky" | custom-call | tf_op jit(solution)/shard_map/cholesky | solution.py:101
  83.9 0.6 compare_reduce_fusion
  84.6 0.7 fusion.38
  85.2 9.8 %custom-call.7 = f32[1,128,128]{1,2,0:T(8,128)S(1)} custom-call(f32[1,128,128]{2,1,0:T(8,128)S(1)} %fusion.38), custom_call_target="InvertDiagBlocksLowerTriangular" | custom-call | tf_op jit(solution)/shard_map/triangular_solve | solution.py:105
  95.5 0.7 copy.38
  96.2 0.6 fusion.26
  97.4 0.9 fusion.8
  98.3 1.6 %copy.37 = f32[32,4,8,256]{3,2,1,0:T(8,128)} copy(f32[32,4,8,256]{3,0,2,1:T(8,128)S(1)} %fusion.8) | data formatting | bytes 2097152
  (47 shorter events, 3.3 us)
Async XLA Ops:
  0.6 36.9 %copy-start = (f32[1024]{0:T(1024)S(1)}, f32[1024]{0:T(1024)}, u32[]{:S(2)}) copy-start(f32[1024]{0:T(1024)} %param.17) | copy-start | bytes 12292
  1.5 1.9 %copy-start.4 = (f32[4,4,8,256]{3,2,1,0:T(8,128)}, f32[4,4,8,256]{3,2,1,0:T(8,128)S(1)}, u32[]{:S(2)}) copy-start(f32[4,4,8,256]{3,2,1,0:T(8,128)S(1)} %pad_maximum_fusion.3.f_mid) | copy-start | bytes 393220
  5.2 11.5 %copy-start.1 = (f32[32,4,8,256]{3,2,1,0:T(8,128)S(1)}, f32[32,4,8,256]{3,2,1,0:T(8,128)}, u32[]{:S(2)}) copy-start(f32[32,4,8,256]{3,2,1,0:T(8,128)} %lp_mid.1) | copy-start | bytes 3145732
  16.7 6.2 %copy-start.8 = (s32[256]{0:T(256)S(1)}, s32[256]{0:T(256)}, u32[]{:S(2)}) copy-start(s32[256]{0:T(256)} %param.18) | copy-start | bytes 3076
  17.4 80.0 %collective-permute-start = (bf16[4,8,32,256]{3,2,1,0:T(8,128)(2,1)S(1)}, bf16[4,8,32,256]{3,2,1,0:T(8,128)(2,1)S(1)}, u32[]{:S(2)}, u32[]{:S(2)}) collective-permute-start(bf16[4,8,32,256]{3,2,1,0:T(8,128)(2,1)S(1)} %fusion.21), channel_id=1, source_target_pairs={{0,1},{1,2},{2,3},{3,0},{4,5},{5,6},{6,7},{7,4},{8,9},{9,10},{10,1... | collective-permute-start | bytes 1572872 | tf_op jit(solution)/shard_map/ppermute | solution.py:441
  18.7 78.6 %collective-permute-start.1 = (bf16[4,8,32,256]{3,2,1,0:T(8,128)(2,1)S(1)}, bf16[4,8,32,256]{3,2,1,0:T(8,128)(2,1)S(1)}, u32[]{:S(2)}, u32[]{:S(2)}) collective-permute-start(bf16[4,8,32,256]{3,2,1,0:T(8,128)(2,1)S(1)} %fusion.21), channel_id=1, source_target_pairs={{0,2},{1,3},{2,0},{3,1},{4,6},{5,7},{6,4},{7,5},{8,10},{9,11},{10,... | collective-permute-start | bytes 1572872 | tf_op jit(solution)/shard_map/ppermute | solution.py:441
  21.3 76.0 %collective-permute-start.2 = (bf16[4,8,32,256]{3,2,1,0:T(8,128)(2,1)S(1)}, bf16[4,8,32,256]{3,2,1,0:T(8,128)(2,1)S(1)}, u32[]{:S(2)}, u32[]{:S(2)}) collective-permute-start(bf16[4,8,32,256]{3,2,1,0:T(8,128)(2,1)S(1)} %fusion.21), channel_id=1, source_target_pairs={{0,3},{1,0},{2,1},{3,2},{4,7},{5,4},{6,5},{7,6},{8,11},{9,8},{10,9... | collective-permute-start | bytes 1572872 | tf_op jit(solution)/shard_map/ppermute | solution.py:441
  34.3 2.0 %copy-start.5 = (f32[32,4,8,256]{3,2,1,0:T(8,128)S(1)}, f32[32,4,8,256]{3,2,1,0:T(8,128)}, u32[]{:S(2)}) copy-start(f32[32,4,8,256]{3,2,1,0:T(8,128)} %get-tuple-element.10) | copy-start | bytes 3145732
  34.3 3.3 %copy-start.7 = (s32[256]{0:T(256)S(1)}, s32[256]{0:T(256)}, u32[]{:S(2)}) copy-start(s32[256]{0:T(256)} %param.19) | copy-start | bytes 3076
  39.0 30.1 %copy-start.6 = (f32[1024]{0:T(1024)S(1)}, f32[1024]{0:T(1024)}, u32[]{:S(2)}) copy-start(f32[1024]{0:T(1024)} %param.22) | copy-start | bytes 12292
  69.3 25.8 %copy-start.3 = (f32[32,32,128]{2,1,0:T(8,128)S(1)}, f32[32,32,128]{2,1,0:T(8,128)}, u32[]{:S(2)}) copy-start(f32[32,32,128]{2,1,0:T(8,128)} %shard_map.149) | copy-start | bytes 1572868
  72.1 24.0 %copy-start.9 = (f32[32,1024]{1,0:T(8,128)S(1)}, f32[32,1024]{1,0:T(8,128)}, u32[]{:S(2)}) copy-start(f32[32,1024]{1,0:T(8,128)} %param.23) | copy-start | bytes 393220
  72.2 24.0 %copy-start.10 = (f32[1024]{0:T(1024)S(1)}, f32[1024]{0:T(1024)}, u32[]{:S(2)}) copy-start(f32[1024]{0:T(1024)} %param.21) | copy-start | bytes 12292
  96.2 1.2 %copy-start.2 = (f32[32,4,8,256]{3,2,1,0:T(8,128)S(1)}, f32[32,4,8,256]{3,2,1,0:T(8,128)}, u32[]{:S(2)}) copy-start(f32[32,4,8,256]{3,2,1,0:T(8,128)} %lp_mid.1) | copy-start | bytes 3145732

commit v20 on v19

--- a/solution.py
+++ b/solution.py
@@ -281,7 +281,13 @@
     )(halo, log_perm, fields, inside)
 
 
-def halo_kernel(out_ref, in_ref, send_sem, recv_sem):
+def halo_kernel(rim, lp_ref, fields_ref, in_ref, out_ref, send_sem, recv_sem):
+    members, layers, rows, depth = lp_ref.shape
+    lp_count = members * layers
+    for side, first in ((0, 0), (1, rows - rim)):
+        for r in range(rim):
+            out_ref[side, r, 0:lp_count, :] = lp_ref[:, :, first + r, :].reshape(lp_count, depth)
+            out_ref[side, r, lp_count:, :] = fields_ref[:, :, first + r, :].reshape(-1, depth)
     tile_count = lax.axis_size("tile")
     me_t = lax.axis_index("tile")
     me_m = lax.axis_index("member")
@@ -306,16 +312,22 @@
     to_left.wait()
 
 
-def halo_exchange(outgoing):
+def halo_exchange(log_perm, fields, rim):
+    members, layers, rows, depth = log_perm.shape
+    halo_shape = (2, rim, (members + fields.shape[0]) * layers, depth)
     vmem = pl.BlockSpec(memory_space=pltpu.VMEM)
     return pl.pallas_call(
-        halo_kernel,
-        out_shape=jax.ShapeDtypeStruct(outgoing.shape, outgoing.dtype),
-        in_specs=[vmem],
+        functools.partial(halo_kernel, rim),
+        out_shape=jax.ShapeDtypeStruct(halo_shape, log_perm.dtype),
+        in_specs=[vmem, vmem],
         out_specs=vmem,
-        scratch_shapes=[pltpu.SemaphoreType.DMA((2,)), pltpu.SemaphoreType.DMA((2,))],
+        scratch_shapes=[
+            pltpu.VMEM(halo_shape, log_perm.dtype),
+            pltpu.SemaphoreType.DMA((2,)),
+            pltpu.SemaphoreType.DMA((2,)),
+        ],
         compiler_params=pltpu.CompilerParams(collective_id=1, has_side_effects=True),
-    )(outgoing)
+    )(log_perm, fields)
 
 
 def rates_exchange(pieces, member_count):
@@ -366,19 +378,9 @@
     fields = jnp.stack([start_pressure, start_sat, source, storage])
     halo_rows = local_count * layers * rim + fields.shape[0] * layers * rim
 
-    def rim_rows(first):
-        return jnp.concatenate(
-            [
-                lax.slice_in_dim(log_perm, first, first + rim, axis=2).transpose(2, 0, 1, 3),
-                lax.slice_in_dim(fields, first, first + rim, axis=2).transpose(2, 0, 1, 3),
-            ],
-            axis=1,
-        ).reshape(-1, strip_depth)
-
-    outgoing = jnp.stack([rim_rows(0), rim_rows(strip_width - rim)])
-    incoming = halo_exchange(outgoing)
+    incoming = halo_exchange(log_perm, fields, rim)
     incoming, log_perm_after = lax.optimization_barrier((incoming, log_perm))
-    halo = incoming.reshape(2, rim, -1, strip_depth)
+    halo = incoming
     column = tile_rank * strip_width - rim + jnp.arange(strip_width + 2 * rim, dtype=jnp.int32)
     inside = ((column >= 0) & (column < strip_width * tile_count)).astype(jnp.float32)
     pressure, saturation, mobility = stencil(halo, log_perm, fields, inside, rim)

time: 100 us -> 97.6 us (0.976)
  local copies, waits for them, and re-layouts: 6.28 us -> 3.9 us
    transpose x2 -> x0, local copies, waits for them, and re-layouts: 1.83 us -> none  [the longest x1 1.81 us: rim_rows(): lax.slice_in_dim(log_perm, first, first + rim, axis=2).transpose(2, 0, 1, 3)]
    unnamed x25 -> x23, local copies, waits for them, and re-layouts: 2.55 us -> 2.55 us
  transfers between devices with their start and end apart: 3 -> 3, of which waited for: 0 -> 0; matrix products, arithmetic and copies ran while one was open for 35% -> 36% of each run, Pallas kernels for 39% -> 40%
where the time goes in v20:
time: 97.6 us; the launch traced here: 97.2 us
  Pallas kernels  51.1 us (52%)
  other arithmetic  26.7 us (27%)
  matrix products  8.82 us (9%)
  starting transfers between devices  5.05 us (5%)
  local copies, waits for them, and re-layouts  3.9 us (4%)
  between operations  1.53 us (2%)
    pallas_call x1, Pallas kernels, rates_exchange(): pl.pallas_call(functools.partial(exchange_kernel, member_count), out_shap...  28 us
    another operation x3, other arithmetic, solve_spd(): lax.linalg.cholesky(gram_matrix + jnp.eye(gram_matrix.shape[0], dtype=jnp...  12.4 us
    pallas_call x1, Pallas kernels, halo_exchange(): pl.pallas_call(functools.partial(halo_kernel, rim), out_shape=jax.ShapeDt...  11.9 us
    pallas_call x1, Pallas kernels, stencil(): pl.pallas_call(functools.partial(stencil_kernel, rim), grid=(members // b...  11.3 us
    another operation x2, other arithmetic, solve_spd(): lax.linalg.triangular_solve(factor, halfway, left_side=True, lower=True,...  10.5 us
    ppermute x3, starting transfers between devices, per_device(): anomaly_parts.append(lax.ppermute(anomaly, 'member', pairs))  5.05 us
    dot_general x1, matrix products, per_device(): lax.dot_general(scaled_t, scaled_t, contract_wells, precision=lax.Precisi...  2.88 us
    dot_general x2, matrix products, pick_cells(): jnp.dot(values_in.reshape(local_count * plane_rows, strip_depth), col_pic...  2.61 us
  transfers between devices with their start and end apart: 3, of which 0 were waited for; matrix products, arithmetic and copies ran while one was open for 36% of the time, Pallas kernels for 40%

profile of v20, /device:TPU:1, one launch (start us, length us, event | category | flops | bytes accessed | tf_op | source)
XLA Modules:
  0.0 97.2 jit_solution(8602012554343105671)
XLA Ops:
  0.6 1.5 %pad_maximum_fusion.fields_ref.f_mid = f32[4,4,8,256]{3,2,1,0:T(8,128)} fusion(f32[1,4,8,256]{3,2,1,0:T(8,128)} %bitcast.50, f32[1,4,8,256]{3,2,1,0:T(8,128)} %bitcast.51, f32[1,4,8,256]{3,2,1,0:T(8,128)} %bitcast.52, f32[1,4,8,256]{3,2,1,0:T(8,128)} %bitcast.53), kind=kLoop, calls=%fused_computation.37 | loop fusion | flops 98304 | bytes 262144 | tf_op jit(solution)/shard_map/stack | solution.py:378
  2.1 11.9 %shard_map.147.halo_ref = f32[2,3,144,256]{3,2,1,0:T(8,128)} custom-call(f32[32,4,8,256]{3,2,1,0:T(8,128)} %lp_mid.1, f32[4,4,8,256]{3,2,1,0:T(8,128)} %pad_maximum_fusion.fields_ref.f_mid), custom_call_target="tpu_custom_call" | custom-call | tf_op jit(solution)/shard_map/pallas_call | solution.py:319
  14.0 0.6 fusion.21
  14.6 1.4 %collective-permute-start = (bf16[4,8,32,256]{3,2,1,0:T(8,128)(2,1)S(1)}, bf16[4,8,32,256]{3,2,1,0:T(8,128)(2,1)S(1)}, u32[]{:S(2)}, u32[]{:S(2)}) collective-permute-start(bf16[4,8,32,256]{3,2,1,0:T(8,128)(2,1)S(1)} %fusion.21), channel_id=1, source_target_pairs={{0,1},{1,2},{2,3},{3,0},{4,5},{5,6},{6,7},{7,4},{8,9},{9,10},{10,1... | collective-permute-start | bytes 1572872 | tf_op jit(solution)/shard_map/ppermute | solution.py:443
  16.0 2.6 %collective-permute-start.1 = (bf16[4,8,32,256]{3,2,1,0:T(8,128)(2,1)S(1)}, bf16[4,8,32,256]{3,2,1,0:T(8,128)(2,1)S(1)}, u32[]{:S(2)}, u32[]{:S(2)}) collective-permute-start(bf16[4,8,32,256]{3,2,1,0:T(8,128)(2,1)S(1)} %fusion.21), channel_id=1, source_target_pairs={{0,2},{1,3},{2,0},{3,1},{4,6},{5,7},{6,4},{7,5},{8,10},{9,11},{10,... | collective-permute-start | bytes 1572872 | tf_op jit(solution)/shard_map/ppermute | solution.py:443
  18.6 1.1 %collective-permute-start.2 = (bf16[4,8,32,256]{3,2,1,0:T(8,128)(2,1)S(1)}, bf16[4,8,32,256]{3,2,1,0:T(8,128)(2,1)S(1)}, u32[]{:S(2)}, u32[]{:S(2)}) collective-permute-start(bf16[4,8,32,256]{3,2,1,0:T(8,128)(2,1)S(1)} %fusion.21), channel_id=1, source_target_pairs={{0,3},{1,0},{2,1},{3,2},{4,7},{5,4},{6,5},{7,6},{8,11},{9,8},{10,9... | collective-permute-start | bytes 1572872 | tf_op jit(solution)/shard_map/ppermute | solution.py:443
  19.7 0.5 and_convert_fusion.inside_ref
  20.2 11.3 %shard_map.148 = (f32[32,4,8,256]{3,2,1,0:T(8,128)}, f32[32,4,8,256]{3,2,1,0:T(8,128)}, f32[32,4,8,256]{3,2,1,0:T(8,128)}) custom-call(f32[2,3,144,256]{3,2,1,0:T(8,128)} %shard_map.147.halo_ref, f32[32,4,8,256]{3,2,1,0:T(8,128)} %lp_mid.1, f32[4,4,8,256]{3,2,1,0:T(8,128)} %pad_maximum_fusion.fields_ref.f_mid, f32[14]{0:T(128)} %and_convert_fusion.inside_ref), custom_call_target="tpu_custom_call" | custom-call | tf_op jit(solution)/shard_map/pallas_call | solution.py:270
  31.6 2.0 %fusion.12 = f32[32,256]{1,0:T(8,128)S(1)} fusion(f32[32,4,8,256]{3,2,1,0:T(8,128)} %get-tuple-element.23, pred[32,256]{1,0:T(8,128)(4,1)S(1)} %iota_compare_fusion.5, s32[256]{0:T(256)S(1)} %get-tuple-element.32), kind=kOutput, calls=%fused_computation.12 | convolution fusion | flops 805888000 | bytes 1090560 | tf_op jit(solution)/shard_map/dot_general | solution.py:397
  33.5 0.7 fusion.11
  34.9 0.6 fusion.18
  35.5 0.8 fusion.19
  36.3 0.8 reshape.95.part_ref
  37.1 28.0 %shard_map.149 = f32[32,32,128]{2,1,0:T(8,128)} custom-call(f32[32,8,128]{2,1,0:T(8,128)} %reshape.95.part_ref), custom_call_target="tpu_custom_call" | custom-call | tf_op jit(solution)/shard_map/pallas_call | solution.py:336
  65.1 1.2 %reduce_sum.29 = f32[32,32]{1,0:T(8,128)S(1)} reduce(f32[32,32,128]{2,1,0:T(8,128)} %shard_map.149, f32[]{:T(128)} %constant.107.clone.1), dimensions={2}, to_apply=%region_2.3 | reduce | flops 130048 | bytes 528388 | tf_op jit(solution)/shard_map/reduce_sum | solution.py:425
  66.5 2.9 %fusion.13 = f32[128,128]{1,0:T(8,128)S(1)} fusion(f32[32,32,128]{2,1,0:T(8,128)} %shard_map.149, f32[32,32]{1,0:T(8,128)S(1)} %div.56, f32[32,32]{1,0:T(8,128)S(1)} %broadcast_multiply_fusion), kind=kOutput, calls=%fused_computation.14 | convolution fusion | flops 201637888 | bytes 598016 | tf_op jit(solution)/shard_map/dot_general | solution.py:430
  69.4 11.7 %cholesky.17 = f32[128,128]{1,0:T(8,128)S(1)} custom-call(f32[128,128]{1,0:T(8,128)S(1)} %fusion.13), custom_call_target="Cholesky" | custom-call | tf_op jit(solution)/shard_map/cholesky | solution.py:101
  81.2 0.6 compare_reduce_fusion
  81.8 0.7 fusion.38
  82.5 9.8 %custom-call.7 = f32[1,128,128]{1,2,0:T(8,128)S(1)} custom-call(f32[1,128,128]{2,1,0:T(8,128)S(1)} %fusion.38), custom_call_target="InvertDiagBlocksLowerTriangular" | custom-call | tf_op jit(solution)/shard_map/triangular_solve | solution.py:105
  92.8 0.7 copy.32
  93.5 0.6 fusion.26
  94.7 0.9 fusion.8
  95.6 1.6 %copy.31 = f32[32,4,8,256]{3,2,1,0:T(8,128)} copy(f32[32,4,8,256]{3,0,2,1:T(8,128)S(1)} %fusion.8) | data formatting | bytes 2097152
  (37 shorter events, 1.3 us)
Async XLA Ops:
  0.6 34.2 %copy-start = (f32[1024]{0:T(1024)S(1)}, f32[1024]{0:T(1024)}, u32[]{:S(2)}) copy-start(f32[1024]{0:T(1024)} %param.17) | copy-start | bytes 12292
  2.1 11.9 %copy-start.1 = (f32[32,4,8,256]{3,2,1,0:T(8,128)S(1)}, f32[32,4,8,256]{3,2,1,0:T(8,128)}, u32[]{:S(2)}) copy-start(f32[32,4,8,256]{3,2,1,0:T(8,128)} %lp_mid.1) | copy-start | bytes 3145732
  14.0 6.2 %copy-start.7 = (s32[256]{0:T(256)S(1)}, s32[256]{0:T(256)}, u32[]{:S(2)}) copy-start(s32[256]{0:T(256)} %param.18) | copy-start | bytes 3076
  14.6 80.0 %collective-permute-start = (bf16[4,8,32,256]{3,2,1,0:T(8,128)(2,1)S(1)}, bf16[4,8,32,256]{3,2,1,0:T(8,128)(2,1)S(1)}, u32[]{:S(2)}, u32[]{:S(2)}) collective-permute-start(bf16[4,8,32,256]{3,2,1,0:T(8,128)(2,1)S(1)} %fusion.21), channel_id=1, source_target_pairs={{0,1},{1,2},{2,3},{3,0},{4,5},{5,6},{6,7},{7,4},{8,9},{9,10},{10,1... | collective-permute-start | bytes 1572872 | tf_op jit(solution)/shard_map/ppermute | solution.py:443
  16.0 78.6 %collective-permute-start.1 = (bf16[4,8,32,256]{3,2,1,0:T(8,128)(2,1)S(1)}, bf16[4,8,32,256]{3,2,1,0:T(8,128)(2,1)S(1)}, u32[]{:S(2)}, u32[]{:S(2)}) collective-permute-start(bf16[4,8,32,256]{3,2,1,0:T(8,128)(2,1)S(1)} %fusion.21), channel_id=1, source_target_pairs={{0,2},{1,3},{2,0},{3,1},{4,6},{5,7},{6,4},{7,5},{8,10},{9,11},{10,... | collective-permute-start | bytes 1572872 | tf_op jit(solution)/shard_map/ppermute | solution.py:443
  18.6 76.0 %collective-permute-start.2 = (bf16[4,8,32,256]{3,2,1,0:T(8,128)(2,1)S(1)}, bf16[4,8,32,256]{3,2,1,0:T(8,128)(2,1)S(1)}, u32[]{:S(2)}, u32[]{:S(2)}) collective-permute-start(bf16[4,8,32,256]{3,2,1,0:T(8,128)(2,1)S(1)} %fusion.21), channel_id=1, source_target_pairs={{0,3},{1,0},{2,1},{3,2},{4,7},{5,4},{6,5},{7,6},{8,11},{9,8},{10,9... | collective-permute-start | bytes 1572872 | tf_op jit(solution)/shard_map/ppermute | solution.py:443
  31.5 2.0 %copy-start.4 = (f32[32,4,8,256]{3,2,1,0:T(8,128)S(1)}, f32[32,4,8,256]{3,2,1,0:T(8,128)}, u32[]{:S(2)}) copy-start(f32[32,4,8,256]{3,2,1,0:T(8,128)} %get-tuple-element.10) | copy-start | bytes 3145732
  31.5 3.3 %copy-start.6 = (s32[256]{0:T(256)S(1)}, s32[256]{0:T(256)}, u32[]{:S(2)}) copy-start(s32[256]{0:T(256)} %param.19) | copy-start | bytes 3076
  36.3 30.1 %copy-start.5 = (f32[1024]{0:T(1024)S(1)}, f32[1024]{0:T(1024)}, u32[]{:S(2)}) copy-start(f32[1024]{0:T(1024)} %param.22) | copy-start | bytes 12292
  66.5 25.8 %copy-start.3 = (f32[32,32,128]{2,1,0:T(8,128)S(1)}, f32[32,32,128]{2,1,0:T(8,128)}, u32[]{:S(2)}) copy-start(f32[32,32,128]{2,1,0:T(8,128)} %shard_map.149) | copy-start | bytes 1572868
  69.4 24.0 %copy-start.8 = (f32[32,1024]{1,0:T(8,128)S(1)}, f32[32,1024]{1,0:T(8,128)}, u32[]{:S(2)}) copy-start(f32[32,1024]{1,0:T(8,128)} %param.23) | copy-start | bytes 393220
  69.4 24.0 %copy-start.9 = (f32[1024]{0:T(1024)S(1)}, f32[1024]{0:T(1024)}, u32[]{:S(2)}) copy-start(f32[1024]{0:T(1024)} %param.21) | copy-start | bytes 12292
  93.5 1.2 %copy-start.2 = (f32[32,4,8,256]{3,2,1,0:T(8,128)S(1)}, f32[32,4,8,256]{3,2,1,0:T(8,128)}, u32[]{:S(2)}) copy-start(f32[32,4,8,256]{3,2,1,0:T(8,128)} %lp_mid.1) | copy-start | bytes 3145732

commit v21 on v20

--- a/solution.py
+++ b/solution.py
@@ -223,10 +223,11 @@
     lax.fori_loop(1, tile_count, wait_t_send, 0)
 
 
-def stencil_kernel(rim, halo_ref, lp_mid, f_mid, inside_ref, press_ref, sat_ref, mob_ref):
+def stencil_kernel(rim, halo_ref, lp_mid, f0, f1, f2, f3, inside_ref, press_ref, sat_ref, mob_ref):
+    f_mid = jnp.stack([f0[...], f1[...], f2[...], f3[...]])
     inside = inside_ref[...]
     block, layers = lp_mid.shape[0], lp_mid.shape[1]
-    field_count = f_mid.shape[0]
+    field_count = 4
     lp_rows = pl.ds(pl.multiple_of(pl.program_id(0) * block * layers, block * layers), block * layers)
     field_first = halo_ref.shape[2] - field_count * layers
 
@@ -241,7 +242,7 @@
     ))
     face_sets = face_terms(permeab, inside)
     fields = jnp.concatenate(
-        halo_piece(0, f_rows, f_shape) + [f_mid[...]] + halo_piece(1, f_rows, f_shape), axis=2
+        halo_piece(0, f_rows, f_shape) + [f_mid] + halo_piece(1, f_rows, f_shape), axis=2
     )
     press_ext = fields[0]
     sat_ext = fields[1]
@@ -273,21 +274,23 @@
         in_specs=[
             whole(halo),
             pl.BlockSpec((block, layers, out_rows, depth), lambda i: (i, 0, 0, 0)),
-            whole(fields),
+            *[whole(f) for f in fields],
             whole(inside),
         ],
         out_specs=[out_spec, out_spec, out_spec],
         out_shape=[out_shape, out_shape, out_shape],
-    )(halo, log_perm, fields, inside)
-
-
-def halo_kernel(rim, lp_ref, fields_ref, in_ref, out_ref, send_sem, recv_sem):
+    )(halo, log_perm, *fields, inside)
+
+
+def halo_kernel(rim, lp_ref, f0, f1, f2, f3, in_ref, out_ref, send_sem, recv_sem):
     members, layers, rows, depth = lp_ref.shape
     lp_count = members * layers
     for side, first in ((0, 0), (1, rows - rim)):
         for r in range(rim):
             out_ref[side, r, 0:lp_count, :] = lp_ref[:, :, first + r, :].reshape(lp_count, depth)
-            out_ref[side, r, lp_count:, :] = fields_ref[:, :, first + r, :].reshape(-1, depth)
+            for fi, f_ref in enumerate((f0, f1, f2, f3)):
+                at = lp_count + fi * layers
+                out_ref[side, r, at:at + layers, :] = f_ref[:, first + r, :]
     tile_count = lax.axis_size("tile")
     me_t = lax.axis_index("tile")
     me_m = lax.axis_index("member")
@@ -314,12 +317,12 @@
 
 def halo_exchange(log_perm, fields, rim):
     members, layers, rows, depth = log_perm.shape
-    halo_shape = (2, rim, (members + fields.shape[0]) * layers, depth)
+    halo_shape = (2, rim, (members + len(fields)) * layers, depth)
     vmem = pl.BlockSpec(memory_space=pltpu.VMEM)
     return pl.pallas_call(
         functools.partial(halo_kernel, rim),
         out_shape=jax.ShapeDtypeStruct(halo_shape, log_perm.dtype),
-        in_specs=[vmem, vmem],
+        in_specs=[vmem] * (1 + len(fields)),
         out_specs=vmem,
         scratch_shapes=[
             pltpu.VMEM(halo_shape, log_perm.dtype),
@@ -327,7 +330,7 @@
             pltpu.SemaphoreType.DMA((2,)),
         ],
         compiler_params=pltpu.CompilerParams(collective_id=1, has_side_effects=True),
-    )(log_perm, fields)
+    )(log_perm, *fields)
 
 
 def rates_exchange(pieces, member_count):
@@ -375,8 +378,7 @@
     tile_rank = lax.axis_index("tile")
     member_rank = lax.axis_index("member")
     rim = SWEEPS + 1
-    fields = jnp.stack([start_pressure, start_sat, source, storage])
-    halo_rows = local_count * layers * rim + fields.shape[0] * layers * rim
+    fields = (start_pressure, start_sat, source, storage)
 
     incoming = halo_exchange(log_perm, fields, rim)
     incoming, log_perm_after = lax.optimization_barrier((incoming, log_perm))

time: 97.6 us -> 96.2 us (0.986)
  other arithmetic: 26.7 us -> 25.3 us
    another operation x1 -> x0, other arithmetic: 1.48 us -> none  [per_device(): fields = jnp.stack([start_pressure, start_sat, source, storage])]
  transfers between devices with their start and end apart: 3 -> 3, of which waited for: 0 -> 0; matrix products, arithmetic and copies ran while one was open for 36% -> 36% of each run, Pallas kernels for 40% -> 41%
where the time goes in v21:
time: 96.2 us; the launch traced here: 95.8 us
  Pallas kernels  51.2 us (53%)
  other arithmetic  25.3 us (26%)
  matrix products  8.82 us (9%)
  starting transfers between devices  5.05 us (5%)
  local copies, waits for them, and re-layouts  3.91 us (4%)
  between operations  1.54 us (2%)
    pallas_call x1, Pallas kernels, rates_exchange(): pl.pallas_call(functools.partial(exchange_kernel, member_count), out_shap...  28 us
    another operation x3, other arithmetic, solve_spd(): lax.linalg.cholesky(gram_matrix + jnp.eye(gram_matrix.shape[0], dtype=jnp...  12.4 us
    pallas_call x1, Pallas kernels, halo_exchange(): pl.pallas_call(functools.partial(halo_kernel, rim), out_shape=jax.ShapeDt...  12 us
    pallas_call x1, Pallas kernels, stencil(): pl.pallas_call(functools.partial(stencil_kernel, rim), grid=(members // b...  11.3 us
    another operation x2, other arithmetic, solve_spd(): lax.linalg.triangular_solve(factor, halfway, left_side=True, lower=True,...  10.5 us
    ppermute x3, starting transfers between devices, per_device(): anomaly_parts.append(lax.ppermute(anomaly, 'member', pairs))  5.05 us
    dot_general x1, matrix products, per_device(): lax.dot_general(scaled_t, scaled_t, contract_wells, precision=lax.Precisi...  2.88 us
    dot_general x2, matrix products, pick_cells(): jnp.dot(values_in.reshape(local_count * plane_rows, strip_depth), col_pic...  2.61 us
  transfers between devices with their start and end apart: 3, of which 0 were waited for; matrix products, arithmetic and copies ran while one was open for 36% of the time, Pallas kernels for 41%

profile of v21, /device:TPU:1, one launch (start us, length us, event | category | flops | bytes accessed | tf_op | source)
XLA Modules:
  0.0 95.8 jit_solution(10187238333938844256)
XLA Ops:
  0.7 12.0 %shard_map.147.halo_ref = f32[2,3,144,256]{3,2,1,0:T(8,128)} custom-call(f32[32,4,8,256]{3,2,1,0:T(8,128)} %lp_mid.1, f32[4,8,256]{2,1,0:T(8,128)} %f0.3, f32[4,8,256]{2,1,0:T(8,128)} %f1.3, f32[4,8,256]{2,1,0:T(8,128)} %f2.3, f32[4,8,256]{2,1,0:T(8,128)} %f3.3), custom_call_target="tpu_custom_call" | custom-call | tf_op jit(solution)/shard_map/pallas_call | solution.py:322
  12.7 0.6 fusion.21
  13.3 1.4 %collective-permute-start = (bf16[4,8,32,256]{3,2,1,0:T(8,128)(2,1)S(1)}, bf16[4,8,32,256]{3,2,1,0:T(8,128)(2,1)S(1)}, u32[]{:S(2)}, u32[]{:S(2)}) collective-permute-start(bf16[4,8,32,256]{3,2,1,0:T(8,128)(2,1)S(1)} %fusion.21), channel_id=1, source_target_pairs={{0,1},{1,2},{2,3},{3,0},{4,5},{5,6},{6,7},{7,4},{8,9},{9,10},{10,1... | collective-permute-start | bytes 1572872 | tf_op jit(solution)/shard_map/ppermute | solution.py:445
  14.6 2.6 %collective-permute-start.1 = (bf16[4,8,32,256]{3,2,1,0:T(8,128)(2,1)S(1)}, bf16[4,8,32,256]{3,2,1,0:T(8,128)(2,1)S(1)}, u32[]{:S(2)}, u32[]{:S(2)}) collective-permute-start(bf16[4,8,32,256]{3,2,1,0:T(8,128)(2,1)S(1)} %fusion.21), channel_id=1, source_target_pairs={{0,2},{1,3},{2,0},{3,1},{4,6},{5,7},{6,4},{7,5},{8,10},{9,11},{10,... | collective-permute-start | bytes 1572872 | tf_op jit(solution)/shard_map/ppermute | solution.py:445
  17.3 1.1 %collective-permute-start.2 = (bf16[4,8,32,256]{3,2,1,0:T(8,128)(2,1)S(1)}, bf16[4,8,32,256]{3,2,1,0:T(8,128)(2,1)S(1)}, u32[]{:S(2)}, u32[]{:S(2)}) collective-permute-start(bf16[4,8,32,256]{3,2,1,0:T(8,128)(2,1)S(1)} %fusion.21), channel_id=1, source_target_pairs={{0,3},{1,0},{2,1},{3,2},{4,7},{5,4},{6,5},{7,6},{8,11},{9,8},{10,9... | collective-permute-start | bytes 1572872 | tf_op jit(solution)/shard_map/ppermute | solution.py:445
  18.3 0.5 and_convert_fusion.inside_ref
  18.9 11.3 %shard_map.148 = (f32[32,4,8,256]{3,2,1,0:T(8,128)}, f32[32,4,8,256]{3,2,1,0:T(8,128)}, f32[32,4,8,256]{3,2,1,0:T(8,128)}) custom-call(f32[2,3,144,256]{3,2,1,0:T(8,128)} %shard_map.147.halo_ref, f32[32,4,8,256]{3,2,1,0:T(8,128)} %lp_mid.1, f32[4,8,256]{2,1,0:T(8,128)} %f0.3, f32[4,8,256]{2,1,0:T(8,128)} %f1.3, f32[4,8,256]{2,1,0:T(8,128)} %f2.3, ...), custom_call_target="tpu_custom_call" | custom-call | tf_op jit(solution)/shard_map/pallas_call | solution.py:271
  30.2 2.0 %fusion.12 = f32[32,256]{1,0:T(8,128)S(1)} fusion(f32[32,4,8,256]{3,2,1,0:T(8,128)} %get-tuple-element.23, pred[32,256]{1,0:T(8,128)(4,1)S(1)} %iota_compare_fusion.5, s32[256]{0:T(256)S(1)} %get-tuple-element.32), kind=kOutput, calls=%fused_computation.12 | convolution fusion | flops 805888000 | bytes 1090560 | tf_op jit(solution)/shard_map/dot_general | solution.py:399
  32.2 0.7 fusion.11
  33.5 0.6 fusion.18
  34.1 0.8 fusion.19
  34.9 0.8 reshape.95.part_ref
  35.8 28.0 %shard_map.149 = f32[32,32,128]{2,1,0:T(8,128)} custom-call(f32[32,8,128]{2,1,0:T(8,128)} %reshape.95.part_ref), custom_call_target="tpu_custom_call" | custom-call | tf_op jit(solution)/shard_map/pallas_call | solution.py:339
  63.7 1.2 %reduce_sum.29 = f32[32,32]{1,0:T(8,128)S(1)} reduce(f32[32,32,128]{2,1,0:T(8,128)} %shard_map.149, f32[]{:T(128)} %constant.107.clone.1), dimensions={2}, to_apply=%region_2.3 | reduce | flops 130048 | bytes 528388 | tf_op jit(solution)/shard_map/reduce_sum | solution.py:427
  65.2 2.9 %fusion.13 = f32[128,128]{1,0:T(8,128)S(1)} fusion(f32[32,32,128]{2,1,0:T(8,128)} %shard_map.149, f32[32,32]{1,0:T(8,128)S(1)} %div.56, f32[32,32]{1,0:T(8,128)S(1)} %broadcast_multiply_fusion), kind=kOutput, calls=%fused_computation.14 | convolution fusion | flops 201637888 | bytes 598016 | tf_op jit(solution)/shard_map/dot_general | solution.py:432
  68.1 11.7 %cholesky.17 = f32[128,128]{1,0:T(8,128)S(1)} custom-call(f32[128,128]{1,0:T(8,128)S(1)} %fusion.13), custom_call_target="Cholesky" | custom-call | tf_op jit(solution)/shard_map/cholesky | solution.py:101
  79.8 0.6 compare_reduce_fusion
  80.5 0.7 fusion.38
  81.1 9.8 %custom-call.7 = f32[1,128,128]{1,2,0:T(8,128)S(1)} custom-call(f32[1,128,128]{2,1,0:T(8,128)S(1)} %fusion.38), custom_call_target="InvertDiagBlocksLowerTriangular" | custom-call | tf_op jit(solution)/shard_map/triangular_solve | solution.py:105
  91.0 0.2 constant_dynamic-slice_fusion.4
  91.4 0.7 copy.32
  92.1 0.6 fusion.26
  93.3 0.9 fusion.8
  94.3 1.6 %copy.31 = f32[32,4,8,256]{3,2,1,0:T(8,128)} copy(f32[32,4,8,256]{3,0,2,1:T(8,128)S(1)} %fusion.8) | data formatting | bytes 2097152
  (36 shorter events, 1.1 us)
Async XLA Ops:
  0.6 32.9 %copy-start = (f32[1024]{0:T(1024)S(1)}, f32[1024]{0:T(1024)}, u32[]{:S(2)}) copy-start(f32[1024]{0:T(1024)} %param.17) | copy-start | bytes 12292
  0.6 12.0 %copy-start.1 = (f32[32,4,8,256]{3,2,1,0:T(8,128)S(1)}, f32[32,4,8,256]{3,2,1,0:T(8,128)}, u32[]{:S(2)}) copy-start(f32[32,4,8,256]{3,2,1,0:T(8,128)} %lp_mid.1) | copy-start | bytes 3145732
  12.6 6.2 %copy-start.7 = (s32[256]{0:T(256)S(1)}, s32[256]{0:T(256)}, u32[]{:S(2)}) copy-start(s32[256]{0:T(256)} %param.18) | copy-start | bytes 3076
  13.3 80.0 %collective-permute-start = (bf16[4,8,32,256]{3,2,1,0:T(8,128)(2,1)S(1)}, bf16[4,8,32,256]{3,2,1,0:T(8,128)(2,1)S(1)}, u32[]{:S(2)}, u32[]{:S(2)}) collective-permute-start(bf16[4,8,32,256]{3,2,1,0:T(8,128)(2,1)S(1)} %fusion.21), channel_id=1, source_target_pairs={{0,1},{1,2},{2,3},{3,0},{4,5},{5,6},{6,7},{7,4},{8,9},{9,10},{10,1... | collective-permute-start | bytes 1572872 | tf_op jit(solution)/shard_map/ppermute | solution.py:445
  14.6 78.6 %collective-permute-start.1 = (bf16[4,8,32,256]{3,2,1,0:T(8,128)(2,1)S(1)}, bf16[4,8,32,256]{3,2,1,0:T(8,128)(2,1)S(1)}, u32[]{:S(2)}, u32[]{:S(2)}) collective-permute-start(bf16[4,8,32,256]{3,2,1,0:T(8,128)(2,1)S(1)} %fusion.21), channel_id=1, source_target_pairs={{0,2},{1,3},{2,0},{3,1},{4,6},{5,7},{6,4},{7,5},{8,10},{9,11},{10,... | collective-permute-start | bytes 1572872 | tf_op jit(solution)/shard_map/ppermute | solution.py:445
  17.3 76.0 %collective-permute-start.2 = (bf16[4,8,32,256]{3,2,1,0:T(8,128)(2,1)S(1)}, bf16[4,8,32,256]{3,2,1,0:T(8,128)(2,1)S(1)}, u32[]{:S(2)}, u32[]{:S(2)}) collective-permute-start(bf16[4,8,32,256]{3,2,1,0:T(8,128)(2,1)S(1)} %fusion.21), channel_id=1, source_target_pairs={{0,3},{1,0},{2,1},{3,2},{4,7},{5,4},{6,5},{7,6},{8,11},{9,8},{10,9... | collective-permute-start | bytes 1572872 | tf_op jit(solution)/shard_map/ppermute | solution.py:445
  30.2 2.0 %copy-start.4 = (f32[32,4,8,256]{3,2,1,0:T(8,128)S(1)}, f32[32,4,8,256]{3,2,1,0:T(8,128)}, u32[]{:S(2)}) copy-start(f32[32,4,8,256]{3,2,1,0:T(8,128)} %get-tuple-element.10) | copy-start | bytes 3145732
  30.2 3.3 %copy-start.6 = (s32[256]{0:T(256)S(1)}, s32[256]{0:T(256)}, u32[]{:S(2)}) copy-start(s32[256]{0:T(256)} %param.19) | copy-start | bytes 3076
  34.9 30.1 %copy-start.5 = (f32[1024]{0:T(1024)S(1)}, f32[1024]{0:T(1024)}, u32[]{:S(2)}) copy-start(f32[1024]{0:T(1024)} %param.22) | copy-start | bytes 12292
  65.2 25.8 %copy-start.3 = (f32[32,32,128]{2,1,0:T(8,128)S(1)}, f32[32,32,128]{2,1,0:T(8,128)}, u32[]{:S(2)}) copy-start(f32[32,32,128]{2,1,0:T(8,128)} %shard_map.149) | copy-start | bytes 1572868
  68.1 24.0 %copy-start.8 = (f32[32,1024]{1,0:T(8,128)S(1)}, f32[32,1024]{1,0:T(8,128)}, u32[]{:S(2)}) copy-start(f32[32,1024]{1,0:T(8,128)} %param.23) | copy-start | bytes 393220
  68.1 24.0 %copy-start.9 = (f32[1024]{0:T(1024)S(1)}, f32[1024]{0:T(1024)}, u32[]{:S(2)}) copy-start(f32[1024]{0:T(1024)} %param.21) | copy-start | bytes 12292
  92.1 1.2 %copy-start.2 = (f32[32,4,8,256]{3,2,1,0:T(8,128)S(1)}, f32[32,4,8,256]{3,2,1,0:T(8,128)}, u32[]{:S(2)}) copy-start(f32[32,4,8,256]{3,2,1,0:T(8,128)} %lp_mid.1) | copy-start | bytes 3145732

commit v22 on v21

--- a/solution.py
+++ b/solution.py
@@ -223,9 +223,13 @@
     lax.fori_loop(1, tile_count, wait_t_send, 0)
 
 
-def stencil_kernel(rim, halo_ref, lp_mid, f0, f1, f2, f3, inside_ref, press_ref, sat_ref, mob_ref):
+def stencil_kernel(rim, halo_ref, lp_mid, f0, f1, f2, f3, press_ref, sat_ref, mob_ref):
     f_mid = jnp.stack([f0[...], f1[...], f2[...], f3[...]])
-    inside = inside_ref[...]
+    strip_width = lp_mid.shape[2]
+    column = lax.axis_index("tile") * strip_width - rim + jnp.arange(
+        strip_width + 2 * rim, dtype=jnp.int32
+    )
+    inside = ((column >= 0) & (column < strip_width * lax.axis_size("tile"))).astype(jnp.float32)
     block, layers = lp_mid.shape[0], lp_mid.shape[1]
     field_count = 4
     lp_rows = pl.ds(pl.multiple_of(pl.program_id(0) * block * layers, block * layers), block * layers)
@@ -259,7 +263,7 @@
     mob_ref[...] = trim_rim(permeab, rim) * water_frac(saturation)
 
 
-def stencil(halo, log_perm, fields, inside, rim):
+def stencil(halo, log_perm, fields, rim):
     members, layers, out_rows, depth = log_perm.shape
     block = 4
 
@@ -275,11 +279,10 @@
             whole(halo),
             pl.BlockSpec((block, layers, out_rows, depth), lambda i: (i, 0, 0, 0)),
             *[whole(f) for f in fields],
-            whole(inside),
         ],
         out_specs=[out_spec, out_spec, out_spec],
         out_shape=[out_shape, out_shape, out_shape],
-    )(halo, log_perm, *fields, inside)
+    )(halo, log_perm, *fields)
 
 
 def halo_kernel(rim, lp_ref, f0, f1, f2, f3, in_ref, out_ref, send_sem, recv_sem):
@@ -385,7 +388,7 @@
     halo = incoming
     column = tile_rank * strip_width - rim + jnp.arange(strip_width + 2 * rim, dtype=jnp.int32)
     inside = ((column >= 0) & (column < strip_width * tile_count)).astype(jnp.float32)
-    pressure, saturation, mobility = stencil(halo, log_perm, fields, inside, rim)
+    pressure, saturation, mobility = stencil(halo, log_perm, fields, rim)
     cell_count = layers * strip_width * strip_depth
     plane_rows = layers * strip_width
     cell_row = perf_cell // strip_depth

time: 96.2 us -> 94.4 us (0.981)
  other arithmetic: 25.3 us -> 23.7 us
  matrix products: 8.82 us -> 7.58 us
  local copies, waits for them, and re-layouts: 3.91 us -> 4.99 us
    dot_general x1, matrix products: 2.88 us -> 1.64 us  [per_device(): lax.dot_general(scaled_t, scaled_t, contract_wells, precision=lax.Precisi...]
    dynamic_slice x1, local copies, waits for them, and re-layouts: 0.2 us -> 1.3 us  [per_device(): lax.dynamic_slice_in_dim(rates_t, member_rank * local_count, local_count, 1)]
    reduce_sum x1, other arithmetic: 1.25 us -> 0.22 us  [per_device(): mean_rate = jnp.sum(rates_t, 1) / members]
  transfers between devices with their start and end apart: 3 -> 3, of which waited for: 0 -> 0; matrix products, arithmetic and copies ran while one was open for 36% -> 35% of each run, Pallas kernels for 41% -> 42%
where the time goes in v22:
time: 94.4 us; the launch traced here: 94.1 us
  Pallas kernels  51.2 us (54%)
  other arithmetic  23.7 us (25%)
  matrix products  7.58 us (8%)
  starting transfers between devices  5.05 us (5%)
  local copies, waits for them, and re-layouts  4.99 us (5%)
  between operations  1.53 us (2%)
    pallas_call x1, Pallas kernels, rates_exchange(): pl.pallas_call(functools.partial(exchange_kernel, member_count), out_shap...  28 us
    another operation x3, other arithmetic, solve_spd(): lax.linalg.cholesky(gram_matrix + jnp.eye(gram_matrix.shape[0], dtype=jnp...  12.4 us
    pallas_call x1, Pallas kernels, halo_exchange(): pl.pallas_call(functools.partial(halo_kernel, rim), out_shape=jax.ShapeDt...  12 us
    pallas_call x1, Pallas kernels, stencil(): pl.pallas_call(functools.partial(stencil_kernel, rim), grid=(members // b...  11.3 us
    another operation x2, other arithmetic, solve_spd(): lax.linalg.triangular_solve(factor, halfway, left_side=True, lower=True,...  10.5 us
    ppermute x3, starting transfers between devices, per_device(): anomaly_parts.append(lax.ppermute(anomaly, 'member', pairs))  5.05 us
    dot_general x2, matrix products, pick_cells(): jnp.dot(values_in.reshape(local_count * plane_rows, strip_depth), col_pic...  2.6 us
    unnamed x23, local copies, waits for them, and re-layouts  2.54 us
  transfers between devices with their start and end apart: 3, of which 0 were waited for; matrix products, arithmetic and copies ran while one was open for 35% of the time, Pallas kernels for 42%

profile of v22, /device:TPU:1, one launch (start us, length us, event | category | flops | bytes accessed | tf_op | source)
XLA Modules:
  0.0 94.1 jit_solution(1290174810955212509)
XLA Ops:
  0.7 12.0 %shard_map.147.halo_ref = f32[2,3,144,256]{3,2,1,0:T(8,128)} custom-call(f32[32,4,8,256]{3,2,1,0:T(8,128)} %lp_mid.1, f32[4,8,256]{2,1,0:T(8,128)} %f0.3, f32[4,8,256]{2,1,0:T(8,128)} %f1.3, f32[4,8,256]{2,1,0:T(8,128)} %f2.3, f32[4,8,256]{2,1,0:T(8,128)} %f3.3), custom_call_target="tpu_custom_call" | custom-call | tf_op jit(solution)/shard_map/pallas_call | solution.py:325
  12.6 0.6 fusion.21
  13.3 1.4 %collective-permute-start = (bf16[4,8,32,256]{3,2,1,0:T(8,128)(2,1)S(1)}, bf16[4,8,32,256]{3,2,1,0:T(8,128)(2,1)S(1)}, u32[]{:S(2)}, u32[]{:S(2)}) collective-permute-start(bf16[4,8,32,256]{3,2,1,0:T(8,128)(2,1)S(1)} %fusion.21), channel_id=1, source_target_pairs={{0,1},{1,2},{2,3},{3,0},{4,5},{5,6},{6,7},{7,4},{8,9},{9,10},{10,1... | collective-permute-start | bytes 1572872 | tf_op jit(solution)/shard_map/ppermute | solution.py:448
  14.6 2.6 %collective-permute-start.1 = (bf16[4,8,32,256]{3,2,1,0:T(8,128)(2,1)S(1)}, bf16[4,8,32,256]{3,2,1,0:T(8,128)(2,1)S(1)}, u32[]{:S(2)}, u32[]{:S(2)}) collective-permute-start(bf16[4,8,32,256]{3,2,1,0:T(8,128)(2,1)S(1)} %fusion.21), channel_id=1, source_target_pairs={{0,2},{1,3},{2,0},{3,1},{4,6},{5,7},{6,4},{7,5},{8,10},{9,11},{10,... | collective-permute-start | bytes 1572872 | tf_op jit(solution)/shard_map/ppermute | solution.py:448
  17.2 1.1 %collective-permute-start.2 = (bf16[4,8,32,256]{3,2,1,0:T(8,128)(2,1)S(1)}, bf16[4,8,32,256]{3,2,1,0:T(8,128)(2,1)S(1)}, u32[]{:S(2)}, u32[]{:S(2)}) collective-permute-start(bf16[4,8,32,256]{3,2,1,0:T(8,128)(2,1)S(1)} %fusion.21), channel_id=1, source_target_pairs={{0,3},{1,0},{2,1},{3,2},{4,7},{5,4},{6,5},{7,6},{8,11},{9,8},{10,9... | collective-permute-start | bytes 1572872 | tf_op jit(solution)/shard_map/ppermute | solution.py:448
  18.3 11.3 %shard_map.148 = (f32[32,4,8,256]{3,2,1,0:T(8,128)}, f32[32,4,8,256]{3,2,1,0:T(8,128)}, f32[32,4,8,256]{3,2,1,0:T(8,128)}) custom-call(f32[2,3,144,256]{3,2,1,0:T(8,128)} %shard_map.147.halo_ref, f32[32,4,8,256]{3,2,1,0:T(8,128)} %lp_mid.1, f32[4,8,256]{2,1,0:T(8,128)} %f0.3, f32[4,8,256]{2,1,0:T(8,128)} %f1.3, f32[4,8,256]{2,1,0:T(8,128)} %f2.3, ...), custom_call_target="tpu_custom_call" | custom-call | tf_op jit(solution)/shard_map/pallas_call | solution.py:275
  29.6 1.9 %fusion.12 = f32[32,256]{1,0:T(8,128)S(1)} fusion(f32[32,4,8,256]{3,2,1,0:T(8,128)} %get-tuple-element.23, pred[32,256]{1,0:T(8,128)(4,1)S(1)} %iota_compare_fusion.5, s32[256]{0:T(256)S(1)} %get-tuple-element.32), kind=kOutput, calls=%fused_computation.12 | convolution fusion | flops 805888000 | bytes 1090560 | tf_op jit(solution)/shard_map/dot_general | solution.py:402
  31.6 0.7 fusion.11
  32.9 0.6 fusion.18
  33.6 0.8 fusion.19
  34.3 0.8 reshape.95.part_ref
  35.2 28.0 %shard_map.149 = f32[32,32,128]{2,1,0:T(8,128)} custom-call(f32[32,8,128]{2,1,0:T(8,128)} %reshape.95.part_ref), custom_call_target="tpu_custom_call" | custom-call | tf_op jit(solution)/shard_map/pallas_call | solution.py:342
  63.2 1.3 %constant_dynamic-slice_fusion.4 = f32[1024,32]{1,0:T(8,128)S(1)} fusion(f32[1024,128]{1,0:T(8,128)} %bitcast.44, s32[]{:T(128)S(6)} %select_n.43), kind=kLoop, calls=%fused_computation.79 | loop fusion | bytes 262148 | tf_op jit(solution)/shard_map/dynamic_slice | solution.py:432
  64.6 0.2 reduce_sum.29
  65.0 1.6 %fusion.13 = f32[128,128]{1,0:T(8,128)S(1)} fusion(f32[32,32,128]{2,1,0:T(8,128)S(1)} %copy-done.3, f32[32,32]{1,0:T(8,128)S(1)} %div.56, f32[32,32]{1,0:T(8,128)S(1)} %broadcast_multiply_fusion), kind=kOutput, calls=%fused_computation.14 | convolution fusion | flops 201637888 | bytes 598016 | tf_op jit(solution)/shard_map/dot_general | solution.py:435
  66.7 11.7 %cholesky.17 = f32[128,128]{1,0:T(8,128)S(1)} custom-call(f32[128,128]{1,0:T(8,128)S(1)} %fusion.13), custom_call_target="Cholesky" | custom-call | tf_op jit(solution)/shard_map/cholesky | solution.py:101
  78.4 0.6 compare_reduce_fusion
  79.1 0.7 fusion.38
  79.7 9.8 %custom-call.7 = f32[1,128,128]{1,2,0:T(8,128)S(1)} custom-call(f32[1,128,128]{2,1,0:T(8,128)S(1)} %fusion.38), custom_call_target="InvertDiagBlocksLowerTriangular" | custom-call | tf_op jit(solution)/shard_map/triangular_solve | solution.py:105
  89.6 0.7 copy.32
  90.3 0.6 fusion.26
  91.1 0.2 convolution_convert_fusion
  91.6 0.9 fusion.8
  92.5 1.6 %copy.31 = f32[32,4,8,256]{3,2,1,0:T(8,128)} copy(f32[32,4,8,256]{3,0,2,1:T(8,128)S(1)} %fusion.8) | data formatting | bytes 2097152
  (35 shorter events, 0.8 us)
Async XLA Ops:
  0.6 32.3 %copy-start = (f32[1024]{0:T(1024)S(1)}, f32[1024]{0:T(1024)}, u32[]{:S(2)}) copy-start(f32[1024]{0:T(1024)} %param.17) | copy-start | bytes 12292
  0.6 12.0 %copy-start.1 = (f32[32,4,8,256]{3,2,1,0:T(8,128)S(1)}, f32[32,4,8,256]{3,2,1,0:T(8,128)}, u32[]{:S(2)}) copy-start(f32[32,4,8,256]{3,2,1,0:T(8,128)} %lp_mid.1) | copy-start | bytes 3145732
  13.3 78.2 %collective-permute-start = (bf16[4,8,32,256]{3,2,1,0:T(8,128)(2,1)S(1)}, bf16[4,8,32,256]{3,2,1,0:T(8,128)(2,1)S(1)}, u32[]{:S(2)}, u32[]{:S(2)}) collective-permute-start(bf16[4,8,32,256]{3,2,1,0:T(8,128)(2,1)S(1)} %fusion.21), channel_id=1, source_target_pairs={{0,1},{1,2},{2,3},{3,0},{4,5},{5,6},{6,7},{7,4},{8,9},{9,10},{10,1... | collective-permute-start | bytes 1572872 | tf_op jit(solution)/shard_map/ppermute | solution.py:448
  14.6 76.9 %collective-permute-start.1 = (bf16[4,8,32,256]{3,2,1,0:T(8,128)(2,1)S(1)}, bf16[4,8,32,256]{3,2,1,0:T(8,128)(2,1)S(1)}, u32[]{:S(2)}, u32[]{:S(2)}) collective-permute-start(bf16[4,8,32,256]{3,2,1,0:T(8,128)(2,1)S(1)} %fusion.21), channel_id=1, source_target_pairs={{0,2},{1,3},{2,0},{3,1},{4,6},{5,7},{6,4},{7,5},{8,10},{9,11},{10,... | collective-permute-start | bytes 1572872 | tf_op jit(solution)/shard_map/ppermute | solution.py:448
  17.2 74.2 %collective-permute-start.2 = (bf16[4,8,32,256]{3,2,1,0:T(8,128)(2,1)S(1)}, bf16[4,8,32,256]{3,2,1,0:T(8,128)(2,1)S(1)}, u32[]{:S(2)}, u32[]{:S(2)}) collective-permute-start(bf16[4,8,32,256]{3,2,1,0:T(8,128)(2,1)S(1)} %fusion.21), channel_id=1, source_target_pairs={{0,3},{1,0},{2,1},{3,2},{4,7},{5,4},{6,5},{7,6},{8,11},{9,8},{10,9... | collective-permute-start | bytes 1572872 | tf_op jit(solution)/shard_map/ppermute | solution.py:448
  18.3 11.3 %copy-start.7 = (s32[256]{0:T(256)S(1)}, s32[256]{0:T(256)}, u32[]{:S(2)}) copy-start(s32[256]{0:T(256)} %param.18) | copy-start | bytes 3076
  29.6 2.0 %copy-start.4 = (f32[32,4,8,256]{3,2,1,0:T(8,128)S(1)}, f32[32,4,8,256]{3,2,1,0:T(8,128)}, u32[]{:S(2)}) copy-start(f32[32,4,8,256]{3,2,1,0:T(8,128)} %get-tuple-element.10) | copy-start | bytes 3145732
  29.6 3.3 %copy-start.6 = (s32[256]{0:T(256)S(1)}, s32[256]{0:T(256)}, u32[]{:S(2)}) copy-start(s32[256]{0:T(256)} %param.19) | copy-start | bytes 3076
  63.2 1.5 %copy-start.3 = (f32[32,32,128]{2,1,0:T(8,128)S(1)}, f32[32,32,128]{2,1,0:T(8,128)}, u32[]{:S(2)}) copy-start(f32[32,32,128]{2,1,0:T(8,128)} %shard_map.149) | copy-start | bytes 1572868
  63.2 1.8 %copy-start.5 = (f32[1024]{0:T(1024)S(1)}, f32[1024]{0:T(1024)}, u32[]{:S(2)}) copy-start(f32[1024]{0:T(1024)} %param.22) | copy-start | bytes 12292
  65.0 25.3 %copy-start.8 = (f32[32,1024]{1,0:T(8,128)S(1)}, f32[32,1024]{1,0:T(8,128)}, u32[]{:S(2)}) copy-start(f32[32,1024]{1,0:T(8,128)} %param.23) | copy-start | bytes 393220
  65.0 25.3 %copy-start.9 = (f32[1024]{0:T(1024)S(1)}, f32[1024]{0:T(1024)}, u32[]{:S(2)}) copy-start(f32[1024]{0:T(1024)} %param.21) | copy-start | bytes 12292
  90.3 1.2 %copy-start.2 = (f32[32,4,8,256]{3,2,1,0:T(8,128)S(1)}, f32[32,4,8,256]{3,2,1,0:T(8,128)}, u32[]{:S(2)}) copy-start(f32[32,4,8,256]{3,2,1,0:T(8,128)} %lp_mid.1) | copy-start | bytes 3145732

commit v23 on v22

--- a/solution.py
+++ b/solution.py
@@ -384,7 +384,6 @@
     fields = (start_pressure, start_sat, source, storage)
 
     incoming = halo_exchange(log_perm, fields, rim)
-    incoming, log_perm_after = lax.optimization_barrier((incoming, log_perm))
     halo = incoming
     column = tile_rank * strip_width - rim + jnp.arange(strip_width + 2 * rim, dtype=jnp.int32)
     inside = ((column >= 0) & (column < strip_width * tile_count)).astype(jnp.float32)
@@ -441,7 +440,7 @@
         preferred_element_type=jnp.float32,
     )
     weights_low = solve_spd(gram_matrix, cross_matrix).astype(jnp.bfloat16)
-    anomaly = (log_perm_after / member_root).astype(jnp.bfloat16).transpose(1, 2, 0, 3)
+    anomaly = (log_perm / member_root).astype(jnp.bfloat16).transpose(1, 2, 0, 3)
     anomaly_parts = [anomaly]
     for shift in range(1, member_count):
         pairs = [(i, (i + shift) % member_count) for i in range(member_count)]

time: 94.4 us -> 95.5 us (1.012)
  other arithmetic: 23.7 us -> 24.9 us
  Pallas kernels: 51.2 us -> 50.2 us
    transpose x1, other arithmetic: 0.62 us -> 1.84 us  [per_device(): (log_perm / member_root).astype(jnp.bfloat16).transpose(1, 2, 0, 3)]
    unnamed x23 -> x21, local copies, waits for them, and re-layouts: 2.54 us -> 2.54 us
  transfers between devices with their start and end apart: 3 -> 3, of which waited for: 0 -> 0; matrix products, arithmetic and copies ran while one was open for 35% -> 35% of each run, Pallas kernels for 42% -> 53%
where the time goes in v23:
time: 95.5 us; the launch traced here: 95.1 us
  Pallas kernels  50.2 us (53%)
  other arithmetic  24.9 us (26%)
  matrix products  7.58 us (8%)
  starting transfers between devices  5.88 us (6%)
  local copies, waits for them, and re-layouts  4.99 us (5%)
  between operations  1.52 us (2%)
    pallas_call x1, Pallas kernels, rates_exchange(): pl.pallas_call(functools.partial(exchange_kernel, member_count), out_shap...  27.1 us
    another operation x3, other arithmetic, solve_spd(): lax.linalg.cholesky(gram_matrix + jnp.eye(gram_matrix.shape[0], dtype=jnp...  12.4 us
    pallas_call x1, Pallas kernels, halo_exchange(): pl.pallas_call(functools.partial(halo_kernel, rim), out_shape=jax.ShapeDt...  11.8 us
    pallas_call x1, Pallas kernels, stencil(): pl.pallas_call(functools.partial(stencil_kernel, rim), grid=(members // b...  11.3 us
    another operation x2, other arithmetic, solve_spd(): lax.linalg.triangular_solve(factor, halfway, left_side=True, lower=True,...  10.5 us
    ppermute x3, starting transfers between devices, per_device(): anomaly_parts.append(lax.ppermute(anomaly, 'member', pairs))  5.88 us
    dot_general x2, matrix products, pick_cells(): jnp.dot(values_in.reshape(local_count * plane_rows, strip_depth), col_pic...  2.6 us
    unnamed x21, local copies, waits for them, and re-layouts  2.54 us
  transfers between devices with their start and end apart: 3, of which 0 were waited for; matrix products, arithmetic and copies ran while one was open for 35% of the time, Pallas kernels for 53%

profile of v23, /device:TPU:1, one launch (start us, length us, event | category | flops | bytes accessed | tf_op | source)
XLA Modules:
  0.0 95.1 jit_solution(7303107355744844611)
XLA Ops:
  0.6 1.8 %fusion.20 = bf16[4,8,32,256]{3,2,1,0:T(8,128)(2,1)S(1)} fusion(f32[32,4,8,256]{3,2,1,0:T(8,128)} %lp_mid.1), kind=kLoop, calls=%fused_computation.23 | loop fusion | flops 524288 | bytes 1572864 | tf_op jit(solution)/shard_map/transpose | solution.py:443
  2.5 2.2 %collective-permute-start = (bf16[4,8,32,256]{3,2,1,0:T(8,128)(2,1)S(1)}, bf16[4,8,32,256]{3,2,1,0:T(8,128)(2,1)S(1)}, u32[]{:S(2)}, u32[]{:S(2)}) collective-permute-start(bf16[4,8,32,256]{3,2,1,0:T(8,128)(2,1)S(1)} %fusion.20), channel_id=1, source_target_pairs={{0,1},{1,2},{2,3},{3,0},{4,5},{5,6},{6,7},{7,4},{8,9},{9,10},{10,1... | collective-permute-start | bytes 1572872 | tf_op jit(solution)/shard_map/ppermute | solution.py:447
  4.7 2.6 %collective-permute-start.1 = (bf16[4,8,32,256]{3,2,1,0:T(8,128)(2,1)S(1)}, bf16[4,8,32,256]{3,2,1,0:T(8,128)(2,1)S(1)}, u32[]{:S(2)}, u32[]{:S(2)}) collective-permute-start(bf16[4,8,32,256]{3,2,1,0:T(8,128)(2,1)S(1)} %fusion.20), channel_id=1, source_target_pairs={{0,2},{1,3},{2,0},{3,1},{4,6},{5,7},{6,4},{7,5},{8,10},{9,11},{10,... | collective-permute-start | bytes 1572872 | tf_op jit(solution)/shard_map/ppermute | solution.py:447
  7.3 1.1 %collective-permute-start.2 = (bf16[4,8,32,256]{3,2,1,0:T(8,128)(2,1)S(1)}, bf16[4,8,32,256]{3,2,1,0:T(8,128)(2,1)S(1)}, u32[]{:S(2)}, u32[]{:S(2)}) collective-permute-start(bf16[4,8,32,256]{3,2,1,0:T(8,128)(2,1)S(1)} %fusion.20), channel_id=1, source_target_pairs={{0,3},{1,0},{2,1},{3,2},{4,7},{5,4},{6,5},{7,6},{8,11},{9,8},{10,9... | collective-permute-start | bytes 1572872 | tf_op jit(solution)/shard_map/ppermute | solution.py:447
  8.4 11.8 %shard_map.147.halo_ref = f32[2,3,144,256]{3,2,1,0:T(8,128)} custom-call(f32[32,4,8,256]{3,2,1,0:T(8,128)} %lp_mid.1, f32[4,8,256]{2,1,0:T(8,128)} %f0.3, f32[4,8,256]{2,1,0:T(8,128)} %f1.3, f32[4,8,256]{2,1,0:T(8,128)} %f2.3, f32[4,8,256]{2,1,0:T(8,128)} %f3.3), custom_call_target="tpu_custom_call" | custom-call | tf_op jit(solution)/shard_map/pallas_call | solution.py:325
  20.2 11.3 %shard_map.148 = (f32[32,4,8,256]{3,2,1,0:T(8,128)}, f32[32,4,8,256]{3,2,1,0:T(8,128)}, f32[32,4,8,256]{3,2,1,0:T(8,128)}) custom-call(f32[2,3,144,256]{3,2,1,0:T(8,128)} %shard_map.147.halo_ref, f32[32,4,8,256]{3,2,1,0:T(8,128)} %lp_mid.1, f32[4,8,256]{2,1,0:T(8,128)} %f0.3, f32[4,8,256]{2,1,0:T(8,128)} %f1.3, f32[4,8,256]{2,1,0:T(8,128)} %f2.3, ...), custom_call_target="tpu_custom_call" | custom-call | tf_op jit(solution)/shard_map/pallas_call | solution.py:275
  31.6 1.9 %fusion.12 = f32[32,256]{1,0:T(8,128)S(1)} fusion(f32[32,4,8,256]{3,2,1,0:T(8,128)} %get-tuple-element.19, pred[32,256]{1,0:T(8,128)(4,1)S(1)} %iota_compare_fusion.5, s32[256]{0:T(256)S(1)} %get-tuple-element.28), kind=kOutput, calls=%fused_computation.12 | convolution fusion | flops 805888000 | bytes 1090560 | tf_op jit(solution)/shard_map/dot_general | solution.py:401
  33.5 0.7 fusion.11
  34.9 0.6 fusion.17
  35.5 0.8 fusion.18
  36.3 0.8 reshape.95.part_ref
  37.1 27.1 %shard_map.149 = f32[32,32,128]{2,1,0:T(8,128)} custom-call(f32[32,8,128]{2,1,0:T(8,128)} %reshape.95.part_ref), custom_call_target="tpu_custom_call" | custom-call | tf_op jit(solution)/shard_map/pallas_call | solution.py:342
  64.2 1.3 %constant_dynamic-slice_fusion.4 = f32[1024,32]{1,0:T(8,128)S(1)} fusion(f32[1024,128]{1,0:T(8,128)} %bitcast.44, s32[]{:T(128)S(6)} %select_n.43), kind=kLoop, calls=%fused_computation.78 | loop fusion | bytes 262148 | tf_op jit(solution)/shard_map/dynamic_slice | solution.py:431
  65.7 0.2 reduce_sum.29
  66.1 1.6 %fusion.13 = f32[128,128]{1,0:T(8,128)S(1)} fusion(f32[32,32,128]{2,1,0:T(8,128)S(1)} %copy-done.2, f32[32,32]{1,0:T(8,128)S(1)} %div.56, f32[32,32]{1,0:T(8,128)S(1)} %broadcast_multiply_fusion), kind=kOutput, calls=%fused_computation.14 | convolution fusion | flops 201637888 | bytes 598016 | tf_op jit(solution)/shard_map/dot_general | solution.py:434
  67.8 11.7 %cholesky.17 = f32[128,128]{1,0:T(8,128)S(1)} custom-call(f32[128,128]{1,0:T(8,128)S(1)} %fusion.13), custom_call_target="Cholesky" | custom-call | tf_op jit(solution)/shard_map/cholesky | solution.py:101
  79.5 0.6 compare_reduce_fusion
  80.1 0.7 fusion.37
  80.8 9.8 %custom-call.7 = f32[1,128,128]{1,2,0:T(8,128)S(1)} custom-call(f32[1,128,128]{2,1,0:T(8,128)S(1)} %fusion.37), custom_call_target="InvertDiagBlocksLowerTriangular" | custom-call | tf_op jit(solution)/shard_map/triangular_solve | solution.py:105
  90.7 0.7 copy.32
  91.4 0.6 fusion.25
  92.2 0.2 convolution_convert_fusion
  92.6 0.9 fusion.8
  93.6 1.6 %copy.31 = f32[32,4,8,256]{3,2,1,0:T(8,128)} copy(f32[32,4,8,256]{3,0,2,1:T(8,128)S(1)} %fusion.8) | data formatting | bytes 2097152
  (33 shorter events, 0.8 us)
Async XLA Ops:
  0.6 34.2 %copy-start = (f32[1024]{0:T(1024)S(1)}, f32[1024]{0:T(1024)}, u32[]{:S(2)}) copy-start(f32[1024]{0:T(1024)} %param.17) | copy-start | bytes 12292
  2.5 90.1 %collective-permute-start = (bf16[4,8,32,256]{3,2,1,0:T(8,128)(2,1)S(1)}, bf16[4,8,32,256]{3,2,1,0:T(8,128)(2,1)S(1)}, u32[]{:S(2)}, u32[]{:S(2)}) collective-permute-start(bf16[4,8,32,256]{3,2,1,0:T(8,128)(2,1)S(1)} %fusion.20), channel_id=1, source_target_pairs={{0,1},{1,2},{2,3},{3,0},{4,5},{5,6},{6,7},{7,4},{8,9},{9,10},{10,1... | collective-permute-start | bytes 1572872 | tf_op jit(solution)/shard_map/ppermute | solution.py:447
  4.7 87.9 %collective-permute-start.1 = (bf16[4,8,32,256]{3,2,1,0:T(8,128)(2,1)S(1)}, bf16[4,8,32,256]{3,2,1,0:T(8,128)(2,1)S(1)}, u32[]{:S(2)}, u32[]{:S(2)}) collective-permute-start(bf16[4,8,32,256]{3,2,1,0:T(8,128)(2,1)S(1)} %fusion.20), channel_id=1, source_target_pairs={{0,2},{1,3},{2,0},{3,1},{4,6},{5,7},{6,4},{7,5},{8,10},{9,11},{10,... | collective-permute-start | bytes 1572872 | tf_op jit(solution)/shard_map/ppermute | solution.py:447
  7.3 85.3 %collective-permute-start.2 = (bf16[4,8,32,256]{3,2,1,0:T(8,128)(2,1)S(1)}, bf16[4,8,32,256]{3,2,1,0:T(8,128)(2,1)S(1)}, u32[]{:S(2)}, u32[]{:S(2)}) collective-permute-start(bf16[4,8,32,256]{3,2,1,0:T(8,128)(2,1)S(1)} %fusion.20), channel_id=1, source_target_pairs={{0,3},{1,0},{2,1},{3,2},{4,7},{5,4},{6,5},{7,6},{8,11},{9,8},{10,9... | collective-permute-start | bytes 1572872 | tf_op jit(solution)/shard_map/ppermute | solution.py:447
  20.2 11.3 %copy-start.6 = (s32[256]{0:T(256)S(1)}, s32[256]{0:T(256)}, u32[]{:S(2)}) copy-start(s32[256]{0:T(256)} %param.18) | copy-start | bytes 3076
  31.5 2.0 %copy-start.3 = (f32[32,4,8,256]{3,2,1,0:T(8,128)S(1)}, f32[32,4,8,256]{3,2,1,0:T(8,128)}, u32[]{:S(2)}) copy-start(f32[32,4,8,256]{3,2,1,0:T(8,128)} %get-tuple-element.7) | copy-start | bytes 3145732
  31.5 3.3 %copy-start.5 = (s32[256]{0:T(256)S(1)}, s32[256]{0:T(256)}, u32[]{:S(2)}) copy-start(s32[256]{0:T(256)} %param.19) | copy-start | bytes 3076
  64.2 1.5 %copy-start.2 = (f32[32,32,128]{2,1,0:T(8,128)S(1)}, f32[32,32,128]{2,1,0:T(8,128)}, u32[]{:S(2)}) copy-start(f32[32,32,128]{2,1,0:T(8,128)} %shard_map.149) | copy-start | bytes 1572868
  64.2 1.8 %copy-start.4 = (f32[1024]{0:T(1024)S(1)}, f32[1024]{0:T(1024)}, u32[]{:S(2)}) copy-start(f32[1024]{0:T(1024)} %param.22) | copy-start | bytes 12292
  66.1 25.3 %copy-start.7 = (f32[32,1024]{1,0:T(8,128)S(1)}, f32[32,1024]{1,0:T(8,128)}, u32[]{:S(2)}) copy-start(f32[32,1024]{1,0:T(8,128)} %param.23) | copy-start | bytes 393220
  66.1 25.3 %copy-start.8 = (f32[1024]{0:T(1024)S(1)}, f32[1024]{0:T(1024)}, u32[]{:S(2)}) copy-start(f32[1024]{0:T(1024)} %param.21) | copy-start | bytes 12292
  91.4 1.2 %copy-start.1 = (f32[32,4,8,256]{3,2,1,0:T(8,128)S(1)}, f32[32,4,8,256]{3,2,1,0:T(8,128)}, u32[]{:S(2)}) copy-start(f32[32,4,8,256]{3,2,1,0:T(8,128)} %lp_mid.1) | copy-start | bytes 3145732
